TPU v7x, 32 devices: a whole 2x2x4 slice. The times are simulated.
32 devices in a mesh: fsdp: 8 (over z, x), seq: 4 (over y, core).
Axes of the slice: x: 2, y: 2, z: 4, core: 2. Of those that a mesh axis runs over, the one named last changes fastest.
Arguments:
- block_input: bfloat16 [8, 1024, 2048], P('fsdp', 'seq'), may hold values from -6 to 6
- cotangent: bfloat16 [8, 1024, 2048], P('fsdp', 'seq'), may hold values from -6 to 6
- item_starts: int32 [8, 3], P('fsdp'), may hold values from 0 to 960, as said below
- item_lengths: int32 [8, 3], P('fsdp'), may hold values from 64 to 768, as said below
- pad_mask: int32 [8, 1024], P('fsdp'), may hold values 0 or 1
- ln1_gain: float32 [2048], P('fsdp'), may hold values from 0.5 to 1.5
- ln1_shift: float32 [2048], P('fsdp'), may hold values from -3 to 3
- w_qkv: bfloat16 [2048, 6144], P('fsdp'), may hold values from -0.125 to 0.125
- w_out: bfloat16 [2048, 2048], P('fsdp'), may hold values from -0.5 to 0.5
- ln2_gain: float32 [2048], P('fsdp'), may hold values from 0.5 to 1.5
- ln2_shift: float32 [2048], P('fsdp'), may hold values from -3 to 3
- w_up: bfloat16 [2048, 8192], P('fsdp'), may hold values from -0.125 to 0.125
- up_bias: float32 [8192], P('fsdp'), may hold values from -3 to 3
- w_down: bfloat16 [8192, 2048], P('fsdp'), may hold values from -0.0625 to 0.0625
- down_bias: float32 [2048], P('fsdp'), may hold values from -3 to 3
Outputs:
- block_output: bfloat16 [8, 1024, 2048], P('fsdp', 'seq')
- input_grad: float32 [8, 1024, 2048], P('fsdp', 'seq')
- ln1_gain_grad: float32 [2048], P('fsdp')
- ln1_shift_grad: float32 [2048], P('fsdp')
- w_qkv_grad: float32 [2048, 6144], P('fsdp')
- w_out_grad: float32 [2048, 2048], P('fsdp')
- ln2_gain_grad: float32 [2048], P('fsdp')
- ln2_shift_grad: float32 [2048], P('fsdp')
- w_up_grad: float32 [2048, 8192], P('fsdp')
- up_bias_grad: float32 [8192], P('fsdp')
- w_down_grad: float32 [8192, 2048], P('fsdp')
- down_bias_grad: float32 [2048], P('fsdp')
Inputs may be any that keep to these rules, and one draw needn't show every extreme that they name: `item_starts`: each row holds three items that lie in order inside its 1024 positions without intersection, each starting no earlier than the end of the one before; positions between or after them belong to no item. `item_lengths`: each item has at least 64 positions, the three of a row at most 1024 together.
All inputs are finite; a program needn't handle non-finite values. No bound on the sum of `pad_mask` on one device may be relied on, other than what follows from the above.
Results may differ from a plain program's by a relative error of at most 0.0095.
Values may be sent and summed in bfloat16 or wider, within the bound.
No kernel may reach another device: no remote copies, remote signals or barrier semaphores. Data moves between devices by JAX's collectives and lax.ppermute only.
A program may use at most 512 MiB of HBM per device.

v0:
```python
import jax
import jax.numpy as jnp
from jax import lax
from jax.sharding import PartitionSpec as P

H = 16
HD = 128


EPSILON = 1e-05
MASKED = -1e30


def layer_norm(values, gain_vec, shift_vec):
    center = values - jnp.mean(values, axis=-1, keepdims=True)
    spread = jnp.mean(center * center, axis=-1, keepdims=True)
    return center * lax.rsqrt(spread + EPSILON) * gain_vec + shift_vec


def contract_rows(left, right):
    return lax.dot_general(
        left, right, (((0,), (0,)), ((), ())), preferred_element_type=jnp.float32
    )


def times_transpose(left, right):
    return lax.dot_general(
        left, right, (((1,), (1,)), ((), ())), preferred_element_type=jnp.float32
    )


def item_numbers(starts, lengths, positions):
    inside = (positions[None, :] >= starts[:, None]) & (
        positions[None, :] < (starts + lengths)[:, None]
    )
    labels = jnp.arange(1, starts.shape[0] + 1, dtype=jnp.int32)
    return jnp.sum(jnp.where(inside, labels[:, None], 0), axis=0) - 1


def visible_mask(query_pos, key_pos, query_item, key_item, key_pad):
    same_item = (query_item[:, None] == key_item[None, :]) & (query_item[:, None] >= 0)
    before = key_pos[None, :] < query_pos[:, None]
    return same_item & before & (key_pad[None, :] == 1) | (key_pos[None, :] == query_pos[:, None])


def masked_scores(query_rows, key_rows, visible, score_scale):
    scores = (
        jnp.einsum("qhd,khd->hqk", query_rows, key_rows, preferred_element_type=jnp.float32)
        * score_scale
    )
    return jnp.where(visible[None], scores, MASKED)


def attend_rows(query_rows, key_rows, value_rows, visible, score_scale):
    scores = masked_scores(query_rows, key_rows, visible, score_scale)
    row_peak = jnp.max(scores, axis=-1, keepdims=True)
    exp_scores = jnp.exp(scores - row_peak)
    row_total = jnp.sum(exp_scores, axis=-1, keepdims=True)
    attn_probs = exp_scores / row_total
    mixed_rows = jnp.einsum(
        "hqk,khd->qhd",
        attn_probs.astype(jnp.bfloat16),
        value_rows,
        preferred_element_type=jnp.float32,
    )
    return (mixed_rows, row_peak + jnp.log(row_total))


def attend_back(query_rows, key_rows, value_rows, visible, log_total, mixed_grad, score_scale):
    scores = masked_scores(query_rows, key_rows, visible, score_scale)
    attn_probs = jnp.exp(scores - log_total)
    prob_grad = jnp.einsum(
        "qhd,khd->hqk", mixed_grad, value_rows, preferred_element_type=jnp.float32
    )
    value_part = jnp.einsum(
        "hqk,qhd->khd",
        attn_probs.astype(jnp.bfloat16),
        mixed_grad,
        preferred_element_type=jnp.float32,
    )
    inner_sum = jnp.sum(prob_grad * attn_probs, axis=-1, keepdims=True)
    score_grad = (attn_probs * (prob_grad - inner_sum)).astype(jnp.bfloat16)
    query_grad = (
        jnp.einsum("hqk,khd->qhd", score_grad, key_rows, preferred_element_type=jnp.float32)
        * score_scale
    )
    key_part = (
        jnp.einsum("hqk,qhd->khd", score_grad, query_rows, preferred_element_type=jnp.float32)
        * score_scale
    )
    return (query_grad.astype(jnp.bfloat16), key_part, value_part)


def shards(
    block_input,
    cotangent,
    item_starts,
    item_lengths,
    pad_mask,
    ln1_gain,
    ln1_shift,
    w_qkv,
    w_out,
    ln2_gain,
    ln2_shift,
    w_up,
    up_bias,
    w_down,
    down_bias,
):
    rows_here, tok_count, model_width = block_input.shape
    seq_count = lax.axis_size("seq")
    shard_count = lax.axis_size("fsdp")
    length = tok_count * seq_count
    score_scale = HD ** (-0.5)
    piece_d = ln1_gain.shape[0]
    seq_first = lax.axis_index("seq") * tok_count
    packed = jnp.concatenate([ln1_gain, ln1_shift, ln2_gain, ln2_shift, down_bias, up_bias])
    vector_table = lax.all_gather(packed, "fsdp", axis=0, tiled=True).reshape(shard_count, -1)

    def vector_part(slot):
        return vector_table[:, slot * piece_d : (slot + 1) * piece_d].reshape(-1)

    gain_one, shift_one, gain_two, shift_two, bias_down = [vector_part(slot) for slot in range(5)]
    bias_up = vector_table[:, 5 * piece_d :].reshape(-1)
    qkv_full, out_full = (
        lax.all_gather(w_qkv, "fsdp", axis=0, tiled=True),
        lax.all_gather(w_out, "fsdp", axis=0, tiled=True),
    )
    inputs = block_input.reshape(rows_here * tok_count, model_width).astype(jnp.float32)
    normed_one = layer_norm(inputs, gain_one, shift_one).astype(jnp.bfloat16)
    projected = jnp.dot(normed_one, qkv_full, preferred_element_type=jnp.float32).astype(
        jnp.bfloat16
    )
    query_all = projected[:, :model_width].reshape(rows_here, tok_count, H, HD)
    kv_local = projected[:, model_width:].reshape(rows_here, tok_count, 2 * model_width)
    kv_whole = lax.all_gather(kv_local, "seq", axis=1, tiled=True)
    key_all = kv_whole[:, :, :model_width].reshape(rows_here, length, H, HD)
    value_all = kv_whole[:, :, model_width:].reshape(rows_here, length, H, HD)
    positions = jnp.arange(length, dtype=jnp.int32)
    query_pos = seq_first + jnp.arange(tok_count, dtype=jnp.int32)
    row_index = 0
    item_label = item_numbers(item_starts[row_index], item_lengths[row_index], positions)
    query_item = lax.dynamic_slice_in_dim(item_label, seq_first, tok_count)
    visible = visible_mask(query_pos, positions, query_item, item_label, pad_mask[row_index])
    mixed_part, log_total = attend_rows(
        query_all[row_index], key_all[row_index], value_all[row_index], visible, score_scale
    )
    visible_list = [visible]
    mixed_list = [mixed_part]
    logsum_list = [log_total]
    mixed_all = (
        jnp.stack(mixed_list).reshape(rows_here * tok_count, model_width).astype(jnp.bfloat16)
    )
    residual_one = inputs + jnp.dot(mixed_all, out_full, preferred_element_type=jnp.float32)
    up_full, down_full = (
        lax.all_gather(w_up, "fsdp", axis=0, tiled=True),
        lax.all_gather(w_down, "fsdp", axis=0, tiled=True),
    )
    normed_two = layer_norm(residual_one, gain_two, shift_two).astype(jnp.bfloat16)
    hidden_pre = jnp.dot(normed_two, up_full, preferred_element_type=jnp.float32) + bias_up
    activated = jax.nn.gelu(hidden_pre).astype(jnp.bfloat16)
    block_output = (
        residual_one + jnp.dot(activated, down_full, preferred_element_type=jnp.float32) + bias_down
    )
    output_shard = block_output.astype(jnp.bfloat16).reshape(rows_here, tok_count, model_width)
    up_full, down_full = (
        lax.all_gather(w_up, "fsdp", axis=0, tiled=True),
        lax.all_gather(w_down, "fsdp", axis=0, tiled=True),
    )
    cot_flat = cotangent.reshape(rows_here * tok_count, model_width)
    cot_wide = cot_flat.astype(jnp.float32)
    down_grad = contract_rows(activated, cot_flat)
    down_bias_part = jnp.sum(cot_wide, axis=0)
    act_grad = times_transpose(cot_flat, down_full)
    gelu_back = jax.vjp(jax.nn.gelu, hidden_pre)[1]
    hidden_grad = gelu_back(act_grad)[0].astype(jnp.bfloat16)
    up_grad = contract_rows(normed_two, hidden_grad)
    up_bias_part = jnp.sum(hidden_grad.astype(jnp.float32), axis=0)
    norm_two_grad = times_transpose(hidden_grad, up_full)
    norm_two_back = jax.vjp(layer_norm, residual_one, gain_two, shift_two)[1]
    resid_part, gain_two_grad, shift_two_grad = norm_two_back(norm_two_grad)
    residual_grad = cot_wide + resid_part
    up_sum, down_sum = (
        lax.psum_scatter(up_grad, "fsdp", scatter_dimension=0, tiled=True),
        lax.psum_scatter(down_grad, "fsdp", scatter_dimension=0, tiled=True),
    )
    qkv_full, out_full = (
        lax.all_gather(w_qkv, "fsdp", axis=0, tiled=True),
        lax.all_gather(w_out, "fsdp", axis=0, tiled=True),
    )
    branch_grad = residual_grad.astype(jnp.bfloat16)
    out_grad = contract_rows(mixed_all, branch_grad)
    mixed_grad = (
        times_transpose(branch_grad, out_full)
        .astype(jnp.bfloat16)
        .reshape(rows_here, tok_count, H, HD)
    )
    row_index = 0
    query_grad, key_part, value_part = attend_back(
        query_all[row_index],
        key_all[row_index],
        value_all[row_index],
        visible_list[row_index],
        logsum_list[row_index],
        mixed_grad[row_index],
        score_scale,
    )
    query_list = [query_grad.reshape(tok_count, model_width)]
    kv_list = [
        jnp.concatenate(
            [key_part.reshape(length, model_width), value_part.reshape(length, model_width)], axis=1
        )
    ]
    kv_terms = jnp.stack(kv_list)
    kv_grad = lax.psum_scatter(kv_terms, "seq", scatter_dimension=1, tiled=True).astype(
        jnp.bfloat16
    )
    proj_grad = jnp.concatenate(
        [
            jnp.stack(query_list).reshape(rows_here * tok_count, model_width),
            kv_grad.reshape(rows_here * tok_count, 2 * model_width),
        ],
        axis=1,
    )
    qkv_grad = contract_rows(normed_one, proj_grad)
    norm_one_grad = times_transpose(proj_grad, qkv_full)
    norm_one_back = jax.vjp(layer_norm, inputs, gain_one, shift_one)[1]
    input_part, gain_one_grad, shift_one_grad = norm_one_back(norm_one_grad)
    input_grad = (residual_grad + input_part).reshape(rows_here, tok_count, model_width)
    vector_grad = jnp.concatenate(
        [
            piece_grad.reshape(shard_count, -1)
            for piece_grad in (
                gain_one_grad,
                shift_one_grad,
                gain_two_grad,
                shift_two_grad,
                down_bias_part,
                up_bias_part,
            )
        ],
        axis=1,
    ).reshape(-1)
    qkv_sum, out_sum, vector_sum = (
        lax.psum_scatter(qkv_grad, "fsdp", scatter_dimension=0, tiled=True),
        lax.psum_scatter(out_grad, "fsdp", scatter_dimension=0, tiled=True),
        lax.psum_scatter(vector_grad, "fsdp", scatter_dimension=0, tiled=True),
    )
    up_total, down_total, qkv_total, out_total, vector_total = lax.psum(
        (up_sum, down_sum, qkv_sum, out_sum, vector_sum), "seq"
    )
    gain_one_out = vector_total[0:piece_d]
    shift_one_out = vector_total[piece_d : 2 * piece_d]
    gain_two_out = vector_total[2 * piece_d : 3 * piece_d]
    shift_two_out = vector_total[3 * piece_d : 4 * piece_d]
    down_bias_out = vector_total[4 * piece_d : 5 * piece_d]
    up_bias_out = vector_total[5 * piece_d :]
    return (
        output_shard,
        input_grad,
        gain_one_out,
        shift_one_out,
        qkv_total,
        out_total,
        gain_two_out,
        shift_two_out,
        up_total,
        up_bias_out,
        down_total,
        down_bias_out,
    )


def solution(mesh):
    placed = (
        P("fsdp", "seq", None),
        P("fsdp", "seq", None),
        P("fsdp", None),
        P("fsdp", None),
        P("fsdp", None),
        P("fsdp"),
        P("fsdp"),
        P("fsdp", None),
        P("fsdp", None),
        P("fsdp"),
        P("fsdp"),
        P("fsdp", None),
        P("fsdp"),
        P("fsdp", None),
        P("fsdp"),
    )
    return jax.shard_map(
        shards,
        mesh=mesh,
        in_specs=placed,
        out_specs=(
            P("fsdp", "seq", None),
            P("fsdp", "seq", None),
            P("fsdp"),
            P("fsdp"),
            P("fsdp", None),
            P("fsdp", None),
            P("fsdp"),
            P("fsdp"),
            P("fsdp", None),
            P("fsdp"),
            P("fsdp", None),
            P("fsdp"),
        ),
        check_vma=False,
    )
```

profile of v0, /device:TPU:0, one launch (start us, length us, event | category | flops | bytes accessed | tf_op | source)
XLA Modules:
  0.0 5920.8 jit_solution(13921106561028544226)
XLA Ops:
  12.1 67.2 %all-gather.1 = f32[8,1,2304]{2,1,0:T(1,128)S(1)} all-gather(f32[1,1,2304]{2,1,0:T(1,128)S(1)} %reshape.286), channel_id=1, replica_groups=mesh['fsdp'=8,'seq'=4] {'fsdp'}, dimensions={0}, use_global_device_ids=true | all-gather | bytes 82944 | tf_op jit(solution)/shard_map/all_gather | solution.py:119
  80.7 413.3 %all-gather.8.cloned.1.call-done = bf16[2048,6144]{1,0:T(8,128)(2,1)} async-done(((bf16[256,6144]{1,0:T(8,128)(2,1)}), bf16[2048,6144]{1,0:T(8,128)(2,1)}) %all-gather.8.cloned.1.call-update) | async-done | bytes 25165840 | tf_op jit(solution)/shard_map/all_gather | solution.py:127
  494.0 11.8 convolution_convert_fusion
  512.5 54.8 all-gather.16.cloned.1.call-done
  595.0 9.5 fusion.34
  604.6 89.8 %all-gather.10.cloned.1.call-done = bf16[2048,2048]{1,0:T(8,128)(2,1)} async-done(((bf16[256,2048]{1,0:T(8,128)(2,1)}), bf16[2048,2048]{1,0:T(8,128)(2,1)}) %all-gather.10.cloned.1.call-update) | async-done | bytes 8388624 | tf_op jit(solution)/shard_map/all_gather | solution.py:128
  701.0 630.8 %all-gather.12.cloned.1.call-done = bf16[2048,8192]{1,0:T(8,128)(2,1)} async-done(((bf16[256,8192]{1,0:T(8,128)(2,1)}), bf16[2048,8192]{1,0:T(8,128)(2,1)}) %all-gather.12.cloned.1.call-update) | async-done | bytes 33554448 | tf_op jit(solution)/shard_map/all_gather | solution.py:157
  1331.8 19.1 convolution_add_fusion
  1350.8 620.0 %all-gather.14.cloned.1.call-done = bf16[8192,2048]{1,0:T(8,128)(2,1)} async-done(((bf16[1024,2048]{1,0:T(8,128)(2,1)}), bf16[8192,2048]{1,0:T(8,128)(2,1)}) %all-gather.14.cloned.1.call-update) | async-done | bytes 33554448 | tf_op jit(solution)/shard_map/all_gather | solution.py:158
  1970.9 21.4 convert_reduce_fusion
  1992.3 18.6 multiply_reduce_fusion.1
  2015.8 6.7 convolution_convert_fusion.1
  2025.0 9.4 fusion.9
  2034.4 15.4 multiply_reduce_fusion
  2049.7 11.9 multiply_convert_fusion
  2064.9 6.7 maximum_bitcast_fusion
  2072.8 12.7 fusion.61
  2087.1 30.4 fusion.38
  2118.2 26.7 fusion.55
  2145.0 8.8 multiply_convert_fusion.2
  2153.8 44.1 reduce-scatter.6.cloned.1.call-done
  2201.7 22.4 fusion.32
  2224.9 13.9 fusion.56
  2247.5 237.0 %reduce-scatter.10.cloned.1.call-done = f32[256,2048]{1,0:T(8,128)} async-done(((f32[2048,2048]{1,0:T(8,128)}), f32[256,2048]{1,0:T(8,128)}) %reduce-scatter.10.cloned.1.call-update) | async-done | bytes 2097168 | tf_op jit(solution)/shard_map/reduce_scatter | solution.py:247
  2484.5 1059.0 %reduce-scatter.14.cloned.1.call-done = f32[1024,2048]{1,0:T(8,128)} async-done(((f32[8192,2048]{1,0:T(8,128)}), f32[1024,2048]{1,0:T(8,128)}) %reduce-scatter.14.cloned.1.call-update) | async-done | bytes 8388624 | tf_op jit(solution)/shard_map/reduce_scatter | solution.py:186
  3543.5 1059.2 %reduce-scatter.12.cloned.1.call-done = f32[256,8192]{1,0:T(8,128)} async-done(((f32[2048,8192]{1,0:T(8,128)}), f32[256,8192]{1,0:T(8,128)}) %reduce-scatter.12.cloned.1.call-update) | async-done | bytes 8388624 | tf_op jit(solution)/shard_map/reduce_scatter | solution.py:185
  4602.7 793.1 %reduce-scatter.8.cloned.1.call-done = f32[256,6144]{1,0:T(8,128)} async-done(((f32[2048,6144]{1,0:T(8,128)}), f32[256,6144]{1,0:T(8,128)}) %reduce-scatter.8.cloned.1.call-update) | async-done | bytes 6291472 | tf_op jit(solution)/shard_map/reduce_scatter | solution.py:246
  5397.8 19.6 fusion.24
  5417.4 50.6 all-reduce.5.cloned.1.call-done
  5468.8 10.1 psum.35
  5480.1 415.9 %all-reduce.7.cloned.1.call-done = (f32[256,6144]{1,0:T(8,128)}, f32[256,2048]{1,0:T(8,128)}, f32[256,8192]{1,0:T(8,128)}, f32[1024,2048]{1,0:T(8,128)}) async-done(((f32[256,6144]{1,0:T(8,128)}, f32[256,2048]{1,0:T(8,128)}, f32[256,8192]{1,0:T(8,128)}, f32[1024,2048]{1,0:T(8,128)}), (f32[256,6144]{1,0:T(8,128)}, f32[256,2048]{1,0:T(8,128)}, f32[256,8192]{1,0:T(8,128)}, ...) | async-done | bytes 25165840 | tf_op jit(solution)/shard_map/psum | solution.py:250
  5895.9 6.8 copy.90
  (183 shorter events, 88.2 us)
Async XLA Ops:
  7.2 72.8 %copy-start.2 = (bf16[1,256,2048]{2,1,0:T(8,128)(2,1)S(1)}, bf16[1,256,2048]{2,1,0:T(8,128)(2,1)}, u32[]{:S(2)}) copy-start(bf16[1,256,2048]{2,1,0:T(8,128)(2,1)} %param.15) | copy-start | bytes 3145732
  7.2 486.8 %all-gather.8.cloned.1.call-start = ((), (), s32[]{:S(2)}) async-start(), calls=%async_computation.5 | async-start | bytes 28311552 | tf_op jit(solution)/shard_map/all_gather | solution.py:127
  7.9 559.4 %all-gather.16.cloned.1.call-start = ((), (), s32[]{:S(2)}) async-start(), calls=%async_computation.14 | async-start | bytes 10485760 | tf_op jit(solution)/shard_map/all_gather | solution.py:137
  79.9 425.8 %copy-start.20 = (f32[1,2,8,128]{3,1,2,0:T(2,128)}, f32[1,2,8,128]{3,1,2,0:T(2,128)S(1)}, u32[]{:S(2)}) copy-start(f32[1,2,8,128]{3,1,2,0:T(2,128)S(1)} %copy.56) | copy-start | bytes 24580
  80.0 425.8 %copy-start.18 = (f32[1,2,8,128]{3,1,2,0:T(2,128)}, f32[1,2,8,128]{3,1,2,0:T(2,128)S(1)}, u32[]{:S(2)}) copy-start(f32[1,2,8,128]{3,1,2,0:T(2,128)S(1)} %copy.55) | copy-start | bytes 24580
  80.2 425.6 %copy-start.22 = (f32[256]{0:T(256)}, f32[256]{0:T(256)S(1)}, u32[]{:S(2)}) copy-start(f32[256]{0:T(256)S(1)} %broadcast_multiply_fusion.2) | copy-start | bytes 3076
  80.6 425.1 %copy-start.30 = (f32[256]{0:T(256)}, f32[256]{0:T(256)S(1)}, u32[]{:S(2)}) copy-start(f32[256]{0:T(256)S(1)} %fusion.30) | copy-start | bytes 3076
  80.6 425.1 %copy-start.24 = (f32[256]{0:T(256)}, f32[256]{0:T(256)S(1)}, u32[]{:S(2)}) copy-start(f32[256]{0:T(256)S(1)} %fusion.48) | copy-start | bytes 3076
  508.9 185.5 %all-gather.10.cloned.1.call-start = ((), (), s32[]{:S(2)}) async-start(), calls=%async_computation.6 | async-start | bytes 9437184 | tf_op jit(solution)/shard_map/all_gather | solution.py:128
  509.7 822.1 %all-gather.12.cloned.1.call-start = ((), (), s32[]{:S(2)}) async-start(), calls=%async_computation.7 | async-start | bytes 37748736 | tf_op jit(solution)/shard_map/all_gather | solution.py:157
  510.3 1460.6 %all-gather.14.cloned.1.call-start = ((), (), s32[]{:S(2)}) async-start(), calls=%async_computation.8 | async-start | bytes 37748736 | tf_op jit(solution)/shard_map/all_gather | solution.py:158
  510.9 1687.0 %reduce-scatter.6.cloned.1.call-start = ((), (), s32[]{:S(2)}) async-start(), calls=%async_computation.9 | async-start | bytes 20971520 | tf_op jit(solution)/shard_map/reduce_scatter | solution.py:216
  511.2 820.6 %copy-start.16 = (f32[1,2,8,128]{3,1,2,0:T(2,128)}, f32[1,2,8,128]{3,1,2,0:T(2,128)S(1)}, u32[]{:S(2)}) copy-start(f32[1,2,8,128]{3,1,2,0:T(2,128)S(1)} %copy.59) | copy-start | bytes 24580
  512.5 70.0 %copy-start.6 = (bf16[256,2048]{0,1:T(8,128)(2,1)}, bf16[256,2048]{0,1:T(8,128)(2,1)S(1)}, u32[]{:S(2)}) copy-start(bf16[256,2048]{0,1:T(8,128)(2,1)S(1)} %copy.52) | copy-start | bytes 3145732
  1331.8 639.1 %copy-start.8 = (bf16[1,256,2048]{2,1,0:T(8,128)(2,1)S(1)}, bf16[1,256,2048]{2,1,0:T(8,128)(2,1)}, u32[]{:S(2)}) copy-start(bf16[1,256,2048]{2,1,0:T(8,128)(2,1)} %param.16) | copy-start | bytes 3145732
  2013.2 9.3 copy-start.28
  2034.4 30.6 slice-start
  2049.7 11.9 copy-start.7
  2049.7 15.2 slice-start.1
  2071.6 412.8 %reduce-scatter.10.cloned.1.call-start = ((), (), s32[]{:S(2)}) async-start(), calls=%async_computation.11 | async-start | bytes 18874368 | tf_op jit(solution)/shard_map/reduce_scatter | solution.py:247
  2085.6 1457.9 %reduce-scatter.14.cloned.1.call-start = ((), (), s32[]{:S(2)}) async-start(), calls=%async_computation.13 | async-start | bytes 75497472 | tf_op jit(solution)/shard_map/reduce_scatter | solution.py:186
  2117.5 2485.2 %reduce-scatter.12.cloned.1.call-start = ((), (), s32[]{:S(2)}) async-start(), calls=%async_computation.12 | async-start | bytes 75497472 | tf_op jit(solution)/shard_map/reduce_scatter | solution.py:185
  2144.9 3251.0 %reduce-scatter.8.cloned.1.call-start = ((), (), s32[]{:S(2)}) async-start(), calls=%async_computation.10 | async-start | bytes 56623104 | tf_op jit(solution)/shard_map/reduce_scatter | solution.py:246
  2153.8 47.9 copy-start.3
  2153.8 47.9 copy-start.19
  2153.8 47.9 copy-start.21
  2153.8 47.9 copy-start.23
  2153.8 47.9 copy-start.25
  2224.1 3243.9 %all-reduce.5.cloned.1.call-start = ((), (), s32[]{:S(2)}) async-start(), calls=%async_computation.15 | async-start | bytes 147456
  2224.9 13.9 copy-start.31
  2224.9 16.6 copy-start.29
  2247.4 3648.5 %all-reduce.7.cloned.1.call-start = ((), (), s32[]{:S(2)}) async-start(), calls=%async_computation.16 | async-start | bytes 50331648 | tf_op jit(solution)/shard_map/psum | solution.py:250
  (23 other events, 63.5 us)
Sparse Core Ops, SparseCore 0:
  9.6 484.3 all-gather.7
  509.1 58.2 all-gather.15
  569.5 124.9 all-gather.9
  695.8 635.9 all-gather.11
  1333.1 637.6 all-gather.13
  2071.8 126.1 reduce-scatter.5
  2202.2 282.2 reduce-scatter.9
  2488.3 1055.1 reduce-scatter.13
  3547.3 1055.3 reduce-scatter.11
  4606.5 789.3 reduce-scatter.7
  5400.3 67.6 all-reduce.4
  5470.8 425.0 all-reduce.6
where the time goes:
time: 5920 us
  waiting for transfers between devices  5470 us (92%)
  matrix products  260 us (4%)
  blocking collectives  77.3 us (1%)
    reduce_scatter x1, waiting for transfers between devices, shards(): lax.psum_scatter(up_grad, 'fsdp', scatter_dimension=0, tiled=True)  1060 us
    reduce_scatter x1, waiting for transfers between devices, shards(): lax.psum_scatter(down_grad, 'fsdp', scatter_dimension=0, tiled=True)  1060 us
    reduce_scatter x1, waiting for transfers between devices, shards(): lax.psum_scatter(qkv_grad, 'fsdp', scatter_dimension=0, tiled=True)  793 us
    all_gather x1, waiting for transfers between devices, shards(): lax.all_gather(w_up, 'fsdp', axis=0, tiled=True)  631 us
    all_gather x1, waiting for transfers between devices, shards(): lax.all_gather(w_down, 'fsdp', axis=0, tiled=True)  620 us
    psum x1, waiting for transfers between devices, shards(): lax.psum((up_sum, down_sum, qkv_sum, out_sum, vector_sum), 'seq')  416 us
    all_gather x1, waiting for transfers between devices, shards(): lax.all_gather(w_qkv, 'fsdp', axis=0, tiled=True)  413 us
    reduce_scatter x1, waiting for transfers between devices, shards(): lax.psum_scatter(out_grad, 'fsdp', scatter_dimension=0, tiled=True)  237 us
  transfers between devices with their start and end apart: 12, of which 12 were waited for; matrix products, arithmetic and copies ran while one was open for 4% of the time, Pallas kernels for 0%

commit v1 on v0

--- a/solution.py
+++ b/solution.py
@@ -1,6 +1,12 @@
+import functools
+
 import jax
 import jax.numpy as jnp
+import numpy as np
 from jax import lax
+from jax.experimental import pallas as pl
+from jax.experimental.pallas import tpu as pltpu
+from jax.sharding import Mesh
 from jax.sharding import PartitionSpec as P
 
 H = 16
@@ -9,6 +15,10 @@
 
 EPSILON = 1e-05
 MASKED = -1e30
+SWAP = ((0, 1), (1, 0))
+VMEM_LIMIT = 56 << 20
+GELU_A = float(np.sqrt(2.0 / np.pi))
+GELU_B = 0.044715
 
 
 def layer_norm(values, gain_vec, shift_vec):
@@ -91,7 +101,7 @@
     return (query_grad.astype(jnp.bfloat16), key_part, value_part)
 
 
-def shards(
+def plain_shards(
     block_input,
     cotangent,
     item_starts,
@@ -272,41 +282,775 @@
     )
 
 
+def piece_owner(zi, xi, z_count):
+    return [
+        lax.rem(zi - j + z_count, z_count) * 2 + jnp.bitwise_xor(xi, dx)
+        for dx in range(2)
+        for j in range(z_count)
+    ]
+
+
+def gather_pieces(shard, z_count):
+    line = [shard]
+    for j in range(1, z_count):
+        line.append(lax.ppermute(shard, "z", [(i, (i + j) % z_count) for i in range(z_count)]))
+    return line + [lax.ppermute(piece, "x", SWAP) for piece in line]
+
+
+def reduce_pieces(pieces, z_count):
+    wide = jnp.float32
+    far = [lax.ppermute(piece, "x", SWAP) for piece in pieces[z_count:]]
+    total = pieces[0].astype(wide) + far[0].astype(wide)
+    for j in range(1, z_count):
+        part = (pieces[j].astype(wide) + far[j].astype(wide)).astype(jnp.bfloat16)
+        total = total + lax.ppermute(
+            part, "z", [(i, (i - j) % z_count) for i in range(z_count)]
+        ).astype(wide)
+    return total.astype(jnp.bfloat16)
+
+
+def seq_pieces(block):
+    other = lax.ppermute(block, "y", SWAP)
+    return [block, lax.ppermute(block, "c", SWAP), other, lax.ppermute(other, "c", SWAP)]
+
+
+def by_bit(bit, mine, theirs):
+    return jnp.where(bit == 0, mine, theirs), jnp.where(bit == 0, theirs, mine)
+
+
+def gather_tokens(block, yi, ci):
+    parts = seq_pieces(block)
+    near = by_bit(ci, parts[0], parts[1])
+    far = by_bit(ci, parts[2], parts[3])
+    rows = [jnp.where(yi == 0, n, f) for n, f in zip(near, far)]
+    rows += [jnp.where(yi == 0, f, n) for n, f in zip(near, far)]
+    return jnp.concatenate(rows, axis=0)
+
+
+def scatter_tokens(partial, yi, ci):
+    tokens = partial.shape[0] // 4
+    parts = partial.reshape(2, 2, tokens, partial.shape[1])
+    away = lax.dynamic_index_in_dim(parts, 1 - ci, 1, keepdims=False)
+    home = lax.dynamic_index_in_dim(parts, ci, 1, keepdims=False)
+    total = home.astype(jnp.float32) + lax.ppermute(away, "c", SWAP).astype(jnp.float32)
+    away = lax.dynamic_index_in_dim(total, 1 - yi, 0, keepdims=False).astype(jnp.bfloat16)
+    home = lax.dynamic_index_in_dim(total, yi, 0, keepdims=False)
+    return home + lax.ppermute(away, "y", SWAP).astype(jnp.float32)
+
+
+def params(limit=VMEM_LIMIT):
+    return pltpu.CompilerParams(vmem_limit_bytes=limit)
+
+
+def load_weight(offsets, pieces, held, sems):
+    copies = []
+    for p, piece in enumerate(pieces):
+        rows, cols = piece.shape
+        row = pl.multiple_of(offsets[0, p], rows)
+        col = pl.multiple_of(offsets[1, p], cols)
+        copies.append(
+            pltpu.make_async_copy(
+                piece, held.at[pl.ds(row, rows), pl.ds(col, cols)], sems.at[p]
+            )
+        )
+    for copy in copies:
+        copy.start()
+    for copy in copies:
+        copy.wait()
+
+
+def weight_matmul(left, pieces, offsets, shape, back, body, extras, outs, tile, chunk):
+    rows = left.shape[0]
+    depth, width = shape
+    out_width = depth if back else width
+    n_pieces, n_extras = len(pieces), len(extras)
+
+    def kernel(offs_ref, left_ref, *refs):
+        piece_refs = refs[:n_pieces]
+        extra_refs = refs[n_pieces : n_pieces + n_extras]
+        out_refs = refs[n_pieces + n_extras : -2]
+        held, sems = refs[-2:]
+
+        @pl.when(pl.program_id(0) == 0)
+        def _():
+            load_weight(offs_ref, piece_refs, held, sems)
+
+        for start in range(0, out_width, chunk):
+            cols = pl.ds(start, chunk)
+            if back:
+                values = lax.dot_general(
+                    left_ref[...],
+                    held[cols, :],
+                    (((1,), (1,)), ((), ())),
+                    preferred_element_type=jnp.float32,
+                )
+            else:
+                values = jnp.dot(
+                    left_ref[...], held[:, cols], preferred_element_type=jnp.float32
+                )
+            body(values, cols, extra_refs, out_refs, pl.program_id(0) == 0)
+
+    def tile_spec(array_rows, array_cols):
+        if array_rows == 1:
+            return pl.BlockSpec((1, array_cols), lambda i, offs: (0, 0))
+        return pl.BlockSpec((tile, array_cols), lambda i, offs: (i, 0))
+
+    flops = 2 * rows * depth * width
+    moved = 2 * (left.size + depth * width) + sum(
+        a.size * a.dtype.itemsize for a in list(extras) + list(outs)
+    )
+    return pl.pallas_call(
+        kernel,
+        grid_spec=pltpu.PrefetchScalarGridSpec(
+            num_scalar_prefetch=1,
+            grid=(rows // tile,),
+            in_specs=[pl.BlockSpec((tile, left.shape[1]), lambda i, offs: (i, 0))]
+            + [pl.BlockSpec(memory_space=pl.ANY)] * n_pieces
+            + [tile_spec(*a.shape) for a in extras],
+            out_specs=[tile_spec(*a.shape) for a in outs],
+            scratch_shapes=[
+                pltpu.VMEM((depth, width), jnp.bfloat16),
+                pltpu.SemaphoreType.DMA((n_pieces,)),
+            ],
+        ),
+        out_shape=list(outs),
+        cost_estimate=pl.CostEstimate(flops=flops, bytes_accessed=moved, transcendentals=0),
+        compiler_params=params(),
+    )(offsets, left, *pieces, *extras)
+
+
+def store_low(values, cols, extra_refs, out_refs, first):
+    out_refs[0][:, cols] = values.astype(jnp.bfloat16)
+
+
+def store_gelu(values, cols, extra_refs, out_refs, first):
+    hidden = values + extra_refs[0][:, cols]
+    square = hidden * hidden
+    bend = jnp.tanh(GELU_A * hidden * (1.0 + GELU_B * square))
+    half = 0.5 * (1.0 + bend)
+    out_refs[0][:, cols] = (hidden * half).astype(jnp.bfloat16)
+    slope = half + 0.5 * hidden * (1.0 - bend * bend) * (
+        GELU_A * (1.0 + 3.0 * GELU_B * square)
+    )
+    out_refs[1][:, cols] = slope
+
+
+def store_hidden_grad(values, cols, extra_refs, out_refs, first):
+    low = (values * extra_refs[0][:, cols]).astype(jnp.bfloat16)
+    out_refs[0][:, cols] = low
+    column_sum = jnp.sum(low.astype(jnp.float32), axis=0, keepdims=True)
+    sums = out_refs[1]
+
+    @pl.when(first)
+    def _():
+        sums[:, cols] = column_sum
+
+    @pl.when(jnp.logical_not(first))
+    def _():
+        sums[:, cols] += column_sum
+
+
+def weight_grad(left, right, owners, block):
+    rows, depth = left.shape
+    width = right.shape[1]
+    count = depth // block
+
+    def kernel(owner_ref, left_ref, right_ref, *refs):
+        outs, held, sems = refs[:count], refs[count], refs[count + 1]
+        step = pl.program_id(0)
+        slot = lax.rem(step, 2)
+
+        @pl.when(step >= 2)
+        def _():
+            pltpu.make_async_copy(held.at[slot], outs[0], sems.at[slot]).wait()
+
+        held[slot] = lax.dot_general(
+            left_ref[...],
+            right_ref[...],
+            (((0,), (0,)), ((), ())),
+            preferred_element_type=jnp.float32,
+        ).astype(jnp.bfloat16)
+        for k in range(count):
+
+            @pl.when(step == k)
+            def _():
+                pltpu.make_async_copy(held.at[slot], outs[k], sems.at[slot]).start()
+
+        @pl.when(step == count - 1)
+        def _():
+            pltpu.make_async_copy(held.at[1 - slot], outs[0], sems.at[1 - slot]).wait()
+            pltpu.make_async_copy(held.at[slot], outs[0], sems.at[slot]).wait()
+
+    return pl.pallas_call(
+        kernel,
+        grid_spec=pltpu.PrefetchScalarGridSpec(
+            num_scalar_prefetch=1,
+            grid=(count,),
+            in_specs=[
+                pl.BlockSpec((rows, block), lambda k, owner: (0, owner[k])),
+                pl.BlockSpec((rows, width), lambda k, owner: (0, 0)),
+            ],
+            out_specs=[pl.BlockSpec(memory_space=pl.ANY)] * count,
+            scratch_shapes=[
+                pltpu.VMEM((2, block, width), jnp.bfloat16),
+                pltpu.SemaphoreType.DMA((2,)),
+            ],
+        ),
+        out_shape=[jax.ShapeDtypeStruct((block, width), jnp.bfloat16)] * count,
+        cost_estimate=pl.CostEstimate(
+            flops=2 * rows * depth * width,
+            bytes_accessed=2 * (left.size + right.size + depth * width),
+            transcendentals=0,
+        ),
+        compiler_params=params(),
+    )(owners, left, right)
+
+
+def visible_tile(query_item, key_item, first_query, n_query, n_key):
+    query_pos = first_query + lax.broadcasted_iota(jnp.int32, (n_query, n_key), 0)
+    key_pos = lax.broadcasted_iota(jnp.int32, (n_query, n_key), 1)
+    return ((query_item == key_item) & (key_pos < query_pos)) | (key_pos == query_pos)
+
+
+def head_spec(length, first):
+    return pl.BlockSpec((length, HD), lambda h: (0, first + h))
+
+
+def attention(projected, query_item, key_item, heads, tile):
+    length = projected.shape[0]
+    scale = HD ** (-0.5)
+
+    def kernel(q_ref, k_ref, v_ref, qi_ref, ki_ref, mixed_ref, log_ref):
+        for start in range(0, length, tile):
+            stop = start + tile
+            rows = slice(start, stop)
+            scores = (
+                lax.dot_general(
+                    q_ref[rows, :],
+                    k_ref[:stop, :],
+                    (((1,), (1,)), ((), ())),
+                    preferred_element_type=jnp.float32,
+                )
+                * scale
+            )
+            seen = visible_tile(qi_ref[rows, :], ki_ref[:, :stop], start, tile, stop)
+            scores = jnp.where(seen, scores, MASKED)
+            peak = jnp.max(scores, axis=-1, keepdims=True)
+            weights = jnp.exp(scores - peak)
+            total = jnp.sum(weights, axis=-1, keepdims=True)
+            probs = (weights * (1.0 / total)).astype(jnp.bfloat16)
+            mixed_ref[rows, :] = jnp.dot(
+                probs, v_ref[:stop, :], preferred_element_type=jnp.float32
+            ).astype(jnp.bfloat16)
+            log_ref[0, rows, :] = peak + jnp.log(total)
+
+    whole = lambda rows, cols: pl.BlockSpec((rows, cols), lambda h: (0, 0))
+    return pl.pallas_call(
+        kernel,
+        grid=(heads,),
+        in_specs=[head_spec(length, g * heads) for g in range(3)]
+        + [whole(length, 1), whole(1, length)],
+        out_specs=[head_spec(length, 0), pl.BlockSpec((1, length, 1), lambda h: (h, 0, 0))],
+        out_shape=[
+            jax.ShapeDtypeStruct((length, heads * HD), jnp.bfloat16),
+            jax.ShapeDtypeStruct((heads, length, 1), jnp.float32),
+        ],
+        cost_estimate=pl.CostEstimate(
+            flops=4 * heads * length * length * HD,
+            bytes_accessed=8 * length * heads * HD,
+            transcendentals=heads * length * length,
+        ),
+        compiler_params=params(),
+    )(projected, projected, projected, query_item, key_item)
+
+
+def attention_back(projected, mixed_grad, log_total, query_item, key_item, heads, tile):
+    length = projected.shape[0]
+    scale = HD ** (-0.5)
+
+    def kernel(q_ref, k_ref, v_ref, g_ref, log_ref, qi_ref, ki_ref, grad_ref, dk_ref, dv_ref):
+        head = pl.program_id(0)
+
+        def place(group):
+            return pl.ds(pl.multiple_of((group * heads + head) * HD, HD), HD)
+
+        for start in reversed(range(0, length, tile)):
+            stop = start + tile
+            rows = slice(start, stop)
+            query, grad = q_ref[rows, :], g_ref[rows, :]
+            key, value = k_ref[:stop, :], v_ref[:stop, :]
+            scores = (
+                lax.dot_general(
+                    query, key, (((1,), (1,)), ((), ())), preferred_element_type=jnp.float32
+                )
+                * scale
+            )
+            seen = visible_tile(qi_ref[rows, :], ki_ref[:, :stop], start, tile, stop)
+            probs = jnp.exp(jnp.where(seen, scores, MASKED) - log_ref[0, rows, :])
+            prob_grad = lax.dot_general(
+                grad, value, (((1,), (1,)), ((), ())), preferred_element_type=jnp.float32
+            )
+            inner = jnp.sum(prob_grad * probs, axis=-1, keepdims=True)
+            score_grad = (probs * (prob_grad - inner)).astype(jnp.bfloat16)
+            grad_ref[rows, place(0)] = (
+                jnp.dot(score_grad, key, preferred_element_type=jnp.float32) * scale
+            ).astype(jnp.bfloat16)
+            key_part = lax.dot_general(
+                score_grad, query, (((0,), (0,)), ((), ())), preferred_element_type=jnp.float32
+            )
+            value_part = lax.dot_general(
+                probs.astype(jnp.bfloat16),
+                grad,
+                (((0,), (0,)), ((), ())),
+                preferred_element_type=jnp.float32,
+            )
+            if stop == length:
+                dk_ref[...] = key_part
+                dv_ref[...] = value_part
+            else:
+                dk_ref[:stop, :] += key_part
+                dv_ref[:stop, :] += value_part
+        grad_ref[:, place(1)] = (dk_ref[...] * scale).astype(jnp.bfloat16)
+        grad_ref[:, place(2)] = dv_ref[...].astype(jnp.bfloat16)
+
+    whole = lambda rows, cols: pl.BlockSpec((rows, cols), lambda h: (0, 0))
+    return pl.pallas_call(
+        kernel,
+        grid=(heads,),
+        in_specs=[head_spec(length, g * heads) for g in range(3)]
+        + [
+            head_spec(length, 0),
+            pl.BlockSpec((1, length, 1), lambda h: (h, 0, 0)),
+            whole(length, 1),
+            whole(1, length),
+        ],
+        out_specs=whole(length, 3 * heads * HD),
+        out_shape=jax.ShapeDtypeStruct((length, 3 * heads * HD), jnp.bfloat16),
+        scratch_shapes=[pltpu.VMEM((length, HD), jnp.float32)] * 2,
+        cost_estimate=pl.CostEstimate(
+            flops=10 * heads * length * length * HD,
+            bytes_accessed=16 * length * heads * HD,
+            transcendentals=heads * length * length,
+        ),
+        compiler_params=params(),
+    )(projected, projected, projected, mixed_grad, log_total, query_item, key_item)
+
+
+def widen(pieces, places, grid, piece_block, out_block, out_index, out_shape, write):
+    def kernel(place_ref, *refs):
+        for r in range(4):
+            write(place_ref[r], refs[r], refs[4])
+
+    return pl.pallas_call(
+        kernel,
+        grid_spec=pltpu.PrefetchScalarGridSpec(
+            num_scalar_prefetch=1,
+            grid=(grid,),
+            in_specs=[pl.BlockSpec(piece_block[0], lambda i, pos: piece_block[1](i))] * 4,
+            out_specs=pl.BlockSpec(out_block, lambda i, pos: out_index(i)),
+        ),
+        out_shape=jax.ShapeDtypeStruct(out_shape, jnp.float32),
+        cost_estimate=pl.CostEstimate(
+            flops=0, bytes_accessed=6 * int(np.prod(out_shape)), transcendentals=0
+        ),
+        compiler_params=params(),
+    )(places, *pieces)
+
+
+def widen_columns(pieces, places, blocks):
+    rows, width = pieces[0].shape
+    part = width // blocks
+
+    def write(pos, piece, out):
+        out[:, pl.ds(pl.multiple_of(pos * part, part), part)] = piece[...].astype(jnp.float32)
+
+    return widen(
+        pieces,
+        places,
+        blocks,
+        ((rows, part), lambda i: (0, i)),
+        (rows, 4 * part),
+        lambda i: (0, i),
+        (rows, 4 * width),
+        write,
+    )
+
+
+def widen_rows(pieces, places):
+    rows, width = pieces[0].shape
+
+    def write(pos, piece, out):
+        @pl.when(pos == pl.program_id(0))
+        def _():
+            out[...] = piece[...].astype(jnp.float32)
+
+    return widen(
+        pieces,
+        places,
+        4,
+        ((rows, width), lambda i: (0, 0)),
+        (rows, width),
+        lambda i: (i, 0),
+        (4 * rows, width),
+        write,
+    )
+
+
+def widen_heads(pieces, places):
+    rows, width = pieces[0].shape
+    part = width // 3
+
+    def write(pos, piece, out):
+        first = lax.div(pos, 2) * part * 2 + lax.rem(pos, 2) * HD
+        for i in range(part // HD):
+            cols = pl.ds(pl.multiple_of(first + 2 * i * HD, HD), HD)
+            out[:, cols] = piece[:, i * HD : (i + 1) * HD].astype(jnp.float32)
+
+    return widen(
+        pieces,
+        places,
+        3,
+        ((rows, part), lambda i: (0, i)),
+        (rows, 4 * part),
+        lambda i: (0, i),
+        (rows, 4 * width),
+        write,
+    )
+
+
+def widen_quarters(pieces, places):
+    rows, width = pieces[0].shape
+
+    def write(pos, piece, out):
+        row = pl.multiple_of(lax.rem(pos, 2) * rows, rows)
+        col = pl.multiple_of(lax.div(pos, 2) * width, width)
+        out[pl.ds(row, rows), pl.ds(col, width)] = piece[...].astype(jnp.float32)
+
+    return widen(
+        pieces,
+        places,
+        1,
+        ((rows, width), lambda i: (0, 0)),
+        (2 * rows, 2 * width),
+        lambda i: (0, 0),
+        (2 * rows, 2 * width),
+        write,
+    )
+
+
+def norm_back(values, gain_vec, incoming):
+    center = values - jnp.mean(values, axis=-1, keepdims=True)
+    spread = jnp.mean(center * center, axis=-1, keepdims=True)
+    inverse = lax.rsqrt(spread + EPSILON)
+    unit = center * inverse
+    scaled = incoming * gain_vec
+    inner = jnp.mean(scaled * unit, axis=-1, keepdims=True)
+    grad = (scaled - jnp.mean(scaled, axis=-1, keepdims=True) - unit * inner) * inverse
+    return grad, jnp.sum(incoming * unit, axis=0), jnp.sum(incoming, axis=0)
+
+
+def split_shards(
+    block_input,
+    cotangent,
+    item_starts,
+    item_lengths,
+    pad_mask,
+    ln1_gain,
+    ln1_shift,
+    w_qkv,
+    w_out,
+    ln2_gain,
+    ln2_shift,
+    w_up,
+    up_bias,
+    w_down,
+    down_bias,
+):
+    low, wide = jnp.bfloat16, jnp.float32
+    z_count = lax.axis_size("z")
+    shard_count = 2 * z_count
+    zi, xi, yi, ci = [lax.axis_index(name) for name in ("z", "x", "y", "c")]
+    si = 2 * yi + ci
+    tok_count, model = block_input.shape[1:]
+    length = 4 * tok_count
+    piece_d, ff_piece = ln1_gain.shape[0], up_bias.shape[0]
+    ff_part = ff_piece // 4
+    ff_here = ff_part * shard_count
+    heads = H // 4
+    owners = jnp.stack(piece_owner(zi, xi, z_count)).astype(jnp.int32)
+    zeros = jnp.zeros_like(owners)
+    places = jnp.stack([jnp.bitwise_xor(si, r) for r in range(4)]).astype(jnp.int32)
+
+    packed = jnp.concatenate([ln1_gain, ln1_shift, ln2_gain, ln2_shift, down_bias, up_bias])
+    vector_stack = jnp.stack(gather_pieces(packed, z_count))
+    hit = owners[None, :] == jnp.arange(shard_count, dtype=jnp.int32)[:, None]
+    vector_table = jnp.sum(jnp.where(hit[:, :, None], vector_stack[None], 0.0), axis=1)
+
+    def vector_part(slot):
+        return vector_table[:, slot * piece_d : (slot + 1) * piece_d].reshape(-1)
+
+    gain_one, shift_one, gain_two, shift_two, bias_down = [vector_part(slot) for slot in range(5)]
+    bias_up = lax.dynamic_index_in_dim(
+        vector_table[:, 5 * piece_d :].reshape(shard_count, 4, ff_part), si, 1, keepdims=False
+    ).reshape(1, ff_here)
+
+    qkv_slice = w_qkv.reshape(piece_d, 3, 2, heads, 2, HD)
+    qkv_slice = lax.dynamic_index_in_dim(qkv_slice, yi, 2, keepdims=False)
+    qkv_slice = lax.dynamic_index_in_dim(qkv_slice, ci, 3, keepdims=False)
+    qkv_slice = qkv_slice.reshape(piece_d, 3 * heads * HD)
+    out_slice = w_out.reshape(2, piece_d // 2, 2, model // 2)
+    out_slice = lax.dynamic_index_in_dim(out_slice, yi, 2, keepdims=False)
+    out_slice = lax.dynamic_index_in_dim(out_slice, ci, 0, keepdims=False)
+    up_slice = lax.dynamic_index_in_dim(
+        w_up.reshape(piece_d, shard_count, 4, ff_part), si, 2, keepdims=False
+    ).reshape(piece_d, ff_here)
+    down_slice = lax.dynamic_index_in_dim(
+        w_down.reshape(4, ff_part, model), si, 0, keepdims=False
+    )
+
+    qkv_parts = gather_pieces(qkv_slice, z_count)
+    out_parts = gather_pieces(out_slice, z_count)
+    out_parts = out_parts + [lax.ppermute(piece, "y", SWAP) for piece in out_parts]
+    up_parts = gather_pieces(up_slice, z_count)
+    down_parts = gather_pieces(down_slice, z_count)
+    row_offsets = jnp.stack([owners * piece_d, zeros])
+    out_offsets = jnp.stack(
+        [
+            jnp.concatenate([owners, owners]) * (piece_d // 2),
+            jnp.concatenate([zeros + yi, zeros + 1 - yi]) * (model // 2),
+        ]
+    )
+    ff_offsets = jnp.stack([owners * ff_part, zeros])
+
+    def shape(rows, cols, kind=low):
+        return jax.ShapeDtypeStruct((rows, cols), kind)
+
+    inputs = block_input.reshape(tok_count, model).astype(wide)
+    normed_one = gather_tokens(layer_norm(inputs, gain_one, shift_one).astype(low), yi, ci)
+    (projected,) = weight_matmul(
+        normed_one,
+        qkv_parts,
+        row_offsets,
+        (model, 3 * heads * HD),
+        False,
+        store_low,
+        (),
+        (shape(length, 3 * heads * HD),),
+        256,
+        512,
+    )
+    positions = jnp.arange(length, dtype=jnp.int32)
+    item_label = item_numbers(item_starts[0], item_lengths[0], positions)
+    query_item = item_label[:, None]
+    key_item = jnp.where((item_label >= 0) & (pad_mask[0] == 1), item_label, -2)[None, :]
+    mixed_heads, log_total = attention(projected, query_item, key_item, heads, 256)
+    halves = mixed_heads.reshape(2, 2 * tok_count, heads * HD)
+    away = lax.dynamic_index_in_dim(halves, 1 - yi, 0, keepdims=False)
+    home = lax.dynamic_index_in_dim(halves, yi, 0, keepdims=False)
+    mixed = jnp.concatenate(by_bit(yi, home, lax.ppermute(away, "y", SWAP)), axis=1)
+    (out_partial,) = weight_matmul(
+        mixed,
+        out_parts,
+        out_offsets,
+        (model // 2, model),
+        False,
+        store_low,
+        (),
+        (shape(2 * tok_count, model),),
+        256,
+        512,
+    )
+    halves = out_partial.reshape(2, tok_count, model)
+    away = lax.dynamic_index_in_dim(halves, 1 - ci, 0, keepdims=False)
+    home = lax.dynamic_index_in_dim(halves, ci, 0, keepdims=False)
+    residual_one = (
+        inputs + home.astype(wide) + lax.ppermute(away, "c", SWAP).astype(wide)
+    )
+    normed_two = gather_tokens(
+        layer_norm(residual_one, gain_two, shift_two).astype(low), yi, ci
+    )
+    activated, slope = weight_matmul(
+        normed_two,
+        up_parts,
+        row_offsets,
+        (model, ff_here),
+        False,
+        store_gelu,
+        (bias_up,),
+        (shape(length, ff_here), shape(length, ff_here, wide)),
+        256,
+        512,
+    )
+    (down_partial,) = weight_matmul(
+        activated,
+        down_parts,
+        ff_offsets,
+        (ff_here, model),
+        False,
+        store_low,
+        (),
+        (shape(length, model),),
+        256,
+        512,
+    )
+    block_output = residual_one + scatter_tokens(down_partial, yi, ci) + bias_down
+    output_shard = block_output.astype(low).reshape(1, tok_count, model)
+
+    cot_flat = cotangent.reshape(tok_count, model)
+    cot_wide = cot_flat.astype(wide)
+    cot_all = gather_tokens(cot_flat, yi, ci)
+    down_bias_part = jnp.sum(cot_wide, axis=0)
+    down_grads = weight_grad(activated, cot_all, owners, ff_part)
+    down_shard = reduce_pieces(down_grads, z_count)
+    hidden_grad, up_bias_part = weight_matmul(
+        cot_all,
+        down_parts,
+        ff_offsets,
+        (ff_here, model),
+        True,
+        store_hidden_grad,
+        (slope,),
+        (shape(length, ff_here), shape(1, ff_here, wide)),
+        256,
+        512,
+    )
+    (norm_two_partial,) = weight_matmul(
+        hidden_grad,
+        up_parts,
+        row_offsets,
+        (model, ff_here),
+        True,
+        store_low,
+        (),
+        (shape(length, model),),
+        256,
+        512,
+    )
+    up_grads = weight_grad(normed_two, hidden_grad, owners, piece_d)
+    up_shard = reduce_pieces(up_grads, z_count)
+    norm_two_grad = scatter_tokens(norm_two_partial, yi, ci)
+    resid_part, gain_two_grad, shift_two_grad = norm_back(residual_one, gain_two, norm_two_grad)
+    residual_grad = cot_wide + resid_part
+    branch_grad = residual_grad.astype(low)
+    branch_pair = jnp.concatenate(
+        by_bit(ci, branch_grad, lax.ppermute(branch_grad, "c", SWAP)), axis=0
+    )
+    (mixed_grad_pair,) = weight_matmul(
+        branch_pair,
+        out_parts,
+        out_offsets,
+        (model // 2, model),
+        True,
+        store_low,
+        (),
+        (shape(2 * tok_count, model // 2),),
+        256,
+        512,
+    )
+    halves = mixed_grad_pair.reshape(2 * tok_count, 2, heads * HD)
+    away = lax.dynamic_index_in_dim(halves, 1 - yi, 1, keepdims=False)
+    home = lax.dynamic_index_in_dim(halves, yi, 1, keepdims=False)
+    mixed_grad = jnp.concatenate(by_bit(yi, home, lax.ppermute(away, "y", SWAP)), axis=0)
+    out_grad = contract_rows(mixed, branch_pair).astype(low)
+    out_grad = out_grad.reshape(shard_count, piece_d // 2, 2, model // 2)
+    away = lax.dynamic_index_in_dim(out_grad, 1 - yi, 2, keepdims=False)
+    home = lax.dynamic_index_in_dim(out_grad, yi, 2, keepdims=False)
+    out_grad = (home.astype(wide) + lax.ppermute(away, "y", SWAP).astype(wide)).astype(low)
+    out_grads = [
+        lax.dynamic_index_in_dim(out_grad, owners[k], 0, keepdims=False)
+        for k in range(shard_count)
+    ]
+    out_shard = reduce_pieces(out_grads, z_count)
+    proj_grad = attention_back(
+        projected, mixed_grad, log_total, query_item, key_item, heads, 256
+    )
+    qkv_grads = weight_grad(normed_one, proj_grad, owners, piece_d)
+    qkv_shard = reduce_pieces(qkv_grads, z_count)
+    (norm_one_partial,) = weight_matmul(
+        proj_grad,
+        qkv_parts,
+        row_offsets,
+        (model, 3 * heads * HD),
+        True,
+        store_low,
+        (),
+        (shape(length, model),),
+        256,
+        512,
+    )
+    norm_one_grad = scatter_tokens(norm_one_partial, yi, ci)
+    input_part, gain_one_grad, shift_one_grad = norm_back(inputs, gain_one, norm_one_grad)
+    input_grad = (residual_grad + input_part).reshape(1, tok_count, model)
+
+    up_bias_grad = jnp.where(
+        (jnp.arange(4, dtype=jnp.int32) == si)[None, :, None],
+        up_bias_part.reshape(shard_count, 1, ff_part),
+        0.0,
+    ).reshape(shard_count, ff_piece)
+    vector_grad = jnp.concatenate(
+        [
+            part.reshape(shard_count, -1)
+            for part in (
+                gain_one_grad,
+                shift_one_grad,
+                gain_two_grad,
+                shift_two_grad,
+                down_bias_part,
+                up_bias_grad,
+            )
+        ],
+        axis=1,
+    )
+    vector_total = lax.dynamic_index_in_dim(
+        lax.psum(vector_grad, ("z", "x", "y", "c")), 2 * zi + xi, 0, keepdims=False
+    )
+    down_total = widen_rows(seq_pieces(down_shard), places)
+    up_total = widen_columns(seq_pieces(up_shard), places, shard_count)
+    out_total = widen_quarters(seq_pieces(out_shard), places)
+    qkv_total = widen_heads(seq_pieces(qkv_shard), places)
+    vectors = [vector_total[slot * piece_d : (slot + 1) * piece_d] for slot in range(5)]
+    return (
+        output_shard,
+        input_grad,
+        vectors[0],
+        vectors[1],
+        qkv_total,
+        out_total,
+        vectors[2],
+        vectors[3],
+        up_total,
+        vector_total[5 * piece_d :],
+        down_total,
+        vectors[4],
+    )
+
+
 def solution(mesh):
-    placed = (
-        P("fsdp", "seq", None),
-        P("fsdp", "seq", None),
-        P("fsdp", None),
-        P("fsdp", None),
-        P("fsdp", None),
-        P("fsdp"),
-        P("fsdp"),
-        P("fsdp", None),
-        P("fsdp", None),
-        P("fsdp"),
-        P("fsdp"),
-        P("fsdp", None),
-        P("fsdp"),
-        P("fsdp", None),
-        P("fsdp"),
-    )
-    return jax.shard_map(
-        shards,
-        mesh=mesh,
-        in_specs=placed,
-        out_specs=(
-            P("fsdp", "seq", None),
-            P("fsdp", "seq", None),
-            P("fsdp"),
-            P("fsdp"),
-            P("fsdp", None),
-            P("fsdp", None),
-            P("fsdp"),
-            P("fsdp"),
-            P("fsdp", None),
-            P("fsdp"),
-            P("fsdp", None),
-            P("fsdp"),
-        ),
-        check_vma=False,
-    )
+    shard_count, seq_count = mesh.shape["fsdp"], mesh.shape["seq"]
+
+    def step(*args):
+        model, hidden = args[0].shape[2], args[12].shape[0]
+        rows_each = args[0].shape[0] // shard_count
+        if (
+            rows_each == 1
+            and seq_count == 4
+            and model // shard_count == 2 * HD
+            and hidden // (4 * shard_count) % 256 == 0
+        ):
+            fsdp, seq = ("z", "x"), ("y", "c")
+            devices = mesh.devices.reshape(shard_count // 2, 2, 2, 2)
+            inner, body = Mesh(devices, fsdp + seq), split_shards
+        else:
+            fsdp, seq = "fsdp", "seq"
+            inner, body = mesh, plain_shards
+        rows, tokens = P(fsdp, None), P(fsdp, seq, None)
+        vector = P(fsdp)
+        placed = (tokens, tokens, rows, rows, rows, vector, vector, rows, rows)
+        placed += (vector, vector, rows, vector, rows, vector)
+        given = (tokens, tokens, vector, vector, rows, rows, vector, vector)
+        given += (rows, vector, rows, vector)
+        return jax.shard_map(
+            body, mesh=inner, in_specs=placed, out_specs=given, check_vma=False
+        )(*args)
+
+    return step

time: 5920 us -> 1450 us (0.24)
  waiting for transfers between devices: 5470 us -> 757 us
  starting transfers between devices: 1.04 us -> 298 us
  matrix products: 260 us -> 4.42 us
  Pallas kernels: 0 us -> 209 us
  blocking collectives: 77.3 us -> 0 us
    reduce_scatter x5 -> x0, waiting for transfers between devices: 3190 us -> none  [the longest x1 1060 us: shards(): lax.psum_scatter(up_grad, 'fsdp', scatter_dimension=0, tiled=True)]
    all_gather x5 -> x0, waiting for transfers between devices: 1810 us -> none  [the longest x1 631 us: shards(): lax.all_gather(w_up, 'fsdp', axis=0, tiled=True)]
    ppermute x0 -> x103, waiting for transfers between devices: none -> 640 us  [the longest x15 162 us: gather_pieces(): lax.ppermute(shard, 'z', [(i, (i + j) % z_count) for i in range(z_count)])]
    psum x1, waiting for transfers between devices: 416 us -> 118 us  [split_shards(): lax.psum(vector_grad, ('z', 'x', 'y', 'c'))]
    ppermute x0 -> x103, starting transfers between devices: none -> 298 us  [the longest x12 173 us: reduce_pieces(): lax.ppermute(part, 'z', [(i, (i - j) % z_count) for i in range(z_count)])]
    pallas_call x0 -> x17, Pallas kernels: none -> 209 us  [the longest x8 115 us: weight_matmul(): pl.pallas_call(kernel, grid_spec=pltpu.PrefetchScalarGridSpec(num_scalar_...]
    dot_general x14 -> x0, matrix products: 167 us -> none  [the longest x4 60.6 us: times_transpose(): lax.dot_general(left, right, (((1,), (1,)), ((), ())), preferred_element_...]
    dot_general x4 -> x1, matrix products: 92.2 us -> 4.42 us  [contract_rows(): lax.dot_general(left, right, (((0,), (0,)), ((), ())), preferred_element_...]
  transfers between devices with their start and end apart: 12 -> 104, of which waited for: 12 -> 48; matrix products, arithmetic and copies ran while one was open for 4% -> 10% of each run, Pallas kernels for 0% -> 11%
where the time goes in v1:
time: 1450 us; the launch traced here: 1440 us
  waiting for transfers between devices  757 us (52%)
  starting transfers between devices  298 us (21%)
  Pallas kernels  209 us (14%)
  local copies, waits for them, and re-layouts  88.1 us (6%)
  other arithmetic  64.3 us (4%)
  between operations  15.7 us (1%)
    ppermute x12, starting transfers between devices, reduce_pieces(): lax.ppermute(part, 'z', [(i, (i - j) % z_count) for i in range(z_count)])  173 us
    ppermute x15, waiting for transfers between devices, gather_pieces(): lax.ppermute(shard, 'z', [(i, (i + j) % z_count) for i in range(z_count)])  162 us
    ppermute x20, waiting for transfers between devices, gather_pieces(): return line + [lax.ppermute(piece, 'x', SWAP) for piece in line]  149 us
    ppermute x16, waiting for transfers between devices, reduce_pieces(): far = [lax.ppermute(piece, 'x', SWAP) for piece in pieces[z_count:]]  134 us
    psum x1, waiting for transfers between devices, split_shards(): lax.psum(vector_grad, ('z', 'x', 'y', 'c'))  118 us
    pallas_call x8, Pallas kernels, weight_matmul(): pl.pallas_call(kernel, grid_spec=pltpu.PrefetchScalarGridSpec(num_scalar_...  115 us
    ppermute x12, waiting for transfers between devices, reduce_pieces(): lax.ppermute(part, 'z', [(i, (i - j) % z_count) for i in range(z_count)])  106 us
    ppermute x15, starting transfers between devices, gather_pieces(): lax.ppermute(shard, 'z', [(i, (i + j) % z_count) for i in range(z_count)])  69.9 us
  transfers between devices with their start and end apart: 104, of which 48 were waited for; matrix products, arithmetic and copies ran while one was open for 10% of the time, Pallas kernels for 11%

profile of v1, /device:TPU:0, one launch (start us, length us, event | category | flops | bytes accessed | tf_op | source)
XLA Modules:
  0.0 1436.9 jit_solution(13778186612890035113)
XLA Ops:
  71.2 29.0 %collective-permute-done.11.refs_2_ = bf16[256,1536]{1,0:T(8,128)(2,1)} collective-permute-done((bf16[256,1536]{1,0:T(8,128)(2,1)}, bf16[256,1536]{1,0:T(8,128)(2,1)}, u32[]{:S(2)}, u32[]{:S(2)}) %collective-permute-start.11) | collective-permute-done | bytes 786464 | tf_op jit(solution)/shard_map/ppermute | solution.py:296
  100.2 16.3 %collective-permute-start.18 = (bf16[128,1024]{1,0:T(8,128)(2,1)S(1)}, bf16[128,1024]{1,0:T(8,128)(2,1)}, u32[]{:S(2)}, u32[]{:S(2)}) collective-permute-start(bf16[128,1024]{1,0:T(8,128)(2,1)S(1)} %bitcast.224), channel_id=1, source_target_pairs={{0,8},{8,16},{16,24},{24,0},{1,9},{9,17},{17,25},{25,1},{2,10},{10... | collective-permute-start | bytes 786440 | tf_op jit(solution)/shard_map/ppermute | solution.py:296
  137.8 16.3 %collective-permute-done.15.refs_6_ = bf16[256,1536]{1,0:T(8,128)(2,1)S(1)} collective-permute-done((bf16[256,1536]{1,0:T(8,128)(2,1)}, bf16[256,1536]{1,0:T(8,128)(2,1)S(1)}, u32[]{:S(2)}, u32[]{:S(2)}) %collective-permute-start.15) | collective-permute-done | bytes 786464 | tf_op jit(solution)/shard_map/ppermute | solution.py:297
  295.2 20.9 %collective-permute-start.38 = (bf16[256,2048]{1,0:T(8,128)(2,1)}, bf16[256,2048]{1,0:T(8,128)(2,1)}, u32[]{:S(2)}, u32[]{:S(2)}) collective-permute-start(bf16[256,2048]{1,0:T(8,128)(2,1)} %bitcast.97.refs_0_), channel_id=1, source_target_pairs={{0,16},{8,24},{16,0},{24,8},{1,17},{9,25},{17,1},{25,9},{2,18},{10... | collective-permute-start | bytes 3145736 | tf_op jit(solution)/shard_map/ppermute | solution.py:296
  316.1 59.4 %collective-permute-done.45.refs_2_ = bf16[256,2048]{1,0:T(8,128)(2,1)} collective-permute-done((bf16[256,2048]{1,0:T(8,128)(2,1)}, bf16[256,2048]{1,0:T(8,128)(2,1)}, u32[]{:S(2)}, u32[]{:S(2)}) %collective-permute-start.45) | collective-permute-done | bytes 1048608 | tf_op jit(solution)/shard_map/ppermute | solution.py:296
  380.5 17.6 %collective-permute-done.38.refs_2_ = bf16[256,2048]{1,0:T(8,128)(2,1)} collective-permute-done((bf16[256,2048]{1,0:T(8,128)(2,1)}, bf16[256,2048]{1,0:T(8,128)(2,1)}, u32[]{:S(2)}, u32[]{:S(2)}) %collective-permute-start.38) | collective-permute-done | bytes 1048608 | tf_op jit(solution)/shard_map/ppermute | solution.py:296
  399.0 21.5 %collective-permute-done.39.refs_3_ = bf16[256,2048]{1,0:T(8,128)(2,1)} collective-permute-done((bf16[256,2048]{1,0:T(8,128)(2,1)}, bf16[256,2048]{1,0:T(8,128)(2,1)}, u32[]{:S(2)}, u32[]{:S(2)}) %collective-permute-start.39) | collective-permute-done | bytes 1048608 | tf_op jit(solution)/shard_map/ppermute | solution.py:296
  427.9 21.5 %collective-permute-done.46.refs_3_ = bf16[256,2048]{1,0:T(8,128)(2,1)S(1)} collective-permute-done((bf16[256,2048]{1,0:T(8,128)(2,1)}, bf16[256,2048]{1,0:T(8,128)(2,1)S(1)}, u32[]{:S(2)}, u32[]{:S(2)}) %collective-permute-start.46) | collective-permute-done | bytes 1048608 | tf_op jit(solution)/shard_map/ppermute | solution.py:296
  452.5 16.6 %collective-permute-done.42.refs_6_ = bf16[256,2048]{1,0:T(8,128)(2,1)S(1)} collective-permute-done((bf16[256,2048]{1,0:T(8,128)(2,1)}, bf16[256,2048]{1,0:T(8,128)(2,1)S(1)}, u32[]{:S(2)}, u32[]{:S(2)}) %collective-permute-start.42) | collective-permute-done | bytes 1048608 | tf_op jit(solution)/shard_map/ppermute | solution.py:297
  472.3 19.3 %collective-permute-done.43.refs_7_ = bf16[256,2048]{1,0:T(8,128)(2,1)S(1)} collective-permute-done((bf16[256,2048]{1,0:T(8,128)(2,1)}, bf16[256,2048]{1,0:T(8,128)(2,1)S(1)}, u32[]{:S(2)}, u32[]{:S(2)}) %collective-permute-start.43) | collective-permute-done | bytes 1048608 | tf_op jit(solution)/shard_map/ppermute | solution.py:297
  492.6 21.3 %shard_map.241 = (bf16[1024,2048]{1,0:T(8,128)(2,1)}, f32[1024,2048]{1,0:T(8,128)}) custom-call(s32[2,8]{1,0:T(2,128)} %stack.87.offs_ref, bf16[1024,2048]{1,0:T(8,128)(2,1)} %pad_maximum_fusion.1.left_ref, bf16[256,2048]{1,0:T(8,128)(2,1)} %bitcast.97.refs_0_, bf16[256,2048]{1,0:T(8,128)(2,1)} %collective-permute-done.37.refs_1_, ...), custom_call_target="tpu_custom_call" | custom-call | flops 8589934592 | bytes 25174016 | tf_op jit(solution)/shard_map/pallas_call | solution.py:402
  514.2 22.5 %collective-permute-done.48.refs_5_ = bf16[256,2048]{1,0:T(8,128)(2,1)} collective-permute-done((bf16[256,2048]{1,0:T(8,128)(2,1)}, bf16[256,2048]{1,0:T(8,128)(2,1)}, u32[]{:S(2)}, u32[]{:S(2)}) %collective-permute-start.48) | collective-permute-done | bytes 1048608 | tf_op jit(solution)/shard_map/ppermute | solution.py:297
  536.6 22.5 %collective-permute-done.49.refs_6_ = bf16[256,2048]{1,0:T(8,128)(2,1)} collective-permute-done((bf16[256,2048]{1,0:T(8,128)(2,1)}, bf16[256,2048]{1,0:T(8,128)(2,1)}, u32[]{:S(2)}, u32[]{:S(2)}) %collective-permute-start.49) | collective-permute-done | bytes 1048608 | tf_op jit(solution)/shard_map/ppermute | solution.py:297
  559.1 21.6 %collective-permute-done.50.refs_7_ = bf16[256,2048]{1,0:T(8,128)(2,1)} collective-permute-done((bf16[256,2048]{1,0:T(8,128)(2,1)S(1)}, bf16[256,2048]{1,0:T(8,128)(2,1)}, u32[]{:S(2)}, u32[]{:S(2)}) %collective-permute-start.50) | collective-permute-done | bytes 1048608 | tf_op jit(solution)/shard_map/ppermute | solution.py:297
  580.7 19.6 %shard_map.243 = (bf16[1024,2048]{1,0:T(8,128)(2,1)}, f32[1,2048]{1,0:T(1,128)}) custom-call(s32[2,8]{1,0:T(2,128)} %stack.87.offs_ref, bf16[1024,2048]{1,0:T(8,128)(2,1)} %pad_maximum_fusion.2.left_ref.right_ref, bf16[256,2048]{1,0:T(8,128)(2,1)} %dynamic-slice_bitcast_fusion.3.refs_0_, bf16[256,2048]{1,0:T(8,128)(2,1)} %collective-permute-done.44.refs_1_, ...), custom_call_target="tpu_custom_call" | custom-call | flops 8589934592 | bytes 25174016 | tf_op jit(solution)/shard_map/pallas_call | solution.py:402
  615.1 16.0 %shard_map.244 = bf16[1024,2048]{1,0:T(8,128)(2,1)} custom-call(s32[2,8]{1,0:T(2,128)} %stack.87.offs_ref, bf16[1024,2048]{1,0:T(8,128)(2,1)} %get-tuple-element.45.left_ref.right_ref, bf16[256,2048]{1,0:T(8,128)(2,1)} %bitcast.97.refs_0_, bf16[256,2048]{1,0:T(8,128)(2,1)} %collective-permute-done.37.refs_1_, ...), custom_call_target="tpu_custom_call" | custom-call | flops 8589934592 | bytes 16777216 | tf_op jit(solution)/shard_map/pallas_call | solution.py:402
  634.1 16.3 %shard_map.242 = bf16[1024,2048]{1,0:T(8,128)(2,1)} custom-call(s32[2,8]{1,0:T(2,128)} %stack.87.offs_ref, bf16[1024,2048]{1,0:T(8,128)(2,1)} %get-tuple-element.43.left_ref, bf16[256,2048]{1,0:T(8,128)(2,1)} %dynamic-slice_bitcast_fusion.3.refs_0_, bf16[256,2048]{1,0:T(8,128)(2,1)} %collective-permute-done.44.refs_1_, ...), custom_call_target="tpu_custom_call" | custom-call | flops 8589934592 | bytes 16777216 | tf_op jit(solution)/shard_map/pallas_call | solution.py:402
  684.5 19.9 %collective-permute-done.84 = bf16[256,2048]{1,0:T(8,128)(2,1)} collective-permute-done((bf16[256,2048]{1,0:T(8,128)(2,1)}, bf16[256,2048]{1,0:T(8,128)(2,1)}, u32[]{:S(2)}, u32[]{:S(2)}) %collective-permute-start.84) | collective-permute-done | bytes 1048608 | tf_op jit(solution)/shard_map/ppermute | solution.py:302
  706.9 42.3 %collective-permute-done.98 = bf16[256,2048]{1,0:T(8,128)(2,1)S(1)} collective-permute-done((bf16[256,2048]{1,0:T(8,128)(2,1)S(1)}, bf16[256,2048]{1,0:T(8,128)(2,1)S(1)}, u32[]{:S(2)}, u32[]{:S(2)}) %collective-permute-start.98) | collective-permute-done | bytes 1048608 | tf_op jit(solution)/shard_map/ppermute | solution.py:302
  750.5 21.2 %collective-permute-done.96 = bf16[256,2048]{1,0:T(8,128)(2,1)S(1)} collective-permute-done((bf16[256,2048]{1,0:T(8,128)(2,1)S(1)}, bf16[256,2048]{1,0:T(8,128)(2,1)S(1)}, u32[]{:S(2)}, u32[]{:S(2)}) %collective-permute-start.96) | collective-permute-done | bytes 1048608 | tf_op jit(solution)/shard_map/ppermute | solution.py:302
  771.7 50.1 %collective-permute-start.89 = (bf16[256,2048]{1,0:T(8,128)(2,1)S(1)}, bf16[256,2048]{1,0:T(8,128)(2,1)S(1)}, u32[]{:S(2)}, u32[]{:S(2)}) collective-permute-start(bf16[256,2048]{1,0:T(8,128)(2,1)S(1)} %add_convert_fusion.5), channel_id=1, source_target_pairs={{0,8},{8,16},{16,24},{24,0},{1,9},{9,17},{17,25},{25,1},{2,10},{10... | collective-permute-start | bytes 3145736 | tf_op jit(solution)/shard_map/ppermute | solution.py:306
  833.5 21.1 %collective-permute-done.57 = bf16[256,2048]{1,0:T(8,128)(2,1)S(1)} collective-permute-done((bf16[256,2048]{1,0:T(8,128)(2,1)S(1)}, bf16[256,2048]{1,0:T(8,128)(2,1)S(1)}, u32[]{:S(2)}, u32[]{:S(2)}) %collective-permute-start.57) | collective-permute-done | bytes 1048608 | tf_op jit(solution)/shard_map/ppermute | solution.py:338
  859.0 34.8 %collective-permute-done.87 = bf16[256,2048]{1,0:T(8,128)(2,1)S(1)} collective-permute-done((bf16[256,2048]{1,0:T(8,128)(2,1)S(1)}, bf16[256,2048]{1,0:T(8,128)(2,1)S(1)}, u32[]{:S(2)}, u32[]{:S(2)}) %collective-permute-start.87) | collective-permute-done | bytes 1048608 | tf_op jit(solution)/shard_map/ppermute | solution.py:306
  893.8 55.6 %collective-permute-start.95 = (bf16[256,2048]{1,0:T(8,128)(2,1)S(1)}, bf16[256,2048]{1,0:T(8,128)(2,1)S(1)}, u32[]{:S(2)}, u32[]{:S(2)}) collective-permute-start(bf16[256,2048]{1,0:T(8,128)(2,1)S(1)} %add_convert_fusion.3), channel_id=1, source_target_pairs={{0,24},{8,0},{16,8},{24,16},{1,25},{9,1},{17,9},{25,17},{2,26},{10... | collective-permute-start | bytes 3145736 | tf_op jit(solution)/shard_map/ppermute | solution.py:306
  957.1 25.1 %collective-permute-done.97 = bf16[256,2048]{1,0:T(8,128)(2,1)S(1)} collective-permute-done((bf16[256,2048]{1,0:T(8,128)(2,1)S(1)}, bf16[256,2048]{1,0:T(8,128)(2,1)S(1)}, u32[]{:S(2)}, u32[]{:S(2)}) %collective-permute-start.97) | collective-permute-done | bytes 1048608 | tf_op jit(solution)/shard_map/ppermute | solution.py:306
  1026.3 15.6 %shard_map.246.left_ref.right_ref = bf16[1024,1536]{1,0:T(8,128)(2,1)} custom-call(bf16[1024,1536]{1,0:T(8,128)(2,1)} %shard_map.238.q_ref.k_ref.v_ref, bf16[1024,1536]{1,0:T(8,128)(2,1)} %shard_map.238.q_ref.k_ref.v_ref, bf16[1024,1536]{1,0:T(8,128)(2,1)} %shard_map.238.q_ref.k_ref.v_ref, bf16[1024,512]{1,0:T(8,128)(2,1)} %pad_maximum_fusion.5.g_ref, ...), custom_call_target="tpu_custom_call" | custom-call | flops 5368709120 | bytes 8388608 | tf_op jit(solution)/shard_map/pallas_call | solution.py:617
  1116.4 23.0 %collective-permute-start.68 = (bf16[256,1536]{1,0:T(8,128)(2,1)S(1)}, bf16[256,1536]{1,0:T(8,128)(2,1)S(1)}, u32[]{:S(2)}, u32[]{:S(2)}) collective-permute-start(bf16[256,1536]{1,0:T(8,128)(2,1)S(1)} %add_convert_fusion.10), channel_id=1, source_target_pairs={{0,8},{8,16},{16,24},{24,0},{1,9},{9,17},{17,25},{25,1},{2,10},{10... | collective-permute-start | bytes 2359304 | tf_op jit(solution)/shard_map/ppermute | solution.py:306
  1145.8 18.2 %collective-permute-start.66 = (bf16[256,1536]{1,0:T(8,128)(2,1)S(1)}, bf16[256,1536]{1,0:T(8,128)(2,1)S(1)}, u32[]{:S(2)}, u32[]{:S(2)}) collective-permute-start(bf16[256,1536]{1,0:T(8,128)(2,1)S(1)} %add_convert_fusion.11), channel_id=1, source_target_pairs={{0,16},{8,24},{16,0},{24,8},{1,17},{9,25},{17,1},{25,9},{2,18},{10... | collective-permute-start | bytes 2359304 | tf_op jit(solution)/shard_map/ppermute | solution.py:306
  1170.4 32.3 %collective-permute-done.66 = bf16[256,1536]{1,0:T(8,128)(2,1)S(1)} collective-permute-done((bf16[256,1536]{1,0:T(8,128)(2,1)S(1)}, bf16[256,1536]{1,0:T(8,128)(2,1)S(1)}, u32[]{:S(2)}, u32[]{:S(2)}) %collective-permute-start.66) | collective-permute-done | bytes 786464 | tf_op jit(solution)/shard_map/ppermute | solution.py:306
  1207.9 16.2 %collective-permute-start.75 = (bf16[128,1024]{1,0:T(8,128)(2,1)S(1)}, bf16[128,1024]{1,0:T(8,128)(2,1)S(1)}, u32[]{:S(2)}, u32[]{:S(2)}) collective-permute-start(bf16[128,1024]{1,0:T(8,128)(2,1)S(1)} %get-tuple-element.104), channel_id=1, source_target_pairs={{0,24},{8,0},{16,8},{24,16},{1,25},{9,1},{17,9},{25,17},{2,26},{10... | collective-permute-start | bytes 786440 | tf_op jit(solution)/shard_map/ppermute | solution.py:306
  1239.8 34.6 %collective-permute-done.81.refs_2_ = bf16[128,1024]{1,0:T(8,128)(2,1)S(1)} collective-permute-done((bf16[128,1024]{1,0:T(8,128)(2,1)S(1)}, bf16[128,1024]{1,0:T(8,128)(2,1)S(1)}, u32[]{:S(2)}, u32[]{:S(2)}) %collective-permute-start.81) | collective-permute-done | bytes 262176 | tf_op jit(solution)/shard_map/ppermute | solution.py:313
  1309.4 117.6 %all-reduce.4.cloned.1.call-done = f32[8,2304]{1,0:T(8,128)} async-done(((f32[8,2304]{1,0:T(8,128)}), f32[8,2304]{1,0:T(8,128)}) %all-reduce.4.cloned.1.call-update) | async-done | bytes 73744 | tf_op jit(solution)/shard_map/psum | solution.py:1005
  (466 shorter events, 515.5 us)
Async XLA Ops:
  7.2 1419.8 %all-reduce.4.cloned.1.call-start = ((), (), s32[]{:S(2)}) async-start(), calls=%async_computation | async-start | bytes 147456 | tf_op jit(solution)/shard_map/psum | solution.py:1005
  49.0 67.5 %collective-permute-start.12 = (bf16[256,1536]{1,0:T(8,128)(2,1)}, bf16[256,1536]{1,0:T(8,128)(2,1)}, u32[]{:S(2)}, u32[]{:S(2)}) collective-permute-start(bf16[256,1536]{1,0:T(8,128)(2,1)} %reshape.583.refs_0_), channel_id=1, source_target_pairs={{0,24},{8,0},{16,8},{24,16},{1,25},{9,1},{17,9},{25,17},{2,26},{10... | collective-permute-start | bytes 2359304 | tf_op jit(solution)/shard_map/ppermute | solution.py:296
  123.9 70.8 %collective-permute-start.19 = (bf16[128,1024]{1,0:T(8,128)(2,1)S(1)}, bf16[128,1024]{1,0:T(8,128)(2,1)S(1)}, u32[]{:S(2)}, u32[]{:S(2)}) collective-permute-start(bf16[128,1024]{1,0:T(8,128)(2,1)S(1)} %bitcast.225), channel_id=1, source_target_pairs={{0,16},{8,24},{16,0},{24,8},{1,17},{9,25},{17,1},{25,9},{2,18},{10... | collective-permute-start | bytes 786440 | tf_op jit(solution)/shard_map/ppermute | solution.py:296
  127.1 68.3 %collective-permute-start.20 = (bf16[128,1024]{1,0:T(8,128)(2,1)S(1)}, bf16[128,1024]{1,0:T(8,128)(2,1)S(1)}, u32[]{:S(2)}, u32[]{:S(2)}) collective-permute-start(bf16[128,1024]{1,0:T(8,128)(2,1)S(1)} %bitcast.226), channel_id=1, source_target_pairs={{0,24},{8,0},{16,8},{24,16},{1,25},{9,1},{17,9},{25,17},{2,26},{10... | collective-permute-start | bytes 786440 | tf_op jit(solution)/shard_map/ppermute | solution.py:296
  267.8 107.8 %collective-permute-start.45 = (bf16[256,2048]{1,0:T(8,128)(2,1)}, bf16[256,2048]{1,0:T(8,128)(2,1)}, u32[]{:S(2)}, u32[]{:S(2)}) collective-permute-start(bf16[256,2048]{1,0:T(8,128)(2,1)} %dynamic-slice_bitcast_fusion.3.refs_0_), channel_id=1, source_target_pairs={{0,16},{8,24},{16,0},{24,8},{1,17},{9,25},{17,1},{25,9},{2,18},{10... | collective-permute-start | bytes 3145736 | tf_op jit(solution)/shard_map/ppermute | solution.py:296
  268.1 107.5 %collective-permute-start.55 = (bf16[256,2048]{1,0:T(8,128)(2,1)}, bf16[256,2048]{1,0:T(8,128)(2,1)}, u32[]{:S(2)}, u32[]{:S(2)}) collective-permute-start(bf16[256,2048]{1,0:T(8,128)(2,1)} %collective-permute-done.54), channel_id=1, source_target_pairs={{0,1},{1,0},{2,3},{3,2},{4,5},{5,4},{6,7},{7,6},{8,9},{9,8},{10,11... | collective-permute-start | bytes 3145736 | tf_op jit(solution)/shard_map/ppermute | solution.py:314
  272.0 103.6 %collective-permute-start.35 = (bf16[256,2048]{1,0:T(8,128)(2,1)}, bf16[256,2048]{1,0:T(8,128)(2,1)}, u32[]{:S(2)}, u32[]{:S(2)}) collective-permute-start(bf16[256,2048]{1,0:T(8,128)(2,1)} %add_convert_fusion.8), channel_id=1, source_target_pairs={{0,2},{2,0},{1,3},{3,1},{4,6},{6,4},{5,7},{7,5},{8,10},{10,8},{9,1... | collective-permute-start | bytes 3145736 | tf_op jit(solution)/shard_map/ppermute | solution.py:313
  290.0 89.2 %collective-permute-start.37 = (bf16[256,2048]{1,0:T(8,128)(2,1)}, bf16[256,2048]{1,0:T(8,128)(2,1)}, u32[]{:S(2)}, u32[]{:S(2)}) collective-permute-start(bf16[256,2048]{1,0:T(8,128)(2,1)} %bitcast.97.refs_0_), channel_id=1, source_target_pairs={{0,8},{8,16},{16,24},{24,0},{1,9},{9,17},{17,25},{25,1},{2,10},{10... | collective-permute-start | bytes 3145736 | tf_op jit(solution)/shard_map/ppermute | solution.py:296
  295.2 102.9 %collective-permute-start.38 = (bf16[256,2048]{1,0:T(8,128)(2,1)}, bf16[256,2048]{1,0:T(8,128)(2,1)}, u32[]{:S(2)}, u32[]{:S(2)}) collective-permute-start(bf16[256,2048]{1,0:T(8,128)(2,1)} %bitcast.97.refs_0_), channel_id=1, source_target_pairs={{0,16},{8,24},{16,0},{24,8},{1,17},{9,25},{17,1},{25,9},{2,18},{10... | collective-permute-start | bytes 3145736 | tf_op jit(solution)/shard_map/ppermute | solution.py:296
  379.2 70.1 %collective-permute-start.46 = (bf16[256,2048]{1,0:T(8,128)(2,1)}, bf16[256,2048]{1,0:T(8,128)(2,1)S(1)}, u32[]{:S(2)}, u32[]{:S(2)}) collective-permute-start(bf16[256,2048]{1,0:T(8,128)(2,1)} %dynamic-slice_bitcast_fusion.3.refs_0_), channel_id=1, source_target_pairs={{0,24},{8,0},{16,8},{24,16},{1,25},{9,1},{17,9},{25,17},{2,26},{10... | collective-permute-start | bytes 3145736 | tf_op jit(solution)/shard_map/ppermute | solution.py:296
  424.7 66.9 %collective-permute-start.43 = (bf16[256,2048]{1,0:T(8,128)(2,1)}, bf16[256,2048]{1,0:T(8,128)(2,1)S(1)}, u32[]{:S(2)}, u32[]{:S(2)}) collective-permute-start(bf16[256,2048]{1,0:T(8,128)(2,1)} %collective-permute-done.39.refs_3_), channel_id=1, source_target_pairs={{0,4},{4,0},{1,5},{5,1},{2,6},{6,2},{3,7},{7,3},{8,12},{12,8},{9,1... | collective-permute-start | bytes 3145736 | tf_op jit(solution)/shard_map/ppermute | solution.py:297
  450.5 86.1 %collective-permute-start.48 = (bf16[256,2048]{1,0:T(8,128)(2,1)}, bf16[256,2048]{1,0:T(8,128)(2,1)}, u32[]{:S(2)}, u32[]{:S(2)}) collective-permute-start(bf16[256,2048]{1,0:T(8,128)(2,1)} %collective-permute-done.44.refs_1_), channel_id=1, source_target_pairs={{0,4},{4,0},{1,5},{5,1},{2,6},{6,2},{3,7},{7,3},{8,12},{12,8},{9,1... | collective-permute-start | bytes 3145736 | tf_op jit(solution)/shard_map/ppermute | solution.py:297
  451.4 107.7 %collective-permute-start.49 = (bf16[256,2048]{1,0:T(8,128)(2,1)}, bf16[256,2048]{1,0:T(8,128)(2,1)}, u32[]{:S(2)}, u32[]{:S(2)}) collective-permute-start(bf16[256,2048]{1,0:T(8,128)(2,1)} %collective-permute-done.45.refs_2_), channel_id=1, source_target_pairs={{0,4},{4,0},{1,5},{5,1},{2,6},{6,2},{3,7},{7,3},{8,12},{12,8},{9,1... | collective-permute-start | bytes 3145736 | tf_op jit(solution)/shard_map/ppermute | solution.py:297
  469.1 111.6 %collective-permute-start.50 = (bf16[256,2048]{1,0:T(8,128)(2,1)S(1)}, bf16[256,2048]{1,0:T(8,128)(2,1)}, u32[]{:S(2)}, u32[]{:S(2)}) collective-permute-start(bf16[256,2048]{1,0:T(8,128)(2,1)S(1)} %collective-permute-done.46.refs_3_), channel_id=1, source_target_pairs={{0,4},{4,0},{1,5},{5,1},{2,6},{6,2},{3,7},{7,3},{8,12},{12,8},{9,1... | collective-permute-start | bytes 3145736 | tf_op jit(solution)/shard_map/ppermute | solution.py:297
  633.0 189.2 %collective-permute-start.56 = (bf16[2,256,2048]{2,1,0:T(8,128)(2,1)S(1)}, bf16[2,256,2048]{2,1,0:T(8,128)(2,1)}, u32[]{:S(2)}, u32[]{:S(2)}) collective-permute-start(bf16[2,256,2048]{2,1,0:T(8,128)(2,1)S(1)} %dynamic-slice_bitcast_fusion.1), channel_id=1, source_target_pairs={{0,1},{1,0},{2,3},{3,2},{4,5},{5,4},{6,7},{7,6},{8,9},{9,8},{10,11... | collective-permute-start | bytes 6291464 | tf_op jit(solution)/shard_map/ppermute | solution.py:335
  652.2 176.2 %collective-permute-start.51 = (bf16[2,256,2048]{2,1,0:T(8,128)(2,1)S(1)}, bf16[2,256,2048]{2,1,0:T(8,128)(2,1)}, u32[]{:S(2)}, u32[]{:S(2)}) collective-permute-start(bf16[2,256,2048]{2,1,0:T(8,128)(2,1)S(1)} %dynamic-slice_bitcast_fusion.2), channel_id=1, source_target_pairs={{0,1},{1,0},{2,3},{3,2},{4,5},{5,4},{6,7},{7,6},{8,9},{9,8},{10,11... | collective-permute-start | bytes 6291464 | tf_op jit(solution)/shard_map/ppermute | solution.py:335
  669.4 186.3 %collective-permute-start.83 = (bf16[256,2048]{1,0:T(8,128)(2,1)}, bf16[256,2048]{1,0:T(8,128)(2,1)S(1)}, u32[]{:S(2)}, u32[]{:S(2)}) collective-permute-start(bf16[256,2048]{1,0:T(8,128)(2,1)} %get-tuple-element.57), channel_id=1, source_target_pairs={{0,4},{4,0},{1,5},{5,1},{2,6},{6,2},{3,7},{7,3},{8,12},{12,8},{9,1... | collective-permute-start | bytes 3145736 | tf_op jit(solution)/shard_map/ppermute | solution.py:302
  681.9 67.3 %collective-permute-start.98 = (bf16[256,2048]{1,0:T(8,128)(2,1)S(1)}, bf16[256,2048]{1,0:T(8,128)(2,1)S(1)}, u32[]{:S(2)}, u32[]{:S(2)}) collective-permute-start(bf16[256,2048]{1,0:T(8,128)(2,1)S(1)} %copy-done.50), channel_id=1, source_target_pairs={{0,4},{4,0},{1,5},{5,1},{2,6},{6,2},{3,7},{7,3},{8,12},{12,8},{9,1... | collective-permute-start | bytes 3145736 | tf_op jit(solution)/shard_map/ppermute | solution.py:302
  704.4 67.3 %collective-permute-start.96 = (bf16[256,2048]{1,0:T(8,128)(2,1)S(1)}, bf16[256,2048]{1,0:T(8,128)(2,1)S(1)}, u32[]{:S(2)}, u32[]{:S(2)}) collective-permute-start(bf16[256,2048]{1,0:T(8,128)(2,1)S(1)} %copy-done.49), channel_id=1, source_target_pairs={{0,4},{4,0},{1,5},{5,1},{2,6},{6,2},{3,7},{7,3},{8,12},{12,8},{9,1... | collective-permute-start | bytes 3145736 | tf_op jit(solution)/shard_map/ppermute | solution.py:302
  749.2 82.2 %collective-permute-start.94 = (bf16[256,2048]{1,0:T(8,128)(2,1)S(1)}, bf16[256,2048]{1,0:T(8,128)(2,1)S(1)}, u32[]{:S(2)}, u32[]{:S(2)}) collective-permute-start(bf16[256,2048]{1,0:T(8,128)(2,1)S(1)} %copy-done.47), channel_id=1, source_target_pairs={{0,4},{4,0},{1,5},{5,1},{2,6},{6,2},{3,7},{7,3},{8,12},{12,8},{9,1... | collective-permute-start | bytes 3145736 | tf_op jit(solution)/shard_map/ppermute | solution.py:302
  771.7 85.3 %collective-permute-start.89 = (bf16[256,2048]{1,0:T(8,128)(2,1)S(1)}, bf16[256,2048]{1,0:T(8,128)(2,1)S(1)}, u32[]{:S(2)}, u32[]{:S(2)}) collective-permute-start(bf16[256,2048]{1,0:T(8,128)(2,1)S(1)} %add_convert_fusion.5), channel_id=1, source_target_pairs={{0,8},{8,16},{16,24},{24,0},{1,9},{9,17},{17,25},{25,1},{2,10},{10... | collective-permute-start | bytes 3145736 | tf_op jit(solution)/shard_map/ppermute | solution.py:306
  822.3 71.6 %collective-permute-start.87 = (bf16[256,2048]{1,0:T(8,128)(2,1)S(1)}, bf16[256,2048]{1,0:T(8,128)(2,1)S(1)}, u32[]{:S(2)}, u32[]{:S(2)}) collective-permute-start(bf16[256,2048]{1,0:T(8,128)(2,1)S(1)} %add_convert_fusion.6), channel_id=1, source_target_pairs={{0,16},{8,24},{16,0},{24,8},{1,17},{9,25},{17,1},{25,9},{2,18},{10... | collective-permute-start | bytes 3145736 | tf_op jit(solution)/shard_map/ppermute | solution.py:306
  854.5 99.6 %collective-permute-start.85 = (bf16[256,2048]{1,0:T(8,128)(2,1)S(1)}, bf16[256,2048]{1,0:T(8,128)(2,1)S(1)}, u32[]{:S(2)}, u32[]{:S(2)}) collective-permute-start(bf16[256,2048]{1,0:T(8,128)(2,1)S(1)} %add_convert_fusion.7), channel_id=1, source_target_pairs={{0,24},{8,0},{16,8},{24,16},{1,25},{9,1},{17,9},{25,17},{2,26},{10... | collective-permute-start | bytes 3145736 | tf_op jit(solution)/shard_map/ppermute | solution.py:306
  855.7 100.3 %collective-permute-start.93 = (bf16[256,2048]{1,0:T(8,128)(2,1)S(1)}, bf16[256,2048]{1,0:T(8,128)(2,1)S(1)}, u32[]{:S(2)}, u32[]{:S(2)}) collective-permute-start(bf16[256,2048]{1,0:T(8,128)(2,1)S(1)} %copy-done.42), channel_id=1, source_target_pairs={{0,4},{4,0},{1,5},{5,1},{2,6},{6,2},{3,7},{7,3},{8,12},{12,8},{9,1... | collective-permute-start | bytes 3145736 | tf_op jit(solution)/shard_map/ppermute | solution.py:302
  857.0 99.6 %collective-permute-start.99 = (bf16[256,2048]{1,0:T(8,128)(2,1)S(1)}, bf16[256,2048]{1,0:T(8,128)(2,1)S(1)}, u32[]{:S(2)}, u32[]{:S(2)}) collective-permute-start(bf16[256,2048]{1,0:T(8,128)(2,1)S(1)} %add_convert_fusion.1), channel_id=1, source_target_pairs={{0,8},{8,16},{16,24},{24,0},{1,9},{9,17},{17,25},{25,1},{2,10},{10... | collective-permute-start | bytes 3145736 | tf_op jit(solution)/shard_map/ppermute | solution.py:306
  893.8 88.4 %collective-permute-start.97 = (bf16[256,2048]{1,0:T(8,128)(2,1)S(1)}, bf16[256,2048]{1,0:T(8,128)(2,1)S(1)}, u32[]{:S(2)}, u32[]{:S(2)}) collective-permute-start(bf16[256,2048]{1,0:T(8,128)(2,1)S(1)} %add_convert_fusion.2), channel_id=1, source_target_pairs={{0,16},{8,24},{16,0},{24,8},{1,17},{9,25},{17,1},{25,9},{2,18},{10... | collective-permute-start | bytes 3145736 | tf_op jit(solution)/shard_map/ppermute | solution.py:306
  893.8 88.7 %collective-permute-start.95 = (bf16[256,2048]{1,0:T(8,128)(2,1)S(1)}, bf16[256,2048]{1,0:T(8,128)(2,1)S(1)}, u32[]{:S(2)}, u32[]{:S(2)}) collective-permute-start(bf16[256,2048]{1,0:T(8,128)(2,1)S(1)} %add_convert_fusion.3), channel_id=1, source_target_pairs={{0,24},{8,0},{16,8},{24,16},{1,25},{9,1},{17,9},{25,17},{2,26},{10... | collective-permute-start | bytes 3145736 | tf_op jit(solution)/shard_map/ppermute | solution.py:306
  956.1 122.6 %collective-permute-start.90 = (bf16[256,2048]{1,0:T(8,128)(2,1)}, bf16[256,2048]{1,0:T(8,128)(2,1)}, u32[]{:S(2)}, u32[]{:S(2)}) collective-permute-start(bf16[256,2048]{1,0:T(8,128)(2,1)} %add_convert_fusion.4.refs_0_), channel_id=1, source_target_pairs={{0,1},{1,0},{2,3},{3,2},{4,5},{5,4},{6,7},{7,6},{8,9},{9,8},{10,11... | collective-permute-start | bytes 3145736 | tf_op jit(solution)/shard_map/ppermute | solution.py:314
  956.6 122.7 %collective-permute-start.91 = (bf16[256,2048]{1,0:T(8,128)(2,1)}, bf16[256,2048]{1,0:T(8,128)(2,1)}, u32[]{:S(2)}, u32[]{:S(2)}) collective-permute-start(bf16[256,2048]{1,0:T(8,128)(2,1)} %add_convert_fusion.4.refs_0_), channel_id=1, source_target_pairs={{0,2},{2,0},{1,3},{3,1},{4,6},{6,4},{5,7},{7,5},{8,10},{10,8},{9,1... | collective-permute-start | bytes 3145736 | tf_op jit(solution)/shard_map/ppermute | solution.py:313
  1071.2 97.8 %collective-permute-start.60 = (bf16[2,256,2048]{2,1,0:T(8,128)(2,1)S(1)}, bf16[2,256,2048]{2,1,0:T(8,128)(2,1)S(1)}, u32[]{:S(2)}, u32[]{:S(2)}) collective-permute-start(bf16[2,256,2048]{2,1,0:T(8,128)(2,1)S(1)} %dynamic-slice_bitcast_fusion), channel_id=1, source_target_pairs={{0,1},{1,0},{2,3},{3,2},{4,5},{5,4},{6,7},{7,6},{8,9},{9,8},{10,11... | collective-permute-start | bytes 6291464 | tf_op jit(solution)/shard_map/ppermute | solution.py:335
  1078.7 85.7 %collective-permute-start.101 = (bf16[256,2048]{1,0:T(8,128)(2,1)}, bf16[256,2048]{1,0:T(8,128)(2,1)}, u32[]{:S(2)}, u32[]{:S(2)}) collective-permute-start(bf16[256,2048]{1,0:T(8,128)(2,1)} %add_convert_fusion.refs_0_), channel_id=1, source_target_pairs={{0,2},{2,0},{1,3},{3,1},{4,6},{6,4},{5,7},{7,5},{8,10},{10,8},{9,1... | collective-permute-start | bytes 3145736 | tf_op jit(solution)/shard_map/ppermute | solution.py:313
  1204.4 80.1 %collective-permute-start.102 = (bf16[256,2048]{1,0:T(8,128)(2,1)}, bf16[256,2048]{1,0:T(8,128)(2,1)}, u32[]{:S(2)}, u32[]{:S(2)}) collective-permute-start(bf16[256,2048]{1,0:T(8,128)(2,1)} %collective-permute-done.101.refs_2_), channel_id=1, source_target_pairs={{0,1},{1,0},{2,3},{3,2},{4,5},{5,4},{6,7},{7,6},{8,9},{9,8},{10,11... | collective-permute-start | bytes 3145736 | tf_op jit(solution)/shard_map/ppermute | solution.py:314
  (140 other events, 4139.6 us)
Sparse Core Ops, SparseCore 0:
  1300.1 126.8 all-reduce.3

commit v2 on v1

--- a/solution.py
+++ b/solution.py
@@ -282,35 +282,48 @@
     )
 
 
-def piece_owner(zi, xi, z_count):
-    return [
-        lax.rem(zi - j + z_count, z_count) * 2 + jnp.bitwise_xor(xi, dx)
-        for dx in range(2)
-        for j in range(z_count)
-    ]
-
-
-def gather_pieces(shard, z_count):
-    line = [shard]
+def gather_small(vector, z_count):
+    line = [vector]
     for j in range(1, z_count):
-        line.append(lax.ppermute(shard, "z", [(i, (i + j) % z_count) for i in range(z_count)]))
+        line.append(lax.ppermute(vector, "z", [(i, (i + j) % z_count) for i in range(z_count)]))
     return line + [lax.ppermute(piece, "x", SWAP) for piece in line]
 
 
-def reduce_pieces(pieces, z_count):
-    wide = jnp.float32
-    far = [lax.ppermute(piece, "x", SWAP) for piece in pieces[z_count:]]
-    total = pieces[0].astype(wide) + far[0].astype(wide)
-    for j in range(1, z_count):
-        part = (pieces[j].astype(wide) + far[j].astype(wide)).astype(jnp.bfloat16)
-        total = total + lax.ppermute(
-            part, "z", [(i, (i - j) % z_count) for i in range(z_count)]
-        ).astype(wide)
-    return total.astype(jnp.bfloat16)
-
-
-def seq_pieces(block):
-    other = lax.ppermute(block, "y", SWAP)
+def gather_weight(shard, *others):
+    near = lax.all_gather(shard, "z", axis=0, tiled=False)
+    return [near, lax.ppermute(after(near, *others), "x", SWAP)]
+
+
+def stage(flag, work, *args):
+    shapes = jax.eval_shape(work, *args)
+
+    def nothing(*_):
+        return jax.tree.map(lambda a: jnp.zeros(a.shape, a.dtype), shapes)
+
+    return lax.cond(flag, work, nothing, *args)
+
+
+class Line:
+    def __init__(self):
+        self.last = ()
+
+    def enter(self, value):
+        return after(value, *self.last)
+
+    def leave(self, *results):
+        self.last = results[:1]
+        return results
+
+
+def after(value, *others):
+    return lax.optimization_barrier((value,) + others)[0]
+
+
+def seq_pieces(block, *others):
+    return core_pieces(block, after(lax.ppermute(block, "y", SWAP), *others))
+
+
+def core_pieces(block, other):
     return [block, lax.ppermute(block, "c", SWAP), other, lax.ppermute(other, "c", SWAP)]
 
 
@@ -318,8 +331,8 @@
     return jnp.where(bit == 0, mine, theirs), jnp.where(bit == 0, theirs, mine)
 
 
-def gather_tokens(block, yi, ci):
-    parts = seq_pieces(block)
+def gather_tokens(block, yi, ci, *others):
+    parts = seq_pieces(block, *others)
     near = by_bit(ci, parts[0], parts[1])
     far = by_bit(ci, parts[2], parts[3])
     rows = [jnp.where(yi == 0, n, f) for n, f in zip(near, far)]
@@ -327,15 +340,34 @@
     return jnp.concatenate(rows, axis=0)
 
 
-def scatter_tokens(partial, yi, ci):
+def core_sum(partial, yi, ci):
     tokens = partial.shape[0] // 4
     parts = partial.reshape(2, 2, tokens, partial.shape[1])
     away = lax.dynamic_index_in_dim(parts, 1 - ci, 1, keepdims=False)
     home = lax.dynamic_index_in_dim(parts, ci, 1, keepdims=False)
     total = home.astype(jnp.float32) + lax.ppermute(away, "c", SWAP).astype(jnp.float32)
     away = lax.dynamic_index_in_dim(total, 1 - yi, 0, keepdims=False).astype(jnp.bfloat16)
-    home = lax.dynamic_index_in_dim(total, yi, 0, keepdims=False)
-    return home + lax.ppermute(away, "y", SWAP).astype(jnp.float32)
+    return lax.dynamic_index_in_dim(total, yi, 0, keepdims=False), away
+
+
+def home_sum(home, other):
+    return home + other.astype(jnp.float32)
+
+
+def scatter_tokens(partial, yi, ci, *others):
+    home, away = core_sum(partial, yi, ci)
+    return home_sum(home, after(lax.ppermute(away, "y", SWAP), *others))
+
+
+COST_SCALE = 0.01
+
+
+def cost(flops, bytes_accessed, transcendentals):
+    return pl.CostEstimate(
+        flops=int(flops * COST_SCALE),
+        bytes_accessed=int(bytes_accessed * COST_SCALE),
+        transcendentals=int(transcendentals * COST_SCALE),
+    )
 
 
 def params(limit=VMEM_LIMIT):
@@ -344,15 +376,17 @@
 
 def load_weight(offsets, pieces, held, sems):
     copies = []
-    for p, piece in enumerate(pieces):
-        rows, cols = piece.shape
-        row = pl.multiple_of(offsets[0, p], rows)
-        col = pl.multiple_of(offsets[1, p], cols)
-        copies.append(
-            pltpu.make_async_copy(
-                piece, held.at[pl.ds(row, rows), pl.ds(col, cols)], sems.at[p]
+    for piece in pieces:
+        count, rows, cols = piece.shape
+        for k in range(count):
+            b = len(copies)
+            row = pl.multiple_of(offsets[0, b], rows)
+            col = pl.multiple_of(offsets[1, b], cols)
+            copies.append(
+                pltpu.make_async_copy(
+                    piece.at[k], held.at[pl.ds(row, rows), pl.ds(col, cols)], sems.at[b]
+                )
             )
-        )
     for copy in copies:
         copy.start()
     for copy in copies:
@@ -410,11 +444,11 @@
             out_specs=[tile_spec(*a.shape) for a in outs],
             scratch_shapes=[
                 pltpu.VMEM((depth, width), jnp.bfloat16),
-                pltpu.SemaphoreType.DMA((n_pieces,)),
+                pltpu.SemaphoreType.DMA((sum(p.shape[0] for p in pieces),)),
             ],
         ),
         out_shape=list(outs),
-        cost_estimate=pl.CostEstimate(flops=flops, bytes_accessed=moved, transcendentals=0),
+        cost_estimate=cost(flops=flops, bytes_accessed=moved, transcendentals=0),
         compiler_params=params(),
     )(offsets, left, *pieces, *extras)
 
@@ -450,60 +484,115 @@
         sums[:, cols] += column_sum
 
 
-def weight_grad(left, right, owners, block):
-    rows, depth = left.shape
-    width = right.shape[1]
-    count = depth // block
-
-    def kernel(owner_ref, left_ref, right_ref, *refs):
-        outs, held, sems = refs[:count], refs[count], refs[count + 1]
-        step = pl.program_id(0)
-        slot = lax.rem(step, 2)
-
-        @pl.when(step >= 2)
-        def _():
-            pltpu.make_async_copy(held.at[slot], outs[0], sems.at[slot]).wait()
-
-        held[slot] = lax.dot_general(
-            left_ref[...],
-            right_ref[...],
-            (((0,), (0,)), ((), ())),
-            preferred_element_type=jnp.float32,
-        ).astype(jnp.bfloat16)
-        for k in range(count):
-
-            @pl.when(step == k)
-            def _():
-                pltpu.make_async_copy(held.at[slot], outs[k], sems.at[slot]).start()
-
-        @pl.when(step == count - 1)
-        def _():
-            pltpu.make_async_copy(held.at[1 - slot], outs[0], sems.at[1 - slot]).wait()
-            pltpu.make_async_copy(held.at[slot], outs[0], sems.at[slot]).wait()
-
+def weight_grad(left, right, where, count, block, width, *addends):
+    rows = left.shape[0]
+    parts = max(len(addends), 1)
+    part = width // parts
+
+    def kernel(where_ref, left_ref, right_ref, *refs):
+        for n in range(parts):
+            cols = slice(n * part, (n + 1) * part)
+            value = lax.dot_general(
+                left_ref[...],
+                right_ref[:, cols],
+                (((0,), (0,)), ((), ())),
+                preferred_element_type=jnp.float32,
+            )
+            if addends:
+                value = value + refs[n][0].astype(jnp.float32)
+            refs[-1][0, :, cols] = value.astype(jnp.bfloat16)
+
+    piece = pl.BlockSpec((1, block, width), lambda k, at: (k, 0, 0))
     return pl.pallas_call(
         kernel,
         grid_spec=pltpu.PrefetchScalarGridSpec(
             num_scalar_prefetch=1,
             grid=(count,),
             in_specs=[
-                pl.BlockSpec((rows, block), lambda k, owner: (0, owner[k])),
-                pl.BlockSpec((rows, width), lambda k, owner: (0, 0)),
-            ],
-            out_specs=[pl.BlockSpec(memory_space=pl.ANY)] * count,
-            scratch_shapes=[
-                pltpu.VMEM((2, block, width), jnp.bfloat16),
-                pltpu.SemaphoreType.DMA((2,)),
-            ],
+                pl.BlockSpec((rows, block), lambda k, at: (0, at[k])),
+                pl.BlockSpec((rows, width), lambda k, at: (0, at[count])),
+            ]
+            + [pl.BlockSpec((1, block, part), lambda k, at: (k, 0, 0))] * len(addends),
+            out_specs=piece,
         ),
-        out_shape=[jax.ShapeDtypeStruct((block, width), jnp.bfloat16)] * count,
-        cost_estimate=pl.CostEstimate(
-            flops=2 * rows * depth * width,
-            bytes_accessed=2 * (left.size + right.size + depth * width),
+        out_shape=jax.ShapeDtypeStruct((count, block, width), jnp.bfloat16),
+        cost_estimate=cost(
+            flops=2 * rows * count * block * width,
+            bytes_accessed=2 * rows * (count * block + width)
+            + 4 * count * block * width,
             transcendentals=0,
         ),
         compiler_params=params(),
-    )(owners, left, right)
+    )(where, left, right, *addends)
+
+
+def slice_weights(w_qkv, w_out, w_up, w_down, yi, ci, shard_count):
+    rows, model = w_out.shape
+    heads = H // 4
+    ff_part = w_down.shape[0] // 4
+    half = 3 * heads * HD // 2
+    steps = shard_count
+    part = ff_part // steps
+
+    def kernel(at_ref, qkv_ref, out_ref, up_ref, down_ref, *to):
+        y, c = at_ref[0], at_ref[1]
+        step = pl.program_id(0)
+        for n in range(2):
+            qkv_to, up_to = to[n], to[3 + n]
+
+            @pl.when(step == n)
+            def _():
+                for i in range(half // HD):
+                    head = n * (half // HD) + i
+                    col = (head // heads) * H + 2 * (head % heads) + c + 2 * heads * y
+                    col = pl.ds(pl.multiple_of(col * HD, HD), HD)
+                    qkv_to[:, i * HD : (i + 1) * HD] = qkv_ref[:, col]
+
+            @pl.when(step // (steps // 2) == n)
+            def _():
+                up_to[...] = up_ref[...]
+
+        @pl.when(step == 0)
+        def _():
+            to[2][...] = out_ref[...]
+
+        to[5][...] = down_ref[...]
+
+    def pair(block, index):
+        return [pl.BlockSpec(block, functools.partial(index, n)) for n in range(2)]
+
+    up_half = steps // 2
+    return pl.pallas_call(
+        kernel,
+        grid_spec=pltpu.PrefetchScalarGridSpec(
+            num_scalar_prefetch=1,
+            grid=(steps,),
+            in_specs=[
+                pl.BlockSpec((rows, 3 * model), lambda i, at: (0, 0)),
+                pl.BlockSpec((rows // 2, model // 2), lambda i, at: (at[1], at[0])),
+                pl.BlockSpec((rows, ff_part), lambda i, at: (0, 4 * i + 2 * at[0] + at[1])),
+                pl.BlockSpec(
+                    (part, model), lambda i, at: ((2 * at[0] + at[1]) * steps + i, 0)
+                ),
+            ],
+            out_specs=pair((rows, half), lambda n, i, at: (0, 0))
+            + [pl.BlockSpec((rows // 2, model // 2), lambda i, at: (0, 0))]
+            + pair(
+                (rows, ff_part),
+                lambda n, i, at: (0, jnp.clip(i - n * up_half, 0, up_half - 1)),
+            )
+            + [pl.BlockSpec((part, model), lambda i, at: (i, 0))],
+        ),
+        out_shape=[
+            jax.ShapeDtypeStruct(shape, jnp.bfloat16)
+            for shape in [(rows, half)] * 2
+            + [(rows // 2, model // 2)]
+            + [(rows, ff_part * up_half)] * 2
+            + [(ff_part, model)]
+        ],
+        cost_estimate=cost(flops=0, bytes_accessed=12 << 20, transcendentals=0),
+        compiler_params=params(),
+    )(jnp.stack([yi, ci]).astype(jnp.int32), w_qkv, w_out, w_up, w_down)
 
 
 def visible_tile(query_item, key_item, first_query, n_query, n_key):
@@ -555,7 +644,7 @@
             jax.ShapeDtypeStruct((length, heads * HD), jnp.bfloat16),
             jax.ShapeDtypeStruct((heads, length, 1), jnp.float32),
         ],
-        cost_estimate=pl.CostEstimate(
+        cost_estimate=cost(
             flops=4 * heads * length * length * HD,
             bytes_accessed=8 * length * heads * HD,
             transcendentals=heads * length * length,
@@ -627,7 +716,7 @@
         out_specs=whole(length, 3 * heads * HD),
         out_shape=jax.ShapeDtypeStruct((length, 3 * heads * HD), jnp.bfloat16),
         scratch_shapes=[pltpu.VMEM((length, HD), jnp.float32)] * 2,
-        cost_estimate=pl.CostEstimate(
+        cost_estimate=cost(
             flops=10 * heads * length * length * HD,
             bytes_accessed=16 * length * heads * HD,
             transcendentals=heads * length * length,
@@ -636,39 +725,44 @@
     )(projected, projected, projected, mixed_grad, log_total, query_item, key_item)
 
 
-def widen(pieces, places, grid, piece_block, out_block, out_index, out_shape, write):
+def widen(chunks, places, grid, piece_specs, out_block, out_index, out_shape, write):
     def kernel(place_ref, *refs):
-        for r in range(4):
-            write(place_ref[r], refs[r], refs[4])
+        for n in range(len(chunks)):
+            for r in range(4):
+                write(n, place_ref[r], refs[4 * n + r], refs[-1])
 
     return pl.pallas_call(
         kernel,
         grid_spec=pltpu.PrefetchScalarGridSpec(
             num_scalar_prefetch=1,
             grid=(grid,),
-            in_specs=[pl.BlockSpec(piece_block[0], lambda i, pos: piece_block[1](i))] * 4,
+            in_specs=[
+                pl.BlockSpec(block, functools.partial(lambda at, i, pos: at(i), at))
+                for block, at in piece_specs
+                for _ in range(4)
+            ],
             out_specs=pl.BlockSpec(out_block, lambda i, pos: out_index(i)),
         ),
         out_shape=jax.ShapeDtypeStruct(out_shape, jnp.float32),
-        cost_estimate=pl.CostEstimate(
+        cost_estimate=cost(
             flops=0, bytes_accessed=6 * int(np.prod(out_shape)), transcendentals=0
         ),
         compiler_params=params(),
-    )(places, *pieces)
+    )(places, *[piece for pieces in chunks for piece in pieces])
 
 
 def widen_columns(pieces, places, blocks):
     rows, width = pieces[0].shape
     part = width // blocks
 
-    def write(pos, piece, out):
+    def write(n, pos, piece, out):
         out[:, pl.ds(pl.multiple_of(pos * part, part), part)] = piece[...].astype(jnp.float32)
 
     return widen(
-        pieces,
+        [pieces],
         places,
         blocks,
-        ((rows, part), lambda i: (0, i)),
+        [((rows, part), lambda i: (0, i))],
         (rows, 4 * part),
         lambda i: (0, i),
         (rows, 4 * width),
@@ -679,16 +773,16 @@
 def widen_rows(pieces, places):
     rows, width = pieces[0].shape
 
-    def write(pos, piece, out):
+    def write(n, pos, piece, out):
         @pl.when(pos == pl.program_id(0))
         def _():
             out[...] = piece[...].astype(jnp.float32)
 
     return widen(
-        pieces,
+        [pieces],
         places,
         4,
-        ((rows, width), lambda i: (0, 0)),
+        [((rows, width), lambda i: (0, 0))],
         (rows, width),
         lambda i: (i, 0),
         (4 * rows, width),
@@ -700,17 +794,17 @@
     rows, width = pieces[0].shape
     part = width // 3
 
-    def write(pos, piece, out):
+    def write(n, pos, piece, out):
         first = lax.div(pos, 2) * part * 2 + lax.rem(pos, 2) * HD
         for i in range(part // HD):
             cols = pl.ds(pl.multiple_of(first + 2 * i * HD, HD), HD)
             out[:, cols] = piece[:, i * HD : (i + 1) * HD].astype(jnp.float32)
 
     return widen(
-        pieces,
+        [pieces],
         places,
         3,
-        ((rows, part), lambda i: (0, i)),
+        [((rows, part), lambda i: (0, i))],
         (rows, 4 * part),
         lambda i: (0, i),
         (rows, 4 * width),
@@ -721,16 +815,16 @@
 def widen_quarters(pieces, places):
     rows, width = pieces[0].shape
 
-    def write(pos, piece, out):
+    def write(n, pos, piece, out):
         row = pl.multiple_of(lax.rem(pos, 2) * rows, rows)
         col = pl.multiple_of(lax.div(pos, 2) * width, width)
         out[pl.ds(row, rows), pl.ds(col, width)] = piece[...].astype(jnp.float32)
 
     return widen(
-        pieces,
+        [pieces],
         places,
         1,
-        ((rows, width), lambda i: (0, 0)),
+        [((rows, width), lambda i: (0, 0))],
         (2 * rows, 2 * width),
         lambda i: (0, 0),
         (2 * rows, 2 * width),
@@ -777,12 +871,17 @@
     ff_part = ff_piece // 4
     ff_here = ff_part * shard_count
     heads = H // 4
-    owners = jnp.stack(piece_owner(zi, xi, z_count)).astype(jnp.int32)
-    zeros = jnp.zeros_like(owners)
     places = jnp.stack([jnp.bitwise_xor(si, r) for r in range(4)]).astype(jnp.int32)
 
     packed = jnp.concatenate([ln1_gain, ln1_shift, ln2_gain, ln2_shift, down_bias, up_bias])
-    vector_stack = jnp.stack(gather_pieces(packed, z_count))
+    vector_stack = jnp.stack(gather_small(packed, z_count))
+    owners = jnp.stack(
+        [
+            lax.rem(zi - j + z_count, z_count) * 2 + jnp.bitwise_xor(xi, dx)
+            for dx in range(2)
+            for j in range(z_count)
+        ]
+    )
     hit = owners[None, :] == jnp.arange(shard_count, dtype=jnp.int32)[:, None]
     vector_table = jnp.sum(jnp.where(hit[:, :, None], vector_stack[None], 0.0), axis=1)
 
@@ -794,220 +893,360 @@
         vector_table[:, 5 * piece_d :].reshape(shard_count, 4, ff_part), si, 1, keepdims=False
     ).reshape(1, ff_here)
 
-    qkv_slice = w_qkv.reshape(piece_d, 3, 2, heads, 2, HD)
-    qkv_slice = lax.dynamic_index_in_dim(qkv_slice, yi, 2, keepdims=False)
-    qkv_slice = lax.dynamic_index_in_dim(qkv_slice, ci, 3, keepdims=False)
-    qkv_slice = qkv_slice.reshape(piece_d, 3 * heads * HD)
-    out_slice = w_out.reshape(2, piece_d // 2, 2, model // 2)
-    out_slice = lax.dynamic_index_in_dim(out_slice, yi, 2, keepdims=False)
-    out_slice = lax.dynamic_index_in_dim(out_slice, ci, 0, keepdims=False)
-    up_slice = lax.dynamic_index_in_dim(
-        w_up.reshape(piece_d, shard_count, 4, ff_part), si, 2, keepdims=False
-    ).reshape(piece_d, ff_here)
-    down_slice = lax.dynamic_index_in_dim(
-        w_down.reshape(4, ff_part, model), si, 0, keepdims=False
-    )
-
-    qkv_parts = gather_pieces(qkv_slice, z_count)
-    out_parts = gather_pieces(out_slice, z_count)
+    line = Line()
+    flag = item_lengths[0, 0] > 0
+    slices = slice_weights(w_qkv, w_out, w_up, w_down, yi, ci, shard_count)
+    half = model // 2
+    qkv_width = 3 * heads * HD
+    qkv_parts = gather_weight(slices[0]) + gather_weight(slices[1])
+    down_pair = jnp.stack([slices[5], lax.ppermute(slices[5], "x", SWAP)])
+    inputs = after(block_input, down_pair).reshape(tok_count, model).astype(wide)
+    normed_one = layer_norm(inputs, gain_one, shift_one).astype(low)
+    out_parts = gather_weight(after(slices[2], normed_one), qkv_parts[1])
     out_parts = out_parts + [lax.ppermute(piece, "y", SWAP) for piece in out_parts]
-    up_parts = gather_pieces(up_slice, z_count)
-    down_parts = gather_pieces(down_slice, z_count)
-    row_offsets = jnp.stack([owners * piece_d, zeros])
-    out_offsets = jnp.stack(
-        [
-            jnp.concatenate([owners, owners]) * (piece_d // 2),
-            jnp.concatenate([zeros + yi, zeros + 1 - yi]) * (model // 2),
-        ]
-    )
-    ff_offsets = jnp.stack([owners * ff_part, zeros])
+
+    near_blocks = [2 * z + xi for z in range(z_count)]
+    far_blocks = [2 * z + 1 - xi for z in range(z_count)]
+    split = near_blocks + far_blocks
+    paired = [b for pair in zip(near_blocks, far_blocks) for b in pair]
+    zero = jnp.zeros_like(xi)
+
+    def table(*rows):
+        return jnp.stack([jnp.stack(row) for row in rows]).astype(jnp.int32)
+
+    def halves_at(first, second, rows, width):
+        return table(
+            [b * rows for b in first + second],
+            [zero] * shard_count + [zero + width] * shard_count,
+        )
+
+    qkv_offsets = halves_at(split, split, piece_d, qkv_width // 2)
+    up_offsets = halves_at(split, split, piece_d, ff_here // 2)
+    down_offsets = table([b * ff_part for b in paired], [zero] * shard_count)
+    out_offsets = table(
+        [b * (piece_d // 2) for b in split] * 2,
+        [yi * half] * shard_count + [(1 - yi) * half] * shard_count,
+    )
+
+    def blocks_at(blocks, n):
+        return table(blocks + [zero + n])[0]
+
+    def sum_small(terms):
+        def term(j):
+            return lax.dynamic_index_in_dim(
+                terms, lax.rem(zi - j + z_count, z_count), 0, keepdims=False
+            )
+
+        total = term(0).astype(wide)
+        for j in range(1, z_count):
+            total = total + lax.ppermute(
+                term(j), "z", [(i, (i - j) % z_count) for i in range(z_count)]
+            ).astype(wide)
+        return total
+
+    def plain_matmul(left, pieces, offsets, shape, back, body, extras, outs):
+        return weight_matmul(left, pieces, offsets, shape, back, body, extras, outs, 256, 512)
+
+    def matmul(left, *others):
+        return line.leave(*plain_matmul(line.enter(left), *others))
+
+    def grad_chunk(left, right, blocks, n, block, width, *addends):
+        return line.leave(
+            weight_grad(
+                line.enter(left), right, blocks_at(blocks, n), len(blocks), block, width, *addends
+            )
+        )[0]
+
+    def far_terms(left, right, block):
+        terms = grad_chunk(left, right, far_blocks, 0, block, right.shape[1])
+        return lax.ppermute(terms, "x", SWAP)
+
+    def near_terms(left, right, block, addend):
+        width = right.shape[1]
+        return weight_grad(
+            left, right, blocks_at(near_blocks, 0), z_count, block, width, addend
+        )
+
+    def sum_over_z(total):
+        return lax.psum_scatter(total, "z", scatter_dimension=0, tiled=False)
 
     def shape(rows, cols, kind=low):
         return jax.ShapeDtypeStruct((rows, cols), kind)
 
-    inputs = block_input.reshape(tok_count, model).astype(wide)
-    normed_one = gather_tokens(layer_norm(inputs, gain_one, shift_one).astype(low), yi, ci)
-    (projected,) = weight_matmul(
-        normed_one,
+    normed_one = gather_tokens(normed_one, yi, ci, qkv_parts[0])
+    cot_flat = after(cotangent.reshape(tok_count, model), normed_one)
+    cot_wide = cot_flat.astype(wide)
+    cot_all = gather_tokens(cot_flat, yi, ci, qkv_parts[2])
+    (projected,) = matmul(
+        after(normed_one, cot_all),
         qkv_parts,
-        row_offsets,
-        (model, 3 * heads * HD),
+        qkv_offsets,
+        (model, qkv_width),
         False,
         store_low,
         (),
-        (shape(length, 3 * heads * HD),),
-        256,
-        512,
-    )
+        (shape(length, qkv_width),),
+    )
+    up_parts = gather_weight(slices[3], projected)
+    up_high = lax.all_gather(slices[4], "z", axis=0, tiled=False)
+    down_parts = [lax.all_gather(down_pair, "z", axis=0, tiled=True)]
     positions = jnp.arange(length, dtype=jnp.int32)
     item_label = item_numbers(item_starts[0], item_lengths[0], positions)
     query_item = item_label[:, None]
     key_item = jnp.where((item_label >= 0) & (pad_mask[0] == 1), item_label, -2)[None, :]
-    mixed_heads, log_total = attention(projected, query_item, key_item, heads, 256)
-    halves = mixed_heads.reshape(2, 2 * tok_count, heads * HD)
-    away = lax.dynamic_index_in_dim(halves, 1 - yi, 0, keepdims=False)
-    home = lax.dynamic_index_in_dim(halves, yi, 0, keepdims=False)
-    mixed = jnp.concatenate(by_bit(yi, home, lax.ppermute(away, "y", SWAP)), axis=1)
-    (out_partial,) = weight_matmul(
-        mixed,
-        out_parts,
-        out_offsets,
-        (model // 2, model),
-        False,
-        store_low,
-        (),
-        (shape(2 * tok_count, model),),
-        256,
-        512,
-    )
-    halves = out_partial.reshape(2, tok_count, model)
-    away = lax.dynamic_index_in_dim(halves, 1 - ci, 0, keepdims=False)
-    home = lax.dynamic_index_in_dim(halves, ci, 0, keepdims=False)
-    residual_one = (
-        inputs + home.astype(wide) + lax.ppermute(away, "c", SWAP).astype(wide)
-    )
-    normed_two = gather_tokens(
-        layer_norm(residual_one, gain_two, shift_two).astype(low), yi, ci
-    )
-    activated, slope = weight_matmul(
+    mixed_heads, log_total = line.leave(
+        *attention(line.enter(projected), query_item, key_item, heads, 256)
+    )
+
+    def attend_out(mixed_heads):
+        halves = mixed_heads.reshape(2, 2 * tok_count, heads * HD)
+        away = lax.dynamic_index_in_dim(halves, 1 - yi, 0, keepdims=False)
+        mine = lax.dynamic_index_in_dim(halves, yi, 0, keepdims=False)
+        other = lax.ppermute(away, "y", SWAP)
+        mixed = jnp.concatenate(by_bit(yi, mine, other), axis=1)
+        (out_partial,) = plain_matmul(
+            mixed,
+            out_parts,
+            out_offsets,
+            (half, model),
+            False,
+            store_low,
+            (),
+            (shape(2 * tok_count, model),),
+        )
+        halves = out_partial.reshape(2, tok_count, model)
+        away = lax.dynamic_index_in_dim(halves, 1 - ci, 0, keepdims=False)
+        home = lax.dynamic_index_in_dim(halves, ci, 0, keepdims=False)
+        residual_one = (
+            inputs + home.astype(wide) + lax.ppermute(away, "c", SWAP).astype(wide)
+        )
+        normed_two = layer_norm(residual_one, gain_two, shift_two).astype(low)
+        return normed_two, residual_one, mine, other
+
+    normed_two, residual_one, mixed_home, mixed_other = line.leave(
+        *stage(flag, attend_out, after(line.enter(mixed_heads), up_parts[0]))
+    )
+    normed_two = after(normed_two, up_high)
+    up_parts += [up_high, lax.ppermute(after(up_high, normed_two), "x", SWAP)]
+    normed_two = gather_tokens(normed_two, yi, ci, up_parts[1])
+    mixed_last = lax.ppermute(after(mixed_home, normed_two), "y", SWAP)
+    others_heads = jnp.concatenate(by_bit(yi, mixed_other, mixed_last), axis=0)
+    mixed = jnp.concatenate(by_bit(yi, mixed_heads, others_heads), axis=1)
+    activated, slope = matmul(
         normed_two,
         up_parts,
-        row_offsets,
+        up_offsets,
         (model, ff_here),
         False,
         store_gelu,
         (bias_up,),
         (shape(length, ff_here), shape(length, ff_here, wide)),
-        256,
-        512,
-    )
-    (down_partial,) = weight_matmul(
-        activated,
-        down_parts,
-        ff_offsets,
-        (ff_here, model),
-        False,
-        store_low,
-        (),
-        (shape(length, model),),
-        256,
-        512,
-    )
-    block_output = residual_one + scatter_tokens(down_partial, yi, ci) + bias_down
-    output_shard = block_output.astype(low).reshape(1, tok_count, model)
-
-    cot_flat = cotangent.reshape(tok_count, model)
-    cot_wide = cot_flat.astype(wide)
-    cot_all = gather_tokens(cot_flat, yi, ci)
+    )
+
     down_bias_part = jnp.sum(cot_wide, axis=0)
-    down_grads = weight_grad(activated, cot_all, owners, ff_part)
-    down_shard = reduce_pieces(down_grads, z_count)
-    hidden_grad, up_bias_part = weight_matmul(
+    down_far = far_terms(after(activated, mixed), cot_all, ff_part)
+    hidden_grad, up_bias_part = matmul(
         cot_all,
         down_parts,
-        ff_offsets,
+        down_offsets,
         (ff_here, model),
         True,
         store_hidden_grad,
         (slope,),
         (shape(length, ff_here), shape(1, ff_here, wide)),
-        256,
-        512,
-    )
-    (norm_two_partial,) = weight_matmul(
+    )
+    up_far = far_terms(normed_two, hidden_grad, piece_d)
+    (norm_two_partial,) = matmul(
         hidden_grad,
         up_parts,
-        row_offsets,
+        up_offsets,
         (model, ff_here),
         True,
         store_low,
         (),
         (shape(length, model),),
-        256,
-        512,
-    )
-    up_grads = weight_grad(normed_two, hidden_grad, owners, piece_d)
-    up_shard = reduce_pieces(up_grads, z_count)
-    norm_two_grad = scatter_tokens(norm_two_partial, yi, ci)
-    resid_part, gain_two_grad, shift_two_grad = norm_back(residual_one, gain_two, norm_two_grad)
-    residual_grad = cot_wide + resid_part
-    branch_grad = residual_grad.astype(low)
-    branch_pair = jnp.concatenate(
-        by_bit(ci, branch_grad, lax.ppermute(branch_grad, "c", SWAP)), axis=0
-    )
-    (mixed_grad_pair,) = weight_matmul(
-        branch_pair,
-        out_parts,
-        out_offsets,
-        (model // 2, model),
-        True,
-        store_low,
-        (),
-        (shape(2 * tok_count, model // 2),),
-        256,
-        512,
-    )
-    halves = mixed_grad_pair.reshape(2 * tok_count, 2, heads * HD)
-    away = lax.dynamic_index_in_dim(halves, 1 - yi, 1, keepdims=False)
-    home = lax.dynamic_index_in_dim(halves, yi, 1, keepdims=False)
-    mixed_grad = jnp.concatenate(by_bit(yi, home, lax.ppermute(away, "y", SWAP)), axis=0)
-    out_grad = contract_rows(mixed, branch_pair).astype(low)
-    out_grad = out_grad.reshape(shard_count, piece_d // 2, 2, model // 2)
-    away = lax.dynamic_index_in_dim(out_grad, 1 - yi, 2, keepdims=False)
-    home = lax.dynamic_index_in_dim(out_grad, yi, 2, keepdims=False)
-    out_grad = (home.astype(wide) + lax.ppermute(away, "y", SWAP).astype(wide)).astype(low)
-    out_grads = [
-        lax.dynamic_index_in_dim(out_grad, owners[k], 0, keepdims=False)
-        for k in range(shard_count)
-    ]
-    out_shard = reduce_pieces(out_grads, z_count)
-    proj_grad = attention_back(
-        projected, mixed_grad, log_total, query_item, key_item, heads, 256
-    )
-    qkv_grads = weight_grad(normed_one, proj_grad, owners, piece_d)
-    qkv_shard = reduce_pieces(qkv_grads, z_count)
-    (norm_one_partial,) = weight_matmul(
+    )
+    (down_sum,) = line.leave(
+        near_terms(line.enter(activated), cot_all, ff_part, down_far)
+    )
+    down_shard = sum_over_z(down_sum)
+
+    def norm_two_back(norm_two_partial):
+        norm_two_grad = scatter_tokens(norm_two_partial, yi, ci)
+        resid_part, gain_two_grad, shift_two_grad = norm_back(
+            residual_one, gain_two, norm_two_grad
+        )
+        residual_grad = cot_wide + resid_part
+        branch_grad = residual_grad.astype(low)
+        branch_pair = jnp.concatenate(
+            by_bit(ci, branch_grad, lax.ppermute(branch_grad, "c", SWAP)), axis=0
+        )
+        return branch_pair, residual_grad, gain_two_grad, shift_two_grad
+
+    branch_pair, residual_grad, gain_two_grad, shift_two_grad = line.leave(
+        *stage(flag, norm_two_back, line.enter(norm_two_partial))
+    )
+
+    out_blocks = far_blocks + near_blocks
+
+    def out_back(branch_pair):
+        (mixed_grad_pair,) = plain_matmul(
+            branch_pair,
+            out_parts,
+            out_offsets,
+            (half, model),
+            True,
+            store_low,
+            (),
+            (shape(2 * tok_count, half),),
+        )
+        part = heads * HD
+        away = lax.dynamic_slice_in_dim(mixed_grad_pair, (1 - yi) * part, part, 1)
+        home = lax.dynamic_slice_in_dim(mixed_grad_pair, yi * part, part, 1)
+        theirs = lax.ppermute(away, "y", SWAP)
+        return jnp.concatenate(by_bit(yi, home, theirs), axis=0)
+
+    (mixed_grad,) = line.leave(stage(flag, out_back, line.enter(branch_pair)))
+    away = lax.dynamic_slice_in_dim(branch_pair, (1 - yi) * half, half, 1)
+    home = lax.dynamic_slice_in_dim(branch_pair, yi * half, half, 1)
+    branch_other = lax.ppermute(after(away, mixed_grad), "y", SWAP)
+    branch_all = jnp.concatenate(by_bit(yi, home, branch_other), axis=0)
+    (proj_grad,) = line.leave(
+        attention_back(
+            projected,
+            line.enter(mixed_grad),
+            log_total,
+            query_item,
+            key_item,
+            heads,
+            256,
+        )
+    )
+    qkv_far = far_terms(normed_one, proj_grad, piece_d)
+    (up_sum,) = line.leave(
+        near_terms(line.enter(after(normed_two, branch_other)), hidden_grad, piece_d, up_far)
+    )
+    up_shard = sum_over_z(up_sum)
+    (norm_one_partial,) = matmul(
         proj_grad,
         qkv_parts,
-        row_offsets,
-        (model, 3 * heads * HD),
+        qkv_offsets,
+        (model, qkv_width),
         True,
         store_low,
         (),
         (shape(length, model),),
-        256,
-        512,
-    )
-    norm_one_grad = scatter_tokens(norm_one_partial, yi, ci)
-    input_part, gain_one_grad, shift_one_grad = norm_back(inputs, gain_one, norm_one_grad)
-    input_grad = (residual_grad + input_part).reshape(1, tok_count, model)
-
-    up_bias_grad = jnp.where(
-        (jnp.arange(4, dtype=jnp.int32) == si)[None, :, None],
-        up_bias_part.reshape(shard_count, 1, ff_part),
-        0.0,
-    ).reshape(shard_count, ff_piece)
-    vector_grad = jnp.concatenate(
-        [
-            part.reshape(shard_count, -1)
-            for part in (
-                gain_one_grad,
-                shift_one_grad,
-                gain_two_grad,
-                shift_two_grad,
-                down_bias_part,
-                up_bias_grad,
-            )
-        ],
-        axis=1,
-    )
-    vector_total = lax.dynamic_index_in_dim(
-        lax.psum(vector_grad, ("z", "x", "y", "c")), 2 * zi + xi, 0, keepdims=False
-    )
-    down_total = widen_rows(seq_pieces(down_shard), places)
-    up_total = widen_columns(seq_pieces(up_shard), places, shard_count)
-    out_total = widen_quarters(seq_pieces(out_shard), places)
-    qkv_total = widen_heads(seq_pieces(qkv_shard), places)
+    )
+
+    out_sum = line.leave(
+        weight_grad(
+            line.enter(mixed),
+            branch_all,
+            blocks_at(out_blocks, 0),
+            shard_count,
+            piece_d // 2,
+            half,
+        )
+    )[0]
+    down_other = lax.ppermute(after(down_shard, mixed_grad), "y", SWAP)
+
+    def norm_one_back(norm_one_partial):
+        home, away = core_sum(norm_one_partial, yi, ci)
+        (down_partial,) = plain_matmul(
+            after(activated, away),
+            down_parts,
+            down_offsets,
+            (ff_here, model),
+            False,
+            store_low,
+            (),
+            (shape(length, model),),
+        )
+        away = lax.ppermute(away, "y", SWAP)
+        norm_one_grad = home_sum(home, after(away, down_partial))
+        input_part, gain_one_grad, shift_one_grad = norm_back(inputs, gain_one, norm_one_grad)
+        input_grad = (residual_grad + input_part).reshape(1, tok_count, model)
+        feed_home, feed_away = core_sum(down_partial, yi, ci)
+        return (
+            input_grad,
+            gain_one_grad,
+            shift_one_grad,
+            feed_home,
+            feed_away,
+        )
+
+    (
+        input_grad,
+        gain_one_grad,
+        shift_one_grad,
+        feed_home,
+        feed_away,
+    ) = line.leave(
+        *stage(flag, norm_one_back, after(line.enter(norm_one_partial), down_other))
+    )
+    (qkv_sum,) = line.leave(
+        near_terms(
+            after(line.enter(normed_one), up_shard), proj_grad, piece_d, qkv_far
+        )
+    )
+    qkv_shard = sum_over_z(qkv_sum)
+
+    def ends(up_shard):
+        feed_other = lax.ppermute(feed_away, "y", SWAP)
+        up_other = lax.ppermute(up_shard, "y", SWAP)
+        feed_out = home_sum(feed_home, feed_other)
+        output_shard = (residual_one + feed_out + bias_down).astype(low)
+        output_shard = output_shard.reshape(1, tok_count, model)
+        out_away = lax.ppermute(out_sum[:z_count], "x", SWAP)
+        out_shard = sum_small(
+            (out_sum[z_count:].astype(wide) + out_away.astype(wide)).astype(low)
+        ).astype(low)
+        up_bias_grad = jnp.where(
+            (jnp.arange(4, dtype=jnp.int32) == si)[None, :, None],
+            up_bias_part.reshape(shard_count, 1, ff_part),
+            0.0,
+        ).reshape(shard_count, ff_piece)
+        vector_grad = jnp.concatenate(
+            [
+                part.reshape(shard_count, -1)
+                for part in (
+                    gain_one_grad,
+                    shift_one_grad,
+                    gain_two_grad,
+                    shift_two_grad,
+                    down_bias_part,
+                    up_bias_grad,
+                )
+            ],
+            axis=1,
+        )
+        for name in ("c", "y"):
+            vector_grad = vector_grad + lax.ppermute(vector_grad, name, SWAP)
+        vector_grad = vector_grad.reshape(z_count, 2, -1)
+        away = lax.dynamic_index_in_dim(vector_grad, 1 - xi, 1, keepdims=False)
+        home = lax.dynamic_index_in_dim(vector_grad, xi, 1, keepdims=False)
+        vector_grad = home + lax.ppermute(away, "x", SWAP)
+        vector_total = sum_small(vector_grad)
+        up_pieces = core_pieces(up_shard, up_other)
+        return (
+            output_shard,
+            vector_total,
+            out_shard,
+            widen_columns(up_pieces, places, shard_count),
+        )
+
+    output_shard, vector_total, out_shard, up_total = line.leave(
+        *stage(flag, ends, line.enter(up_shard))
+    )
+
+    def last(qkv_shard):
+        return (
+            widen_heads(seq_pieces(qkv_shard), places),
+            widen_quarters(seq_pieces(out_shard), places),
+            widen_rows(core_pieces(down_shard, down_other), places),
+        )
+
+    qkv_total, out_total, down_total = stage(flag, last, after(qkv_shard, up_total))
     vectors = [vector_total[slot * piece_d : (slot + 1) * piece_d] for slot in range(5)]
     return (
         output_shard,

time: 1450 us -> 813 us (0.56)
  waiting for transfers between devices: 757 us -> 371 us
  starting transfers between devices: 298 us -> 58.3 us
  local copies, waits for them, and re-layouts: 88.1 us -> 40.8 us
  Pallas kernels: 209 us -> 232 us
  loops' own time: 0 us -> 14.7 us
    ppermute x95 -> x59, waiting for transfers between devices: 607 us -> 352 us  [the longest x5 69.6 us: seq_pieces(): return core_pieces(block, after(lax.ppermute(block, 'y', SWAP), *others))]
    ppermute x95 -> x59, starting transfers between devices: 292 us -> 54.9 us  [the longest x6 11.1 us: sum_small(): lax.ppermute(term(j), 'z', [(i, (i - j) % z_count) for i in range(z_count)])]
    psum x1 -> x0, waiting for transfers between devices: 118 us -> none  [split_shards(): lax.psum(vector_grad, ('z', 'x', 'y', 'c'))]
    ppermute x8 -> x2, waiting for transfers between devices: 32.5 us -> 0.01 us  [split_shards(): lax.ppermute(piece, 'y', SWAP)]
    reshape x11 -> x6, local copies, waits for them, and re-layouts: 28.5 us -> 0.07 us  [the longest x1 0.05 us: ends(): vector_grad = vector_grad.reshape(z_count, 2, -1)]
    dynamic_slice x6 -> x4, local copies, waits for them, and re-layouts: 30.1 us -> 2.58 us  [the longest x1 1.32 us: split_shards(): away = lax.dynamic_slice_in_dim(branch_pair, (1 - yi) * half, half, 1)]
    pallas_call x3 -> x7, Pallas kernels: 42.6 us -> 64.3 us  [weight_grad(): pl.pallas_call(kernel, grid_spec=pltpu.PrefetchScalarGridSpec(num_scalar_...]
    all_gather x0 -> x6, waiting for transfers between devices: none -> 17 us  [the longest x4 9.64 us: gather_weight(): near = lax.all_gather(shard, 'z', axis=0, tiled=False)]
  transfers between devices with their start and end apart: 104 -> 70, of which waited for: 48 -> 39; matrix products, arithmetic and copies ran while one was open for 10% -> 13% of each run, Pallas kernels for 11% -> 25%
where the time goes in v2:
time: 813 us; the launch traced here: 810 us
  waiting for transfers between devices  371 us (46%)
  Pallas kernels  232 us (29%)
  other arithmetic  78.6 us (10%)
  starting transfers between devices  58.3 us (7%)
  local copies, waits for them, and re-layouts  40.8 us (5%)
  loops' own time  14.7 us (2%)
  between operations  14.7 us (2%)
    pallas_call x8, Pallas kernels, weight_matmul(): pl.pallas_call(kernel, grid_spec=pltpu.PrefetchScalarGridSpec(num_scalar_...  112 us
    ppermute x5, waiting for transfers between devices, seq_pieces(): return core_pieces(block, after(lax.ppermute(block, 'y', SWAP), *others))  69.6 us
    pallas_call x7, Pallas kernels, weight_grad(): pl.pallas_call(kernel, grid_spec=pltpu.PrefetchScalarGridSpec(num_scalar_...  64.3 us
    ppermute x4, waiting for transfers between devices, gather_weight(): return [near, lax.ppermute(after(near, *others), 'x', SWAP)]  63.6 us
    ppermute x1, waiting for transfers between devices, split_shards(): up_parts += [up_high, lax.ppermute(after(up_high, normed_two), 'x', SWAP)]  39.1 us
    ppermute x3, waiting for transfers between devices, far_terms(): return lax.ppermute(terms, 'x', SWAP)  38.4 us
    ppermute x6, waiting for transfers between devices, sum_small(): lax.ppermute(term(j), 'z', [(i, (i - j) % z_count) for i in range(z_count)])  22.7 us
    pallas_call x4, Pallas kernels, widen(): pl.pallas_call(kernel, grid_spec=pltpu.PrefetchScalarGridSpec(num_scalar_...  20.4 us
  transfers between devices with their start and end apart: 70, of which 39 were waited for; matrix products, arithmetic and copies ran while one was open for 13% of the time, Pallas kernels for 25%

profile of v2, /device:TPU:0, one launch (start us, length us, event | category | flops | bytes accessed | tf_op | source)
XLA Modules:
  0.0 809.7 jit_solution(12015377554335517938)
XLA Ops:
  29.5 13.6 %collective-permute-done.35 = f32[2304]{0:T(1024)S(1)} collective-permute-done((f32[2304]{0:T(1024)S(1)}, f32[2304]{0:T(1024)S(1)}, u32[]{:S(2)}, u32[]{:S(2)}) %collective-permute-start.35) | collective-permute-done | bytes 9248 | tf_op jit(solution)/shard_map/ppermute | solution.py:289
  52.2 22.9 %collective-permute-done.40 = bf16[256,2048]{1,0:T(8,128)(2,1)} collective-permute-done((bf16[256,2048]{1,0:T(8,128)(2,1)}, bf16[256,2048]{1,0:T(8,128)(2,1)}, u32[]{:S(2)}, u32[]{:S(2)}) %collective-permute-start.40) | collective-permute-done | bytes 1048608 | tf_op jit(solution)/shard_map/ppermute | solution.py:323
  84.6 27.4 %collective-permute-done.45.refs_1_ = bf16[4,256,768]{2,1,0:T(8,128)(2,1)S(1)} collective-permute-done((bf16[4,256,768]{2,1,0:T(8,128)(2,1)}, bf16[4,256,768]{2,1,0:T(8,128)(2,1)S(1)}, u32[]{:S(2)}, u32[]{:S(2)}) %collective-permute-start.45) | collective-permute-done | bytes 1572896 | tf_op jit(solution)/shard_map/ppermute | solution.py:294
  113.5 9.6 %all-gather.16.cloned.1.call-done = bf16[1024,768]{1,0:T(8,128)(2,1)} async-done(((bf16[256,768]{1,0:T(8,128)(2,1)}), bf16[1024,768]{1,0:T(8,128)(2,1)}) %all-gather.16.cloned.1.call-update) | async-done | bytes 1572880 | tf_op jit(solution)/shard_map/all_gather | solution.py:293
  126.9 11.5 %collective-permute-done.47 = bf16[4,128,1024]{2,1,0:T(8,128)(2,1)} collective-permute-done((bf16[4,128,1024]{2,1,0:T(8,128)(2,1)}, bf16[4,128,1024]{2,1,0:T(8,128)(2,1)}, u32[]{:S(2)}, u32[]{:S(2)}) %collective-permute-start.47) | collective-permute-done | bytes 1048608 | tf_op jit(solution)/shard_map/ppermute | solution.py:294
  146.3 24.6 %collective-permute-done.46.refs_3_ = bf16[4,256,768]{2,1,0:T(8,128)(2,1)} collective-permute-done((bf16[4,256,768]{2,1,0:T(8,128)(2,1)}, bf16[4,256,768]{2,1,0:T(8,128)(2,1)}, u32[]{:S(2)}, u32[]{:S(2)}) %collective-permute-start.46) | collective-permute-done | bytes 1572896 | tf_op jit(solution)/shard_map/ppermute | solution.py:294
  171.0 13.1 %shard_map.239.q_ref.k_ref.v_ref = bf16[1024,1536]{1,0:T(8,128)(2,1)} custom-call(s32[2,16]{1,0:T(2,128)} %get-tuple-element.401.offs_ref, bf16[1024,2048]{1,0:T(8,128)(2,1)} %pad_maximum_fusion.3.left_ref, bf16[4,256,768]{2,1,0:T(8,128)(2,1)} %bitcast.175, bf16[4,256,768]{2,1,0:T(8,128)(2,1)} %copy-done.13, bf16[4,256,768]{2,1,0:T(8,128)(2,1)} %bitcast.178, ...), custom_call_target="tpu_custom_call" | custom-call | flops 64424508 | bytes 136314 | tf_op jit(solution)/shard_map/pallas_call | solution.py:436
  187.8 11.4 %shard_map.240 = (bf16[1024,512]{1,0:T(8,128)(2,1)}, f32[4,1024,1]{2,1,0:T(8,128)}) custom-call(bf16[1024,1536]{1,0:T(8,128)(2,1)} %shard_map.239.q_ref.k_ref.v_ref, bf16[1024,1536]{1,0:T(8,128)(2,1)} %shard_map.239.q_ref.k_ref.v_ref, bf16[1024,1536]{1,0:T(8,128)(2,1)} %shard_map.239.q_ref.k_ref.v_ref, s32[1024,1]{1,0:T(8,128)} %copy.35.qi_ref, ...), custom_call_target="tpu_custom_call" | custom-call | flops 21474836 | bytes 41943 | tf_op jit(solution)/shard_map/pallas_call | solution.py:637
  199.2 49.9 %conditional.6 = (bf16[256,2048]{1,0:T(8,128)(2,1)}, f32[256,2048]{1,0:T(8,128)}, bf16[512,512]{1,0:T(8,128)(2,1)S(1)}, bf16[512,512]{1,0:T(8,128)(2,1)S(1)}) conditional(s32[]{:T(128)} %bitcast.33, () %tuple.105, (s32[]{:T(128)}, bf16[1024,512]{1,0:T(8,128)(2,1)}, s32[2,16]{1,0:T(2,128)S(1)}, bf16[4,128,1024]{2,1,0:T(8,128)(2,1)}, ...), branch_computations={%region_4.5_spmd, %region_5.8_spmd} | conditional | flops 30912284 | bytes 39470188 | solution.py:303
  215.3 11.0 %collective-permute-done.9 = bf16[512,512]{1,0:T(8,128)(2,1)S(1)} collective-permute-done((bf16[512,512]{1,0:T(8,128)(2,1)S(1)}, bf16[512,512]{1,0:T(8,128)(2,1)S(1)}, u32[]{:S(2)}, u32[]{:S(2)}) %collective-permute-start.9) | collective-permute-done | bytes 524320 | tf_op jit(solution)/shard_map/cond/branch_1_fun/ppermute | solution.py:1005
  250.7 23.9 %collective-permute-done.51 = bf16[256,2048]{1,0:T(8,128)(2,1)S(1)} collective-permute-done((bf16[256,2048]{1,0:T(8,128)(2,1)}, bf16[256,2048]{1,0:T(8,128)(2,1)S(1)}, u32[]{:S(2)}, u32[]{:S(2)}) %collective-permute-start.51) | collective-permute-done | bytes 1048608 | tf_op jit(solution)/shard_map/ppermute | solution.py:323
  283.8 39.1 %collective-permute-done.54.refs_3_ = bf16[4,256,1024]{2,1,0:T(8,128)(2,1)} collective-permute-done((bf16[4,256,1024]{2,1,0:T(8,128)(2,1)}, bf16[4,256,1024]{2,1,0:T(8,128)(2,1)}, u32[]{:S(2)}, u32[]{:S(2)}) %collective-permute-start.54) | collective-permute-done | bytes 2097184 | tf_op jit(solution)/shard_map/ppermute | solution.py:1030
  322.9 20.9 %shard_map.241 = (bf16[1024,2048]{1,0:T(8,128)(2,1)S(1)}, f32[1024,2048]{1,0:T(8,128)}) custom-call(s32[2,16]{1,0:T(2,128)} %get-tuple-element.400.offs_ref, bf16[1024,2048]{1,0:T(8,128)(2,1)} %pad_maximum_fusion.5.left_ref, bf16[4,256,1024]{2,1,0:T(8,128)(2,1)} %bitcast.167, bf16[4,256,1024]{2,1,0:T(8,128)(2,1)} %collective-permute-done.52.refs_1_, ...), custom_call_target="tpu_custom_call" | custom-call | flops 85899344 | bytes 251740 | tf_op jit(solution)/shard_map/pallas_call | solution.py:436
  366.4 19.5 %shard_map.243 = (bf16[1024,2048]{1,0:T(8,128)(2,1)}, f32[1,2048]{1,0:T(1,128)S(1)}) custom-call(s32[2,8]{1,0:T(2,128)S(1)} %stack.347.offs_ref, bf16[1024,2048]{1,0:T(8,128)(2,1)} %pad_maximum_fusion.4.right_ref.left_ref, bf16[8,256,2048]{2,1,0:T(8,128)(2,1)} %all-gather.12.cloned.1.call-done.refs_0_, f32[1024,2048]{1,0:T(8,128)} %get-tuple-element.294.refs_1_), custom_call_target="tpu_custom_call" | custom-call | flops 85899344 | bytes 251740 | tf_op jit(solution)/shard_map/pallas_call | solution.py:436
  395.3 16.5 %shard_map.245 = bf16[1024,2048]{1,0:T(8,128)(2,1)} custom-call(s32[2,16]{1,0:T(2,128)} %get-tuple-element.400.offs_ref, bf16[1024,2048]{1,0:T(8,128)(2,1)} %get-tuple-element.297.right_ref.left_ref, bf16[4,256,1024]{2,1,0:T(8,128)(2,1)} %bitcast.168, bf16[4,256,1024]{2,1,0:T(8,128)(2,1)} %collective-permute-done.52.refs_1_, ...), custom_call_target="tpu_custom_call" | custom-call | flops 85899344 | bytes 167772 | tf_op jit(solution)/shard_map/pallas_call | solution.py:436
  411.8 38.3 %collective-permute-done.56.refs_0_ = bf16[4,256,2048]{2,1,0:T(8,128)(2,1)} collective-permute-done((bf16[4,256,2048]{2,1,0:T(8,128)(2,1)}, bf16[4,256,2048]{2,1,0:T(8,128)(2,1)}, u32[]{:S(2)}, u32[]{:S(2)}) %collective-permute-start.56) | collective-permute-done | bytes 4194336 | tf_op jit(solution)/shard_map/ppermute | solution.py:962
  450.2 9.9 %shard_map.246 = bf16[4,256,2048]{2,1,0:T(8,128)(2,1)} custom-call(s32[5]{0:T(128)} %stack.357.where_ref, bf16[1024,2048]{1,0:T(8,128)(2,1)S(1)} %copy-done.1, bf16[1024,2048]{1,0:T(8,128)(2,1)} %pad_maximum_fusion.4.right_ref.left_ref, bf16[4,256,2048]{2,1,0:T(8,128)(2,1)} %collective-permute-done.56.refs_0_), custom_call_target="tpu_custom_call" | custom-call | flops 42949672 | bytes 146800 | tf_op jit(solution)/shard_map/pallas_call | solution.py:506
  460.9 52.1 %conditional.7 = (bf16[512,2048]{1,0:T(8,128)(2,1)}, f32[256,2048]{1,0:T(8,128)}, f32[2048]{0:T(1024)S(1)}, f32[2048]{0:T(1024)S(1)}) conditional(s32[]{:T(128)} %bitcast.33, () %tuple.104, (s32[]{:T(128)}, bf16[1024,2048]{1,0:T(8,128)(2,1)}, s32[]{:T(128)}, f32[8,256]{1,0:T(8,128)S(1)}, f32[256,2048]{1,0:T(8,128)}, ...), branch_computations={%region_8.9_spmd, %region_9.16_spmd} | conditional | flops 20967696 | bytes 86052232 | solution.py:303
  479.1 20.0 %collective-permute-done.12 = bf16[256,2048]{1,0:T(8,128)(2,1)} collective-permute-done((bf16[256,2048]{1,0:T(8,128)(2,1)S(1)}, bf16[256,2048]{1,0:T(8,128)(2,1)}, u32[]{:S(2)}, u32[]{:S(2)}) %collective-permute-start.12) | collective-permute-done | bytes 1048608 | tf_op jit(solution)/shard_map/cond/branch_1_fun/ppermute | solution.py:359
  513.0 24.0 %conditional.8 = (bf16[1024,512]{1,0:T(8,128)(2,1)S(1)}) conditional(s32[]{:T(128)} %bitcast.33, () %tuple.103, (s32[]{:T(128)}, s32[2,16]{1,0:T(2,128)S(1)}, bf16[512,2048]{1,0:T(8,128)(2,1)}, bf16[4,128,1024]{2,1,0:T(8,128)(2,1)}, bf16[4,128,1024]{2,1,0:T(8,128)(2,1)}, /*index=5*/bf16[4,128,1024]{2,1,0:T(8,128)(2,1)}, ...), branch_computations={%region_16.17_spmd, %region_17.18_spmd} | conditional | flops 24096276 | bytes 7413602 | solution.py:303
  523.1 12.5 %collective-permute-done.8 = bf16[512,512]{1,0:T(8,128)(2,1)S(1)} collective-permute-done((bf16[512,512]{1,0:T(8,128)(2,1)S(1)}, bf16[512,512]{1,0:T(8,128)(2,1)S(1)}, u32[]{:S(2)}, u32[]{:S(2)}) %collective-permute-start.8) | collective-permute-done | bytes 524320 | tf_op jit(solution)/shard_map/cond/branch_1_fun/ppermute | solution.py:1106
  539.8 15.4 %shard_map.247.right_ref.left_ref = bf16[1024,1536]{1,0:T(8,128)(2,1)} custom-call(bf16[1024,1536]{1,0:T(8,128)(2,1)} %shard_map.239.q_ref.k_ref.v_ref, bf16[1024,1536]{1,0:T(8,128)(2,1)} %shard_map.239.q_ref.k_ref.v_ref, bf16[1024,1536]{1,0:T(8,128)(2,1)} %shard_map.239.q_ref.k_ref.v_ref, bf16[1024,512]{1,0:T(8,128)(2,1)S(1)} %get-tuple-element.456.g_ref, ...), custom_call_target="tpu_custom_call" | custom-call | flops 53687092 | bytes 83886 | tf_op jit(solution)/shard_map/pallas_call | solution.py:706
  563.3 10.1 %shard_map.249 = bf16[4,256,2048]{2,1,0:T(8,128)(2,1)} custom-call(s32[5]{0:T(128)} %stack.357.where_ref, bf16[1024,2048]{1,0:T(8,128)(2,1)} %pad_maximum_fusion.5.left_ref, bf16[1024,2048]{1,0:T(8,128)(2,1)} %get-tuple-element.297.right_ref.left_ref, bf16[4,256,2048]{2,1,0:T(8,128)(2,1)} %collective-permute-done.58.refs_0_), custom_call_target="tpu_custom_call" | custom-call | flops 42949672 | bytes 146800 | tf_op jit(solution)/shard_map/pallas_call | solution.py:506
  580.2 13.2 %shard_map.250 = bf16[1024,2048]{1,0:T(8,128)(2,1)} custom-call(s32[2,16]{1,0:T(2,128)} %get-tuple-element.401.offs_ref, bf16[1024,1536]{1,0:T(8,128)(2,1)} %shard_map.247.right_ref.left_ref, bf16[4,256,768]{2,1,0:T(8,128)(2,1)} %bitcast.176, bf16[4,256,768]{2,1,0:T(8,128)(2,1)} %copy-done.13, bf16[4,256,768]{2,1,0:T(8,128)(2,1)} %bitcast.179, ...), custom_call_target="tpu_custom_call" | custom-call | flops 64424508 | bytes 136314 | tf_op jit(solution)/shard_map/pallas_call | solution.py:436
  603.2 50.4 %conditional.9 = (f32[1,256,2048]{2,1,0:T(8,128)}, f32[2048]{0:T(1024)S(1)}, f32[2048]{0:T(1024)S(1)}, f32[256,2048]{1,0:T(8,128)}, bf16[256,2048]{1,0:T(8,128)(2,1)}) conditional(s32[]{:T(128)} %bitcast.33, () %tuple.97, (bf16[1024,2048]{1,0:T(8,128)(2,1)}, s32[]{:T(128)}, s32[]{:T(128)}, bf16[1024,2048]{1,0:T(8,128)(2,1)}, ...), branch_computations={%region_19.20_spmd, %region_20.27_spmd} | conditional | flops 104245600 | bytes 125017352 | solution.py:303
  617.6 14.6 %branch_1_fun.9 = bf16[1024,2048]{1,0:T(8,128)(2,1)} custom-call(s32[2,8]{1,0:T(2,128)S(1)} %get-tuple-element.149.offs_ref, bf16[1024,2048]{1,0:T(8,128)(2,1)S(1)} %copy-done.2, bf16[8,256,2048]{2,1,0:T(8,128)(2,1)} %get-tuple-element.152.refs_0_), custom_call_target="tpu_custom_call" | custom-call | flops 85899344 | bytes 167772 | tf_op jit(solution)/shard_map/cond/branch_1_fun/pallas_call | solution.py:436
  663.8 90.9 %conditional.10 = (bf16[1,256,2048]{2,1,0:T(8,128)(2,1)}, f32[2304]{0:T(1024)}, bf16[128,1024]{1,0:T(8,128)(2,1)S(1)}, f32[256,8192]{1,0:T(8,128)}, f32[256]{0:T...) conditional(s32[]{:T(128)} %bitcast.33, () %tuple.96, ...), branch_computations={%region_28.29_spmd, %region_29.31_spmd} | conditional | flops 6350643 | bytes 64031960 | solution.py:303
  688.3 13.8 %collective-permute-done.29.refs_2_ = bf16[256,2048]{1,0:T(8,128)(2,1)} collective-permute-done((bf16[256,2048]{1,0:T(8,128)(2,1)}, bf16[256,2048]{1,0:T(8,128)(2,1)}, u32[]{:S(2)}, u32[]{:S(2)}) %collective-permute-start.29) | collective-permute-done | bytes 1048608 | tf_op jit(solution)/shard_map/cond/branch_1_fun/ppermute | solution.py:1196
  707.4 14.5 %collective-permute-done.17 = bf16[256,2048]{1,0:T(8,128)(2,1)S(1)} collective-permute-done((bf16[256,2048]{1,0:T(8,128)(2,1)}, bf16[256,2048]{1,0:T(8,128)(2,1)S(1)}, u32[]{:S(2)}, u32[]{:S(2)}) %collective-permute-start.17) | collective-permute-done | bytes 1048608 | tf_op jit(solution)/shard_map/cond/branch_1_fun/ppermute | solution.py:1195
  731.7 13.7 %collective-permute-done.26 = bf16[128,1024]{1,0:T(8,128)(2,1)S(1)} collective-permute-done((bf16[128,1024]{1,0:T(8,128)(2,1)S(1)}, bf16[128,1024]{1,0:T(8,128)(2,1)S(1)}, u32[]{:S(2)}, u32[]{:S(2)}) %collective-permute-start.26) | collective-permute-done | bytes 262176 | tf_op jit(solution)/shard_map/cond/branch_1_fun/ppermute | solution.py:942
  755.3 44.9 %conditional.11 = (f32[256,6144]{1,0:T(8,128)S(1)}, f32[256,2048]{1,0:T(8,128)}, f32[1024,2048]{1,0:T(8,128)}) conditional(s32[]{:T(128)} %bitcast.33, () %tuple.143, (bf16[256,1536]{1,0:T(8,128)(2,1)}, s32[4]{0:T(128)S(1)}, bf16[128,1024]{1,0:T(8,128)(2,1)S(1)}, bf16[256,2048]{1,0:T(8,128)(2,1)S(1)}, bf16[256,2048]{1,0:T(8,128)(2,1)}) %tuple.227), branch_computations={%region_32.33_spmd, %region_33.34_spmd} | conditional | bytes 43243840 | solution.py:303
  758.2 18.1 %collective-permute-done.1.refs_2_ = bf16[256,1536]{1,0:T(8,128)(2,1)S(1)} collective-permute-done((bf16[256,1536]{1,0:T(8,128)(2,1)}, bf16[256,1536]{1,0:T(8,128)(2,1)S(1)}, u32[]{:S(2)}, u32[]{:S(2)}) %collective-permute-start.1) | collective-permute-done | bytes 786464 | tf_op jit(solution)/shard_map/cond/branch_1_fun/ppermute | solution.py:323
  (384 shorter events, 321.2 us)
Async XLA Ops:
  7.2 67.9 %all-gather.14.cloned.1.call-start = ((), (), s32[]{:S(2)}) async-start(), calls=%async_computation.7 | async-start | bytes 1966080 | tf_op jit(solution)/shard_map/all_gather | solution.py:293
  16.0 68.6 %all-gather.20.cloned.1.call-start = ((), (), s32[]{:S(2)}) async-start(), calls=%async_computation.10 | async-start | bytes 1310720 | tf_op jit(solution)/shard_map/all_gather | solution.py:293
  16.0 27.8 %collective-permute-start.31 = (bf16[256,2048]{1,0:T(8,128)(2,1)}, bf16[256,2048]{1,0:T(8,128)(2,1)S(1)}, u32[]{:S(2)}, u32[]{:S(2)}) collective-permute-start(bf16[256,2048]{1,0:T(8,128)(2,1)} %get-tuple-element.264), channel_id=1, source_target_pairs={{0,4},{4,0},{1,5},{5,1},{2,6},{6,2},{3,7},{7,3},{8,12},{12,8},{9,1... | collective-permute-start | bytes 3145736 | tf_op jit(solution)/shard_map/ppermute | solution.py:902
  48.8 74.2 %all-gather.16.cloned.1.call-start = ((), (), s32[]{:S(2)}) async-start(), calls=%async_computation.8 | async-start | bytes 1966080 | tf_op jit(solution)/shard_map/all_gather | solution.py:293
  49.6 134.6 %all-gather.18.cloned.1.call-start = ((), (), s32[]{:S(2)}) async-start(), calls=%async_computation.9 | async-start | bytes 2621440 | tf_op jit(solution)/shard_map/all_gather | solution.py:293
  50.1 198.9 %all-gather.22.cloned.1.call-start = ((), (), s32[]{:S(2)}) async-start(), calls=%async_computation.11 | async-start | bytes 2621440 | tf_op jit(solution)/shard_map/all_gather | solution.py:991
  52.0 314.3 %all-gather.12.cloned.1.call-start = ((), (), s32[]{:S(2)}) async-start(), calls=%async_computation.3 | async-start | bytes 10485760 | tf_op jit(solution)/shard_map/all_gather | solution.py:992
  75.0 37.0 %collective-permute-start.45 = (bf16[4,256,768]{2,1,0:T(8,128)(2,1)}, bf16[4,256,768]{2,1,0:T(8,128)(2,1)S(1)}, u32[]{:S(2)}, u32[]{:S(2)}) collective-permute-start(bf16[4,256,768]{2,1,0:T(8,128)(2,1)} %bitcast.174), channel_id=1, source_target_pairs={{0,4},{4,0},{1,5},{5,1},{2,6},{6,2},{3,7},{7,3},{8,12},{12,8},{9,1... | collective-permute-start | bytes 4718600 | tf_op jit(solution)/shard_map/ppermute | solution.py:294
  82.9 40.2 %collective-permute-start.43 = (bf16[256,2048]{1,0:T(8,128)(2,1)}, bf16[256,2048]{1,0:T(8,128)(2,1)}, u32[]{:S(2)}, u32[]{:S(2)}) collective-permute-start(bf16[256,2048]{1,0:T(8,128)(2,1)} %bitcast.57), channel_id=1, source_target_pairs={{0,2},{2,0},{1,3},{3,1},{4,6},{6,4},{5,7},{7,5},{8,10},{10,8},{9,1... | collective-permute-start | bytes 3145736 | tf_op jit(solution)/shard_map/ppermute | solution.py:323
  84.5 490.5 %reduce-scatter.4.cloned.1.call-start = ((), (), s32[]{:S(2)}) async-start(), calls=%async_computation.4 | async-start | bytes 5242880 | tf_op jit(solution)/shard_map/reduce_scatter | solution.py:971
  84.5 55.4 %collective-permute-start.42 = (bf16[256,2048]{1,0:T(8,128)(2,1)}, bf16[256,2048]{1,0:T(8,128)(2,1)}, u32[]{:S(2)}, u32[]{:S(2)}) collective-permute-start(bf16[256,2048]{1,0:T(8,128)(2,1)} %bitcast.57), channel_id=1, source_target_pairs={{0,1},{1,0},{2,3},{3,2},{4,5},{5,4},{6,7},{7,6},{8,9},{9,8},{10,11... | collective-permute-start | bytes 3145736 | tf_op jit(solution)/shard_map/ppermute | solution.py:327
  112.1 26.4 %collective-permute-start.47 = (bf16[4,128,1024]{2,1,0:T(8,128)(2,1)}, bf16[4,128,1024]{2,1,0:T(8,128)(2,1)}, u32[]{:S(2)}, u32[]{:S(2)}) collective-permute-start(bf16[4,128,1024]{2,1,0:T(8,128)(2,1)} %bitcast.182), channel_id=1, source_target_pairs={{0,4},{4,0},{1,5},{5,1},{2,6},{6,2},{3,7},{7,3},{8,12},{12,8},{9,1... | collective-permute-start | bytes 3145736 | tf_op jit(solution)/shard_map/ppermute | solution.py:294
  123.1 47.9 %collective-permute-start.46 = (bf16[4,256,768]{2,1,0:T(8,128)(2,1)}, bf16[4,256,768]{2,1,0:T(8,128)(2,1)}, u32[]{:S(2)}, u32[]{:S(2)}) collective-permute-start(bf16[4,256,768]{2,1,0:T(8,128)(2,1)} %bitcast.177), channel_id=1, source_target_pairs={{0,4},{4,0},{1,5},{5,1},{2,6},{6,2},{3,7},{7,3},{8,12},{12,8},{9,1... | collective-permute-start | bytes 4718600 | tf_op jit(solution)/shard_map/ppermute | solution.py:294
  125.4 73.8 %collective-permute-start.48 = (bf16[4,128,1024]{2,1,0:T(8,128)(2,1)}, bf16[4,128,1024]{2,1,0:T(8,128)(2,1)}, u32[]{:S(2)}, u32[]{:S(2)}) collective-permute-start(bf16[4,128,1024]{2,1,0:T(8,128)(2,1)} %bitcast.183), channel_id=1, source_target_pairs={{0,2},{2,0},{1,3},{3,1},{4,6},{6,4},{5,7},{7,5},{8,10},{10,8},{9,1... | collective-permute-start | bytes 3145736 | tf_op jit(solution)/shard_map/ppermute | solution.py:906
  138.4 60.8 %collective-permute-start.49 = (bf16[4,128,1024]{2,1,0:T(8,128)(2,1)}, bf16[4,128,1024]{2,1,0:T(8,128)(2,1)}, u32[]{:S(2)}, u32[]{:S(2)}) collective-permute-start(bf16[4,128,1024]{2,1,0:T(8,128)(2,1)} %collective-permute-done.47), channel_id=1, source_target_pairs={{0,2},{2,0},{1,3},{3,1},{4,6},{6,4},{5,7},{7,5},{8,10},{10,8},{9,1... | collective-permute-start | bytes 3145736 | tf_op jit(solution)/shard_map/ppermute | solution.py:906
  184.2 90.4 %collective-permute-start.52 = (bf16[4,256,1024]{2,1,0:T(8,128)(2,1)}, bf16[4,256,1024]{2,1,0:T(8,128)(2,1)}, u32[]{:S(2)}, u32[]{:S(2)}) collective-permute-start(bf16[4,256,1024]{2,1,0:T(8,128)(2,1)} %bitcast.166), channel_id=1, source_target_pairs={{0,4},{4,0},{1,5},{5,1},{2,6},{6,2},{3,7},{7,3},{8,12},{12,8},{9,1... | collective-permute-start | bytes 6291464 | tf_op jit(solution)/shard_map/ppermute | solution.py:294
  274.6 48.4 %collective-permute-start.54 = (bf16[4,256,1024]{2,1,0:T(8,128)(2,1)}, bf16[4,256,1024]{2,1,0:T(8,128)(2,1)}, u32[]{:S(2)}, u32[]{:S(2)}) collective-permute-start(bf16[4,256,1024]{2,1,0:T(8,128)(2,1)} %bitcast.169), channel_id=1, source_target_pairs={{0,4},{4,0},{1,5},{5,1},{2,6},{6,2},{3,7},{7,3},{8,12},{12,8},{9,1... | collective-permute-start | bytes 6291464 | tf_op jit(solution)/shard_map/ppermute | solution.py:1030
  281.1 62.8 %collective-permute-start.55 = (bf16[512,512]{1,0:T(8,128)(2,1)S(1)}, bf16[512,512]{1,0:T(8,128)(2,1)}, u32[]{:S(2)}, u32[]{:S(2)}) collective-permute-start(bf16[512,512]{1,0:T(8,128)(2,1)S(1)} %get-tuple-element.290), channel_id=1, source_target_pairs={{0,2},{2,0},{1,3},{3,1},{4,6},{6,4},{5,7},{7,5},{8,10},{10,8},{9,1... | collective-permute-start | bytes 1572872 | tf_op jit(solution)/shard_map/ppermute | solution.py:1032
  357.7 92.5 %collective-permute-start.56 = (bf16[4,256,2048]{2,1,0:T(8,128)(2,1)}, bf16[4,256,2048]{2,1,0:T(8,128)(2,1)}, u32[]{:S(2)}, u32[]{:S(2)}) collective-permute-start(bf16[4,256,2048]{2,1,0:T(8,128)(2,1)} %shard_map.242), channel_id=1, source_target_pairs={{0,4},{4,0},{1,5},{5,1},{2,6},{6,2},{3,7},{7,3},{8,12},{12,8},{9,1... | collective-permute-start | bytes 12582920 | tf_op jit(solution)/shard_map/ppermute | solution.py:962
  460.1 193.5 %reduce-scatter.6.cloned.1.call-start = ((), (), s32[]{:S(2)}) async-start(), calls=%async_computation.5 | async-start | bytes 5242880 | tf_op jit(solution)/shard_map/reduce_scatter | solution.py:971
  460.2 103.1 %collective-permute-start.58 = (bf16[4,256,2048]{2,1,0:T(8,128)(2,1)}, bf16[4,256,2048]{2,1,0:T(8,128)(2,1)}, u32[]{:S(2)}, u32[]{:S(2)}) collective-permute-start(bf16[4,256,2048]{2,1,0:T(8,128)(2,1)} %shard_map.244), channel_id=1, source_target_pairs={{0,4},{4,0},{1,5},{5,1},{2,6},{6,2},{3,7},{7,3},{8,12},{12,8},{9,1... | collective-permute-start | bytes 12582920 | tf_op jit(solution)/shard_map/ppermute | solution.py:962
  573.4 181.4 %reduce-scatter.8.cloned.1.call-start = ((), (), s32[]{:S(2)}) async-start(), calls=%async_computation.6 | async-start | bytes 3932160 | tf_op jit(solution)/shard_map/reduce_scatter | solution.py:971
  573.5 80.1 %collective-permute-start.60 = (bf16[4,256,1536]{2,1,0:T(8,128)(2,1)}, bf16[4,256,1536]{2,1,0:T(8,128)(2,1)}, u32[]{:S(2)}, u32[]{:S(2)}) collective-permute-start(bf16[4,256,1536]{2,1,0:T(8,128)(2,1)} %shard_map.248), channel_id=1, source_target_pairs={{0,4},{4,0},{1,5},{5,1},{2,6},{6,2},{3,7},{7,3},{8,12},{12,8},{9,1... | collective-permute-start | bytes 9437192 | tf_op jit(solution)/shard_map/ppermute | solution.py:962
  575.0 27.3 %collective-permute-start.59 = (bf16[256,2048]{1,0:T(8,128)(2,1)}, bf16[256,2048]{1,0:T(8,128)(2,1)S(1)}, u32[]{:S(2)}, u32[]{:S(2)}) collective-permute-start(bf16[256,2048]{1,0:T(8,128)(2,1)} %bitcast.186), channel_id=1, source_target_pairs={{0,2},{2,0},{1,3},{3,1},{4,6},{6,4},{5,7},{7,5},{8,10},{10,8},{9,1... | collective-permute-start | bytes 3145736 | tf_op jit(solution)/shard_map/ppermute | solution.py:1151
  674.4 27.7 %collective-permute-start.24 = (bf16[4,128,1024]{2,1,0:T(8,128)(2,1)}, bf16[4,128,1024]{2,1,0:T(8,128)(2,1)}, u32[]{:S(2)}, u32[]{:S(2)}) collective-permute-start(bf16[4,128,1024]{2,1,0:T(8,128)(2,1)} %slice.51), channel_id=1, source_target_pairs={{0,4},{4,0},{1,5},{5,1},{2,6},{6,2},{3,7},{7,3},{8,12},{12,8},{9,1... | collective-permute-start | bytes 3145736 | tf_op jit(solution)/shard_map/cond/branch_1_fun/ppermute | solution.py:1200
  675.7 26.4 %collective-permute-start.29 = (bf16[256,2048]{1,0:T(8,128)(2,1)}, bf16[256,2048]{1,0:T(8,128)(2,1)}, u32[]{:S(2)}, u32[]{:S(2)}) collective-permute-start(bf16[256,2048]{1,0:T(8,128)(2,1)} %get-tuple-element.171.refs_0_), channel_id=1, source_target_pairs={{0,2},{2,0},{1,3},{3,1},{4,6},{6,4},{5,7},{7,5},{8,10},{10,8},{9,1... | collective-permute-start | bytes 3145736 | tf_op jit(solution)/shard_map/cond/branch_1_fun/ppermute | solution.py:1196
  680.5 41.4 %collective-permute-start.17 = (bf16[256,2048]{1,0:T(8,128)(2,1)}, bf16[256,2048]{1,0:T(8,128)(2,1)S(1)}, u32[]{:S(2)}, u32[]{:S(2)}) collective-permute-start(bf16[256,2048]{1,0:T(8,128)(2,1)} %get-tuple-element.158), channel_id=1, source_target_pairs={{0,2},{2,0},{1,3},{3,1},{4,6},{6,4},{5,7},{7,5},{8,10},{10,8},{9,1... | collective-permute-start | bytes 3145736 | tf_op jit(solution)/shard_map/cond/branch_1_fun/ppermute | solution.py:1195
  687.2 58.4 %collective-permute-start.28 = (bf16[256,2048]{1,0:T(8,128)(2,1)}, bf16[256,2048]{1,0:T(8,128)(2,1)S(1)}, u32[]{:S(2)}, u32[]{:S(2)}) collective-permute-start(bf16[256,2048]{1,0:T(8,128)(2,1)} %get-tuple-element.171.refs_0_), channel_id=1, source_target_pairs={{0,1},{1,0},{2,3},{3,2},{4,5},{5,4},{6,7},{7,6},{8,9},{9,8},{10,11... | collective-permute-start | bytes 3145736 | tf_op jit(solution)/shard_map/cond/branch_1_fun/ppermute | solution.py:327
  702.1 43.5 %collective-permute-start.30 = (bf16[256,2048]{1,0:T(8,128)(2,1)}, bf16[256,2048]{1,0:T(8,128)(2,1)S(1)}, u32[]{:S(2)}, u32[]{:S(2)}) collective-permute-start(bf16[256,2048]{1,0:T(8,128)(2,1)} %collective-permute-done.29.refs_2_), channel_id=1, source_target_pairs={{0,1},{1,0},{2,3},{3,2},{4,5},{5,4},{6,7},{7,6},{8,9},{9,8},{10,11... | collective-permute-start | bytes 3145736 | tf_op jit(solution)/shard_map/cond/branch_1_fun/ppermute | solution.py:327
  757.1 30.8 %collective-permute-start.6 = (bf16[256,2048]{1,0:T(8,128)(2,1)S(1)}, bf16[256,2048]{1,0:T(8,128)(2,1)S(1)}, u32[]{:S(2)}, u32[]{:S(2)}) collective-permute-start(bf16[256,2048]{1,0:T(8,128)(2,1)S(1)} %get-tuple-element.175.refs_0_), channel_id=1, source_target_pairs={{0,1},{1,0},{2,3},{3,2},{4,5},{5,4},{6,7},{7,6},{8,9},{9,8},{10,11... | collective-permute-start | bytes 3145736 | tf_op jit(solution)/shard_map/cond/branch_1_fun/ppermute | solution.py:327
  757.1 30.8 %collective-permute-start.7 = (bf16[256,2048]{1,0:T(8,128)(2,1)}, bf16[256,2048]{1,0:T(8,128)(2,1)S(1)}, u32[]{:S(2)}, u32[]{:S(2)}) collective-permute-start(bf16[256,2048]{1,0:T(8,128)(2,1)} %get-tuple-element.176.refs_2_), channel_id=1, source_target_pairs={{0,1},{1,0},{2,3},{3,2},{4,5},{5,4},{6,7},{7,6},{8,9},{9,8},{10,11... | collective-permute-start | bytes 3145736 | tf_op jit(solution)/shard_map/cond/branch_1_fun/ppermute | solution.py:327
  758.2 37.4 %collective-permute-start = (bf16[256,1536]{1,0:T(8,128)(2,1)}, bf16[256,1536]{1,0:T(8,128)(2,1)S(1)}, u32[]{:S(2)}, u32[]{:S(2)}) collective-permute-start(bf16[256,1536]{1,0:T(8,128)(2,1)} %get-tuple-element.173.refs_0_), channel_id=1, source_target_pairs={{0,1},{1,0},{2,3},{3,2},{4,5},{5,4},{6,7},{7,6},{8,9},{9,8},{10,11... | collective-permute-start | bytes 2359304 | tf_op jit(solution)/shard_map/cond/branch_1_fun/ppermute | solution.py:327
  (87 other events, 1129.4 us)
Sparse Core Ops, SparseCore 0:
  16.1 39.7 all-gather.13
  57.5 26.7 all-gather.19
  86.4 36.5 all-gather.15
  125.1 44.7 all-gather.17
  171.3 44.6 all-gather.21
  218.0 148.3 all-gather.11
  460.2 77.0 reduce-scatter.3
  573.6 77.4 reduce-scatter.5
  662.4 73.8 reduce-scatter.7

commit v3 on v2

--- a/solution.py
+++ b/solution.py
@@ -374,60 +374,74 @@
     return pltpu.CompilerParams(vmem_limit_bytes=limit)
 
 
-def load_weight(offsets, pieces, held, sems):
-    copies = []
-    for piece in pieces:
-        count, rows, cols = piece.shape
-        for k in range(count):
-            b = len(copies)
-            row = pl.multiple_of(offsets[0, b], rows)
-            col = pl.multiple_of(offsets[1, b], cols)
-            copies.append(
-                pltpu.make_async_copy(
-                    piece.at[k], held.at[pl.ds(row, rows), pl.ds(col, cols)], sems.at[b]
-                )
-            )
-    for copy in copies:
-        copy.start()
-    for copy in copies:
-        copy.wait()
-
-
-def weight_matmul(left, pieces, offsets, shape, back, body, extras, outs, tile, chunk):
+def weight_matmul(left, pieces, offsets, shape, back, body, extras, outs, chunk):
     rows = left.shape[0]
     depth, width = shape
     out_width = depth if back else width
+    steps = out_width // chunk
     n_pieces, n_extras = len(pieces), len(extras)
+    blocks = [(p, k) for p, piece in enumerate(pieces) for k in range(piece.shape[0])]
+    block_rows, block_cols = pieces[0].shape[1:]
+    row_count, col_count = depth // block_rows, width // block_cols
 
     def kernel(offs_ref, left_ref, *refs):
         piece_refs = refs[:n_pieces]
         extra_refs = refs[n_pieces : n_pieces + n_extras]
         out_refs = refs[n_pieces + n_extras : -2]
         held, sems = refs[-2:]
-
-        @pl.when(pl.program_id(0) == 0)
+        step = pl.program_id(0)
+
+        def slot(row, col):
+            return sems.at[row, col]
+
+        @pl.when(step == 0)
         def _():
-            load_weight(offs_ref, piece_refs, held, sems)
-
-        for start in range(0, out_width, chunk):
-            cols = pl.ds(start, chunk)
-            if back:
-                values = lax.dot_general(
-                    left_ref[...],
-                    held[cols, :],
-                    (((1,), (1,)), ((), ())),
-                    preferred_element_type=jnp.float32,
-                )
-            else:
-                values = jnp.dot(
-                    left_ref[...], held[:, cols], preferred_element_type=jnp.float32
-                )
-            body(values, cols, extra_refs, out_refs, pl.program_id(0) == 0)
-
-    def tile_spec(array_rows, array_cols):
-        if array_rows == 1:
-            return pl.BlockSpec((1, array_cols), lambda i, offs: (0, 0))
-        return pl.BlockSpec((tile, array_cols), lambda i, offs: (i, 0))
+            for b, (p, k) in enumerate(blocks):
+                row, col = offs_ref[0, b], offs_ref[1, b]
+                target = held.at[
+                    pl.ds(pl.multiple_of(row * block_rows, block_rows), block_rows),
+                    pl.ds(pl.multiple_of(col * block_cols, block_cols), block_cols),
+                ]
+                pltpu.make_async_copy(piece_refs[p].at[k], target, slot(row, col)).start()
+
+        def arrive(row, col):
+            target = held.at[
+                pl.ds(row * block_rows, block_rows), pl.ds(col * block_cols, block_cols)
+            ]
+            pltpu.make_async_copy(piece_refs[0].at[0], target, slot(row, col)).wait()
+
+        for n in range(steps):
+            needed = [
+                (row, col)
+                for row in range(row_count)
+                for col in range(col_count)
+                if (
+                    row * block_rows // chunk if back else col * block_cols // chunk
+                ) == n
+            ]
+            if needed:
+
+                @pl.when(step == n)
+                def _():
+                    for row, col in needed:
+                        arrive(row, col)
+
+        start = pl.ds(pl.multiple_of(step * chunk, chunk), chunk)
+        if back:
+            values = lax.dot_general(
+                left_ref[...],
+                held[start, :],
+                (((1,), (1,)), ((), ())),
+                preferred_element_type=jnp.float32,
+            )
+        else:
+            values = jnp.dot(
+                left_ref[...], held[:, start], preferred_element_type=jnp.float32
+            )
+        body(values, extra_refs, out_refs)
+
+    def column_spec(array):
+        return pl.BlockSpec((array.shape[0], chunk), lambda i, offs: (0, i))
 
     flops = 2 * rows * depth * width
     moved = 2 * (left.size + depth * width) + sum(
@@ -437,14 +451,18 @@
         kernel,
         grid_spec=pltpu.PrefetchScalarGridSpec(
             num_scalar_prefetch=1,
-            grid=(rows // tile,),
-            in_specs=[pl.BlockSpec((tile, left.shape[1]), lambda i, offs: (i, 0))]
+            grid=(steps,),
+            in_specs=[
+                pl.BlockSpec(
+                    left.shape, lambda i, offs: (0, 0), pipeline_mode=pl.Buffered(1)
+                )
+            ]
             + [pl.BlockSpec(memory_space=pl.ANY)] * n_pieces
-            + [tile_spec(*a.shape) for a in extras],
-            out_specs=[tile_spec(*a.shape) for a in outs],
+            + [column_spec(a) for a in extras],
+            out_specs=[column_spec(a) for a in outs],
             scratch_shapes=[
                 pltpu.VMEM((depth, width), jnp.bfloat16),
-                pltpu.SemaphoreType.DMA((sum(p.shape[0] for p in pieces),)),
+                pltpu.SemaphoreType.DMA((row_count, col_count)),
             ],
         ),
         out_shape=list(outs),
@@ -453,41 +471,32 @@
     )(offsets, left, *pieces, *extras)
 
 
-def store_low(values, cols, extra_refs, out_refs, first):
-    out_refs[0][:, cols] = values.astype(jnp.bfloat16)
-
-
-def store_gelu(values, cols, extra_refs, out_refs, first):
-    hidden = values + extra_refs[0][:, cols]
+def store_low(values, extra_refs, out_refs):
+    out_refs[0][...] = values.astype(jnp.bfloat16)
+
+
+def store_gelu(values, extra_refs, out_refs):
+    hidden = values + extra_refs[0][...]
     square = hidden * hidden
     bend = jnp.tanh(GELU_A * hidden * (1.0 + GELU_B * square))
     half = 0.5 * (1.0 + bend)
-    out_refs[0][:, cols] = (hidden * half).astype(jnp.bfloat16)
+    out_refs[0][...] = (hidden * half).astype(jnp.bfloat16)
     slope = half + 0.5 * hidden * (1.0 - bend * bend) * (
         GELU_A * (1.0 + 3.0 * GELU_B * square)
     )
-    out_refs[1][:, cols] = slope
-
-
-def store_hidden_grad(values, cols, extra_refs, out_refs, first):
-    low = (values * extra_refs[0][:, cols]).astype(jnp.bfloat16)
-    out_refs[0][:, cols] = low
-    column_sum = jnp.sum(low.astype(jnp.float32), axis=0, keepdims=True)
-    sums = out_refs[1]
-
-    @pl.when(first)
-    def _():
-        sums[:, cols] = column_sum
-
-    @pl.when(jnp.logical_not(first))
-    def _():
-        sums[:, cols] += column_sum
-
-
-def weight_grad(left, right, where, count, block, width, *addends):
+    out_refs[1][...] = slope
+
+
+def store_hidden_grad(values, extra_refs, out_refs):
+    low = (values * extra_refs[0][...]).astype(jnp.bfloat16)
+    out_refs[0][...] = low
+    out_refs[1][...] = jnp.sum(low.astype(jnp.float32), axis=0, keepdims=True)
+
+
+def weight_grad(left, right, where, count, block, width, addend=None, parts=1):
     rows = left.shape[0]
-    parts = max(len(addends), 1)
     part = width // parts
+    added = () if addend is None else (addend,)
 
     def kernel(where_ref, left_ref, right_ref, *refs):
         for n in range(parts):
@@ -498,11 +507,10 @@
                 (((0,), (0,)), ((), ())),
                 preferred_element_type=jnp.float32,
             )
-            if addends:
-                value = value + refs[n][0].astype(jnp.float32)
-            refs[-1][0, :, cols] = value.astype(jnp.bfloat16)
-
-    piece = pl.BlockSpec((1, block, width), lambda k, at: (k, 0, 0))
+            if added:
+                value = value + refs[0][0, :, cols].astype(jnp.float32)
+            refs[len(added) + n][0] = value.astype(jnp.bfloat16)
+
     return pl.pallas_call(
         kernel,
         grid_spec=pltpu.PrefetchScalarGridSpec(
@@ -512,87 +520,99 @@
                 pl.BlockSpec((rows, block), lambda k, at: (0, at[k])),
                 pl.BlockSpec((rows, width), lambda k, at: (0, at[count])),
             ]
-            + [pl.BlockSpec((1, block, part), lambda k, at: (k, 0, 0))] * len(addends),
-            out_specs=piece,
+            + [pl.BlockSpec((1, block, width), lambda k, at: (k, 0, 0))] * len(added),
+            out_specs=[pl.BlockSpec((1, block, part), lambda k, at: (k, 0, 0))] * parts,
         ),
-        out_shape=jax.ShapeDtypeStruct((count, block, width), jnp.bfloat16),
+        out_shape=[jax.ShapeDtypeStruct((count, block, part), jnp.bfloat16)] * parts,
         cost_estimate=cost(
             flops=2 * rows * count * block * width,
-            bytes_accessed=2 * rows * (count * block + width)
-            + 4 * count * block * width,
+            bytes_accessed=2 * rows * (count * block + width) + 4 * count * block * width,
             transcendentals=0,
         ),
         compiler_params=params(),
-    )(where, left, right, *addends)
-
-
-def slice_weights(w_qkv, w_out, w_up, w_down, yi, ci, shard_count):
+    )(where, left, right, *added)
+
+
+def slice_qkv(w_qkv, where, width):
+    rows = w_qkv.shape[0]
+    heads = H // 4
+
+    def kernel(at_ref, from_ref, to_ref):
+        for i in range(heads):
+            col = pl.ds(pl.multiple_of((2 * i + at_ref[1]) * HD, HD), HD)
+            to_ref[:, i * HD : (i + 1) * HD] = from_ref[:, col]
+
+    part = heads * HD
+    return pl.pallas_call(
+        kernel,
+        grid_spec=pltpu.PrefetchScalarGridSpec(
+            num_scalar_prefetch=1,
+            grid=(3,),
+            in_specs=[pl.BlockSpec((rows, 2 * part), lambda g, at: (0, 2 * g + at[0]))],
+            out_specs=pl.BlockSpec((rows, part), lambda g, at: (0, g)),
+        ),
+        out_shape=jax.ShapeDtypeStruct((rows, width), jnp.bfloat16),
+        cost_estimate=cost(flops=0, bytes_accessed=3 << 20, transcendentals=0),
+        compiler_params=params(),
+    )(where, w_qkv)
+
+
+def slice_weights(w_out, w_up, w_down, where, shard_count):
     rows, model = w_out.shape
-    heads = H // 4
     ff_part = w_down.shape[0] // 4
-    half = 3 * heads * HD // 2
     steps = shard_count
     part = ff_part // steps
-
-    def kernel(at_ref, qkv_ref, out_ref, up_ref, down_ref, *to):
-        y, c = at_ref[0], at_ref[1]
+    up_half = steps // 2
+
+    def kernel(at_ref, out_ref, up_ref, down_ref, out_to, low_to, high_to, left_to, right_to):
         step = pl.program_id(0)
-        for n in range(2):
-            qkv_to, up_to = to[n], to[3 + n]
-
-            @pl.when(step == n)
-            def _():
-                for i in range(half // HD):
-                    head = n * (half // HD) + i
-                    col = (head // heads) * H + 2 * (head % heads) + c + 2 * heads * y
-                    col = pl.ds(pl.multiple_of(col * HD, HD), HD)
-                    qkv_to[:, i * HD : (i + 1) * HD] = qkv_ref[:, col]
-
-            @pl.when(step // (steps // 2) == n)
+        for n, up_to in enumerate((low_to, high_to)):
+
+            @pl.when(step // up_half == n)
             def _():
                 up_to[...] = up_ref[...]
 
         @pl.when(step == 0)
         def _():
-            to[2][...] = out_ref[...]
-
-        to[5][...] = down_ref[...]
-
-    def pair(block, index):
-        return [pl.BlockSpec(block, functools.partial(index, n)) for n in range(2)]
-
-    up_half = steps // 2
+            out_to[...] = out_ref[...]
+
+        left_to[...] = down_ref[:, : model // 2]
+        right_to[...] = down_ref[:, model // 2 :]
+
+    def up_spec(n):
+        return pl.BlockSpec(
+            (rows, ff_part), lambda i, at: (0, jnp.clip(i - n * up_half, 0, up_half - 1))
+        )
+
     return pl.pallas_call(
         kernel,
         grid_spec=pltpu.PrefetchScalarGridSpec(
             num_scalar_prefetch=1,
             grid=(steps,),
             in_specs=[
-                pl.BlockSpec((rows, 3 * model), lambda i, at: (0, 0)),
                 pl.BlockSpec((rows // 2, model // 2), lambda i, at: (at[1], at[0])),
                 pl.BlockSpec((rows, ff_part), lambda i, at: (0, 4 * i + 2 * at[0] + at[1])),
                 pl.BlockSpec(
                     (part, model), lambda i, at: ((2 * at[0] + at[1]) * steps + i, 0)
                 ),
             ],
-            out_specs=pair((rows, half), lambda n, i, at: (0, 0))
-            + [pl.BlockSpec((rows // 2, model // 2), lambda i, at: (0, 0))]
-            + pair(
-                (rows, ff_part),
-                lambda n, i, at: (0, jnp.clip(i - n * up_half, 0, up_half - 1)),
-            )
-            + [pl.BlockSpec((part, model), lambda i, at: (i, 0))],
+            out_specs=[
+                pl.BlockSpec((rows // 2, model // 2), lambda i, at: (0, 0)),
+                up_spec(0),
+                up_spec(1),
+                pl.BlockSpec((part, model // 2), lambda i, at: (i, 0)),
+                pl.BlockSpec((part, model // 2), lambda i, at: (i, 0)),
+            ],
         ),
         out_shape=[
             jax.ShapeDtypeStruct(shape, jnp.bfloat16)
-            for shape in [(rows, half)] * 2
-            + [(rows // 2, model // 2)]
+            for shape in [(rows // 2, model // 2)]
             + [(rows, ff_part * up_half)] * 2
-            + [(ff_part, model)]
+            + [(ff_part, model // 2)] * 2
         ],
-        cost_estimate=cost(flops=0, bytes_accessed=12 << 20, transcendentals=0),
+        cost_estimate=cost(flops=0, bytes_accessed=9 << 20, transcendentals=0),
         compiler_params=params(),
-    )(jnp.stack([yi, ci]).astype(jnp.int32), w_qkv, w_out, w_up, w_down)
+    )(where, w_out, w_up, w_down)
 
 
 def visible_tile(query_item, key_item, first_query, n_query, n_key):
@@ -790,24 +810,29 @@
     )
 
 
-def widen_heads(pieces, places):
-    rows, width = pieces[0].shape
-    part = width // 3
+def widen_heads(chunks, places):
+    rows, width = chunks[0][0].shape
+    heads = H // 4
+    part = heads * HD
 
     def write(n, pos, piece, out):
         first = lax.div(pos, 2) * part * 2 + lax.rem(pos, 2) * HD
-        for i in range(part // HD):
-            cols = pl.ds(pl.multiple_of(first + 2 * i * HD, HD), HD)
-            out[:, cols] = piece[:, i * HD : (i + 1) * HD].astype(jnp.float32)
+        for i in range(width // HD):
+            head = n * (width // HD) + i
+
+            @pl.when(pl.program_id(0) == head // heads)
+            def _():
+                cols = pl.ds(pl.multiple_of(first + 2 * (head % heads) * HD, HD), HD)
+                out[:, cols] = piece[:, i * HD : (i + 1) * HD].astype(jnp.float32)
 
     return widen(
-        [pieces],
+        chunks,
         places,
         3,
-        [((rows, part), lambda i: (0, i))],
+        [((rows, width), lambda i: (0, 0))] * 2,
         (rows, 4 * part),
         lambda i: (0, i),
-        (rows, 4 * width),
+        (rows, 12 * part),
         write,
     )
 
@@ -895,14 +920,16 @@
 
     line = Line()
     flag = item_lengths[0, 0] > 0
-    slices = slice_weights(w_qkv, w_out, w_up, w_down, yi, ci, shard_count)
+    where = jnp.stack([yi, ci]).astype(jnp.int32)
+    qkv_slice = slice_qkv(w_qkv, where, 3 * heads * HD)
+    slices = slice_weights(w_out, w_up, w_down, after(where, qkv_slice), shard_count)
     half = model // 2
     qkv_width = 3 * heads * HD
-    qkv_parts = gather_weight(slices[0]) + gather_weight(slices[1])
-    down_pair = jnp.stack([slices[5], lax.ppermute(slices[5], "x", SWAP)])
+    qkv_parts = gather_weight(qkv_slice)
+    down_pair = jnp.stack([slices[4], lax.ppermute(slices[4], "x", SWAP)])
     inputs = after(block_input, down_pair).reshape(tok_count, model).astype(wide)
     normed_one = layer_norm(inputs, gain_one, shift_one).astype(low)
-    out_parts = gather_weight(after(slices[2], normed_one), qkv_parts[1])
+    out_parts = gather_weight(after(slices[0], normed_one), qkv_parts[1])
     out_parts = out_parts + [lax.ppermute(piece, "y", SWAP) for piece in out_parts]
 
     near_blocks = [2 * z + xi for z in range(z_count)]
@@ -914,19 +941,10 @@
     def table(*rows):
         return jnp.stack([jnp.stack(row) for row in rows]).astype(jnp.int32)
 
-    def halves_at(first, second, rows, width):
-        return table(
-            [b * rows for b in first + second],
-            [zero] * shard_count + [zero + width] * shard_count,
-        )
-
-    qkv_offsets = halves_at(split, split, piece_d, qkv_width // 2)
-    up_offsets = halves_at(split, split, piece_d, ff_here // 2)
-    down_offsets = table([b * ff_part for b in paired], [zero] * shard_count)
-    out_offsets = table(
-        [b * (piece_d // 2) for b in split] * 2,
-        [yi * half] * shard_count + [(1 - yi) * half] * shard_count,
-    )
+    qkv_offsets = table(split, [zero] * shard_count)
+    up_offsets = table(split + split, [zero] * shard_count + [zero + 1] * shard_count)
+    down_offsets = table(split + paired, [zero] * shard_count + [zero + 1] * shard_count)
+    out_offsets = table(split + split, [yi] * shard_count + [1 - yi] * shard_count)
 
     def blocks_at(blocks, n):
         return table(blocks + [zero + n])[0]
@@ -945,26 +963,23 @@
         return total
 
     def plain_matmul(left, pieces, offsets, shape, back, body, extras, outs):
-        return weight_matmul(left, pieces, offsets, shape, back, body, extras, outs, 256, 512)
+        return weight_matmul(left, pieces, offsets, shape, back, body, extras, outs, 512)
 
     def matmul(left, *others):
         return line.leave(*plain_matmul(line.enter(left), *others))
 
-    def grad_chunk(left, right, blocks, n, block, width, *addends):
+    def grad_chunk(left, right, blocks, n, block, width):
         return line.leave(
-            weight_grad(
-                line.enter(left), right, blocks_at(blocks, n), len(blocks), block, width, *addends
-            )
+            *weight_grad(line.enter(left), right, blocks_at(blocks, n), len(blocks), block, width)
         )[0]
 
     def far_terms(left, right, block):
         terms = grad_chunk(left, right, far_blocks, 0, block, right.shape[1])
         return lax.ppermute(terms, "x", SWAP)
 
-    def near_terms(left, right, block, addend):
-        width = right.shape[1]
+    def near_terms(left, right, block, addend, parts=1):
         return weight_grad(
-            left, right, blocks_at(near_blocks, 0), z_count, block, width, addend
+            left, right, blocks_at(near_blocks, 0), z_count, block, addend.shape[2], addend, parts
         )
 
     def sum_over_z(total):
@@ -976,7 +991,7 @@
     normed_one = gather_tokens(normed_one, yi, ci, qkv_parts[0])
     cot_flat = after(cotangent.reshape(tok_count, model), normed_one)
     cot_wide = cot_flat.astype(wide)
-    cot_all = gather_tokens(cot_flat, yi, ci, qkv_parts[2])
+    cot_all = gather_tokens(cot_flat, yi, ci)
     (projected,) = matmul(
         after(normed_one, cot_all),
         qkv_parts,
@@ -987,9 +1002,10 @@
         (),
         (shape(length, qkv_width),),
     )
-    up_parts = gather_weight(slices[3], projected)
-    up_high = lax.all_gather(slices[4], "z", axis=0, tiled=False)
-    down_parts = [lax.all_gather(down_pair, "z", axis=0, tiled=True)]
+    up_parts = gather_weight(slices[1], projected)
+    up_high = lax.all_gather(slices[2], "z", axis=0, tiled=False)
+    down_parts = gather_weight(slices[3], projected)
+    down_parts.append(lax.all_gather(down_pair, "z", axis=0, tiled=True))
     positions = jnp.arange(length, dtype=jnp.int32)
     item_label = item_numbers(item_starts[0], item_lengths[0], positions)
     query_item = item_label[:, None]
@@ -1023,15 +1039,11 @@
         normed_two = layer_norm(residual_one, gain_two, shift_two).astype(low)
         return normed_two, residual_one, mine, other
 
+    up_parts += [up_high, lax.ppermute(after(up_high, mixed_heads), "x", SWAP)]
     normed_two, residual_one, mixed_home, mixed_other = line.leave(
-        *stage(flag, attend_out, after(line.enter(mixed_heads), up_parts[0]))
-    )
-    normed_two = after(normed_two, up_high)
-    up_parts += [up_high, lax.ppermute(after(up_high, normed_two), "x", SWAP)]
-    normed_two = gather_tokens(normed_two, yi, ci, up_parts[1])
-    mixed_last = lax.ppermute(after(mixed_home, normed_two), "y", SWAP)
-    others_heads = jnp.concatenate(by_bit(yi, mixed_other, mixed_last), axis=0)
-    mixed = jnp.concatenate(by_bit(yi, mixed_heads, others_heads), axis=1)
+        *stage(flag, attend_out, after(line.enter(mixed_heads), up_parts[0], up_high))
+    )
+    normed_two = gather_tokens(normed_two, yi, ci, up_parts[1], up_parts[3])
     activated, slope = matmul(
         normed_two,
         up_parts,
@@ -1043,8 +1055,17 @@
         (shape(length, ff_here), shape(length, ff_here, wide)),
     )
 
+    mixed_last = lax.ppermute(after(mixed_home, activated), "y", SWAP)
+    others_heads = jnp.concatenate(by_bit(yi, mixed_other, mixed_last), axis=0)
+    mixed = jnp.concatenate(by_bit(yi, mixed_heads, others_heads), axis=1)
+
     down_bias_part = jnp.sum(cot_wide, axis=0)
-    down_far = far_terms(after(activated, mixed), cot_all, ff_part)
+    down_sum = grad_chunk(
+        after(activated, down_parts[1], mixed), cot_all, paired, 0, ff_part, model
+    )
+    down_pair = lax.psum_scatter(
+        down_sum.reshape(z_count, 2, ff_part, model), "z", scatter_dimension=0, tiled=False
+    )
     hidden_grad, up_bias_part = matmul(
         cot_all,
         down_parts,
@@ -1066,13 +1087,20 @@
         (),
         (shape(length, model),),
     )
-    (down_sum,) = line.leave(
-        near_terms(line.enter(activated), cot_all, ff_part, down_far)
-    )
-    down_shard = sum_over_z(down_sum)
-
     def norm_two_back(norm_two_partial):
-        norm_two_grad = scatter_tokens(norm_two_partial, yi, ci)
+        home, away = core_sum(norm_two_partial, yi, ci)
+        other = lax.ppermute(away, "y", SWAP)
+        (down_partial,) = plain_matmul(
+            after(activated, away),
+            down_parts,
+            down_offsets,
+            (ff_here, model),
+            False,
+            store_low,
+            (),
+            (shape(length, model),),
+        )
+        norm_two_grad = home_sum(home, after(other, down_partial))
         resid_part, gain_two_grad, shift_two_grad = norm_back(
             residual_one, gain_two, norm_two_grad
         )
@@ -1081,9 +1109,9 @@
         branch_pair = jnp.concatenate(
             by_bit(ci, branch_grad, lax.ppermute(branch_grad, "c", SWAP)), axis=0
         )
-        return branch_pair, residual_grad, gain_two_grad, shift_two_grad
-
-    branch_pair, residual_grad, gain_two_grad, shift_two_grad = line.leave(
+        return branch_pair, residual_grad, gain_two_grad, shift_two_grad, down_partial
+
+    branch_pair, residual_grad, gain_two_grad, shift_two_grad, down_partial = line.leave(
         *stage(flag, norm_two_back, line.enter(norm_two_partial))
     )
 
@@ -1104,9 +1132,13 @@
         away = lax.dynamic_slice_in_dim(mixed_grad_pair, (1 - yi) * part, part, 1)
         home = lax.dynamic_slice_in_dim(mixed_grad_pair, yi * part, part, 1)
         theirs = lax.ppermute(away, "y", SWAP)
-        return jnp.concatenate(by_bit(yi, home, theirs), axis=0)
-
-    (mixed_grad,) = line.leave(stage(flag, out_back, line.enter(branch_pair)))
+        feed_home, feed_away = core_sum(after(down_partial, away), yi, ci)
+        theirs = after(theirs, feed_away)
+        return jnp.concatenate(by_bit(yi, home, theirs), axis=0), feed_home, feed_away
+
+    mixed_grad, feed_home, feed_away = line.leave(
+        *stage(flag, out_back, line.enter(branch_pair))
+    )
     away = lax.dynamic_slice_in_dim(branch_pair, (1 - yi) * half, half, 1)
     home = lax.dynamic_slice_in_dim(branch_pair, yi * half, half, 1)
     branch_other = lax.ppermute(after(away, mixed_grad), "y", SWAP)
@@ -1124,9 +1156,11 @@
     )
     qkv_far = far_terms(normed_one, proj_grad, piece_d)
     (up_sum,) = line.leave(
-        near_terms(line.enter(after(normed_two, branch_other)), hidden_grad, piece_d, up_far)
-    )
-    up_shard = sum_over_z(up_sum)
+        near_terms(
+            line.enter(after(normed_two, branch_other)), hidden_grad, piece_d, up_far
+        )[0]
+    )
+    up_shard = sum_over_z(after(up_sum, down_pair))
     (norm_one_partial,) = matmul(
         proj_grad,
         qkv_parts,
@@ -1139,7 +1173,7 @@
     )
 
     out_sum = line.leave(
-        weight_grad(
+        *weight_grad(
             line.enter(mixed),
             branch_all,
             blocks_at(out_blocks, 0),
@@ -1148,59 +1182,30 @@
             half,
         )
     )[0]
-    down_other = lax.ppermute(after(down_shard, mixed_grad), "y", SWAP)
+    feed_other = lax.ppermute(after(feed_away, up_sum), "y", SWAP)
 
     def norm_one_back(norm_one_partial):
         home, away = core_sum(norm_one_partial, yi, ci)
-        (down_partial,) = plain_matmul(
-            after(activated, away),
-            down_parts,
-            down_offsets,
-            (ff_here, model),
-            False,
-            store_low,
-            (),
-            (shape(length, model),),
-        )
         away = lax.ppermute(away, "y", SWAP)
-        norm_one_grad = home_sum(home, after(away, down_partial))
+        norm_one_grad = home_sum(home, away)
         input_part, gain_one_grad, shift_one_grad = norm_back(inputs, gain_one, norm_one_grad)
         input_grad = (residual_grad + input_part).reshape(1, tok_count, model)
-        feed_home, feed_away = core_sum(down_partial, yi, ci)
-        return (
-            input_grad,
-            gain_one_grad,
-            shift_one_grad,
-            feed_home,
-            feed_away,
+        return input_grad, gain_one_grad, shift_one_grad
+
+    input_grad, gain_one_grad, shift_one_grad = line.leave(
+        *stage(flag, norm_one_back, after(line.enter(norm_one_partial), feed_other))
+    )
+    qkv_sums = line.leave(
+        *near_terms(
+            line.enter(after(normed_one, up_shard)), proj_grad, piece_d, qkv_far, 2
         )
-
-    (
-        input_grad,
-        gain_one_grad,
-        shift_one_grad,
-        feed_home,
-        feed_away,
-    ) = line.leave(
-        *stage(flag, norm_one_back, after(line.enter(norm_one_partial), down_other))
-    )
-    (qkv_sum,) = line.leave(
-        near_terms(
-            after(line.enter(normed_one), up_shard), proj_grad, piece_d, qkv_far
-        )
-    )
-    qkv_shard = sum_over_z(qkv_sum)
+    )
+    qkv_shards = [sum_over_z(total) for total in qkv_sums]
 
     def ends(up_shard):
-        feed_other = lax.ppermute(feed_away, "y", SWAP)
-        up_other = lax.ppermute(up_shard, "y", SWAP)
         feed_out = home_sum(feed_home, feed_other)
         output_shard = (residual_one + feed_out + bias_down).astype(low)
         output_shard = output_shard.reshape(1, tok_count, model)
-        out_away = lax.ppermute(out_sum[:z_count], "x", SWAP)
-        out_shard = sum_small(
-            (out_sum[z_count:].astype(wide) + out_away.astype(wide)).astype(low)
-        ).astype(low)
         up_bias_grad = jnp.where(
             (jnp.arange(4, dtype=jnp.int32) == si)[None, :, None],
             up_bias_part.reshape(shard_count, 1, ff_part),
@@ -1222,31 +1227,38 @@
         )
         for name in ("c", "y"):
             vector_grad = vector_grad + lax.ppermute(vector_grad, name, SWAP)
+        up_shard = after(up_shard, vector_grad)
         vector_grad = vector_grad.reshape(z_count, 2, -1)
         away = lax.dynamic_index_in_dim(vector_grad, 1 - xi, 1, keepdims=False)
         home = lax.dynamic_index_in_dim(vector_grad, xi, 1, keepdims=False)
         vector_grad = home + lax.ppermute(away, "x", SWAP)
+        up_other = lax.ppermute(up_shard, "y", SWAP)
+        down_far = lax.ppermute(after(down_pair[1], vector_grad), "x", SWAP)
+        down_shard = (down_pair[0].astype(wide) + down_far.astype(wide)).astype(low)
+        down_other = lax.ppermute(after(down_shard, up_other), "y", SWAP)
+        out_away = lax.ppermute(after(out_sum[:z_count], down_far), "x", SWAP)
+        out_both = (out_sum[z_count:].astype(wide) + out_away.astype(wide)).astype(low)
         vector_total = sum_small(vector_grad)
         up_pieces = core_pieces(up_shard, up_other)
         return (
             output_shard,
             vector_total,
-            out_shard,
+            out_both,
+            widen_rows(core_pieces(down_shard, down_other), places),
             widen_columns(up_pieces, places, shard_count),
         )
 
-    output_shard, vector_total, out_shard, up_total = line.leave(
+    output_shard, vector_total, out_both, down_total, up_total = line.leave(
         *stage(flag, ends, line.enter(up_shard))
     )
 
-    def last(qkv_shard):
-        return (
-            widen_heads(seq_pieces(qkv_shard), places),
-            widen_quarters(seq_pieces(out_shard), places),
-            widen_rows(core_pieces(down_shard, down_other), places),
-        )
-
-    qkv_total, out_total, down_total = stage(flag, last, after(qkv_shard, up_total))
+    out_shard = sum_over_z(after(out_both, *qkv_shards))
+
+    def last(qkv_low, qkv_high):
+        return widen_heads([seq_pieces(qkv_low), seq_pieces(qkv_high)], places)
+
+    qkv_total = stage(flag, last, after(qkv_shards[0], up_total), qkv_shards[1])
+    out_total = widen_quarters(seq_pieces(after(out_shard, qkv_total)), places)
     vectors = [vector_total[slot * piece_d : (slot + 1) * piece_d] for slot in range(5)]
     return (
         output_shard,

time: 813 us -> 723 us (0.89)
  waiting for transfers between devices: 371 us -> 290 us
  loops' own time: 14.7 us -> 1.54 us
    ppermute x3 -> x2, waiting for transfers between devices: 38.4 us -> 0.01 us  [far_terms(): return lax.ppermute(terms, 'x', SWAP)]
    ppermute x4, waiting for transfers between devices: 63.6 us -> 37.8 us  [gather_weight(): return [near, lax.ppermute(after(near, *others), 'x', SWAP)]]
    ppermute x6 -> x3, waiting for transfers between devices: 22.7 us -> 1.86 us  [sum_small(): lax.ppermute(term(j), 'z', [(i, (i - j) % z_count) for i in range(z_count)])]
    ppermute x1, waiting for transfers between devices: 5.82 us -> 23.8 us  [norm_one_back(): away = lax.ppermute(away, 'y', SWAP)]
    another operation x6, loops' own time: 14.7 us -> 1.54 us  [stage(): return lax.cond(flag, work, nothing, *args)]
    ppermute x1, waiting for transfers between devices: 13.8 us -> 1.2 us  [ends(): up_other = lax.ppermute(up_shard, 'y', SWAP)]
    all_gather x2, waiting for transfers between devices: 7.34 us -> 17.1 us  [the longest x1 17.1 us: split_shards(): up_high = lax.all_gather(slices[2], 'z', axis=0, tiled=False)]
    ppermute x1, waiting for transfers between devices: 12.5 us -> 4.2 us  [out_back(): theirs = lax.ppermute(away, 'y', SWAP)]
  transfers between devices with their start and end apart: 70 -> 72, of which waited for: 39 -> 38; matrix products, arithmetic and copies ran while one was open for 13% -> 14% of each run, Pallas kernels for 25% -> 31%
where the time goes in v3:
time: 723 us; the launch traced here: 714 us
  waiting for transfers between devices  290 us (40%)
  Pallas kernels  233 us (32%)
  other arithmetic  75.7 us (10%)
  starting transfers between devices  57.3 us (8%)
  local copies, waits for them, and re-layouts  40.7 us (6%)
  between operations  14.9 us (2%)
    pallas_call x8, Pallas kernels, weight_matmul(): pl.pallas_call(kernel, grid_spec=pltpu.PrefetchScalarGridSpec(num_scalar_...  113 us
    ppermute x6, waiting for transfers between devices, seq_pieces(): return core_pieces(block, after(lax.ppermute(block, 'y', SWAP), *others))  74.1 us
    pallas_call x6, Pallas kernels, weight_grad(): pl.pallas_call(kernel, grid_spec=pltpu.PrefetchScalarGridSpec(num_scalar_...  59.7 us
    ppermute x4, waiting for transfers between devices, gather_weight(): return [near, lax.ppermute(after(near, *others), 'x', SWAP)]  37.8 us
    ppermute x1, waiting for transfers between devices, norm_one_back(): away = lax.ppermute(away, 'y', SWAP)  23.8 us
    pallas_call x4, Pallas kernels, widen(): pl.pallas_call(kernel, grid_spec=pltpu.PrefetchScalarGridSpec(num_scalar_...  23.2 us
    ppermute x1, waiting for transfers between devices, ends(): down_far = lax.ppermute(after(down_pair[1], vector_grad), 'x', SWAP)  20.4 us
    ppermute x1, waiting for transfers between devices, split_shards(): up_parts += [up_high, lax.ppermute(after(up_high, mixed_heads), 'x', SWAP)]  19 us
  transfers between devices with their start and end apart: 72, of which 38 were waited for; matrix products, arithmetic and copies ran while one was open for 14% of the time, Pallas kernels for 31%

profile of v3, /device:TPU:0, one launch (start us, length us, event | category | flops | bytes accessed | tf_op | source)
XLA Modules:
  0.0 713.5 jit_solution(1473990312917431551)
XLA Ops:
  30.8 8.9 %collective-permute-done.36 = f32[2304]{0:T(1024)S(1)} collective-permute-done((f32[2304]{0:T(1024)S(1)}, f32[2304]{0:T(1024)S(1)}, u32[]{:S(2)}, u32[]{:S(2)}) %collective-permute-start.36) | collective-permute-done | bytes 9248 | tf_op jit(solution)/shard_map/ppermute | solution.py:289
  47.6 21.6 %collective-permute-done.38 = bf16[256,2048]{1,0:T(8,128)(2,1)S(1)} collective-permute-done((bf16[256,2048]{1,0:T(8,128)(2,1)}, bf16[256,2048]{1,0:T(8,128)(2,1)S(1)}, u32[]{:S(2)}, u32[]{:S(2)}) %collective-permute-start.38) | collective-permute-done | bytes 1048608 | tf_op jit(solution)/shard_map/ppermute | solution.py:323
  69.2 8.9 %all-gather.14.cloned.1.call-done = bf16[1024,1536]{1,0:T(8,128)(2,1)} async-done(((bf16[256,1536]{1,0:T(8,128)(2,1)}), bf16[1024,1536]{1,0:T(8,128)(2,1)}) %all-gather.14.cloned.1.call-update) | async-done | bytes 3145744 | tf_op jit(solution)/shard_map/all_gather | solution.py:293
  86.7 23.7 %collective-permute-done.41 = bf16[256,2048]{1,0:T(8,128)(2,1)S(1)} collective-permute-done((bf16[256,2048]{1,0:T(8,128)(2,1)S(1)}, bf16[256,2048]{1,0:T(8,128)(2,1)S(1)}, u32[]{:S(2)}, u32[]{:S(2)}) %collective-permute-start.41) | collective-permute-done | bytes 1048608 | tf_op jit(solution)/shard_map/ppermute | solution.py:323
  114.5 34.6 %collective-permute-done.43.refs_1_ = bf16[4,256,1536]{2,1,0:T(8,128)(2,1)} collective-permute-done((bf16[4,256,1536]{2,1,0:T(8,128)(2,1)}, bf16[4,256,1536]{2,1,0:T(8,128)(2,1)}, u32[]{:S(2)}, u32[]{:S(2)}) %collective-permute-start.43) | collective-permute-done | bytes 3145760 | tf_op jit(solution)/shard_map/ppermute | solution.py:294
  156.1 14.0 %shard_map.240.q_ref.k_ref.v_ref = bf16[1024,1536]{1,0:T(8,128)(2,1)} custom-call(s32[2,8]{1,0:T(2,128)} %stack.306.offs_ref, bf16[1024,2048]{1,0:T(8,128)(2,1)} %pad_maximum_fusion.3.left_ref, bf16[4,256,1536]{2,1,0:T(8,128)(2,1)} %bitcast.146, bf16[4,256,1536]{2,1,0:T(8,128)(2,1)} %collective-permute-done.43.refs_1_), custom_call_target="tpu_custom_call" | custom-call | flops 64424508 | bytes 136314 | tf_op jit(solution)/shard_map/pallas_call | solution.py:450
  170.6 11.4 %shard_map.241 = (bf16[1024,512]{1,0:T(8,128)(2,1)}, f32[4,1024,1]{2,1,0:T(8,128)}) custom-call(bf16[1024,1536]{1,0:T(8,128)(2,1)} %shard_map.240.q_ref.k_ref.v_ref, bf16[1024,1536]{1,0:T(8,128)(2,1)} %shard_map.240.q_ref.k_ref.v_ref, bf16[1024,1536]{1,0:T(8,128)(2,1)} %shard_map.240.q_ref.k_ref.v_ref, s32[1024,1]{1,0:T(8,128)} %copy.31.qi_ref, ...), custom_call_target="tpu_custom_call" | custom-call | flops 21474836 | bytes 41943 | tf_op jit(solution)/shard_map/pallas_call | solution.py:657
  183.6 17.1 %all-gather.18.cloned.1.call-done = bf16[1024,1024]{1,0:T(8,128)(2,1)} async-done(((bf16[256,1024]{1,0:T(8,128)(2,1)}), bf16[1024,1024]{1,0:T(8,128)(2,1)}) %all-gather.18.cloned.1.call-update) | async-done | bytes 2097168 | tf_op jit(solution)/shard_map/all_gather | solution.py:1006
  206.7 36.4 %conditional.6 = (bf16[256,2048]{1,0:T(8,128)(2,1)}, f32[256,2048]{1,0:T(8,128)}, bf16[512,512]{1,0:T(8,128)(2,1)S(1)}, bf16[512,512]{1,0:T(8,128)(2,1)S(1)}) conditional(s32[]{:T(128)} %bitcast.31, () %tuple.111, (s32[]{:T(128)}, bf16[1024,512]{1,0:T(8,128)(2,1)}, s32[2,16]{1,0:T(2,128)S(1)}, bf16[4,128,1024]{2,1,0:T(8,128)(2,1)}, ...), branch_computations={%region_4.5_spmd, %region_5.8_spmd} | conditional | flops 30912284 | bytes 39470188 | solution.py:303
  209.8 10.6 %collective-permute-done.8 = bf16[512,512]{1,0:T(8,128)(2,1)S(1)} collective-permute-done((bf16[512,512]{1,0:T(8,128)(2,1)S(1)}, bf16[512,512]{1,0:T(8,128)(2,1)S(1)}, u32[]{:S(2)}, u32[]{:S(2)}) %collective-permute-start.8) | collective-permute-done | bytes 524320 | tf_op jit(solution)/shard_map/cond/branch_1_fun/ppermute | solution.py:1021
  245.1 19.0 %collective-permute-done.50.refs_3_ = bf16[4,256,1024]{2,1,0:T(8,128)(2,1)} collective-permute-done((bf16[4,256,1024]{2,1,0:T(8,128)(2,1)}, bf16[4,256,1024]{2,1,0:T(8,128)(2,1)}, u32[]{:S(2)}, u32[]{:S(2)}) %collective-permute-start.50) | collective-permute-done | bytes 2097184 | tf_op jit(solution)/shard_map/ppermute | solution.py:1042
  276.8 20.7 %shard_map.242 = (bf16[1024,2048]{1,0:T(8,128)(2,1)}, f32[1024,2048]{1,0:T(8,128)}) custom-call(s32[2,16]{1,0:T(2,128)} %get-tuple-element.417.offs_ref, bf16[1024,2048]{1,0:T(8,128)(2,1)} %pad_maximum_fusion.5.left_ref, bf16[4,256,1024]{2,1,0:T(8,128)(2,1)} %bitcast.149, bf16[4,256,1024]{2,1,0:T(8,128)(2,1)} %collective-permute-done.49.refs_1_, ...), custom_call_target="tpu_custom_call" | custom-call | flops 85899344 | bytes 251740 | tf_op jit(solution)/shard_map/pallas_call | solution.py:450
  299.9 11.7 %collective-permute-done.53 = bf16[512,512]{1,0:T(8,128)(2,1)} collective-permute-done((bf16[512,512]{1,0:T(8,128)(2,1)S(1)}, bf16[512,512]{1,0:T(8,128)(2,1)}, u32[]{:S(2)}, u32[]{:S(2)}) %collective-permute-start.53) | collective-permute-done | bytes 524320 | tf_op jit(solution)/shard_map/ppermute | solution.py:1058
  317.9 14.8 %shard_map.243 = bf16[8,256,2048]{2,1,0:T(8,128)(2,1)} custom-call(s32[9]{0:T(128)} %stack.150.where_ref, bf16[1024,2048]{1,0:T(8,128)(2,1)S(1)} %copy-done.3, bf16[1024,2048]{1,0:T(8,128)(2,1)} %pad_maximum_fusion.4.right_ref.left_ref), custom_call_target="tpu_custom_call" | custom-call | flops 85899344 | bytes 251658 | tf_op jit(solution)/shard_map/pallas_call | solution.py:514
  333.5 17.6 %shard_map.244 = (bf16[1024,2048]{1,0:T(8,128)(2,1)}, f32[1,2048]{1,0:T(1,128)S(1)}) custom-call(s32[2,16]{1,0:T(2,128)S(1)} %get-tuple-element.416.offs_ref, bf16[1024,2048]{1,0:T(8,128)(2,1)} %pad_maximum_fusion.4.right_ref.left_ref, bf16[4,256,1024]{2,1,0:T(8,128)(2,1)} %bitcast.157, bf16[4,256,1024]{2,1,0:T(8,128)(2,1)} %collective-permute-done.52.refs_1_, ...), custom_call_target="tpu_custom_call" | custom-call | flops 85899344 | bytes 251740 | tf_op jit(solution)/shard_map/pallas_call | solution.py:450
  351.0 9.5 %shard_map.245 = bf16[4,256,2048]{2,1,0:T(8,128)(2,1)} custom-call(s32[5]{0:T(128)} %stack.307.where_ref, bf16[1024,2048]{1,0:T(8,128)(2,1)} %pad_maximum_fusion.5.left_ref, bf16[1024,2048]{1,0:T(8,128)(2,1)} %get-tuple-element.313.right_ref.left_ref), custom_call_target="tpu_custom_call" | custom-call | flops 42949672 | bytes 146800 | tf_op jit(solution)/shard_map/pallas_call | solution.py:514
  362.1 16.6 %shard_map.246 = bf16[1024,2048]{1,0:T(8,128)(2,1)} custom-call(s32[2,16]{1,0:T(2,128)} %get-tuple-element.417.offs_ref, bf16[1024,2048]{1,0:T(8,128)(2,1)} %get-tuple-element.313.right_ref.left_ref, bf16[4,256,1024]{2,1,0:T(8,128)(2,1)} %bitcast.150, bf16[4,256,1024]{2,1,0:T(8,128)(2,1)} %collective-permute-done.49.refs_1_, ...), custom_call_target="tpu_custom_call" | custom-call | flops 85899344 | bytes 167772 | tf_op jit(solution)/shard_map/pallas_call | solution.py:450
  378.7 51.7 %conditional.7 = (bf16[512,2048]{1,0:T(8,128)(2,1)}, f32[256,2048]{1,0:T(8,128)S(1)}, f32[2048]{0:T(1024)S(1)}, f32[2048]{0:T(1024)S(1)}, bf16[1024,2048]{1,0:T(8,128)(2,1)}) conditional(s32[]{:T(128)} %bitcast.31, () %tuple.106, (s32[]{:T(128)}, bf16[1024,2048]{1,0:T(8,128)(2,1)}, s32[]{:T(128)}, bf16[1024,2048]{1,0:T(8,128)(2,1)}, ...), branch_computations={%region_8.9_spmd, %region_9.16_spmd} | conditional | flops 106867040 | bytes 111385880 | solution.py:303
  397.0 15.9 %branch_1_fun.7 = bf16[1024,2048]{1,0:T(8,128)(2,1)} custom-call(s32[2,16]{1,0:T(2,128)S(1)} %get-tuple-element.142.offs_ref, bf16[1024,2048]{1,0:T(8,128)(2,1)} %get-tuple-element.144.left_ref, bf16[4,256,1024]{2,1,0:T(8,128)(2,1)} %get-tuple-element.145.refs_0_, bf16[4,256,1024]{2,1,0:T(8,128)(2,1)} %get-tuple-element.146.refs_1_, ...), custom_call_target="tpu_custom_call" | custom-call | flops 85899344 | bytes 167772 | tf_op jit(solution)/shard_map/cond/branch_1_fun/pallas_call | solution.py:450
  431.7 26.9 %conditional.8 = (bf16[1024,512]{1,0:T(8,128)(2,1)S(1)}, f32[256,2048]{1,0:T(8,128)}, bf16[256,2048]{1,0:T(8,128)(2,1)}) conditional(s32[]{:T(128)} %bitcast.31, () %tuple.105, (s32[]{:T(128)}, s32[2,16]{1,0:T(2,128)S(1)}, bf16[512,2048]{1,0:T(8,128)(2,1)}, bf16[4,128,1024]{2,1,0:T(8,128)(2,1)}, bf16[4,128,1024]{2,1,0:T(8,128)(2,1)}, ...), branch_computations={%region_16.17_spmd, %region_17.18_spmd} | conditional | flops 27242004 | bytes 38871124 | solution.py:303
  463.3 15.5 %shard_map.247.right_ref.left_ref = bf16[1024,1536]{1,0:T(8,128)(2,1)} custom-call(bf16[1024,1536]{1,0:T(8,128)(2,1)} %shard_map.240.q_ref.k_ref.v_ref, bf16[1024,1536]{1,0:T(8,128)(2,1)} %shard_map.240.q_ref.k_ref.v_ref, bf16[1024,1536]{1,0:T(8,128)(2,1)} %shard_map.240.q_ref.k_ref.v_ref, bf16[1024,512]{1,0:T(8,128)(2,1)S(1)} %get-tuple-element.322.g_ref, ...), custom_call_target="tpu_custom_call" | custom-call | flops 53687092 | bytes 83886 | tf_op jit(solution)/shard_map/pallas_call | solution.py:726
  486.8 10.1 %shard_map.249 = bf16[4,256,2048]{2,1,0:T(8,128)(2,1)} custom-call(s32[5]{0:T(128)} %stack.308.where_ref, bf16[1024,2048]{1,0:T(8,128)(2,1)} %pad_maximum_fusion.5.left_ref, bf16[1024,2048]{1,0:T(8,128)(2,1)} %get-tuple-element.313.right_ref.left_ref, bf16[4,256,2048]{2,1,0:T(8,128)(2,1)} %collective-permute-done.55.refs_0_), custom_call_target="tpu_custom_call" | custom-call | flops 42949672 | bytes 146800 | tf_op jit(solution)/shard_map/pallas_call | solution.py:514
  503.3 13.1 %shard_map.250 = bf16[1024,2048]{1,0:T(8,128)(2,1)} custom-call(s32[2,8]{1,0:T(2,128)} %stack.306.offs_ref, bf16[1024,1536]{1,0:T(8,128)(2,1)} %shard_map.247.right_ref.left_ref, bf16[4,256,1536]{2,1,0:T(8,128)(2,1)} %bitcast.147, bf16[4,256,1536]{2,1,0:T(8,128)(2,1)} %collective-permute-done.43.refs_1_), custom_call_target="tpu_custom_call" | custom-call | flops 64424508 | bytes 136314 | tf_op jit(solution)/shard_map/pallas_call | solution.py:450
  516.4 8.8 %shard_map.251 = bf16[8,128,1024]{2,1,0:T(8,128)(2,1)} custom-call(s32[9]{0:T(128)} %stack.309.where_ref, bf16[1024,1024]{1,0:T(8,128)(2,1)} %pad_maximum_fusion.6.left_ref, bf16[1024,1024]{1,0:T(8,128)(2,1)} %pad_maximum_fusion.7.right_ref), custom_call_target="tpu_custom_call" | custom-call | flops 21474836 | bytes 83886 | tf_op jit(solution)/shard_map/pallas_call | solution.py:514
  526.2 43.8 %conditional.9 = (f32[1,256,2048]{2,1,0:T(8,128)}, f32[2048]{0:T(1024)S(1)}, f32[2048]{0:T(1024)S(1)}) conditional(s32[]{:T(128)} %bitcast.31, () %tuple.139, (bf16[1024,2048]{1,0:T(8,128)(2,1)}, s32[]{:T(128)}, s32[]{:T(128)}, f32[8,256]{1,0:T(8,128)S(1)}, f32[256,2048]{1,0:T(8,128)S(1)}, /*index=5*/f32[256,2048]{1,0:T(8,128)}) %tuple.233), branch_computations={%region_18.19_spmd, %region_19.26_spmd} | conditional | flops 15200526 | bytes 72420688 | solution.py:303
  541.0 23.8 %collective-permute-done.14 = bf16[256,2048]{1,0:T(8,128)(2,1)} collective-permute-done((bf16[256,2048]{1,0:T(8,128)(2,1)S(1)}, bf16[256,2048]{1,0:T(8,128)(2,1)}, u32[]{:S(2)}, u32[]{:S(2)}) %collective-permute-start.14) | collective-permute-done | bytes 1048608 | tf_op jit(solution)/shard_map/cond/branch_1_fun/ppermute | solution.py:1189
  570.6 8.4 %shard_map.252 = (bf16[4,256,768]{2,1,0:T(8,128)(2,1)}, bf16[4,256,768]{2,1,0:T(8,128)(2,1)}) custom-call(s32[5]{0:T(128)} %stack.308.where_ref, bf16[1024,2048]{1,0:T(8,128)(2,1)} %pad_maximum_fusion.3.left_ref, bf16[1024,1536]{1,0:T(8,128)(2,1)} %shard_map.247.right_ref.left_ref, bf16[4,256,1536]{2,1,0:T(8,128)(2,1)} %collective-permute-done.57.refs_0_), custom_call_target="tpu_custom_call" | custom-call | flops 32212254 | bytes 115343 | tf_op jit(solution)/shard_map/pallas_call | solution.py:514
  580.5 83.7 %conditional.10 = (bf16[1,256,2048]{2,1,0:T(8,128)(2,1)}, f32[2304]{0:T(1024)}, bf16[4,128,1024]{2,1,0:T(8,128)(2,1)}, f32[1024,2048]{1,0:T(8,128)}, f32[256,819...) conditional(s32[]{:T(128)} %bitcast.31, () %tuple.104, ...), branch_computations={%region_28.29_spmd, %region_29.31_spmd} | conditional | flops 7399219 | bytes 96925912 | solution.py:303
  595.1 20.4 %collective-permute-done.21 = bf16[256,2048]{1,0:T(8,128)(2,1)S(1)} collective-permute-done((bf16[256,2048]{1,0:T(8,128)(2,1)S(1)}, bf16[256,2048]{1,0:T(8,128)(2,1)S(1)}, u32[]{:S(2)}, u32[]{:S(2)}) %collective-permute-start.21) | collective-permute-done | bytes 1048608 | tf_op jit(solution)/shard_map/cond/branch_1_fun/ppermute | solution.py:1236
  627.6 11.8 %collective-permute-done.25.refs_2_ = bf16[256,2048]{1,0:T(8,128)(2,1)} collective-permute-done((bf16[256,2048]{1,0:T(8,128)(2,1)S(1)}, bf16[256,2048]{1,0:T(8,128)(2,1)}, u32[]{:S(2)}, u32[]{:S(2)}) %collective-permute-start.25) | collective-permute-done | bytes 1048608 | tf_op jit(solution)/shard_map/cond/branch_1_fun/ppermute | solution.py:1238
  664.8 27.7 %conditional.11 = (f32[256,6144]{1,0:T(8,128)}) conditional(s32[]{:T(128)} %bitcast.31, () %tuple.150, (bf16[256,768]{1,0:T(8,128)(2,1)}, bf16[256,768]{1,0:T(8,128)(2,1)}, s32[4]{0:T(128)S(1)}) %tuple.240), branch_computations={%region_33.34_spmd, %region_34.35_spmd} | conditional | bytes 18969156 | solution.py:303
  667.4 9.7 %collective-permute-done.1.refs_2_ = bf16[256,768]{1,0:T(8,128)(2,1)S(1)} collective-permute-done((bf16[256,768]{1,0:T(8,128)(2,1)}, bf16[256,768]{1,0:T(8,128)(2,1)S(1)}, u32[]{:S(2)}, u32[]{:S(2)}) %collective-permute-start.1) | collective-permute-done | bytes 393248 | tf_op jit(solution)/shard_map/cond/branch_1_fun/ppermute | solution.py:323
  (398 shorter events, 298.8 us)
Async XLA Ops:
  7.2 71.0 %all-gather.14.cloned.1.call-start = ((), (), s32[]{:S(2)}) async-start(), calls=%async_computation.11 | async-start | bytes 3932160 | tf_op jit(solution)/shard_map/all_gather | solution.py:293
  11.8 101.1 %all-gather.20.cloned.1.call-start = ((), (), s32[]{:S(2)}) async-start(), calls=%async_computation.14 | async-start | bytes 1310720 | tf_op jit(solution)/shard_map/all_gather | solution.py:293
  44.7 125.5 %all-gather.16.cloned.1.call-start = ((), (), s32[]{:S(2)}) async-start(), calls=%async_computation.12 | async-start | bytes 2621440 | tf_op jit(solution)/shard_map/all_gather | solution.py:293
  45.4 155.2 %all-gather.18.cloned.1.call-start = ((), (), s32[]{:S(2)}) async-start(), calls=%async_computation.13 | async-start | bytes 2621440 | tf_op jit(solution)/shard_map/all_gather | solution.py:1006
  46.0 223.5 %all-gather.22.cloned.1.call-start = ((), (), s32[]{:S(2)}) async-start(), calls=%async_computation.15 | async-start | bytes 2621440 | tf_op jit(solution)/shard_map/all_gather | solution.py:293
  47.6 32.2 %collective-permute-start.37 = (bf16[256,2048]{1,0:T(8,128)(2,1)}, bf16[256,2048]{1,0:T(8,128)(2,1)S(1)}, u32[]{:S(2)}, u32[]{:S(2)}) collective-permute-start(bf16[256,2048]{1,0:T(8,128)(2,1)} %add_convert_fusion.3), channel_id=1, source_target_pairs={{0,1},{1,0},{2,3},{3,2},{4,5},{5,4},{6,7},{7,6},{8,9},{9,8},{10,11... | collective-permute-start | bytes 3145736 | tf_op jit(solution)/shard_map/ppermute | solution.py:327
  78.2 255.3 %all-gather.12.cloned.1.call-start = ((), (), s32[]{:S(2)}) async-start(), calls=%async_computation.5 | async-start | bytes 5242880 | tf_op jit(solution)/shard_map/all_gather | solution.py:1008
  78.3 70.9 %collective-permute-start.43 = (bf16[4,256,1536]{2,1,0:T(8,128)(2,1)}, bf16[4,256,1536]{2,1,0:T(8,128)(2,1)}, u32[]{:S(2)}, u32[]{:S(2)}) collective-permute-start(bf16[4,256,1536]{2,1,0:T(8,128)(2,1)} %bitcast.145), channel_id=1, source_target_pairs={{0,4},{4,0},{1,5},{5,1},{2,6},{6,2},{3,7},{7,3},{8,12},{12,8},{9,1... | collective-permute-start | bytes 9437192 | tf_op jit(solution)/shard_map/ppermute | solution.py:294
  85.3 25.2 %collective-permute-start.41 = (bf16[256,2048]{1,0:T(8,128)(2,1)S(1)}, bf16[256,2048]{1,0:T(8,128)(2,1)S(1)}, u32[]{:S(2)}, u32[]{:S(2)}) collective-permute-start(bf16[256,2048]{1,0:T(8,128)(2,1)S(1)} %bitcast.166), channel_id=1, source_target_pairs={{0,2},{2,0},{1,3},{3,1},{4,6},{6,4},{5,7},{7,5},{8,10},{10,8},{9,1... | collective-permute-start | bytes 3145736 | tf_op jit(solution)/shard_map/ppermute | solution.py:323
  86.7 63.9 %collective-permute-start.40 = (bf16[256,2048]{1,0:T(8,128)(2,1)S(1)}, bf16[256,2048]{1,0:T(8,128)(2,1)}, u32[]{:S(2)}, u32[]{:S(2)}) collective-permute-start(bf16[256,2048]{1,0:T(8,128)(2,1)S(1)} %bitcast.167), channel_id=1, source_target_pairs={{0,1},{1,0},{2,3},{3,2},{4,5},{5,4},{6,7},{7,6},{8,9},{9,8},{10,11... | collective-permute-start | bytes 3145736 | tf_op jit(solution)/shard_map/ppermute | solution.py:327
  110.5 40.2 %collective-permute-start.42 = (bf16[256,2048]{1,0:T(8,128)(2,1)S(1)}, bf16[256,2048]{1,0:T(8,128)(2,1)}, u32[]{:S(2)}, u32[]{:S(2)}) collective-permute-start(bf16[256,2048]{1,0:T(8,128)(2,1)S(1)} %collective-permute-done.41), channel_id=1, source_target_pairs={{0,1},{1,0},{2,3},{3,2},{4,5},{5,4},{6,7},{7,6},{8,9},{9,8},{10,11... | collective-permute-start | bytes 3145736 | tf_op jit(solution)/shard_map/ppermute | solution.py:327
  112.9 384.1 %reduce-scatter.6.cloned.1.call-start = ((), (), s32[]{:S(2)}) async-start(), calls=%async_computation.6 | async-start | bytes 10485760 | tf_op jit(solution)/shard_map/reduce_scatter | solution.py:1066
  113.0 90.3 %collective-permute-start.45 = (bf16[4,128,1024]{2,1,0:T(8,128)(2,1)}, bf16[4,128,1024]{2,1,0:T(8,128)(2,1)}, u32[]{:S(2)}, u32[]{:S(2)}) collective-permute-start(bf16[4,128,1024]{2,1,0:T(8,128)(2,1)} %bitcast.161), channel_id=1, source_target_pairs={{0,2},{2,0},{1,3},{3,1},{4,6},{6,4},{5,7},{7,5},{8,10},{10,8},{9,1... | collective-permute-start | bytes 3145736 | tf_op jit(solution)/shard_map/ppermute | solution.py:933
  149.2 32.9 %collective-permute-start.44 = (bf16[4,128,1024]{2,1,0:T(8,128)(2,1)}, bf16[4,128,1024]{2,1,0:T(8,128)(2,1)}, u32[]{:S(2)}, u32[]{:S(2)}) collective-permute-start(bf16[4,128,1024]{2,1,0:T(8,128)(2,1)} %bitcast.162), channel_id=1, source_target_pairs={{0,4},{4,0},{1,5},{5,1},{2,6},{6,2},{3,7},{7,3},{8,12},{12,8},{9,1... | collective-permute-start | bytes 3145736 | tf_op jit(solution)/shard_map/ppermute | solution.py:294
  170.2 74.9 %collective-permute-start.49 = (bf16[4,256,1024]{2,1,0:T(8,128)(2,1)}, bf16[4,256,1024]{2,1,0:T(8,128)(2,1)}, u32[]{:S(2)}, u32[]{:S(2)}) collective-permute-start(bf16[4,256,1024]{2,1,0:T(8,128)(2,1)} %bitcast.148), channel_id=1, source_target_pairs={{0,4},{4,0},{1,5},{5,1},{2,6},{6,2},{3,7},{7,3},{8,12},{12,8},{9,1... | collective-permute-start | bytes 6291464 | tf_op jit(solution)/shard_map/ppermute | solution.py:294
  182.0 24.6 %collective-permute-start.46 = (bf16[4,128,1024]{2,1,0:T(8,128)(2,1)}, bf16[4,128,1024]{2,1,0:T(8,128)(2,1)}, u32[]{:S(2)}, u32[]{:S(2)}) collective-permute-start(bf16[4,128,1024]{2,1,0:T(8,128)(2,1)} %collective-permute-done.44), channel_id=1, source_target_pairs={{0,2},{2,0},{1,3},{3,1},{4,6},{6,4},{5,7},{7,5},{8,10},{10,8},{9,1... | collective-permute-start | bytes 3145736 | tf_op jit(solution)/shard_map/ppermute | solution.py:933
  200.6 63.5 %collective-permute-start.50 = (bf16[4,256,1024]{2,1,0:T(8,128)(2,1)}, bf16[4,256,1024]{2,1,0:T(8,128)(2,1)}, u32[]{:S(2)}, u32[]{:S(2)}) collective-permute-start(bf16[4,256,1024]{2,1,0:T(8,128)(2,1)} %bitcast.151), channel_id=1, source_target_pairs={{0,4},{4,0},{1,5},{5,1},{2,6},{6,2},{3,7},{7,3},{8,12},{12,8},{9,1... | collective-permute-start | bytes 6291464 | tf_op jit(solution)/shard_map/ppermute | solution.py:1042
  243.0 25.9 %collective-permute-start.48 = (bf16[256,2048]{1,0:T(8,128)(2,1)}, bf16[256,2048]{1,0:T(8,128)(2,1)}, u32[]{:S(2)}, u32[]{:S(2)}) collective-permute-start(bf16[256,2048]{1,0:T(8,128)(2,1)} %get-tuple-element.296), channel_id=1, source_target_pairs={{0,2},{2,0},{1,3},{3,1},{4,6},{6,4},{5,7},{7,5},{8,10},{10,8},{9,1... | collective-permute-start | bytes 3145736 | tf_op jit(solution)/shard_map/ppermute | solution.py:323
  245.1 25.8 %collective-permute-start.47 = (bf16[256,2048]{1,0:T(8,128)(2,1)}, bf16[256,2048]{1,0:T(8,128)(2,1)}, u32[]{:S(2)}, u32[]{:S(2)}) collective-permute-start(bf16[256,2048]{1,0:T(8,128)(2,1)} %get-tuple-element.296), channel_id=1, source_target_pairs={{0,1},{1,0},{2,3},{3,2},{4,5},{5,4},{6,7},{7,6},{8,9},{9,8},{10,11... | collective-permute-start | bytes 3145736 | tf_op jit(solution)/shard_map/ppermute | solution.py:327
  269.5 48.4 %collective-permute-start.52 = (bf16[4,256,1024]{2,1,0:T(8,128)(2,1)}, bf16[4,256,1024]{2,1,0:T(8,128)(2,1)}, u32[]{:S(2)}, u32[]{:S(2)}) collective-permute-start(bf16[4,256,1024]{2,1,0:T(8,128)(2,1)} %bitcast.156), channel_id=1, source_target_pairs={{0,4},{4,0},{1,5},{5,1},{2,6},{6,2},{3,7},{7,3},{8,12},{12,8},{9,1... | collective-permute-start | bytes 6291464 | tf_op jit(solution)/shard_map/ppermute | solution.py:294
  332.7 237.9 %reduce-scatter.8.cloned.1.call-start = ((), (), s32[]{:S(2)}) async-start(), calls=%async_computation.7 | async-start | bytes 5242880 | tf_op jit(solution)/shard_map/reduce_scatter | solution.py:986
  360.6 126.3 %collective-permute-start.55 = (bf16[4,256,2048]{2,1,0:T(8,128)(2,1)}, bf16[4,256,2048]{2,1,0:T(8,128)(2,1)}, u32[]{:S(2)}, u32[]{:S(2)}) collective-permute-start(bf16[4,256,2048]{2,1,0:T(8,128)(2,1)} %shard_map.245), channel_id=1, source_target_pairs={{0,4},{4,0},{1,5},{5,1},{2,6},{6,2},{3,7},{7,3},{8,12},{12,8},{9,1... | collective-permute-start | bytes 12582920 | tf_op jit(solution)/shard_map/ppermute | solution.py:978
  391.5 25.4 %collective-permute-start.11 = (bf16[256,2048]{1,0:T(8,128)(2,1)S(1)}, bf16[256,2048]{1,0:T(8,128)(2,1)}, u32[]{:S(2)}, u32[]{:S(2)}) collective-permute-start(bf16[256,2048]{1,0:T(8,128)(2,1)S(1)} %fusion.1), channel_id=1, source_target_pairs={{0,2},{2,0},{1,3},{3,1},{4,6},{6,4},{5,7},{7,5},{8,10},{10,8},{9,1... | collective-permute-start | bytes 3145736 | tf_op jit(solution)/shard_map/cond/branch_1_fun/ppermute | solution.py:1092
  460.9 25.9 %collective-permute-start.54 = (bf16[512,1024]{1,0:T(8,128)(2,1)}, bf16[512,1024]{1,0:T(8,128)(2,1)}, u32[]{:S(2)}, u32[]{:S(2)}) collective-permute-start(bf16[512,1024]{1,0:T(8,128)(2,1)} %constant_dynamic-slice_fusion.3), channel_id=1, source_target_pairs={{0,2},{2,0},{1,3},{3,1},{4,6},{6,4},{5,7},{7,5},{8,10},{10,8},{9,1... | collective-permute-start | bytes 3145736 | tf_op jit(solution)/shard_map/ppermute | solution.py:1144
  497.0 167.3 %reduce-scatter.12.cloned.1.call-start = ((), (), s32[]{:S(2)}) async-start(), calls=%async_computation.9 | async-start | bytes 1966080 | tf_op jit(solution)/shard_map/reduce_scatter | solution.py:986
  497.0 73.5 %collective-permute-start.57 = (bf16[4,256,1536]{2,1,0:T(8,128)(2,1)}, bf16[4,256,1536]{2,1,0:T(8,128)(2,1)}, u32[]{:S(2)}, u32[]{:S(2)}) collective-permute-start(bf16[4,256,1536]{2,1,0:T(8,128)(2,1)} %shard_map.248), channel_id=1, source_target_pairs={{0,4},{4,0},{1,5},{5,1},{2,6},{6,2},{3,7},{7,3},{8,12},{12,8},{9,1... | collective-permute-start | bytes 9437192 | tf_op jit(solution)/shard_map/ppermute | solution.py:978
  497.7 27.5 %collective-permute-start.56 = (bf16[256,2048]{1,0:T(8,128)(2,1)}, bf16[256,2048]{1,0:T(8,128)(2,1)S(1)}, u32[]{:S(2)}, u32[]{:S(2)}) collective-permute-start(bf16[256,2048]{1,0:T(8,128)(2,1)} %get-tuple-element.326), channel_id=1, source_target_pairs={{0,2},{2,0},{1,3},{3,1},{4,6},{6,4},{5,7},{7,5},{8,10},{10,8},{9,1... | collective-permute-start | bytes 3145736 | tf_op jit(solution)/shard_map/ppermute | solution.py:1185
  539.4 25.4 %collective-permute-start.14 = (bf16[256,2048]{1,0:T(8,128)(2,1)S(1)}, bf16[256,2048]{1,0:T(8,128)(2,1)}, u32[]{:S(2)}, u32[]{:S(2)}) collective-permute-start(bf16[256,2048]{1,0:T(8,128)(2,1)S(1)} %fusion.3), channel_id=1, source_target_pairs={{0,2},{2,0},{1,3},{3,1},{4,6},{6,4},{5,7},{7,5},{8,10},{10,8},{9,1... | collective-permute-start | bytes 3145736 | tf_op jit(solution)/shard_map/cond/branch_1_fun/ppermute | solution.py:1189
  579.0 85.3 %reduce-scatter.10.cloned.1.call-start = ((), (), s32[]{:S(2)}) async-start(), calls=%async_computation.8 | async-start | bytes 1966080 | tf_op jit(solution)/shard_map/reduce_scatter | solution.py:986
  579.6 113.0 %reduce-scatter.14.cloned.1.call-start = ((), (), s32[]{:S(2)}) async-start(), calls=%async_computation.10 | async-start | bytes 1310720 | tf_op jit(solution)/shard_map/reduce_scatter | solution.py:986
  627.4 28.5 %collective-permute-start.23 = (bf16[256,2048]{1,0:T(8,128)(2,1)S(1)}, bf16[256,2048]{1,0:T(8,128)(2,1)S(1)}, u32[]{:S(2)}, u32[]{:S(2)}) collective-permute-start(bf16[256,2048]{1,0:T(8,128)(2,1)S(1)} %fusion.4.refs_0_), channel_id=1, source_target_pairs={{0,1},{1,0},{2,3},{3,2},{4,5},{5,4},{6,7},{7,6},{8,9},{9,8},{10,11... | collective-permute-start | bytes 3145736 | tf_op jit(solution)/shard_map/cond/branch_1_fun/ppermute | solution.py:327
  627.4 25.9 %collective-permute-start.22 = (bf16[4,128,1024]{2,1,0:T(8,128)(2,1)}, bf16[4,128,1024]{2,1,0:T(8,128)(2,1)}, u32[]{:S(2)}, u32[]{:S(2)}) collective-permute-start(bf16[4,128,1024]{2,1,0:T(8,128)(2,1)} %slice.55), channel_id=1, source_target_pairs={{0,4},{4,0},{1,5},{5,1},{2,6},{6,2},{3,7},{7,3},{8,12},{12,8},{9,1... | collective-permute-start | bytes 3145736 | tf_op jit(solution)/shard_map/cond/branch_1_fun/ppermute | solution.py:1239
  (93 other events, 817.2 us)
Sparse Core Ops, SparseCore 0:
  11.9 66.1 all-gather.13
  80.3 26.5 all-gather.19
  109.1 45.4 all-gather.15
  156.0 44.6 all-gather.17
  202.1 44.6 all-gather.21
  248.8 79.4 all-gather.11
  332.8 143.3 reduce-scatter.5
  497.1 73.4 reduce-scatter.7
  579.1 35.8 reduce-scatter.11
  617.8 34.5 reduce-scatter.9
  664.4 27.1 reduce-scatter.13

commit v4 on v3

--- a/solution.py
+++ b/solution.py
@@ -340,23 +340,42 @@
     return jnp.concatenate(rows, axis=0)
 
 
-def core_sum(partial, yi, ci):
-    tokens = partial.shape[0] // 4
-    parts = partial.reshape(2, 2, tokens, partial.shape[1])
-    away = lax.dynamic_index_in_dim(parts, 1 - ci, 1, keepdims=False)
-    home = lax.dynamic_index_in_dim(parts, ci, 1, keepdims=False)
-    total = home.astype(jnp.float32) + lax.ppermute(away, "c", SWAP).astype(jnp.float32)
-    away = lax.dynamic_index_in_dim(total, 1 - yi, 0, keepdims=False).astype(jnp.bfloat16)
-    return lax.dynamic_index_in_dim(total, yi, 0, keepdims=False), away
+def core_sum(parts, yi):
+    away, home = parts
+    other = lax.ppermute(away, "c", SWAP)
+    tokens, model = home.shape[0] // 2, home.shape[1]
+    steps = 4
+    block = (tokens // steps, model)
+
+    def kernel(at_ref, *refs):
+        wide = jnp.float32
+        refs[4][...] = refs[0][...].astype(wide) + refs[1][...].astype(wide)
+        refs[5][...] = (refs[2][...].astype(wide) + refs[3][...].astype(wide)).astype(
+            jnp.bfloat16
+        )
+
+    here = pl.BlockSpec(block, lambda i, at: (at[0] * steps + i, 0))
+    there = pl.BlockSpec(block, lambda i, at: ((1 - at[0]) * steps + i, 0))
+    out = pl.BlockSpec(block, lambda i, at: (i, 0))
+    return pl.pallas_call(
+        kernel,
+        grid_spec=pltpu.PrefetchScalarGridSpec(
+            num_scalar_prefetch=1,
+            grid=(steps,),
+            in_specs=[here, here, there, there],
+            out_specs=[out, out],
+        ),
+        out_shape=[
+            jax.ShapeDtypeStruct((tokens, model), jnp.float32),
+            jax.ShapeDtypeStruct((tokens, model), jnp.bfloat16),
+        ],
+        cost_estimate=cost(flops=0, bytes_accessed=7 * tokens * model, transcendentals=0),
+        compiler_params=params(),
+    )(jnp.reshape(yi, (1,)).astype(jnp.int32), home, other, home, other)
 
 
 def home_sum(home, other):
     return home + other.astype(jnp.float32)
-
-
-def scatter_tokens(partial, yi, ci, *others):
-    home, away = core_sum(partial, yi, ci)
-    return home_sum(home, after(lax.ppermute(away, "y", SWAP), *others))
 
 
 COST_SCALE = 0.01
@@ -374,7 +393,7 @@
     return pltpu.CompilerParams(vmem_limit_bytes=limit)
 
 
-def weight_matmul(left, pieces, offsets, shape, back, body, extras, outs, chunk):
+def weight_matmul(left, pieces, offsets, shape, back, body, extras, outs, chunk, groups=None):
     rows = left.shape[0]
     depth, width = shape
     out_width = depth if back else width
@@ -384,7 +403,11 @@
     block_rows, block_cols = pieces[0].shape[1:]
     row_count, col_count = depth // block_rows, width // block_cols
 
-    def kernel(offs_ref, left_ref, *refs):
+    tables = (offsets,) if groups is None else (offsets, groups)
+
+    def kernel(*refs):
+        table_refs, left_ref, refs = refs[: len(tables)], refs[len(tables)], refs[len(tables) + 1 :]
+        offs_ref = table_refs[0]
         piece_refs = refs[:n_pieces]
         extra_refs = refs[n_pieces : n_pieces + n_extras]
         out_refs = refs[n_pieces + n_extras : -2]
@@ -427,21 +450,30 @@
                         arrive(row, col)
 
         start = pl.ds(pl.multiple_of(step * chunk, chunk), chunk)
-        if back:
-            values = lax.dot_general(
-                left_ref[...],
-                held[start, :],
-                (((1,), (1,)), ((), ())),
-                preferred_element_type=jnp.float32,
-            )
+
+        def product(part):
+            if back:
+                return lax.dot_general(
+                    part,
+                    held[start, :],
+                    (((1,), (1,)), ((), ())),
+                    preferred_element_type=jnp.float32,
+                )
+            return jnp.dot(part, held[:, start], preferred_element_type=jnp.float32)
+
+        if groups is None:
+            body(product(left_ref[...]), extra_refs, out_refs)
         else:
-            values = jnp.dot(
-                left_ref[...], held[:, start], preferred_element_type=jnp.float32
-            )
-        body(values, extra_refs, out_refs)
+            size = rows // groups.shape[0]
+            each = out_refs[0].shape[0] // size
+            for g in range(groups.shape[0]):
+                at = pl.multiple_of(table_refs[1][g] * size, size)
+                values = product(left_ref[pl.ds(at, size), :])
+                to = (g % each) * size
+                out_refs[g // each][to : to + size, :] = values.astype(jnp.bfloat16)
 
     def column_spec(array):
-        return pl.BlockSpec((array.shape[0], chunk), lambda i, offs: (0, i))
+        return pl.BlockSpec((array.shape[0], chunk), lambda i, *tabs: (0, i))
 
     flops = 2 * rows * depth * width
     moved = 2 * (left.size + depth * width) + sum(
@@ -450,11 +482,11 @@
     return pl.pallas_call(
         kernel,
         grid_spec=pltpu.PrefetchScalarGridSpec(
-            num_scalar_prefetch=1,
+            num_scalar_prefetch=len(tables),
             grid=(steps,),
             in_specs=[
                 pl.BlockSpec(
-                    left.shape, lambda i, offs: (0, 0), pipeline_mode=pl.Buffered(1)
+                    left.shape, lambda i, *tabs: (0, 0), pipeline_mode=pl.Buffered(1)
                 )
             ]
             + [pl.BlockSpec(memory_space=pl.ANY)] * n_pieces
@@ -468,7 +500,7 @@
         out_shape=list(outs),
         cost_estimate=cost(flops=flops, bytes_accessed=moved, transcendentals=0),
         compiler_params=params(),
-    )(offsets, left, *pieces, *extras)
+    )(*tables, left, *pieces, *extras)
 
 
 def store_low(values, extra_refs, out_refs):
@@ -810,29 +842,24 @@
     )
 
 
-def widen_heads(chunks, places):
-    rows, width = chunks[0][0].shape
-    heads = H // 4
-    part = heads * HD
+def widen_heads(pieces, places):
+    rows, width = pieces[0].shape
+    part = width // 3
 
     def write(n, pos, piece, out):
         first = lax.div(pos, 2) * part * 2 + lax.rem(pos, 2) * HD
-        for i in range(width // HD):
-            head = n * (width // HD) + i
-
-            @pl.when(pl.program_id(0) == head // heads)
-            def _():
-                cols = pl.ds(pl.multiple_of(first + 2 * (head % heads) * HD, HD), HD)
-                out[:, cols] = piece[:, i * HD : (i + 1) * HD].astype(jnp.float32)
+        for i in range(part // HD):
+            cols = pl.ds(pl.multiple_of(first + 2 * i * HD, HD), HD)
+            out[:, cols] = piece[:, i * HD : (i + 1) * HD].astype(jnp.float32)
 
     return widen(
-        chunks,
+        [pieces],
         places,
         3,
-        [((rows, width), lambda i: (0, 0))] * 2,
+        [((rows, part), lambda i: (0, i))],
         (rows, 4 * part),
         lambda i: (0, i),
-        (rows, 12 * part),
+        (rows, 4 * width),
         write,
     )
 
@@ -965,6 +992,11 @@
     def plain_matmul(left, pieces, offsets, shape, back, body, extras, outs):
         return weight_matmul(left, pieces, offsets, shape, back, body, extras, outs, 512)
 
+    def row_groups(left, pieces, offsets, shape_, back):
+        groups = jnp.stack([1 - ci, 3 - ci, ci, 2 + ci]).astype(jnp.int32)
+        outs = (shape(2 * tok_count, shape_[0] if back else shape_[1]),) * 2
+        return weight_matmul(left, pieces, offsets, shape_, back, None, (), outs, 512, groups)
+
     def matmul(left, *others):
         return line.leave(*plain_matmul(line.enter(left), *others))
 
@@ -1077,30 +1109,17 @@
         (shape(length, ff_here), shape(1, ff_here, wide)),
     )
     up_far = far_terms(normed_two, hidden_grad, piece_d)
-    (norm_two_partial,) = matmul(
-        hidden_grad,
-        up_parts,
-        up_offsets,
-        (model, ff_here),
-        True,
-        store_low,
-        (),
-        (shape(length, model),),
-    )
-    def norm_two_back(norm_two_partial):
-        home, away = core_sum(norm_two_partial, yi, ci)
+    norm_two_parts = line.leave(
+        *row_groups(line.enter(hidden_grad), up_parts, up_offsets, (model, ff_here), True)
+    )
+
+    def norm_two_back(*norm_two_parts):
+        home, away = core_sum(norm_two_parts, yi)
         other = lax.ppermute(away, "y", SWAP)
-        (down_partial,) = plain_matmul(
-            after(activated, away),
-            down_parts,
-            down_offsets,
-            (ff_here, model),
-            False,
-            store_low,
-            (),
-            (shape(length, model),),
+        feed_parts = row_groups(
+            after(activated, away), down_parts, down_offsets, (ff_here, model), False
         )
-        norm_two_grad = home_sum(home, after(other, down_partial))
+        norm_two_grad = home_sum(home, after(other, *feed_parts))
         resid_part, gain_two_grad, shift_two_grad = norm_back(
             residual_one, gain_two, norm_two_grad
         )
@@ -1109,10 +1128,10 @@
         branch_pair = jnp.concatenate(
             by_bit(ci, branch_grad, lax.ppermute(branch_grad, "c", SWAP)), axis=0
         )
-        return branch_pair, residual_grad, gain_two_grad, shift_two_grad, down_partial
-
-    branch_pair, residual_grad, gain_two_grad, shift_two_grad, down_partial = line.leave(
-        *stage(flag, norm_two_back, line.enter(norm_two_partial))
+        return branch_pair, residual_grad, gain_two_grad, shift_two_grad, feed_parts
+
+    branch_pair, residual_grad, gain_two_grad, shift_two_grad, feed_parts = line.leave(
+        *stage(flag, norm_two_back, line.enter(norm_two_parts[0]), norm_two_parts[1])
     )
 
     out_blocks = far_blocks + near_blocks
@@ -1132,7 +1151,7 @@
         away = lax.dynamic_slice_in_dim(mixed_grad_pair, (1 - yi) * part, part, 1)
         home = lax.dynamic_slice_in_dim(mixed_grad_pair, yi * part, part, 1)
         theirs = lax.ppermute(away, "y", SWAP)
-        feed_home, feed_away = core_sum(after(down_partial, away), yi, ci)
+        feed_home, feed_away = core_sum([after(feed_parts[0], away), feed_parts[1]], yi)
         theirs = after(theirs, feed_away)
         return jnp.concatenate(by_bit(yi, home, theirs), axis=0), feed_home, feed_away
 
@@ -1161,17 +1180,9 @@
         )[0]
     )
     up_shard = sum_over_z(after(up_sum, down_pair))
-    (norm_one_partial,) = matmul(
-        proj_grad,
-        qkv_parts,
-        qkv_offsets,
-        (model, qkv_width),
-        True,
-        store_low,
-        (),
-        (shape(length, model),),
-    )
-
+    norm_one_parts = line.leave(
+        *row_groups(line.enter(proj_grad), qkv_parts, qkv_offsets, (model, qkv_width), True)
+    )
     out_sum = line.leave(
         *weight_grad(
             line.enter(mixed),
@@ -1184,8 +1195,8 @@
     )[0]
     feed_other = lax.ppermute(after(feed_away, up_sum), "y", SWAP)
 
-    def norm_one_back(norm_one_partial):
-        home, away = core_sum(norm_one_partial, yi, ci)
+    def norm_one_back(*norm_one_parts):
+        home, away = core_sum(norm_one_parts, yi)
         away = lax.ppermute(away, "y", SWAP)
         norm_one_grad = home_sum(home, away)
         input_part, gain_one_grad, shift_one_grad = norm_back(inputs, gain_one, norm_one_grad)
@@ -1193,14 +1204,12 @@
         return input_grad, gain_one_grad, shift_one_grad
 
     input_grad, gain_one_grad, shift_one_grad = line.leave(
-        *stage(flag, norm_one_back, after(line.enter(norm_one_partial), feed_other))
-    )
-    qkv_sums = line.leave(
-        *near_terms(
-            line.enter(after(normed_one, up_shard)), proj_grad, piece_d, qkv_far, 2
-        )
-    )
-    qkv_shards = [sum_over_z(total) for total in qkv_sums]
+        *stage(flag, norm_one_back, after(line.enter(norm_one_parts[0]), feed_other), norm_one_parts[1])
+    )
+    (qkv_sum,) = line.leave(
+        *near_terms(line.enter(after(normed_one, up_shard)), proj_grad, piece_d, qkv_far)
+    )
+    qkv_shard = sum_over_z(qkv_sum)
 
     def ends(up_shard):
         feed_out = home_sum(feed_home, feed_other)
@@ -1235,29 +1244,29 @@
         up_other = lax.ppermute(up_shard, "y", SWAP)
         down_far = lax.ppermute(after(down_pair[1], vector_grad), "x", SWAP)
         down_shard = (down_pair[0].astype(wide) + down_far.astype(wide)).astype(low)
-        down_other = lax.ppermute(after(down_shard, up_other), "y", SWAP)
-        out_away = lax.ppermute(after(out_sum[:z_count], down_far), "x", SWAP)
+        return output_shard, sum_small(vector_grad), down_shard, up_other
+
+    output_shard, vector_total, down_shard, up_other = line.leave(
+        *stage(flag, ends, line.enter(up_shard))
+    )
+
+    def more_ends(down_shard):
+        down_other = lax.ppermute(down_shard, "y", SWAP)
+        out_away = lax.ppermute(out_sum[:z_count], "x", SWAP)
+        up_total = widen_columns(core_pieces(up_shard, up_other), places, shard_count)
         out_both = (out_sum[z_count:].astype(wide) + out_away.astype(wide)).astype(low)
-        vector_total = sum_small(vector_grad)
-        up_pieces = core_pieces(up_shard, up_other)
-        return (
-            output_shard,
-            vector_total,
-            out_both,
-            widen_rows(core_pieces(down_shard, down_other), places),
-            widen_columns(up_pieces, places, shard_count),
-        )
-
-    output_shard, vector_total, out_both, down_total, up_total = line.leave(
-        *stage(flag, ends, line.enter(up_shard))
-    )
-
-    out_shard = sum_over_z(after(out_both, *qkv_shards))
-
-    def last(qkv_low, qkv_high):
-        return widen_heads([seq_pieces(qkv_low), seq_pieces(qkv_high)], places)
-
-    qkv_total = stage(flag, last, after(qkv_shards[0], up_total), qkv_shards[1])
+        return out_both, up_total, after(down_other, up_total)
+
+    out_both, up_total, down_other = stage(flag, more_ends, line.enter(down_shard))
+    out_shard = sum_over_z(after(out_both, qkv_shard))
+
+    def last(qkv_shard):
+        other = lax.ppermute(qkv_shard, "y", SWAP)
+        down_total = widen_rows(core_pieces(down_shard, down_other), places)
+        qkv_pieces = core_pieces(qkv_shard, after(other, down_total))
+        return widen_heads(qkv_pieces, places), down_total
+
+    qkv_total, down_total = stage(flag, last, after(qkv_shard, up_total))
     out_total = widen_quarters(seq_pieces(after(out_shard, qkv_total)), places)
     vectors = [vector_total[slot * piece_d : (slot + 1) * piece_d] for slot in range(5)]
     return (

time: 723 us -> 707 us (0.978)
  local copies, waits for them, and re-layouts: 40.7 us -> 29.6 us
  Pallas kernels: 233 us -> 243 us
  waiting for transfers between devices: 290 us -> 282 us
    ppermute x6 -> x4, waiting for transfers between devices: 74.1 us -> 59.7 us  [seq_pieces(): return core_pieces(block, after(lax.ppermute(block, 'y', SWAP), *others))]
    pallas_call x0 -> x3, Pallas kernels: none -> 12.3 us  [core_sum(): pl.pallas_call(kernel, grid_spec=pltpu.PrefetchScalarGridSpec(num_scalar_...]
    squeeze x4 -> x0, local copies, waits for them, and re-layouts: 11 us -> none  [the longest x3 9.5 us: core_sum(): away = lax.dynamic_index_in_dim(parts, 1 - ci, 1, keepdims=False)]
    ppermute x5 -> x6, waiting for transfers between devices: 24.2 us -> 34.2 us  [the longest x1 11.5 us: more_ends(): down_other = lax.ppermute(down_shard, 'y', SWAP)]
    add x3 -> x0, other arithmetic: 9.12 us -> none  [core_sum(): home.astype(jnp.float32) + lax.ppermute(away, 'c', SWAP).astype(jnp.float32)]
  transfers between devices with their start and end apart: 72 -> 68, of which waited for: 38 -> 37; matrix products, arithmetic and copies ran while one was open for 14% -> 13% of each run, Pallas kernels for 31% -> 33%
where the time goes in v4:
time: 707 us; the launch traced here: 697 us
  waiting for transfers between devices  282 us (40%)
  Pallas kernels  243 us (34%)
  other arithmetic  70.6 us (10%)
  starting transfers between devices  55.8 us (8%)
  local copies, waits for them, and re-layouts  29.6 us (4%)
  between operations  15.2 us (2%)
    pallas_call x8, Pallas kernels, weight_matmul(): pl.pallas_call(kernel, grid_spec=pltpu.PrefetchScalarGridSpec(num_scalar_...  110 us
    pallas_call x6, Pallas kernels, weight_grad(): pl.pallas_call(kernel, grid_spec=pltpu.PrefetchScalarGridSpec(num_scalar_...  59.9 us
    ppermute x4, waiting for transfers between devices, seq_pieces(): return core_pieces(block, after(lax.ppermute(block, 'y', SWAP), *others))  59.7 us
    ppermute x4, waiting for transfers between devices, gather_weight(): return [near, lax.ppermute(after(near, *others), 'x', SWAP)]  36.9 us
    ppermute x1, waiting for transfers between devices, norm_one_back(): away = lax.ppermute(away, 'y', SWAP)  24.1 us
    pallas_call x4, Pallas kernels, widen(): pl.pallas_call(kernel, grid_spec=pltpu.PrefetchScalarGridSpec(num_scalar_...  22.6 us
    ppermute x1, waiting for transfers between devices, split_shards(): up_parts += [up_high, lax.ppermute(after(up_high, mixed_heads), 'x', SWAP)]  17.6 us
    all_gather x1, waiting for transfers between devices, split_shards(): up_high = lax.all_gather(slices[2], 'z', axis=0, tiled=False)  15.6 us
  transfers between devices with their start and end apart: 68, of which 37 were waited for; matrix products, arithmetic and copies ran while one was open for 13% of the time, Pallas kernels for 33%

profile of v4, /device:TPU:0, one launch (start us, length us, event | category | flops | bytes accessed | tf_op | source)
XLA Modules:
  0.0 697.3 jit_solution(1044111186536587426)
XLA Ops:
  30.8 8.9 %collective-permute-done.33 = f32[2304]{0:T(1024)S(1)} collective-permute-done((f32[2304]{0:T(1024)S(1)}, f32[2304]{0:T(1024)S(1)}, u32[]{:S(2)}, u32[]{:S(2)}) %collective-permute-start.33) | collective-permute-done | bytes 9248 | tf_op jit(solution)/shard_map/ppermute | solution.py:289
  47.6 21.6 %collective-permute-done.35 = bf16[256,2048]{1,0:T(8,128)(2,1)S(1)} collective-permute-done((bf16[256,2048]{1,0:T(8,128)(2,1)}, bf16[256,2048]{1,0:T(8,128)(2,1)S(1)}, u32[]{:S(2)}, u32[]{:S(2)}) %collective-permute-start.35) | collective-permute-done | bytes 1048608 | tf_op jit(solution)/shard_map/ppermute | solution.py:323
  69.2 8.9 %all-gather.14.cloned.1.call-done = bf16[1024,1536]{1,0:T(8,128)(2,1)} async-done(((bf16[256,1536]{1,0:T(8,128)(2,1)}), bf16[1024,1536]{1,0:T(8,128)(2,1)}) %all-gather.14.cloned.1.call-update) | async-done | bytes 3145744 | tf_op jit(solution)/shard_map/all_gather | solution.py:293
  87.4 23.9 %collective-permute-done.38 = bf16[256,2048]{1,0:T(8,128)(2,1)S(1)} collective-permute-done((bf16[256,2048]{1,0:T(8,128)(2,1)}, bf16[256,2048]{1,0:T(8,128)(2,1)S(1)}, u32[]{:S(2)}, u32[]{:S(2)}) %collective-permute-start.38) | collective-permute-done | bytes 1048608 | tf_op jit(solution)/shard_map/ppermute | solution.py:323
  115.5 33.7 %collective-permute-done.40.refs_3_.refs_4_ = bf16[4,256,1536]{2,1,0:T(8,128)(2,1)} collective-permute-done((bf16[4,256,1536]{2,1,0:T(8,128)(2,1)}, bf16[4,256,1536]{2,1,0:T(8,128)(2,1)}, u32[]{:S(2)}, u32[]{:S(2)}) %collective-permute-start.40) | collective-permute-done | bytes 3145760 | tf_op jit(solution)/shard_map/ppermute | solution.py:294
  158.1 14.2 %shard_map.240.q_ref.k_ref.v_ref = bf16[1024,1536]{1,0:T(8,128)(2,1)} custom-call(s32[2,8]{1,0:T(2,128)} %stack.343.refs_0_, bf16[1024,2048]{1,0:T(8,128)(2,1)} %pad_maximum_fusion.3.refs_1_.left_ref, bf16[4,256,1536]{2,1,0:T(8,128)(2,1)} %bitcast.119, bf16[4,256,1536]{2,1,0:T(8,128)(2,1)} %collective-permute-done.40.refs_3_.refs_4_), custom_call_target="tpu_custom_call" | custom-call | flops 64424508 | bytes 136314 | tf_op jit(solution)/shard_map/pallas_call | solution.py:482
  172.7 11.4 %shard_map.241 = (bf16[1024,512]{1,0:T(8,128)(2,1)}, f32[4,1024,1]{2,1,0:T(8,128)}) custom-call(bf16[1024,1536]{1,0:T(8,128)(2,1)} %shard_map.240.q_ref.k_ref.v_ref, bf16[1024,1536]{1,0:T(8,128)(2,1)} %shard_map.240.q_ref.k_ref.v_ref, bf16[1024,1536]{1,0:T(8,128)(2,1)} %shard_map.240.q_ref.k_ref.v_ref, s32[1024,1]{1,0:T(8,128)} %copy.31.qi_ref, ...), custom_call_target="tpu_custom_call" | custom-call | flops 21474836 | bytes 41943 | tf_op jit(solution)/shard_map/pallas_call | solution.py:689
  185.7 15.6 %all-gather.18.cloned.1.call-done = bf16[1024,1024]{1,0:T(8,128)(2,1)} async-done(((bf16[256,1024]{1,0:T(8,128)(2,1)}), bf16[1024,1024]{1,0:T(8,128)(2,1)}) %all-gather.18.cloned.1.call-update) | async-done | bytes 2097168 | tf_op jit(solution)/shard_map/all_gather | solution.py:1038
  208.6 36.2 %conditional.7 = (bf16[256,2048]{1,0:T(8,128)(2,1)}, f32[256,2048]{1,0:T(8,128)}, bf16[512,512]{1,0:T(8,128)(2,1)S(1)}, bf16[512,512]{1,0:T(8,128)(2,1)S(1)}) conditional(s32[]{:T(128)} %bitcast.20, () %tuple.122, (s32[]{:T(128)}, bf16[1024,512]{1,0:T(8,128)(2,1)}, s32[2,16]{1,0:T(2,128)S(1)}, bf16[4,128,1024]{2,1,0:T(8,128)(2,1)}, ...), branch_computations={%region_4.5_spmd, %region_5.8_spmd} | conditional | flops 30912284 | bytes 39470188 | solution.py:303
  211.7 10.5 %collective-permute-done.13 = bf16[512,512]{1,0:T(8,128)(2,1)S(1)} collective-permute-done((bf16[512,512]{1,0:T(8,128)(2,1)S(1)}, bf16[512,512]{1,0:T(8,128)(2,1)S(1)}, u32[]{:S(2)}, u32[]{:S(2)}) %collective-permute-start.13) | collective-permute-done | bytes 524320 | tf_op jit(solution)/shard_map/cond/branch_1_fun/ppermute | solution.py:1053
  246.9 17.6 %collective-permute-done.47.refs_5_.refs_6_ = bf16[4,256,1024]{2,1,0:T(8,128)(2,1)} collective-permute-done((bf16[4,256,1024]{2,1,0:T(8,128)(2,1)}, bf16[4,256,1024]{2,1,0:T(8,128)(2,1)}, u32[]{:S(2)}, u32[]{:S(2)}) %collective-permute-start.47) | collective-permute-done | bytes 2097184 | tf_op jit(solution)/shard_map/ppermute | solution.py:1074
  278.5 20.6 %shard_map.242 = (bf16[1024,2048]{1,0:T(8,128)(2,1)}, f32[1024,2048]{1,0:T(8,128)}) custom-call(s32[2,16]{1,0:T(2,128)} %get-tuple-element.451.refs_0_, bf16[1024,2048]{1,0:T(8,128)(2,1)} %pad_maximum_fusion.5.refs_1_.left_ref, bf16[4,256,1024]{2,1,0:T(8,128)(2,1)} %bitcast.122, bf16[4,256,1024]{2,1,0:T(8,128)(2,1)} %collective-permute-done.46.refs_3_.refs_4_, ...), custom_call_target="tpu_custom_call" | custom-call | flops 85899344 | bytes 251740 | tf_op jit(solution)/shard_map/pallas_call | solution.py:482
  301.7 11.6 %collective-permute-done.50 = bf16[512,512]{1,0:T(8,128)(2,1)} collective-permute-done((bf16[512,512]{1,0:T(8,128)(2,1)S(1)}, bf16[512,512]{1,0:T(8,128)(2,1)}, u32[]{:S(2)}, u32[]{:S(2)}) %collective-permute-start.50) | collective-permute-done | bytes 524320 | tf_op jit(solution)/shard_map/ppermute | solution.py:1090
  319.7 14.8 %shard_map.243 = bf16[8,256,2048]{2,1,0:T(8,128)(2,1)} custom-call(s32[9]{0:T(128)} %stack.340.where_ref, bf16[1024,2048]{1,0:T(8,128)(2,1)S(1)} %copy-done.3, bf16[1024,2048]{1,0:T(8,128)(2,1)} %pad_maximum_fusion.4.right_ref.refs_1_), custom_call_target="tpu_custom_call" | custom-call | flops 85899344 | bytes 251658 | tf_op jit(solution)/shard_map/pallas_call | solution.py:546
  335.3 17.5 %shard_map.244 = (bf16[1024,2048]{1,0:T(8,128)(2,1)}, f32[1,2048]{1,0:T(1,128)S(1)}) custom-call(s32[2,16]{1,0:T(2,128)S(1)} %get-tuple-element.450.refs_0_, bf16[1024,2048]{1,0:T(8,128)(2,1)} %pad_maximum_fusion.4.right_ref.refs_1_, bf16[4,256,1024]{2,1,0:T(8,128)(2,1)} %bitcast.130, bf16[4,256,1024]{2,1,0:T(8,128)(2,1)} %collective-permute-done.49.refs_3_, ...), custom_call_target="tpu_custom_call" | custom-call | flops 85899344 | bytes 251740 | tf_op jit(solution)/shard_map/pallas_call | solution.py:482
  352.9 9.5 %shard_map.245 = bf16[4,256,2048]{2,1,0:T(8,128)(2,1)} custom-call(s32[5]{0:T(128)} %stack.344.where_ref, bf16[1024,2048]{1,0:T(8,128)(2,1)} %pad_maximum_fusion.5.refs_1_.left_ref, bf16[1024,2048]{1,0:T(8,128)(2,1)} %get-tuple-element.341.right_ref.refs_2_), custom_call_target="tpu_custom_call" | custom-call | flops 42949672 | bytes 146800 | tf_op jit(solution)/shard_map/pallas_call | solution.py:546
  364.6 15.8 %shard_map.246 = (bf16[512,2048]{1,0:T(8,128)(2,1)}, bf16[512,2048]{1,0:T(8,128)(2,1)S(1)}) custom-call(s32[2,16]{1,0:T(2,128)} %get-tuple-element.451.refs_0_, s32[4]{0:T(128)} %pad_add_fusion.4.refs_1_, bf16[1024,2048]{1,0:T(8,128)(2,1)} %get-tuple-element.341.right_ref.refs_2_, bf16[4,256,1024]{2,1,0:T(8,128)(2,1)} %bitcast.123, ...), custom_call_target="tpu_custom_call" | custom-call | flops 85899344 | bytes 167772 | tf_op jit(solution)/shard_map/pallas_call | solution.py:482
  380.4 48.6 %conditional.8 = (bf16[512,2048]{1,0:T(8,128)(2,1)}, f32[256,2048]{1,0:T(8,128)}, f32[2048]{0:T(1024)S(1)}, f32[2048]{0:T(1024)S(1)}, bf16[512,2048]{1,0:T(8,128)(2,1)}, /*index=5*/bf16[512,2048]{1,0:T(8,128)(2,1)}) conditional(s32[]{:T(128)} %bitcast.20, () %tuple.117, (s32[]{:T(128)}, s32[]{:T(128)}, bf16[512,2048]{1,0:T(8,128)(2,1)}, ...), branch_computations={%region_8.9_spmd, %region_9.16_spmd} | conditional | flops 104769888 | bytes 87305296 | solution.py:303
  396.3 15.3 %branch_1_fun.11 = (bf16[512,2048]{1,0:T(8,128)(2,1)}, bf16[512,2048]{1,0:T(8,128)(2,1)}) custom-call(s32[2,16]{1,0:T(2,128)S(1)} %get-tuple-element.152.refs_0_, s32[4]{0:T(128)} %pad_add_fusion.refs_1_, bf16[1024,2048]{1,0:T(8,128)(2,1)} %get-tuple-element.154.refs_2_, bf16[4,256,1024]{2,1,0:T(8,128)(2,1)S(1)} %copy-done.9, ...), custom_call_target="tpu_custom_call" | custom-call | flops 85899344 | bytes 167772 | tf_op jit(solution)/shard_map/cond/branch_1_fun/pallas_call | solution.py:482
  429.0 25.8 %conditional.9 = (bf16[1024,512]{1,0:T(8,128)(2,1)S(1)}, f32[256,2048]{1,0:T(8,128)}, bf16[256,2048]{1,0:T(8,128)(2,1)}) conditional(s32[]{:T(128)} %bitcast.20, () %tuple.116, (s32[]{:T(128)}, s32[2,16]{1,0:T(2,128)S(1)}, bf16[512,2048]{1,0:T(8,128)(2,1)}, bf16[4,128,1024]{2,1,0:T(8,128)(2,1)}, bf16[4,128,1024]{2,1,0:T(8,128)(2,1)}, ...), branch_computations={%region_16.17_spmd, %region_17.18_spmd} | conditional | flops 24096276 | bytes 20033298 | solution.py:303
  459.2 15.4 %shard_map.247.right_ref.refs_2_ = bf16[1024,1536]{1,0:T(8,128)(2,1)} custom-call(bf16[1024,1536]{1,0:T(8,128)(2,1)} %shard_map.240.q_ref.k_ref.v_ref, bf16[1024,1536]{1,0:T(8,128)(2,1)} %shard_map.240.q_ref.k_ref.v_ref, bf16[1024,1536]{1,0:T(8,128)(2,1)} %shard_map.240.q_ref.k_ref.v_ref, bf16[1024,512]{1,0:T(8,128)(2,1)S(1)} %get-tuple-element.353.g_ref, ...), custom_call_target="tpu_custom_call" | custom-call | flops 53687092 | bytes 83886 | tf_op jit(solution)/shard_map/pallas_call | solution.py:758
  482.8 10.1 %shard_map.249 = bf16[4,256,2048]{2,1,0:T(8,128)(2,1)} custom-call(s32[5]{0:T(128)} %stack.345.where_ref, bf16[1024,2048]{1,0:T(8,128)(2,1)} %pad_maximum_fusion.5.refs_1_.left_ref, bf16[1024,2048]{1,0:T(8,128)(2,1)} %get-tuple-element.341.right_ref.refs_2_, bf16[4,256,2048]{2,1,0:T(8,128)(2,1)} %collective-permute-done.52.refs_0_), custom_call_target="tpu_custom_call" | custom-call | flops 42949672 | bytes 146800 | tf_op jit(solution)/shard_map/pallas_call | solution.py:546
  499.1 12.3 %shard_map.250 = (bf16[512,2048]{1,0:T(8,128)(2,1)}, bf16[512,2048]{1,0:T(8,128)(2,1)S(1)}) custom-call(s32[2,8]{1,0:T(2,128)} %stack.343.refs_0_, s32[4]{0:T(128)} %pad_add_fusion.4.refs_1_, bf16[1024,1536]{1,0:T(8,128)(2,1)} %shard_map.247.right_ref.refs_2_, bf16[4,256,1536]{2,1,0:T(8,128)(2,1)} %bitcast.120, ...), custom_call_target="tpu_custom_call" | custom-call | flops 64424508 | bytes 136314 | tf_op jit(solution)/shard_map/pallas_call | solution.py:482
  511.4 8.8 %shard_map.251 = bf16[8,128,1024]{2,1,0:T(8,128)(2,1)} custom-call(s32[9]{0:T(128)} %stack.346.where_ref, bf16[1024,1024]{1,0:T(8,128)(2,1)} %pad_maximum_fusion.6.left_ref, bf16[1024,1024]{1,0:T(8,128)(2,1)} %pad_maximum_fusion.7.right_ref), custom_call_target="tpu_custom_call" | custom-call | flops 21474836 | bytes 83886 | tf_op jit(solution)/shard_map/pallas_call | solution.py:546
  520.2 40.3 %conditional.10 = (f32[1,256,2048]{2,1,0:T(8,128)}, f32[2048]{0:T(1024)S(1)}, f32[2048]{0:T(1024)S(1)}) conditional(s32[]{:T(128)} %bitcast.20, () %tuple.150, (s32[]{:T(128)}, bf16[512,2048]{1,0:T(8,128)(2,1)}, bf16[512,2048]{1,0:T(8,128)(2,1)S(1)}, f32[8,256]{1,0:T(8,128)S(1)}, f32[256,2048]{1,0:T(8,128)S(1)}, ...), branch_computations={%region_18.19_spmd, %region_19.26_spmd} | conditional | flops 13103360 | bytes 48339968 | solution.py:303
  531.1 24.1 %collective-permute-done.8 = bf16[256,2048]{1,0:T(8,128)(2,1)S(1)} collective-permute-done((bf16[256,2048]{1,0:T(8,128)(2,1)}, bf16[256,2048]{1,0:T(8,128)(2,1)S(1)}, u32[]{:S(2)}, u32[]{:S(2)}) %collective-permute-start.8) | collective-permute-done | bytes 1048608 | tf_op jit(solution)/shard_map/cond/branch_1_fun/ppermute | solution.py:1200
  577.0 39.9 %conditional.11 = (bf16[1,256,2048]{2,1,0:T(8,128)(2,1)}, f32[2304]{0:T(1024)}, bf16[256,2048]{1,0:T(8,128)(2,1)S(1)}, bf16[256,2048]{1,0:T(8,128)(2,1)}, f32[25...) conditional(s32[]{:T(128)} %bitcast.20, () %tuple.115, ...), branch_computations={%region_28.29_spmd, %region_29.31_spmd} | conditional | flops 5302067 | bytes 32673764 | solution.py:303
  601.4 15.1 %collective-permute-done.24 = bf16[256,2048]{1,0:T(8,128)(2,1)S(1)} collective-permute-done((bf16[256,2048]{1,0:T(8,128)(2,1)S(1)}, bf16[256,2048]{1,0:T(8,128)(2,1)S(1)}, u32[]{:S(2)}, u32[]{:S(2)}) %collective-permute-start.24) | collective-permute-done | bytes 1048608 | tf_op jit(solution)/shard_map/cond/branch_1_fun/ppermute | solution.py:1245
  617.5 29.7 %conditional.12 = (bf16[4,128,1024]{2,1,0:T(8,128)(2,1)}, f32[256,8192]{1,0:T(8,128)}, bf16[256,2048]{1,0:T(8,128)(2,1)}) conditional(s32[]{:T(128)} %bitcast.20, () %tuple.162, (bf16[8,128,1024]{2,1,0:T(8,128)(2,1)}, bf16[256,2048]{1,0:T(8,128)(2,1)}, bf16[256,2048]{1,0:T(8,128)(2,1)}, s32[4]{0:T(128)S(1)}, ...), branch_computations={%region_32.33_spmd, %region_33.34_spmd} | conditional | flops 2097152 | bytes 38923408 | solution.py:303
  631.9 11.5 %collective-permute-done.12 = bf16[256,2048]{1,0:T(8,128)(2,1)} collective-permute-done((bf16[256,2048]{1,0:T(8,128)(2,1)S(1)}, bf16[256,2048]{1,0:T(8,128)(2,1)}, u32[]{:S(2)}, u32[]{:S(2)}) %collective-permute-start.12) | collective-permute-done | bytes 1048608 | tf_op jit(solution)/shard_map/cond/branch_1_fun/ppermute | solution.py:1254
  647.2 28.8 %conditional.13 = (f32[256,6144]{1,0:T(8,128)}, f32[1024,2048]{1,0:T(8,128)}) conditional(s32[]{:T(128)} %bitcast.20, () %tuple.161, (bf16[256,1536]{1,0:T(8,128)(2,1)}, bf16[256,2048]{1,0:T(8,128)(2,1)S(1)}, bf16[256,2048]{1,0:T(8,128)(2,1)}, s32[4]{0:T(128)S(1)}) %tuple.249), branch_computations={%region_34.35_spmd, %region_35.36_spmd} | conditional | bytes 39017896 | solution.py:303
  658.7 8.9 %collective-permute-done.1.refs_2_ = bf16[256,1536]{1,0:T(8,128)(2,1)S(1)} collective-permute-done((bf16[256,1536]{1,0:T(8,128)(2,1)}, bf16[256,1536]{1,0:T(8,128)(2,1)S(1)}, u32[]{:S(2)}, u32[]{:S(2)}) %collective-permute-start.1) | collective-permute-done | bytes 786464 | tf_op jit(solution)/shard_map/cond/branch_1_fun/ppermute | solution.py:1264
  (381 shorter events, 302.8 us)
Async XLA Ops:
  7.2 71.0 %all-gather.14.cloned.1.call-start = ((), (), s32[]{:S(2)}) async-start(), calls=%async_computation.9 | async-start | bytes 3932160 | tf_op jit(solution)/shard_map/all_gather | solution.py:293
  11.8 102.1 %all-gather.20.cloned.1.call-start = ((), (), s32[]{:S(2)}) async-start(), calls=%async_computation.12 | async-start | bytes 1310720 | tf_op jit(solution)/shard_map/all_gather | solution.py:293
  44.7 127.6 %all-gather.16.cloned.1.call-start = ((), (), s32[]{:S(2)}) async-start(), calls=%async_computation.10 | async-start | bytes 2621440 | tf_op jit(solution)/shard_map/all_gather | solution.py:293
  45.4 155.9 %all-gather.18.cloned.1.call-start = ((), (), s32[]{:S(2)}) async-start(), calls=%async_computation.11 | async-start | bytes 2621440 | tf_op jit(solution)/shard_map/all_gather | solution.py:1038
  46.0 225.3 %all-gather.22.cloned.1.call-start = ((), (), s32[]{:S(2)}) async-start(), calls=%async_computation.13 | async-start | bytes 2621440 | tf_op jit(solution)/shard_map/all_gather | solution.py:293
  47.6 32.2 %collective-permute-start.34 = (bf16[256,2048]{1,0:T(8,128)(2,1)}, bf16[256,2048]{1,0:T(8,128)(2,1)S(1)}, u32[]{:S(2)}, u32[]{:S(2)}) collective-permute-start(bf16[256,2048]{1,0:T(8,128)(2,1)} %add_convert_fusion.3), channel_id=1, source_target_pairs={{0,1},{1,0},{2,3},{3,2},{4,5},{5,4},{6,7},{7,6},{8,9},{9,8},{10,11... | collective-permute-start | bytes 3145736 | tf_op jit(solution)/shard_map/ppermute | solution.py:327
  78.2 257.1 %all-gather.12.cloned.1.call-start = ((), (), s32[]{:S(2)}) async-start(), calls=%async_computation.4 | async-start | bytes 5242880 | tf_op jit(solution)/shard_map/all_gather | solution.py:1040
  78.3 70.9 %collective-permute-start.40 = (bf16[4,256,1536]{2,1,0:T(8,128)(2,1)}, bf16[4,256,1536]{2,1,0:T(8,128)(2,1)}, u32[]{:S(2)}, u32[]{:S(2)}) collective-permute-start(bf16[4,256,1536]{2,1,0:T(8,128)(2,1)} %bitcast.118), channel_id=1, source_target_pairs={{0,4},{4,0},{1,5},{5,1},{2,6},{6,2},{3,7},{7,3},{8,12},{12,8},{9,1... | collective-permute-start | bytes 9437192 | tf_op jit(solution)/shard_map/ppermute | solution.py:294
  85.9 25.4 %collective-permute-start.38 = (bf16[256,2048]{1,0:T(8,128)(2,1)}, bf16[256,2048]{1,0:T(8,128)(2,1)S(1)}, u32[]{:S(2)}, u32[]{:S(2)}) collective-permute-start(bf16[256,2048]{1,0:T(8,128)(2,1)} %bitcast.38), channel_id=1, source_target_pairs={{0,2},{2,0},{1,3},{3,1},{4,6},{6,4},{5,7},{7,5},{8,10},{10,8},{9,1... | collective-permute-start | bytes 3145736 | tf_op jit(solution)/shard_map/ppermute | solution.py:323
  87.4 63.2 %collective-permute-start.37 = (bf16[256,2048]{1,0:T(8,128)(2,1)}, bf16[256,2048]{1,0:T(8,128)(2,1)S(1)}, u32[]{:S(2)}, u32[]{:S(2)}) collective-permute-start(bf16[256,2048]{1,0:T(8,128)(2,1)} %bitcast.38), channel_id=1, source_target_pairs={{0,1},{1,0},{2,3},{3,2},{4,5},{5,4},{6,7},{7,6},{8,9},{9,8},{10,11... | collective-permute-start | bytes 3145736 | tf_op jit(solution)/shard_map/ppermute | solution.py:327
  111.3 40.3 %collective-permute-start.39 = (bf16[256,2048]{1,0:T(8,128)(2,1)S(1)}, bf16[256,2048]{1,0:T(8,128)(2,1)}, u32[]{:S(2)}, u32[]{:S(2)}) collective-permute-start(bf16[256,2048]{1,0:T(8,128)(2,1)S(1)} %collective-permute-done.38), channel_id=1, source_target_pairs={{0,1},{1,0},{2,3},{3,2},{4,5},{5,4},{6,7},{7,6},{8,9},{9,8},{10,11... | collective-permute-start | bytes 3145736 | tf_op jit(solution)/shard_map/ppermute | solution.py:327
  113.9 379.0 %reduce-scatter.5.cloned.1.call-start = ((), (), s32[]{:S(2)}) async-start(), calls=%async_computation.5 | async-start | bytes 10485760 | tf_op jit(solution)/shard_map/reduce_scatter | solution.py:1098
  113.9 90.0 %collective-permute-start.42 = (bf16[4,128,1024]{2,1,0:T(8,128)(2,1)}, bf16[4,128,1024]{2,1,0:T(8,128)(2,1)}, u32[]{:S(2)}, u32[]{:S(2)}) collective-permute-start(bf16[4,128,1024]{2,1,0:T(8,128)(2,1)} %bitcast.134), channel_id=1, source_target_pairs={{0,2},{2,0},{1,3},{3,1},{4,6},{6,4},{5,7},{7,5},{8,10},{10,8},{9,1... | collective-permute-start | bytes 3145736 | tf_op jit(solution)/shard_map/ppermute | solution.py:960
  149.2 35.0 %collective-permute-start.41 = (bf16[4,128,1024]{2,1,0:T(8,128)(2,1)}, bf16[4,128,1024]{2,1,0:T(8,128)(2,1)}, u32[]{:S(2)}, u32[]{:S(2)}) collective-permute-start(bf16[4,128,1024]{2,1,0:T(8,128)(2,1)} %bitcast.135), channel_id=1, source_target_pairs={{0,4},{4,0},{1,5},{5,1},{2,6},{6,2},{3,7},{7,3},{8,12},{12,8},{9,1... | collective-permute-start | bytes 3145736 | tf_op jit(solution)/shard_map/ppermute | solution.py:294
  172.3 74.6 %collective-permute-start.46 = (bf16[4,256,1024]{2,1,0:T(8,128)(2,1)}, bf16[4,256,1024]{2,1,0:T(8,128)(2,1)}, u32[]{:S(2)}, u32[]{:S(2)}) collective-permute-start(bf16[4,256,1024]{2,1,0:T(8,128)(2,1)} %bitcast.121), channel_id=1, source_target_pairs={{0,4},{4,0},{1,5},{5,1},{2,6},{6,2},{3,7},{7,3},{8,12},{12,8},{9,1... | collective-permute-start | bytes 6291464 | tf_op jit(solution)/shard_map/ppermute | solution.py:294
  184.1 24.5 %collective-permute-start.43 = (bf16[4,128,1024]{2,1,0:T(8,128)(2,1)}, bf16[4,128,1024]{2,1,0:T(8,128)(2,1)}, u32[]{:S(2)}, u32[]{:S(2)}) collective-permute-start(bf16[4,128,1024]{2,1,0:T(8,128)(2,1)} %collective-permute-done.41), channel_id=1, source_target_pairs={{0,2},{2,0},{1,3},{3,1},{4,6},{6,4},{5,7},{7,5},{8,10},{10,8},{9,1... | collective-permute-start | bytes 3145736 | tf_op jit(solution)/shard_map/ppermute | solution.py:960
  201.3 63.2 %collective-permute-start.47 = (bf16[4,256,1024]{2,1,0:T(8,128)(2,1)}, bf16[4,256,1024]{2,1,0:T(8,128)(2,1)}, u32[]{:S(2)}, u32[]{:S(2)}) collective-permute-start(bf16[4,256,1024]{2,1,0:T(8,128)(2,1)} %bitcast.124), channel_id=1, source_target_pairs={{0,4},{4,0},{1,5},{5,1},{2,6},{6,2},{3,7},{7,3},{8,12},{12,8},{9,1... | collective-permute-start | bytes 6291464 | tf_op jit(solution)/shard_map/ppermute | solution.py:1074
  244.8 25.9 %collective-permute-start.45 = (bf16[256,2048]{1,0:T(8,128)(2,1)}, bf16[256,2048]{1,0:T(8,128)(2,1)}, u32[]{:S(2)}, u32[]{:S(2)}) collective-permute-start(bf16[256,2048]{1,0:T(8,128)(2,1)} %get-tuple-element.324), channel_id=1, source_target_pairs={{0,2},{2,0},{1,3},{3,1},{4,6},{6,4},{5,7},{7,5},{8,10},{10,8},{9,1... | collective-permute-start | bytes 3145736 | tf_op jit(solution)/shard_map/ppermute | solution.py:323
  246.9 26.0 %collective-permute-start.44 = (bf16[256,2048]{1,0:T(8,128)(2,1)}, bf16[256,2048]{1,0:T(8,128)(2,1)}, u32[]{:S(2)}, u32[]{:S(2)}) collective-permute-start(bf16[256,2048]{1,0:T(8,128)(2,1)} %get-tuple-element.324), channel_id=1, source_target_pairs={{0,1},{1,0},{2,3},{3,2},{4,5},{5,4},{6,7},{7,6},{8,9},{9,8},{10,11... | collective-permute-start | bytes 3145736 | tf_op jit(solution)/shard_map/ppermute | solution.py:327
  271.3 48.4 %collective-permute-start.49 = (bf16[4,256,1024]{2,1,0:T(8,128)(2,1)}, bf16[4,256,1024]{2,1,0:T(8,128)(2,1)}, u32[]{:S(2)}, u32[]{:S(2)}) collective-permute-start(bf16[4,256,1024]{2,1,0:T(8,128)(2,1)} %bitcast.129), channel_id=1, source_target_pairs={{0,4},{4,0},{1,5},{5,1},{2,6},{6,2},{3,7},{7,3},{8,12},{12,8},{9,1... | collective-permute-start | bytes 6291464 | tf_op jit(solution)/shard_map/ppermute | solution.py:294
  334.5 232.3 %reduce-scatter.7.cloned.1.call-start = ((), (), s32[]{:S(2)}) async-start(), calls=%async_computation.6 | async-start | bytes 5242880 | tf_op jit(solution)/shard_map/reduce_scatter | solution.py:1018
  362.3 120.4 %collective-permute-start.52 = (bf16[4,256,2048]{2,1,0:T(8,128)(2,1)}, bf16[4,256,2048]{2,1,0:T(8,128)(2,1)}, u32[]{:S(2)}, u32[]{:S(2)}) collective-permute-start(bf16[4,256,2048]{2,1,0:T(8,128)(2,1)} %shard_map.245), channel_id=1, source_target_pairs={{0,4},{4,0},{1,5},{5,1},{2,6},{6,2},{3,7},{7,3},{8,12},{12,8},{9,1... | collective-permute-start | bytes 12582920 | tf_op jit(solution)/shard_map/ppermute | solution.py:1010
  390.2 25.4 %collective-permute-start.16 = (bf16[256,2048]{1,0:T(8,128)(2,1)}, bf16[256,2048]{1,0:T(8,128)(2,1)S(1)}, u32[]{:S(2)}, u32[]{:S(2)}) collective-permute-start(bf16[256,2048]{1,0:T(8,128)(2,1)} %get-tuple-element.151), channel_id=1, source_target_pairs={{0,2},{2,0},{1,3},{3,1},{4,6},{6,4},{5,7},{7,5},{8,10},{10,8},{9,1... | collective-permute-start | bytes 3145736 | tf_op jit(solution)/shard_map/cond/branch_1_fun/ppermute | solution.py:1118
  457.0 25.8 %collective-permute-start.51 = (bf16[512,1024]{1,0:T(8,128)(2,1)}, bf16[512,1024]{1,0:T(8,128)(2,1)}, u32[]{:S(2)}, u32[]{:S(2)}) collective-permute-start(bf16[512,1024]{1,0:T(8,128)(2,1)} %constant_dynamic-slice_fusion.3), channel_id=1, source_target_pairs={{0,2},{2,0},{1,3},{3,1},{4,6},{6,4},{5,7},{7,5},{8,10},{10,8},{9,1... | collective-permute-start | bytes 3145736 | tf_op jit(solution)/shard_map/ppermute | solution.py:1163
  492.9 154.3 %reduce-scatter.9.cloned.1.call-start = ((), (), s32[]{:S(2)}) async-start(), calls=%async_computation.7 | async-start | bytes 3932160 | tf_op jit(solution)/shard_map/reduce_scatter | solution.py:1018
  493.0 73.8 %collective-permute-start.54 = (bf16[4,256,1536]{2,1,0:T(8,128)(2,1)}, bf16[4,256,1536]{2,1,0:T(8,128)(2,1)}, u32[]{:S(2)}, u32[]{:S(2)}) collective-permute-start(bf16[4,256,1536]{2,1,0:T(8,128)(2,1)} %shard_map.248), channel_id=1, source_target_pairs={{0,4},{4,0},{1,5},{5,1},{2,6},{6,2},{3,7},{7,3},{8,12},{12,8},{9,1... | collective-permute-start | bytes 9437192 | tf_op jit(solution)/shard_map/ppermute | solution.py:1010
  493.5 26.7 %collective-permute-start.53 = (bf16[256,2048]{1,0:T(8,128)(2,1)}, bf16[256,2048]{1,0:T(8,128)(2,1)}, u32[]{:S(2)}, u32[]{:S(2)}) collective-permute-start(bf16[256,2048]{1,0:T(8,128)(2,1)} %get-tuple-element.357), channel_id=1, source_target_pairs={{0,2},{2,0},{1,3},{3,1},{4,6},{6,4},{5,7},{7,5},{8,10},{10,8},{9,1... | collective-permute-start | bytes 3145736 | tf_op jit(solution)/shard_map/ppermute | solution.py:1196
  529.9 25.4 %collective-permute-start.8 = (bf16[256,2048]{1,0:T(8,128)(2,1)}, bf16[256,2048]{1,0:T(8,128)(2,1)S(1)}, u32[]{:S(2)}, u32[]{:S(2)}) collective-permute-start(bf16[256,2048]{1,0:T(8,128)(2,1)} %get-tuple-element.181), channel_id=1, source_target_pairs={{0,2},{2,0},{1,3},{3,1},{4,6},{6,4},{5,7},{7,5},{8,10},{10,8},{9,1... | collective-permute-start | bytes 3145736 | tf_op jit(solution)/shard_map/cond/branch_1_fun/ppermute | solution.py:1200
  575.4 100.6 %reduce-scatter.11.cloned.1.call-start = ((), (), s32[]{:S(2)}) async-start(), calls=%async_computation.8 | async-start | bytes 1310720 | tf_op jit(solution)/shard_map/reduce_scatter | solution.py:1018
  586.0 30.9 %collective-permute-start.25 = (bf16[256,2048]{1,0:T(8,128)(2,1)}, bf16[256,2048]{1,0:T(8,128)(2,1)}, u32[]{:S(2)}, u32[]{:S(2)}) collective-permute-start(bf16[256,2048]{1,0:T(8,128)(2,1)} %get-tuple-element.200), channel_id=1, source_target_pairs={{0,2},{2,0},{1,3},{3,1},{4,6},{6,4},{5,7},{7,5},{8,10},{10,8},{9,1... | collective-permute-start | bytes 3145736 | tf_op jit(solution)/shard_map/cond/branch_1_fun/ppermute | solution.py:1244
  618.1 25.2 %collective-permute-start.12 = (bf16[256,2048]{1,0:T(8,128)(2,1)S(1)}, bf16[256,2048]{1,0:T(8,128)(2,1)}, u32[]{:S(2)}, u32[]{:S(2)}) collective-permute-start(bf16[256,2048]{1,0:T(8,128)(2,1)S(1)} %get-tuple-element.205), channel_id=1, source_target_pairs={{0,2},{2,0},{1,3},{3,1},{4,6},{6,4},{5,7},{7,5},{8,10},{10,8},{9,1... | collective-permute-start | bytes 3145736 | tf_op jit(solution)/shard_map/cond/branch_1_fun/ppermute | solution.py:1254
  620.9 24.9 %collective-permute-start.9 = (bf16[4,128,1024]{2,1,0:T(8,128)(2,1)S(1)}, bf16[4,128,1024]{2,1,0:T(8,128)(2,1)S(1)}, u32[]{:S(2)}, u32[]{:S(2)}) collective-permute-start(bf16[4,128,1024]{2,1,0:T(8,128)(2,1)S(1)} %slice.63), channel_id=1, source_target_pairs={{0,4},{4,0},{1,5},{5,1},{2,6},{6,2},{3,7},{7,3},{8,12},{12,8},{9,1... | collective-permute-start | bytes 3145736 | tf_op jit(solution)/shard_map/cond/branch_1_fun/ppermute | solution.py:1255
  (87 other events, 718.4 us)
Sparse Core Ops, SparseCore 0:
  11.9 66.1 all-gather.13
  80.3 26.5 all-gather.19
  109.1 45.4 all-gather.15
  156.6 44.6 all-gather.17
  202.7 44.5 all-gather.21
  248.7 79.4 all-gather.11
  334.6 143.3 reduce-scatter.4
  493.0 73.6 reduce-scatter.6
  575.5 61.5 reduce-scatter.8
  647.4 25.6 reduce-scatter.10

commit v5 on v4

--- a/solution.py
+++ b/solution.py
@@ -976,7 +976,7 @@
     def blocks_at(blocks, n):
         return table(blocks + [zero + n])[0]
 
-    def sum_small(terms):
+    def sum_small(terms, *others):
         def term(j):
             return lax.dynamic_index_in_dim(
                 terms, lax.rem(zi - j + z_count, z_count), 0, keepdims=False
@@ -984,9 +984,10 @@
 
         total = term(0).astype(wide)
         for j in range(1, z_count):
-            total = total + lax.ppermute(
+            theirs = lax.ppermute(
                 term(j), "z", [(i, (i - j) % z_count) for i in range(z_count)]
-            ).astype(wide)
+            )
+            total = total + after(theirs, *others).astype(wide)
         return total
 
     def plain_matmul(left, pieces, offsets, shape, back, body, extras, outs):
@@ -1152,16 +1153,18 @@
         home = lax.dynamic_slice_in_dim(mixed_grad_pair, yi * part, part, 1)
         theirs = lax.ppermute(away, "y", SWAP)
         feed_home, feed_away = core_sum([after(feed_parts[0], away), feed_parts[1]], yi)
-        theirs = after(theirs, feed_away)
-        return jnp.concatenate(by_bit(yi, home, theirs), axis=0), feed_home, feed_away
-
-    mixed_grad, feed_home, feed_away = line.leave(
+        pair = after(branch_pair, away)
+        branch_away = lax.dynamic_slice_in_dim(pair, (1 - yi) * half, half, 1)
+        branch_home = lax.dynamic_slice_in_dim(pair, yi * half, half, 1)
+        theirs = after(theirs, feed_away, branch_away, branch_home)
+        mixed_grad = jnp.concatenate(by_bit(yi, home, theirs), axis=0)
+        return mixed_grad, feed_home, feed_away, branch_away, branch_home
+
+    mixed_grad, feed_home, feed_away, branch_away, branch_home = line.leave(
         *stage(flag, out_back, line.enter(branch_pair))
     )
-    away = lax.dynamic_slice_in_dim(branch_pair, (1 - yi) * half, half, 1)
-    home = lax.dynamic_slice_in_dim(branch_pair, yi * half, half, 1)
-    branch_other = lax.ppermute(after(away, mixed_grad), "y", SWAP)
-    branch_all = jnp.concatenate(by_bit(yi, home, branch_other), axis=0)
+    branch_other = lax.ppermute(after(branch_away, mixed_grad), "y", SWAP)
+    branch_all = jnp.concatenate(by_bit(yi, branch_home, branch_other), axis=0)
     (proj_grad,) = line.leave(
         attention_back(
             projected,
@@ -1212,9 +1215,18 @@
     qkv_shard = sum_over_z(qkv_sum)
 
     def ends(up_shard):
-        feed_out = home_sum(feed_home, feed_other)
-        output_shard = (residual_one + feed_out + bias_down).astype(low)
+        up_other = lax.ppermute(up_shard, "y", SWAP)
+        down_far = lax.ppermute(down_pair[1], "x", SWAP)
+        output_shard = (residual_one + home_sum(feed_home, feed_other) + bias_down).astype(low)
         output_shard = output_shard.reshape(1, tok_count, model)
+        down_shard = (down_pair[0].astype(wide) + down_far.astype(wide)).astype(low)
+        return output_shard, down_shard, up_other
+
+    output_shard, down_shard, up_other = line.leave(
+        *stage(flag, ends, line.enter(up_shard))
+    )
+
+    def more_ends(down_shard):
         up_bias_grad = jnp.where(
             (jnp.arange(4, dtype=jnp.int32) == si)[None, :, None],
             up_bias_part.reshape(shard_count, 1, ff_part),
@@ -1236,29 +1248,21 @@
         )
         for name in ("c", "y"):
             vector_grad = vector_grad + lax.ppermute(vector_grad, name, SWAP)
-        up_shard = after(up_shard, vector_grad)
+        down_shard = after(down_shard, vector_grad)
         vector_grad = vector_grad.reshape(z_count, 2, -1)
         away = lax.dynamic_index_in_dim(vector_grad, 1 - xi, 1, keepdims=False)
         home = lax.dynamic_index_in_dim(vector_grad, xi, 1, keepdims=False)
         vector_grad = home + lax.ppermute(away, "x", SWAP)
-        up_other = lax.ppermute(up_shard, "y", SWAP)
-        down_far = lax.ppermute(after(down_pair[1], vector_grad), "x", SWAP)
-        down_shard = (down_pair[0].astype(wide) + down_far.astype(wide)).astype(low)
-        return output_shard, sum_small(vector_grad), down_shard, up_other
-
-    output_shard, vector_total, down_shard, up_other = line.leave(
-        *stage(flag, ends, line.enter(up_shard))
-    )
-
-    def more_ends(down_shard):
         down_other = lax.ppermute(down_shard, "y", SWAP)
-        out_away = lax.ppermute(out_sum[:z_count], "x", SWAP)
+        out_away = lax.ppermute(after(out_sum[:z_count], vector_grad), "x", SWAP)
         up_total = widen_columns(core_pieces(up_shard, up_other), places, shard_count)
         out_both = (out_sum[z_count:].astype(wide) + out_away.astype(wide)).astype(low)
-        return out_both, up_total, after(down_other, up_total)
-
-    out_both, up_total, down_other = stage(flag, more_ends, line.enter(down_shard))
-    out_shard = sum_over_z(after(out_both, qkv_shard))
+        return out_both, up_total, after(down_other, up_total), sum_small(vector_grad, up_total)
+
+    out_both, up_total, down_other, vector_total = stage(
+        flag, more_ends, after(line.enter(down_shard), down_shard)
+    )
+    out_shard = sum_over_z(after(out_both, qkv_sum))
 
     def last(qkv_shard):
         other = lax.ppermute(qkv_shard, "y", SWAP)

time: 707 us -> 701 us (level)
  transfers between devices with their start and end apart: 68 -> 68, of which waited for: 37 -> 36; matrix products, arithmetic and copies ran while one was open for 13% -> 13% of each run, Pallas kernels for 33% -> 33%
where the time goes in v5:
time: 701 us; the launch traced here: 691 us
  waiting for transfers between devices  280 us (40%)
  Pallas kernels  243 us (35%)
  other arithmetic  69.6 us (10%)
  starting transfers between devices  56 us (8%)
  local copies, waits for them, and re-layouts  26 us (4%)
  between operations  15.2 us (2%)
    pallas_call x8, Pallas kernels, weight_matmul(): pl.pallas_call(kernel, grid_spec=pltpu.PrefetchScalarGridSpec(num_scalar_...  110 us
    pallas_call x6, Pallas kernels, weight_grad(): pl.pallas_call(kernel, grid_spec=pltpu.PrefetchScalarGridSpec(num_scalar_...  59.9 us
    ppermute x4, waiting for transfers between devices, seq_pieces(): return core_pieces(block, after(lax.ppermute(block, 'y', SWAP), *others))  58 us
    ppermute x4, waiting for transfers between devices, gather_weight(): return [near, lax.ppermute(after(near, *others), 'x', SWAP)]  37.8 us
    ppermute x1, waiting for transfers between devices, norm_one_back(): away = lax.ppermute(away, 'y', SWAP)  23.5 us
    pallas_call x4, Pallas kernels, widen(): pl.pallas_call(kernel, grid_spec=pltpu.PrefetchScalarGridSpec(num_scalar_...  22.6 us
    ppermute x1, waiting for transfers between devices, split_shards(): up_parts += [up_high, lax.ppermute(after(up_high, mixed_heads), 'x', SWAP)]  19.1 us
    ppermute x1, waiting for transfers between devices, ends(): down_far = lax.ppermute(down_pair[1], 'x', SWAP)  18.2 us
  transfers between devices with their start and end apart: 68, of which 36 were waited for; matrix products, arithmetic and copies ran while one was open for 13% of the time, Pallas kernels for 33%

profile of v5, /device:TPU:0, one launch (start us, length us, event | category | flops | bytes accessed | tf_op | source)
XLA Modules:
  0.0 691.3 jit_solution(15521520543917064036)
XLA Ops:
  30.8 8.9 %collective-permute-done.33 = f32[2304]{0:T(1024)S(1)} collective-permute-done((f32[2304]{0:T(1024)S(1)}, f32[2304]{0:T(1024)S(1)}, u32[]{:S(2)}, u32[]{:S(2)}) %collective-permute-start.33) | collective-permute-done | bytes 9248 | tf_op jit(solution)/shard_map/ppermute | solution.py:289
  47.6 21.6 %collective-permute-done.35 = bf16[256,2048]{1,0:T(8,128)(2,1)S(1)} collective-permute-done((bf16[256,2048]{1,0:T(8,128)(2,1)}, bf16[256,2048]{1,0:T(8,128)(2,1)S(1)}, u32[]{:S(2)}, u32[]{:S(2)}) %collective-permute-start.35) | collective-permute-done | bytes 1048608 | tf_op jit(solution)/shard_map/ppermute | solution.py:323
  69.2 8.9 %all-gather.14.cloned.1.call-done = bf16[1024,1536]{1,0:T(8,128)(2,1)} async-done(((bf16[256,1536]{1,0:T(8,128)(2,1)}), bf16[1024,1536]{1,0:T(8,128)(2,1)}) %all-gather.14.cloned.1.call-update) | async-done | bytes 3145744 | tf_op jit(solution)/shard_map/all_gather | solution.py:293
  86.8 23.7 %collective-permute-done.38 = bf16[256,2048]{1,0:T(8,128)(2,1)S(1)} collective-permute-done((bf16[256,2048]{1,0:T(8,128)(2,1)S(1)}, bf16[256,2048]{1,0:T(8,128)(2,1)S(1)}, u32[]{:S(2)}, u32[]{:S(2)}) %collective-permute-start.38) | collective-permute-done | bytes 1048608 | tf_op jit(solution)/shard_map/ppermute | solution.py:323
  114.6 34.6 %collective-permute-done.40.refs_3_.refs_4_ = bf16[4,256,1536]{2,1,0:T(8,128)(2,1)} collective-permute-done((bf16[4,256,1536]{2,1,0:T(8,128)(2,1)}, bf16[4,256,1536]{2,1,0:T(8,128)(2,1)}, u32[]{:S(2)}, u32[]{:S(2)}) %collective-permute-start.40) | collective-permute-done | bytes 3145760 | tf_op jit(solution)/shard_map/ppermute | solution.py:294
  156.1 13.9 %shard_map.240.q_ref.k_ref.v_ref = bf16[1024,1536]{1,0:T(8,128)(2,1)} custom-call(s32[2,8]{1,0:T(2,128)} %stack.343.refs_0_, bf16[1024,2048]{1,0:T(8,128)(2,1)} %pad_maximum_fusion.3.refs_1_.left_ref, bf16[4,256,1536]{2,1,0:T(8,128)(2,1)} %bitcast.119, bf16[4,256,1536]{2,1,0:T(8,128)(2,1)} %collective-permute-done.40.refs_3_.refs_4_), custom_call_target="tpu_custom_call" | custom-call | flops 64424508 | bytes 136314 | tf_op jit(solution)/shard_map/pallas_call | solution.py:482
  170.6 11.4 %shard_map.241 = (bf16[1024,512]{1,0:T(8,128)(2,1)}, f32[4,1024,1]{2,1,0:T(8,128)}) custom-call(bf16[1024,1536]{1,0:T(8,128)(2,1)} %shard_map.240.q_ref.k_ref.v_ref, bf16[1024,1536]{1,0:T(8,128)(2,1)} %shard_map.240.q_ref.k_ref.v_ref, bf16[1024,1536]{1,0:T(8,128)(2,1)} %shard_map.240.q_ref.k_ref.v_ref, s32[1024,1]{1,0:T(8,128)} %copy.31.qi_ref, ...), custom_call_target="tpu_custom_call" | custom-call | flops 21474836 | bytes 41943 | tf_op jit(solution)/shard_map/pallas_call | solution.py:689
  183.5 17.2 %all-gather.18.cloned.1.call-done = bf16[1024,1024]{1,0:T(8,128)(2,1)} async-done(((bf16[256,1024]{1,0:T(8,128)(2,1)}), bf16[1024,1024]{1,0:T(8,128)(2,1)}) %all-gather.18.cloned.1.call-update) | async-done | bytes 2097168 | tf_op jit(solution)/shard_map/all_gather | solution.py:1039
  206.6 36.3 %conditional.7 = (bf16[256,2048]{1,0:T(8,128)(2,1)}, f32[256,2048]{1,0:T(8,128)}, bf16[512,512]{1,0:T(8,128)(2,1)S(1)}, bf16[512,512]{1,0:T(8,128)(2,1)S(1)}) conditional(s32[]{:T(128)} %bitcast.20, () %tuple.127, (s32[]{:T(128)}, bf16[1024,512]{1,0:T(8,128)(2,1)}, s32[2,16]{1,0:T(2,128)S(1)}, bf16[4,128,1024]{2,1,0:T(8,128)(2,1)}, ...), branch_computations={%region_4.5_spmd, %region_5.8_spmd} | conditional | flops 30912284 | bytes 39470188 | solution.py:303
  209.7 10.6 %collective-permute-done.11 = bf16[512,512]{1,0:T(8,128)(2,1)S(1)} collective-permute-done((bf16[512,512]{1,0:T(8,128)(2,1)S(1)}, bf16[512,512]{1,0:T(8,128)(2,1)S(1)}, u32[]{:S(2)}, u32[]{:S(2)}) %collective-permute-start.11) | collective-permute-done | bytes 524320 | tf_op jit(solution)/shard_map/cond/branch_1_fun/ppermute | solution.py:1054
  245.0 19.1 %collective-permute-done.47.refs_5_.refs_6_ = bf16[4,256,1024]{2,1,0:T(8,128)(2,1)} collective-permute-done((bf16[4,256,1024]{2,1,0:T(8,128)(2,1)}, bf16[4,256,1024]{2,1,0:T(8,128)(2,1)}, u32[]{:S(2)}, u32[]{:S(2)}) %collective-permute-start.47) | collective-permute-done | bytes 2097184 | tf_op jit(solution)/shard_map/ppermute | solution.py:1075
  276.7 20.7 %shard_map.242 = (bf16[1024,2048]{1,0:T(8,128)(2,1)}, f32[1024,2048]{1,0:T(8,128)}) custom-call(s32[2,16]{1,0:T(2,128)} %get-tuple-element.461.refs_0_, bf16[1024,2048]{1,0:T(8,128)(2,1)} %pad_maximum_fusion.5.refs_1_.left_ref, bf16[4,256,1024]{2,1,0:T(8,128)(2,1)} %bitcast.122, bf16[4,256,1024]{2,1,0:T(8,128)(2,1)} %collective-permute-done.46.refs_3_.refs_4_, ...), custom_call_target="tpu_custom_call" | custom-call | flops 85899344 | bytes 251740 | tf_op jit(solution)/shard_map/pallas_call | solution.py:482
  299.8 11.7 %collective-permute-done.50 = bf16[512,512]{1,0:T(8,128)(2,1)} collective-permute-done((bf16[512,512]{1,0:T(8,128)(2,1)S(1)}, bf16[512,512]{1,0:T(8,128)(2,1)}, u32[]{:S(2)}, u32[]{:S(2)}) %collective-permute-start.50) | collective-permute-done | bytes 524320 | tf_op jit(solution)/shard_map/ppermute | solution.py:1091
  317.8 14.8 %shard_map.243 = bf16[8,256,2048]{2,1,0:T(8,128)(2,1)} custom-call(s32[9]{0:T(128)} %stack.340.where_ref, bf16[1024,2048]{1,0:T(8,128)(2,1)S(1)} %copy-done.3, bf16[1024,2048]{1,0:T(8,128)(2,1)} %pad_maximum_fusion.4.right_ref.refs_1_), custom_call_target="tpu_custom_call" | custom-call | flops 85899344 | bytes 251658 | tf_op jit(solution)/shard_map/pallas_call | solution.py:546
  333.4 17.6 %shard_map.244 = (bf16[1024,2048]{1,0:T(8,128)(2,1)}, f32[1,2048]{1,0:T(1,128)S(1)}) custom-call(s32[2,16]{1,0:T(2,128)S(1)} %get-tuple-element.460.refs_0_, bf16[1024,2048]{1,0:T(8,128)(2,1)} %pad_maximum_fusion.4.right_ref.refs_1_, bf16[4,256,1024]{2,1,0:T(8,128)(2,1)} %bitcast.130, bf16[4,256,1024]{2,1,0:T(8,128)(2,1)} %collective-permute-done.49.refs_3_, ...), custom_call_target="tpu_custom_call" | custom-call | flops 85899344 | bytes 251740 | tf_op jit(solution)/shard_map/pallas_call | solution.py:482
  351.0 9.5 %shard_map.245 = bf16[4,256,2048]{2,1,0:T(8,128)(2,1)} custom-call(s32[5]{0:T(128)} %stack.344.where_ref, bf16[1024,2048]{1,0:T(8,128)(2,1)} %pad_maximum_fusion.5.refs_1_.left_ref, bf16[1024,2048]{1,0:T(8,128)(2,1)} %get-tuple-element.347.right_ref.refs_2_), custom_call_target="tpu_custom_call" | custom-call | flops 42949672 | bytes 146800 | tf_op jit(solution)/shard_map/pallas_call | solution.py:546
  362.5 15.8 %shard_map.246 = (bf16[512,2048]{1,0:T(8,128)(2,1)}, bf16[512,2048]{1,0:T(8,128)(2,1)S(1)}) custom-call(s32[2,16]{1,0:T(2,128)} %get-tuple-element.461.refs_0_, s32[4]{0:T(128)} %pad_add_fusion.4.refs_1_, bf16[1024,2048]{1,0:T(8,128)(2,1)} %get-tuple-element.347.right_ref.refs_2_, bf16[4,256,1024]{2,1,0:T(8,128)(2,1)} %bitcast.123, ...), custom_call_target="tpu_custom_call" | custom-call | flops 85899344 | bytes 167772 | tf_op jit(solution)/shard_map/pallas_call | solution.py:482
  378.4 48.3 %conditional.8 = (bf16[512,2048]{1,0:T(8,128)(2,1)}, f32[256,2048]{1,0:T(8,128)}, f32[2048]{0:T(1024)S(1)}, f32[2048]{0:T(1024)S(1)}, bf16[512,2048]{1,0:T(8,128)(2,1)}, /*index=5*/bf16[512,2048]{1,0:T(8,128)(2,1)}) conditional(s32[]{:T(128)} %bitcast.20, () %tuple.122, (s32[]{:T(128)}, s32[]{:T(128)}, bf16[512,2048]{1,0:T(8,128)(2,1)}, ...), branch_computations={%region_8.9_spmd, %region_9.16_spmd} | conditional | flops 104769888 | bytes 83110976 | solution.py:303
  394.2 15.3 %branch_1_fun.11 = (bf16[512,2048]{1,0:T(8,128)(2,1)}, bf16[512,2048]{1,0:T(8,128)(2,1)}) custom-call(s32[2,16]{1,0:T(2,128)S(1)} %get-tuple-element.152.refs_0_, s32[4]{0:T(128)} %pad_add_fusion.refs_1_, bf16[1024,2048]{1,0:T(8,128)(2,1)} %get-tuple-element.154.refs_2_, bf16[4,256,1024]{2,1,0:T(8,128)(2,1)S(1)} %copy-done.9, ...), custom_call_target="tpu_custom_call" | custom-call | flops 85899344 | bytes 167772 | tf_op jit(solution)/shard_map/cond/branch_1_fun/pallas_call | solution.py:482
  426.6 26.8 %conditional.9 = (bf16[1024,512]{1,0:T(8,128)(2,1)}, f32[256,2048]{1,0:T(8,128)}, bf16[256,2048]{1,0:T(8,128)(2,1)}, bf16[512,1024]{1,0:T(8,128)(2,1)}, bf16[512,1024]{1,0:T(8,128)(2,1)S(1)}) conditional(s32[]{:T(128)} %bitcast.20, () %tuple.121, (s32[]{:T(128)}, s32[2,16]{1,0:T(2,128)S(1)}, bf16[512,2048]{1,0:T(8,128)(2,1)}, ...), branch_computations={%region_16.17_spmd, %region_17.18_spmd} | conditional | flops 24096276 | bytes 24227716 | solution.py:303
  455.7 15.6 %shard_map.247.right_ref.refs_2_ = bf16[1024,1536]{1,0:T(8,128)(2,1)} custom-call(bf16[1024,1536]{1,0:T(8,128)(2,1)} %shard_map.240.q_ref.k_ref.v_ref, bf16[1024,1536]{1,0:T(8,128)(2,1)} %shard_map.240.q_ref.k_ref.v_ref, bf16[1024,1536]{1,0:T(8,128)(2,1)} %shard_map.240.q_ref.k_ref.v_ref, bf16[1024,512]{1,0:T(8,128)(2,1)} %get-tuple-element.359.g_ref, ...), custom_call_target="tpu_custom_call" | custom-call | flops 53687092 | bytes 83886 | tf_op jit(solution)/shard_map/pallas_call | solution.py:758
  479.4 10.1 %shard_map.249 = bf16[4,256,2048]{2,1,0:T(8,128)(2,1)} custom-call(s32[5]{0:T(128)} %stack.345.where_ref, bf16[1024,2048]{1,0:T(8,128)(2,1)} %pad_maximum_fusion.5.refs_1_.left_ref, bf16[1024,2048]{1,0:T(8,128)(2,1)} %get-tuple-element.347.right_ref.refs_2_, bf16[4,256,2048]{2,1,0:T(8,128)(2,1)} %collective-permute-done.52.refs_0_), custom_call_target="tpu_custom_call" | custom-call | flops 42949672 | bytes 146800 | tf_op jit(solution)/shard_map/pallas_call | solution.py:546
  494.6 12.3 %shard_map.250 = (bf16[512,2048]{1,0:T(8,128)(2,1)}, bf16[512,2048]{1,0:T(8,128)(2,1)S(1)}) custom-call(s32[2,8]{1,0:T(2,128)} %stack.343.refs_0_, s32[4]{0:T(128)} %pad_add_fusion.4.refs_1_, bf16[1024,1536]{1,0:T(8,128)(2,1)} %shard_map.247.right_ref.refs_2_, bf16[4,256,1536]{2,1,0:T(8,128)(2,1)} %bitcast.120, ...), custom_call_target="tpu_custom_call" | custom-call | flops 64424508 | bytes 136314 | tf_op jit(solution)/shard_map/pallas_call | solution.py:482
  506.9 8.8 %shard_map.251 = bf16[8,128,1024]{2,1,0:T(8,128)(2,1)} custom-call(s32[9]{0:T(128)} %stack.346.where_ref, bf16[1024,1024]{1,0:T(8,128)(2,1)} %pad_maximum_fusion.6.left_ref, bf16[1024,1024]{1,0:T(8,128)(2,1)} %pad_maximum_fusion.7.right_ref), custom_call_target="tpu_custom_call" | custom-call | flops 21474836 | bytes 83886 | tf_op jit(solution)/shard_map/pallas_call | solution.py:546
  515.7 40.3 %conditional.10 = (f32[1,256,2048]{2,1,0:T(8,128)}, f32[2048]{0:T(1024)S(1)}, f32[2048]{0:T(1024)S(1)}) conditional(s32[]{:T(128)} %bitcast.20, () %tuple.156, (s32[]{:T(128)}, bf16[512,2048]{1,0:T(8,128)(2,1)}, bf16[512,2048]{1,0:T(8,128)(2,1)S(1)}, f32[8,256]{1,0:T(8,128)S(1)}, f32[256,2048]{1,0:T(8,128)S(1)}, ...), branch_computations={%region_20.21_spmd, %region_21.28_spmd} | conditional | flops 13103360 | bytes 48339968 | solution.py:303
  527.3 23.5 %collective-permute-done.8 = bf16[256,2048]{1,0:T(8,128)(2,1)S(1)} collective-permute-done((bf16[256,2048]{1,0:T(8,128)(2,1)}, bf16[256,2048]{1,0:T(8,128)(2,1)S(1)}, u32[]{:S(2)}, u32[]{:S(2)}) %collective-permute-start.8) | collective-permute-done | bytes 1048608 | tf_op jit(solution)/shard_map/cond/branch_1_fun/ppermute | solution.py:1203
  562.9 8.6 %shard_map.252 = bf16[4,256,1536]{2,1,0:T(8,128)(2,1)} custom-call(s32[5]{0:T(128)} %stack.345.where_ref, bf16[1024,2048]{1,0:T(8,128)(2,1)} %pad_maximum_fusion.3.refs_1_.left_ref, bf16[1024,1536]{1,0:T(8,128)(2,1)} %shard_map.247.right_ref.refs_2_, bf16[4,256,1536]{2,1,0:T(8,128)(2,1)} %collective-permute-done.54.refs_0_), custom_call_target="tpu_custom_call" | custom-call | flops 32212254 | bytes 115343 | tf_op jit(solution)/shard_map/pallas_call | solution.py:546
  571.7 27.8 %conditional.11 = (bf16[1,256,2048]{2,1,0:T(8,128)(2,1)S(1)}, bf16[256,2048]{1,0:T(8,128)(2,1)S(1)}, bf16[256,2048]{1,0:T(8,128)(2,1)}) conditional(s32[]{:T(128)} %bitcast.20, () %tuple.120, (bf16[256,2048]{1,0:T(8,128)(2,1)}, f32[256,2048]{1,0:T(8,128)}, f32[256,2048]{1,0:T(8,128)}, f32[8,2304]{1,0:T(8,128)S(1)}, ...), branch_computations={%region_28.29_spmd, %region_29.30_spmd} | conditional | flops 4718592 | bytes 32546976 | solution.py:303
  580.0 18.2 %collective-permute-done.9 = bf16[256,2048]{1,0:T(8,128)(2,1)S(1)} collective-permute-done((bf16[256,2048]{1,0:T(8,128)(2,1)S(1)}, bf16[256,2048]{1,0:T(8,128)(2,1)S(1)}, u32[]{:S(2)}, u32[]{:S(2)}) %collective-permute-start.9) | collective-permute-done | bytes 1048608 | tf_op jit(solution)/shard_map/cond/branch_1_fun/ppermute | solution.py:1219
  600.5 40.2 %conditional.12 = (bf16[4,128,1024]{2,1,0:T(8,128)(2,1)}, f32[256,8192]{1,0:T(8,128)}, bf16[256,2048]{1,0:T(8,128)(2,1)}, f32[2304]{0:T(1024)}, f32[256]{0:T(256...) conditional(s32[]{:T(128)} %bitcast.20, () %tuple.165, ...), branch_computations={%region_30.31_spmd, %region_31.33_spmd} | conditional | flops 2680627 | bytes 43244504 | solution.py:303
  641.2 28.8 %conditional.13 = (f32[256,6144]{1,0:T(8,128)}, f32[1024,2048]{1,0:T(8,128)}) conditional(s32[]{:T(128)} %bitcast.20, () %tuple.169, (bf16[256,1536]{1,0:T(8,128)(2,1)}, bf16[256,2048]{1,0:T(8,128)(2,1)S(1)}, bf16[256,2048]{1,0:T(8,128)(2,1)}, s32[4]{0:T(128)S(1)}) %tuple.257), branch_computations={%region_34.35_spmd, %region_35.36_spmd} | conditional | bytes 39017896 | solution.py:303
  652.7 8.9 %collective-permute-done.1.refs_2_ = bf16[256,1536]{1,0:T(8,128)(2,1)S(1)} collective-permute-done((bf16[256,1536]{1,0:T(8,128)(2,1)}, bf16[256,1536]{1,0:T(8,128)(2,1)S(1)}, u32[]{:S(2)}, u32[]{:S(2)}) %collective-permute-start.1) | collective-permute-done | bytes 786464 | tf_op jit(solution)/shard_map/cond/branch_1_fun/ppermute | solution.py:1268
  (377 shorter events, 293.4 us)
Async XLA Ops:
  7.2 71.0 %all-gather.14.cloned.1.call-start = ((), (), s32[]{:S(2)}) async-start(), calls=%async_computation.9 | async-start | bytes 3932160 | tf_op jit(solution)/shard_map/all_gather | solution.py:293
  11.8 101.2 %all-gather.20.cloned.1.call-start = ((), (), s32[]{:S(2)}) async-start(), calls=%async_computation.12 | async-start | bytes 1310720 | tf_op jit(solution)/shard_map/all_gather | solution.py:293
  44.7 125.4 %all-gather.16.cloned.1.call-start = ((), (), s32[]{:S(2)}) async-start(), calls=%async_computation.10 | async-start | bytes 2621440 | tf_op jit(solution)/shard_map/all_gather | solution.py:293
  45.4 155.3 %all-gather.18.cloned.1.call-start = ((), (), s32[]{:S(2)}) async-start(), calls=%async_computation.11 | async-start | bytes 2621440 | tf_op jit(solution)/shard_map/all_gather | solution.py:1039
  46.0 223.4 %all-gather.22.cloned.1.call-start = ((), (), s32[]{:S(2)}) async-start(), calls=%async_computation.13 | async-start | bytes 2621440 | tf_op jit(solution)/shard_map/all_gather | solution.py:293
  47.6 32.2 %collective-permute-start.34 = (bf16[256,2048]{1,0:T(8,128)(2,1)}, bf16[256,2048]{1,0:T(8,128)(2,1)S(1)}, u32[]{:S(2)}, u32[]{:S(2)}) collective-permute-start(bf16[256,2048]{1,0:T(8,128)(2,1)} %add_convert_fusion.3), channel_id=1, source_target_pairs={{0,1},{1,0},{2,3},{3,2},{4,5},{5,4},{6,7},{7,6},{8,9},{9,8},{10,11... | collective-permute-start | bytes 3145736 | tf_op jit(solution)/shard_map/ppermute | solution.py:327
  78.2 255.2 %all-gather.12.cloned.1.call-start = ((), (), s32[]{:S(2)}) async-start(), calls=%async_computation.4 | async-start | bytes 5242880 | tf_op jit(solution)/shard_map/all_gather | solution.py:1041
  78.3 70.9 %collective-permute-start.40 = (bf16[4,256,1536]{2,1,0:T(8,128)(2,1)}, bf16[4,256,1536]{2,1,0:T(8,128)(2,1)}, u32[]{:S(2)}, u32[]{:S(2)}) collective-permute-start(bf16[4,256,1536]{2,1,0:T(8,128)(2,1)} %bitcast.118), channel_id=1, source_target_pairs={{0,4},{4,0},{1,5},{5,1},{2,6},{6,2},{3,7},{7,3},{8,12},{12,8},{9,1... | collective-permute-start | bytes 9437192 | tf_op jit(solution)/shard_map/ppermute | solution.py:294
  85.3 25.2 %collective-permute-start.38 = (bf16[256,2048]{1,0:T(8,128)(2,1)S(1)}, bf16[256,2048]{1,0:T(8,128)(2,1)S(1)}, u32[]{:S(2)}, u32[]{:S(2)}) collective-permute-start(bf16[256,2048]{1,0:T(8,128)(2,1)S(1)} %bitcast.141), channel_id=1, source_target_pairs={{0,2},{2,0},{1,3},{3,1},{4,6},{6,4},{5,7},{7,5},{8,10},{10,8},{9,1... | collective-permute-start | bytes 3145736 | tf_op jit(solution)/shard_map/ppermute | solution.py:323
  86.8 63.8 %collective-permute-start.37 = (bf16[256,2048]{1,0:T(8,128)(2,1)S(1)}, bf16[256,2048]{1,0:T(8,128)(2,1)}, u32[]{:S(2)}, u32[]{:S(2)}) collective-permute-start(bf16[256,2048]{1,0:T(8,128)(2,1)S(1)} %bitcast.142), channel_id=1, source_target_pairs={{0,1},{1,0},{2,3},{3,2},{4,5},{5,4},{6,7},{7,6},{8,9},{9,8},{10,11... | collective-permute-start | bytes 3145736 | tf_op jit(solution)/shard_map/ppermute | solution.py:327
  110.5 40.1 %collective-permute-start.39 = (bf16[256,2048]{1,0:T(8,128)(2,1)S(1)}, bf16[256,2048]{1,0:T(8,128)(2,1)}, u32[]{:S(2)}, u32[]{:S(2)}) collective-permute-start(bf16[256,2048]{1,0:T(8,128)(2,1)S(1)} %collective-permute-done.38), channel_id=1, source_target_pairs={{0,1},{1,0},{2,3},{3,2},{4,5},{5,4},{6,7},{7,6},{8,9},{9,8},{10,11... | collective-permute-start | bytes 3145736 | tf_op jit(solution)/shard_map/ppermute | solution.py:327
  113.0 376.6 %reduce-scatter.5.cloned.1.call-start = ((), (), s32[]{:S(2)}) async-start(), calls=%async_computation.5 | async-start | bytes 10485760 | tf_op jit(solution)/shard_map/reduce_scatter | solution.py:1099
  113.0 90.3 %collective-permute-start.42 = (bf16[4,128,1024]{2,1,0:T(8,128)(2,1)}, bf16[4,128,1024]{2,1,0:T(8,128)(2,1)}, u32[]{:S(2)}, u32[]{:S(2)}) collective-permute-start(bf16[4,128,1024]{2,1,0:T(8,128)(2,1)} %bitcast.134), channel_id=1, source_target_pairs={{0,2},{2,0},{1,3},{3,1},{4,6},{6,4},{5,7},{7,5},{8,10},{10,8},{9,1... | collective-permute-start | bytes 3145736 | tf_op jit(solution)/shard_map/ppermute | solution.py:960
  149.2 32.8 %collective-permute-start.41 = (bf16[4,128,1024]{2,1,0:T(8,128)(2,1)}, bf16[4,128,1024]{2,1,0:T(8,128)(2,1)}, u32[]{:S(2)}, u32[]{:S(2)}) collective-permute-start(bf16[4,128,1024]{2,1,0:T(8,128)(2,1)} %bitcast.135), channel_id=1, source_target_pairs={{0,4},{4,0},{1,5},{5,1},{2,6},{6,2},{3,7},{7,3},{8,12},{12,8},{9,1... | collective-permute-start | bytes 3145736 | tf_op jit(solution)/shard_map/ppermute | solution.py:294
  170.1 74.9 %collective-permute-start.46 = (bf16[4,256,1024]{2,1,0:T(8,128)(2,1)}, bf16[4,256,1024]{2,1,0:T(8,128)(2,1)}, u32[]{:S(2)}, u32[]{:S(2)}) collective-permute-start(bf16[4,256,1024]{2,1,0:T(8,128)(2,1)} %bitcast.121), channel_id=1, source_target_pairs={{0,4},{4,0},{1,5},{5,1},{2,6},{6,2},{3,7},{7,3},{8,12},{12,8},{9,1... | collective-permute-start | bytes 6291464 | tf_op jit(solution)/shard_map/ppermute | solution.py:294
  200.7 63.4 %collective-permute-start.47 = (bf16[4,256,1024]{2,1,0:T(8,128)(2,1)}, bf16[4,256,1024]{2,1,0:T(8,128)(2,1)}, u32[]{:S(2)}, u32[]{:S(2)}) collective-permute-start(bf16[4,256,1024]{2,1,0:T(8,128)(2,1)} %bitcast.124), channel_id=1, source_target_pairs={{0,4},{4,0},{1,5},{5,1},{2,6},{6,2},{3,7},{7,3},{8,12},{12,8},{9,1... | collective-permute-start | bytes 6291464 | tf_op jit(solution)/shard_map/ppermute | solution.py:1075
  242.9 25.9 %collective-permute-start.45 = (bf16[256,2048]{1,0:T(8,128)(2,1)}, bf16[256,2048]{1,0:T(8,128)(2,1)}, u32[]{:S(2)}, u32[]{:S(2)}) collective-permute-start(bf16[256,2048]{1,0:T(8,128)(2,1)} %get-tuple-element.330), channel_id=1, source_target_pairs={{0,2},{2,0},{1,3},{3,1},{4,6},{6,4},{5,7},{7,5},{8,10},{10,8},{9,1... | collective-permute-start | bytes 3145736 | tf_op jit(solution)/shard_map/ppermute | solution.py:323
  245.0 25.8 %collective-permute-start.44 = (bf16[256,2048]{1,0:T(8,128)(2,1)}, bf16[256,2048]{1,0:T(8,128)(2,1)}, u32[]{:S(2)}, u32[]{:S(2)}) collective-permute-start(bf16[256,2048]{1,0:T(8,128)(2,1)} %get-tuple-element.330), channel_id=1, source_target_pairs={{0,1},{1,0},{2,3},{3,2},{4,5},{5,4},{6,7},{7,6},{8,9},{9,8},{10,11... | collective-permute-start | bytes 3145736 | tf_op jit(solution)/shard_map/ppermute | solution.py:327
  269.4 48.4 %collective-permute-start.49 = (bf16[4,256,1024]{2,1,0:T(8,128)(2,1)}, bf16[4,256,1024]{2,1,0:T(8,128)(2,1)}, u32[]{:S(2)}, u32[]{:S(2)}) collective-permute-start(bf16[4,256,1024]{2,1,0:T(8,128)(2,1)} %bitcast.129), channel_id=1, source_target_pairs={{0,4},{4,0},{1,5},{5,1},{2,6},{6,2},{3,7},{7,3},{8,12},{12,8},{9,1... | collective-permute-start | bytes 6291464 | tf_op jit(solution)/shard_map/ppermute | solution.py:294
  332.6 230.3 %reduce-scatter.7.cloned.1.call-start = ((), (), s32[]{:S(2)}) async-start(), calls=%async_computation.6 | async-start | bytes 5242880 | tf_op jit(solution)/shard_map/reduce_scatter | solution.py:1019
  360.5 118.9 %collective-permute-start.52 = (bf16[4,256,2048]{2,1,0:T(8,128)(2,1)}, bf16[4,256,2048]{2,1,0:T(8,128)(2,1)}, u32[]{:S(2)}, u32[]{:S(2)}) collective-permute-start(bf16[4,256,2048]{2,1,0:T(8,128)(2,1)} %shard_map.245), channel_id=1, source_target_pairs={{0,4},{4,0},{1,5},{5,1},{2,6},{6,2},{3,7},{7,3},{8,12},{12,8},{9,1... | collective-permute-start | bytes 12582920 | tf_op jit(solution)/shard_map/ppermute | solution.py:1011
  388.1 25.4 %collective-permute-start.14 = (bf16[256,2048]{1,0:T(8,128)(2,1)}, bf16[256,2048]{1,0:T(8,128)(2,1)S(1)}, u32[]{:S(2)}, u32[]{:S(2)}) collective-permute-start(bf16[256,2048]{1,0:T(8,128)(2,1)} %get-tuple-element.151), channel_id=1, source_target_pairs={{0,2},{2,0},{1,3},{3,1},{4,6},{6,4},{5,7},{7,5},{8,10},{10,8},{9,1... | collective-permute-start | bytes 3145736 | tf_op jit(solution)/shard_map/cond/branch_1_fun/ppermute | solution.py:1119
  453.4 26.0 %collective-permute-start.51 = (bf16[512,1024]{1,0:T(8,128)(2,1)}, bf16[512,1024]{1,0:T(8,128)(2,1)}, u32[]{:S(2)}, u32[]{:S(2)}) collective-permute-start(bf16[512,1024]{1,0:T(8,128)(2,1)} %get-tuple-element.357), channel_id=1, source_target_pairs={{0,2},{2,0},{1,3},{3,1},{4,6},{6,4},{5,7},{7,5},{8,10},{10,8},{9,1... | collective-permute-start | bytes 3145736 | tf_op jit(solution)/shard_map/ppermute | solution.py:1166
  489.5 151.2 %reduce-scatter.9.cloned.1.call-start = ((), (), s32[]{:S(2)}) async-start(), calls=%async_computation.7 | async-start | bytes 3932160 | tf_op jit(solution)/shard_map/reduce_scatter | solution.py:1019
  489.6 73.3 %collective-permute-start.54 = (bf16[4,256,1536]{2,1,0:T(8,128)(2,1)}, bf16[4,256,1536]{2,1,0:T(8,128)(2,1)}, u32[]{:S(2)}, u32[]{:S(2)}) collective-permute-start(bf16[4,256,1536]{2,1,0:T(8,128)(2,1)} %shard_map.248), channel_id=1, source_target_pairs={{0,4},{4,0},{1,5},{5,1},{2,6},{6,2},{3,7},{7,3},{8,12},{12,8},{9,1... | collective-permute-start | bytes 9437192 | tf_op jit(solution)/shard_map/ppermute | solution.py:1011
  490.2 25.5 %collective-permute-start.53 = (bf16[256,2048]{1,0:T(8,128)(2,1)}, bf16[256,2048]{1,0:T(8,128)(2,1)}, u32[]{:S(2)}, u32[]{:S(2)}) collective-permute-start(bf16[256,2048]{1,0:T(8,128)(2,1)} %get-tuple-element.363), channel_id=1, source_target_pairs={{0,2},{2,0},{1,3},{3,1},{4,6},{6,4},{5,7},{7,5},{8,10},{10,8},{9,1... | collective-permute-start | bytes 3145736 | tf_op jit(solution)/shard_map/ppermute | solution.py:1199
  525.4 25.4 %collective-permute-start.8 = (bf16[256,2048]{1,0:T(8,128)(2,1)}, bf16[256,2048]{1,0:T(8,128)(2,1)S(1)}, u32[]{:S(2)}, u32[]{:S(2)}) collective-permute-start(bf16[256,2048]{1,0:T(8,128)(2,1)} %get-tuple-element.182), channel_id=1, source_target_pairs={{0,2},{2,0},{1,3},{3,1},{4,6},{6,4},{5,7},{7,5},{8,10},{10,8},{9,1... | collective-permute-start | bytes 3145736 | tf_op jit(solution)/shard_map/cond/branch_1_fun/ppermute | solution.py:1203
  571.6 98.5 %reduce-scatter.11.cloned.1.call-start = ((), (), s32[]{:S(2)}) async-start(), calls=%async_computation.8 | async-start | bytes 1310720 | tf_op jit(solution)/shard_map/reduce_scatter | solution.py:1019
  573.2 25.0 %collective-permute-start.9 = (bf16[256,2048]{1,0:T(8,128)(2,1)S(1)}, bf16[256,2048]{1,0:T(8,128)(2,1)S(1)}, u32[]{:S(2)}, u32[]{:S(2)}) collective-permute-start(bf16[256,2048]{1,0:T(8,128)(2,1)S(1)} %slice_bitcast_fusion.1), channel_id=1, source_target_pairs={{0,4},{4,0},{1,5},{5,1},{2,6},{6,2},{3,7},{7,3},{8,12},{12,8},{9,1... | collective-permute-start | bytes 3145736 | tf_op jit(solution)/shard_map/cond/branch_1_fun/ppermute | solution.py:1219
  574.7 24.8 %collective-permute-start.10 = (bf16[256,2048]{1,0:T(8,128)(2,1)S(1)}, bf16[256,2048]{1,0:T(8,128)(2,1)}, u32[]{:S(2)}, u32[]{:S(2)}) collective-permute-start(bf16[256,2048]{1,0:T(8,128)(2,1)S(1)} %copy-done.19), channel_id=1, source_target_pairs={{0,2},{2,0},{1,3},{3,1},{4,6},{6,4},{5,7},{7,5},{8,10},{10,8},{9,1... | collective-permute-start | bytes 3145736 | tf_op jit(solution)/shard_map/cond/branch_1_fun/ppermute | solution.py:1218
  611.4 25.2 %collective-permute-start.22 = (bf16[256,2048]{1,0:T(8,128)(2,1)S(1)}, bf16[256,2048]{1,0:T(8,128)(2,1)}, u32[]{:S(2)}, u32[]{:S(2)}) collective-permute-start(bf16[256,2048]{1,0:T(8,128)(2,1)S(1)} %get-tuple-element.205), channel_id=1, source_target_pairs={{0,2},{2,0},{1,3},{3,1},{4,6},{6,4},{5,7},{7,5},{8,10},{10,8},{9,1... | collective-permute-start | bytes 3145736 | tf_op jit(solution)/shard_map/cond/branch_1_fun/ppermute | solution.py:1256
  612.9 25.2 %collective-permute-start.19 = (bf16[4,128,1024]{2,1,0:T(8,128)(2,1)}, bf16[4,128,1024]{2,1,0:T(8,128)(2,1)}, u32[]{:S(2)}, u32[]{:S(2)}) collective-permute-start(bf16[4,128,1024]{2,1,0:T(8,128)(2,1)} %slice.57), channel_id=1, source_target_pairs={{0,4},{4,0},{1,5},{5,1},{2,6},{6,2},{3,7},{7,3},{8,12},{12,8},{9,1... | collective-permute-start | bytes 3145736 | tf_op jit(solution)/shard_map/cond/branch_1_fun/ppermute | solution.py:1257
  (85 other events, 719.5 us)
Sparse Core Ops, SparseCore 0:
  11.9 66.1 all-gather.13
  80.3 26.5 all-gather.19
  109.1 45.4 all-gather.15
  156.0 44.6 all-gather.17
  202.1 44.6 all-gather.21
  248.8 79.4 all-gather.11
  332.7 143.3 reduce-scatter.4
  489.7 73.2 reduce-scatter.6
  571.7 61.4 reduce-scatter.8
  640.8 26.7 reduce-scatter.10

commit v6 on v5

--- a/solution.py
+++ b/solution.py
@@ -1246,32 +1246,34 @@
             ],
             axis=1,
         )
-        for name in ("c", "y"):
-            vector_grad = vector_grad + lax.ppermute(vector_grad, name, SWAP)
-        down_shard = after(down_shard, vector_grad)
-        vector_grad = vector_grad.reshape(z_count, 2, -1)
-        away = lax.dynamic_index_in_dim(vector_grad, 1 - xi, 1, keepdims=False)
-        home = lax.dynamic_index_in_dim(vector_grad, xi, 1, keepdims=False)
-        vector_grad = home + lax.ppermute(away, "x", SWAP)
+        vector_grad = vector_grad + lax.ppermute(vector_grad, "c", SWAP)
+        vector_other = lax.ppermute(vector_grad, "y", SWAP)
         down_other = lax.ppermute(down_shard, "y", SWAP)
-        out_away = lax.ppermute(after(out_sum[:z_count], vector_grad), "x", SWAP)
+        out_away = lax.ppermute(out_sum[:z_count], "x", SWAP)
         up_total = widen_columns(core_pieces(up_shard, up_other), places, shard_count)
         out_both = (out_sum[z_count:].astype(wide) + out_away.astype(wide)).astype(low)
-        return out_both, up_total, after(down_other, up_total), sum_small(vector_grad, up_total)
-
-    out_both, up_total, down_other, vector_total = stage(
+        vector_grad = vector_grad + after(vector_other, up_total)
+        return out_both, up_total, after(down_other, up_total), vector_grad
+
+    out_both, up_total, down_other, vector_grad = stage(
         flag, more_ends, after(line.enter(down_shard), down_shard)
     )
     out_shard = sum_over_z(after(out_both, qkv_sum))
 
     def last(qkv_shard):
         other = lax.ppermute(qkv_shard, "y", SWAP)
+        vector_pair = vector_grad.reshape(z_count, 2, -1)
+        away = lax.dynamic_index_in_dim(vector_pair, 1 - xi, 1, keepdims=False)
+        home = lax.dynamic_index_in_dim(vector_pair, xi, 1, keepdims=False)
+        vector_other = lax.ppermute(away, "x", SWAP)
         down_total = widen_rows(core_pieces(down_shard, down_other), places)
-        qkv_pieces = core_pieces(qkv_shard, after(other, down_total))
-        return widen_heads(qkv_pieces, places), down_total
-
-    qkv_total, down_total = stage(flag, last, after(qkv_shard, up_total))
+        vector_sum = home + after(vector_other, down_total)
+        qkv_pieces = core_pieces(qkv_shard, after(other, vector_sum))
+        return widen_heads(qkv_pieces, places), down_total, vector_sum
+
+    qkv_total, down_total, vector_sum = stage(flag, last, after(qkv_shard, up_total))
     out_total = widen_quarters(seq_pieces(after(out_shard, qkv_total)), places)
+    vector_total = sum_small(after(vector_sum, qkv_total))
     vectors = [vector_total[slot * piece_d : (slot + 1) * piece_d] for slot in range(5)]
     return (
         output_shard,

time: 701 us -> 694 us (0.990)
    ppermute x4, waiting for transfers between devices: 5.63 us -> 14.1 us  [the longest x1 10.7 us: more_ends(): vector_other = lax.ppermute(vector_grad, 'y', SWAP)]
    ppermute x4, waiting for transfers between devices: 58 us -> 50.1 us  [seq_pieces(): return core_pieces(block, after(lax.ppermute(block, 'y', SWAP), *others))]
  transfers between devices with their start and end apart: 68 -> 68, of which waited for: 36 -> 37; matrix products, arithmetic and copies ran while one was open for 13% -> 13% of each run, Pallas kernels for 33% -> 33%
where the time goes in v6:
time: 694 us; the launch traced here: 684 us
  waiting for transfers between devices  276 us (40%)
  Pallas kernels  243 us (35%)
  other arithmetic  69 us (10%)
  starting transfers between devices  54.4 us (8%)
  local copies, waits for them, and re-layouts  25.4 us (4%)
  between operations  15.2 us (2%)
    pallas_call x8, Pallas kernels, weight_matmul(): pl.pallas_call(kernel, grid_spec=pltpu.PrefetchScalarGridSpec(num_scalar_...  110 us
    pallas_call x6, Pallas kernels, weight_grad(): pl.pallas_call(kernel, grid_spec=pltpu.PrefetchScalarGridSpec(num_scalar_...  59.9 us
    ppermute x4, waiting for transfers between devices, seq_pieces(): return core_pieces(block, after(lax.ppermute(block, 'y', SWAP), *others))  50.1 us
    ppermute x4, waiting for transfers between devices, gather_weight(): return [near, lax.ppermute(after(near, *others), 'x', SWAP)]  37.9 us
    ppermute x1, waiting for transfers between devices, norm_one_back(): away = lax.ppermute(away, 'y', SWAP)  23.6 us
    pallas_call x4, Pallas kernels, widen(): pl.pallas_call(kernel, grid_spec=pltpu.PrefetchScalarGridSpec(num_scalar_...  22.6 us
    ppermute x1, waiting for transfers between devices, split_shards(): up_parts += [up_high, lax.ppermute(after(up_high, mixed_heads), 'x', SWAP)]  19.1 us
    ppermute x1, waiting for transfers between devices, ends(): down_far = lax.ppermute(down_pair[1], 'x', SWAP)  18.2 us
  transfers between devices with their start and end apart: 68, of which 37 were waited for; matrix products, arithmetic and copies ran while one was open for 13% of the time, Pallas kernels for 33%

profile of v6, /device:TPU:0, one launch (start us, length us, event | category | flops | bytes accessed | tf_op | source)
XLA Modules:
  0.0 684.2 jit_solution(15087731795439158891)
XLA Ops:
  30.8 8.9 %collective-permute-done.30 = f32[2304]{0:T(1024)S(1)} collective-permute-done((f32[2304]{0:T(1024)S(1)}, f32[2304]{0:T(1024)S(1)}, u32[]{:S(2)}, u32[]{:S(2)}) %collective-permute-start.30) | collective-permute-done | bytes 9248 | tf_op jit(solution)/shard_map/ppermute | solution.py:289
  47.6 21.6 %collective-permute-done.32 = bf16[256,2048]{1,0:T(8,128)(2,1)S(1)} collective-permute-done((bf16[256,2048]{1,0:T(8,128)(2,1)}, bf16[256,2048]{1,0:T(8,128)(2,1)S(1)}, u32[]{:S(2)}, u32[]{:S(2)}) %collective-permute-start.32) | collective-permute-done | bytes 1048608 | tf_op jit(solution)/shard_map/ppermute | solution.py:323
  69.2 8.9 %all-gather.14.cloned.1.call-done = bf16[1024,1536]{1,0:T(8,128)(2,1)} async-done(((bf16[256,1536]{1,0:T(8,128)(2,1)}), bf16[1024,1536]{1,0:T(8,128)(2,1)}) %all-gather.14.cloned.1.call-update) | async-done | bytes 3145744 | tf_op jit(solution)/shard_map/all_gather | solution.py:293
  86.8 23.7 %collective-permute-done.35 = bf16[256,2048]{1,0:T(8,128)(2,1)S(1)} collective-permute-done((bf16[256,2048]{1,0:T(8,128)(2,1)S(1)}, bf16[256,2048]{1,0:T(8,128)(2,1)S(1)}, u32[]{:S(2)}, u32[]{:S(2)}) %collective-permute-start.35) | collective-permute-done | bytes 1048608 | tf_op jit(solution)/shard_map/ppermute | solution.py:323
  114.5 34.6 %collective-permute-done.37.refs_3_.refs_4_ = bf16[4,256,1536]{2,1,0:T(8,128)(2,1)} collective-permute-done((bf16[4,256,1536]{2,1,0:T(8,128)(2,1)}, bf16[4,256,1536]{2,1,0:T(8,128)(2,1)}, u32[]{:S(2)}, u32[]{:S(2)}) %collective-permute-start.37) | collective-permute-done | bytes 3145760 | tf_op jit(solution)/shard_map/ppermute | solution.py:294
  156.1 13.9 %shard_map.240.q_ref.k_ref.v_ref = bf16[1024,1536]{1,0:T(8,128)(2,1)} custom-call(s32[2,8]{1,0:T(2,128)} %stack.343.refs_0_, bf16[1024,2048]{1,0:T(8,128)(2,1)} %pad_maximum_fusion.3.refs_1_.left_ref, bf16[4,256,1536]{2,1,0:T(8,128)(2,1)} %bitcast.121, bf16[4,256,1536]{2,1,0:T(8,128)(2,1)} %collective-permute-done.37.refs_3_.refs_4_), custom_call_target="tpu_custom_call" | custom-call | flops 64424508 | bytes 136314 | tf_op jit(solution)/shard_map/pallas_call | solution.py:482
  170.6 11.4 %shard_map.241 = (bf16[1024,512]{1,0:T(8,128)(2,1)}, f32[4,1024,1]{2,1,0:T(8,128)}) custom-call(bf16[1024,1536]{1,0:T(8,128)(2,1)} %shard_map.240.q_ref.k_ref.v_ref, bf16[1024,1536]{1,0:T(8,128)(2,1)} %shard_map.240.q_ref.k_ref.v_ref, bf16[1024,1536]{1,0:T(8,128)(2,1)} %shard_map.240.q_ref.k_ref.v_ref, s32[1024,1]{1,0:T(8,128)} %copy.39.qi_ref, ...), custom_call_target="tpu_custom_call" | custom-call | flops 21474836 | bytes 41943 | tf_op jit(solution)/shard_map/pallas_call | solution.py:689
  183.5 17.2 %all-gather.18.cloned.1.call-done = bf16[1024,1024]{1,0:T(8,128)(2,1)} async-done(((bf16[256,1024]{1,0:T(8,128)(2,1)}), bf16[1024,1024]{1,0:T(8,128)(2,1)}) %all-gather.18.cloned.1.call-update) | async-done | bytes 2097168 | tf_op jit(solution)/shard_map/all_gather | solution.py:1039
  206.6 36.3 %conditional.7 = (bf16[256,2048]{1,0:T(8,128)(2,1)}, f32[256,2048]{1,0:T(8,128)}, bf16[512,512]{1,0:T(8,128)(2,1)S(1)}, bf16[512,512]{1,0:T(8,128)(2,1)S(1)}) conditional(s32[]{:T(128)} %bitcast.22, () %tuple.123, (s32[]{:T(128)}, bf16[1024,512]{1,0:T(8,128)(2,1)}, s32[2,16]{1,0:T(2,128)S(1)}, bf16[4,128,1024]{2,1,0:T(8,128)(2,1)}, ...), branch_computations={%region_4.5_spmd, %region_5.8_spmd} | conditional | flops 30912284 | bytes 39470188 | solution.py:303
  209.7 10.6 %collective-permute-done.18 = bf16[512,512]{1,0:T(8,128)(2,1)S(1)} collective-permute-done((bf16[512,512]{1,0:T(8,128)(2,1)S(1)}, bf16[512,512]{1,0:T(8,128)(2,1)S(1)}, u32[]{:S(2)}, u32[]{:S(2)}) %collective-permute-start.18) | collective-permute-done | bytes 524320 | tf_op jit(solution)/shard_map/cond/branch_1_fun/ppermute | solution.py:1054
  245.1 19.1 %collective-permute-done.44.refs_5_.refs_6_ = bf16[4,256,1024]{2,1,0:T(8,128)(2,1)} collective-permute-done((bf16[4,256,1024]{2,1,0:T(8,128)(2,1)}, bf16[4,256,1024]{2,1,0:T(8,128)(2,1)}, u32[]{:S(2)}, u32[]{:S(2)}) %collective-permute-start.44) | collective-permute-done | bytes 2097184 | tf_op jit(solution)/shard_map/ppermute | solution.py:1075
  276.7 20.7 %shard_map.242 = (bf16[1024,2048]{1,0:T(8,128)(2,1)}, f32[1024,2048]{1,0:T(8,128)}) custom-call(s32[2,16]{1,0:T(2,128)} %get-tuple-element.446.refs_0_, bf16[1024,2048]{1,0:T(8,128)(2,1)} %pad_maximum_fusion.5.refs_1_.left_ref, bf16[4,256,1024]{2,1,0:T(8,128)(2,1)} %bitcast.124, bf16[4,256,1024]{2,1,0:T(8,128)(2,1)} %collective-permute-done.43.refs_3_.refs_4_, ...), custom_call_target="tpu_custom_call" | custom-call | flops 85899344 | bytes 251740 | tf_op jit(solution)/shard_map/pallas_call | solution.py:482
  299.8 11.7 %collective-permute-done.47 = bf16[512,512]{1,0:T(8,128)(2,1)} collective-permute-done((bf16[512,512]{1,0:T(8,128)(2,1)S(1)}, bf16[512,512]{1,0:T(8,128)(2,1)}, u32[]{:S(2)}, u32[]{:S(2)}) %collective-permute-start.47) | collective-permute-done | bytes 524320 | tf_op jit(solution)/shard_map/ppermute | solution.py:1091
  317.8 14.8 %shard_map.243 = bf16[8,256,2048]{2,1,0:T(8,128)(2,1)} custom-call(s32[9]{0:T(128)} %stack.340.where_ref, bf16[1024,2048]{1,0:T(8,128)(2,1)S(1)} %copy-done.3, bf16[1024,2048]{1,0:T(8,128)(2,1)} %pad_maximum_fusion.4.right_ref.refs_1_), custom_call_target="tpu_custom_call" | custom-call | flops 85899344 | bytes 251658 | tf_op jit(solution)/shard_map/pallas_call | solution.py:546
  333.5 17.5 %shard_map.244 = (bf16[1024,2048]{1,0:T(8,128)(2,1)}, f32[1,2048]{1,0:T(1,128)S(1)}) custom-call(s32[2,16]{1,0:T(2,128)S(1)} %get-tuple-element.445.refs_0_, bf16[1024,2048]{1,0:T(8,128)(2,1)} %pad_maximum_fusion.4.right_ref.refs_1_, bf16[4,256,1024]{2,1,0:T(8,128)(2,1)} %bitcast.132, bf16[4,256,1024]{2,1,0:T(8,128)(2,1)} %collective-permute-done.46.refs_3_, ...), custom_call_target="tpu_custom_call" | custom-call | flops 85899344 | bytes 251740 | tf_op jit(solution)/shard_map/pallas_call | solution.py:482
  351.0 9.4 %shard_map.245 = bf16[4,256,2048]{2,1,0:T(8,128)(2,1)} custom-call(s32[5]{0:T(128)} %stack.344.where_ref, bf16[1024,2048]{1,0:T(8,128)(2,1)} %pad_maximum_fusion.5.refs_1_.left_ref, bf16[1024,2048]{1,0:T(8,128)(2,1)} %get-tuple-element.335.right_ref.refs_2_), custom_call_target="tpu_custom_call" | custom-call | flops 42949672 | bytes 146800 | tf_op jit(solution)/shard_map/pallas_call | solution.py:546
  362.6 15.8 %shard_map.246 = (bf16[512,2048]{1,0:T(8,128)(2,1)}, bf16[512,2048]{1,0:T(8,128)(2,1)S(1)}) custom-call(s32[2,16]{1,0:T(2,128)} %get-tuple-element.446.refs_0_, s32[4]{0:T(128)} %pad_add_fusion.4.refs_1_, bf16[1024,2048]{1,0:T(8,128)(2,1)} %get-tuple-element.335.right_ref.refs_2_, bf16[4,256,1024]{2,1,0:T(8,128)(2,1)} %bitcast.125, ...), custom_call_target="tpu_custom_call" | custom-call | flops 85899344 | bytes 167772 | tf_op jit(solution)/shard_map/pallas_call | solution.py:482
  378.5 48.2 %conditional.8 = (bf16[512,2048]{1,0:T(8,128)(2,1)}, f32[256,2048]{1,0:T(8,128)}, f32[2048]{0:T(1024)S(1)}, f32[2048]{0:T(1024)S(1)}, bf16[512,2048]{1,0:T(8,128)(2,1)}, /*index=5*/bf16[512,2048]{1,0:T(8,128)(2,1)}) conditional(s32[]{:T(128)} %bitcast.22, () %tuple.118, (s32[]{:T(128)}, s32[]{:T(128)}, bf16[512,2048]{1,0:T(8,128)(2,1)}, ...), branch_computations={%region_8.9_spmd, %region_9.16_spmd} | conditional | flops 104769888 | bytes 83110976 | solution.py:303
  394.3 15.3 %branch_1_fun.11 = (bf16[512,2048]{1,0:T(8,128)(2,1)}, bf16[512,2048]{1,0:T(8,128)(2,1)}) custom-call(s32[2,16]{1,0:T(2,128)S(1)} %get-tuple-element.146.refs_0_, s32[4]{0:T(128)} %pad_add_fusion.refs_1_, bf16[1024,2048]{1,0:T(8,128)(2,1)} %get-tuple-element.148.refs_2_, bf16[4,256,1024]{2,1,0:T(8,128)(2,1)S(1)} %copy-done.9, ...), custom_call_target="tpu_custom_call" | custom-call | flops 85899344 | bytes 167772 | tf_op jit(solution)/shard_map/cond/branch_1_fun/pallas_call | solution.py:482
  426.7 26.8 %conditional.9 = (bf16[1024,512]{1,0:T(8,128)(2,1)}, f32[256,2048]{1,0:T(8,128)}, bf16[256,2048]{1,0:T(8,128)(2,1)}, bf16[512,1024]{1,0:T(8,128)(2,1)}, bf16[512,1024]{1,0:T(8,128)(2,1)S(1)}) conditional(s32[]{:T(128)} %bitcast.22, () %tuple.117, (s32[]{:T(128)}, s32[2,16]{1,0:T(2,128)S(1)}, bf16[512,2048]{1,0:T(8,128)(2,1)}, ...), branch_computations={%region_16.17_spmd, %region_17.18_spmd} | conditional | flops 24096276 | bytes 24227716 | solution.py:303
  455.7 15.6 %shard_map.247.right_ref.refs_2_ = bf16[1024,1536]{1,0:T(8,128)(2,1)} custom-call(bf16[1024,1536]{1,0:T(8,128)(2,1)} %shard_map.240.q_ref.k_ref.v_ref, bf16[1024,1536]{1,0:T(8,128)(2,1)} %shard_map.240.q_ref.k_ref.v_ref, bf16[1024,1536]{1,0:T(8,128)(2,1)} %shard_map.240.q_ref.k_ref.v_ref, bf16[1024,512]{1,0:T(8,128)(2,1)} %get-tuple-element.347.g_ref, ...), custom_call_target="tpu_custom_call" | custom-call | flops 53687092 | bytes 83886 | tf_op jit(solution)/shard_map/pallas_call | solution.py:758
  479.4 10.1 %shard_map.249 = bf16[4,256,2048]{2,1,0:T(8,128)(2,1)} custom-call(s32[5]{0:T(128)} %stack.345.where_ref, bf16[1024,2048]{1,0:T(8,128)(2,1)} %pad_maximum_fusion.5.refs_1_.left_ref, bf16[1024,2048]{1,0:T(8,128)(2,1)} %get-tuple-element.335.right_ref.refs_2_, bf16[4,256,2048]{2,1,0:T(8,128)(2,1)} %collective-permute-done.49.refs_0_), custom_call_target="tpu_custom_call" | custom-call | flops 42949672 | bytes 146800 | tf_op jit(solution)/shard_map/pallas_call | solution.py:546
  494.7 12.3 %shard_map.250 = (bf16[512,2048]{1,0:T(8,128)(2,1)}, bf16[512,2048]{1,0:T(8,128)(2,1)S(1)}) custom-call(s32[2,8]{1,0:T(2,128)} %stack.343.refs_0_, s32[4]{0:T(128)} %pad_add_fusion.4.refs_1_, bf16[1024,1536]{1,0:T(8,128)(2,1)} %shard_map.247.right_ref.refs_2_, bf16[4,256,1536]{2,1,0:T(8,128)(2,1)} %bitcast.122, ...), custom_call_target="tpu_custom_call" | custom-call | flops 64424508 | bytes 136314 | tf_op jit(solution)/shard_map/pallas_call | solution.py:482
  507.0 8.8 %shard_map.251 = bf16[8,128,1024]{2,1,0:T(8,128)(2,1)} custom-call(s32[9]{0:T(128)} %stack.346.where_ref, bf16[1024,1024]{1,0:T(8,128)(2,1)} %pad_maximum_fusion.6.left_ref, bf16[1024,1024]{1,0:T(8,128)(2,1)} %pad_maximum_fusion.7.right_ref), custom_call_target="tpu_custom_call" | custom-call | flops 21474836 | bytes 83886 | tf_op jit(solution)/shard_map/pallas_call | solution.py:546
  515.8 40.3 %conditional.10 = (f32[1,256,2048]{2,1,0:T(8,128)}, f32[2048]{0:T(1024)S(1)}, f32[2048]{0:T(1024)S(1)}) conditional(s32[]{:T(128)} %bitcast.22, () %tuple.152, (s32[]{:T(128)}, bf16[512,2048]{1,0:T(8,128)(2,1)}, bf16[512,2048]{1,0:T(8,128)(2,1)S(1)}, f32[8,256]{1,0:T(8,128)S(1)}, f32[256,2048]{1,0:T(8,128)S(1)}, ...), branch_computations={%region_20.21_spmd, %region_21.28_spmd} | conditional | flops 13103360 | bytes 48339968 | solution.py:303
  527.3 23.6 %collective-permute-done.3 = bf16[256,2048]{1,0:T(8,128)(2,1)S(1)} collective-permute-done((bf16[256,2048]{1,0:T(8,128)(2,1)}, bf16[256,2048]{1,0:T(8,128)(2,1)S(1)}, u32[]{:S(2)}, u32[]{:S(2)}) %collective-permute-start.3) | collective-permute-done | bytes 1048608 | tf_op jit(solution)/shard_map/cond/branch_1_fun/ppermute | solution.py:1203
  571.8 27.8 %conditional.11 = (bf16[1,256,2048]{2,1,0:T(8,128)(2,1)S(1)}, bf16[256,2048]{1,0:T(8,128)(2,1)S(1)}, bf16[256,2048]{1,0:T(8,128)(2,1)}) conditional(s32[]{:T(128)} %bitcast.22, () %tuple.116, (bf16[256,2048]{1,0:T(8,128)(2,1)}, f32[256,2048]{1,0:T(8,128)}, f32[256,2048]{1,0:T(8,128)}, f32[8,2304]{1,0:T(8,128)S(1)}, ...), branch_computations={%region_28.29_spmd, %region_29.30_spmd} | conditional | flops 4718592 | bytes 32546976 | solution.py:303
  580.1 18.2 %collective-permute-done.4 = bf16[256,2048]{1,0:T(8,128)(2,1)S(1)} collective-permute-done((bf16[256,2048]{1,0:T(8,128)(2,1)S(1)}, bf16[256,2048]{1,0:T(8,128)(2,1)S(1)}, u32[]{:S(2)}, u32[]{:S(2)}) %collective-permute-start.4) | collective-permute-done | bytes 1048608 | tf_op jit(solution)/shard_map/cond/branch_1_fun/ppermute | solution.py:1219
  600.6 31.9 %conditional.12 = (bf16[4,128,1024]{2,1,0:T(8,128)(2,1)}, f32[256,8192]{1,0:T(8,128)}, bf16[256,2048]{1,0:T(8,128)(2,1)}, f32[8,2304]{1,0:T(8,128)S(1)}) conditional(s32[]{:T(128)} %bitcast.22, () %tuple.162, (bf16[8,128,1024]{2,1,0:T(8,128)(2,1)}, bf16[256,2048]{1,0:T(8,128)(2,1)}, bf16[256,2048]{1,0:T(8,128)(2,1)}, s32[4]{0:T(128)S(1)}, ...), branch_computations={%region_31.32_spmd, %region_32.34_spmd} | conditional | flops 2664452 | bytes 33979596 | solution.py:303
  617.0 10.7 %collective-permute-done.17 = f32[8,2304]{1,0:T(8,128)S(1)} collective-permute-done((f32[8,2304]{1,0:T(8,128)S(1)}, f32[8,2304]{1,0:T(8,128)S(1)}, u32[]{:S(2)}, u32[]{:S(2)}) %collective-permute-start.17) | collective-permute-done | bytes 73760 | tf_op jit(solution)/shard_map/cond/branch_1_fun/ppermute | solution.py:1250
  632.6 29.1 %conditional.13 = (f32[256,6144]{1,0:T(8,128)}, f32[1024,2048]{1,0:T(8,128)}, f32[4,2304]{1,0:T(4,128)S(1)}) conditional(s32[]{:T(128)} %bitcast.22, () %tuple.161, (bf16[256,1536]{1,0:T(8,128)(2,1)}, f32[8,2304]{1,0:T(8,128)S(1)}, s32[]{:T(128)}, bf16[256,2048]{1,0:T(8,128)(2,1)S(1)}, bf16[256,2048]{1,0:T(8,128)(2,1)}, ...), branch_computations={%region_34.35_spmd, %region_35.36_spmd} | conditional | flops 9223 | bytes 36498960 | solution.py:303
  644.0 8.9 %collective-permute-done.7.refs_2_ = bf16[256,1536]{1,0:T(8,128)(2,1)} collective-permute-done((bf16[256,1536]{1,0:T(8,128)(2,1)}, bf16[256,1536]{1,0:T(8,128)(2,1)}, u32[]{:S(2)}, u32[]{:S(2)}) %collective-permute-start.7) | collective-permute-done | bytes 786464 | tf_op jit(solution)/shard_map/cond/branch_1_fun/ppermute | solution.py:1264
  (359 shorter events, 284.1 us)
Async XLA Ops:
  7.2 71.0 %all-gather.14.cloned.1.call-start = ((), (), s32[]{:S(2)}) async-start(), calls=%async_computation.9 | async-start | bytes 3932160 | tf_op jit(solution)/shard_map/all_gather | solution.py:293
  11.8 101.2 %all-gather.20.cloned.1.call-start = ((), (), s32[]{:S(2)}) async-start(), calls=%async_computation.12 | async-start | bytes 1310720 | tf_op jit(solution)/shard_map/all_gather | solution.py:293
  44.7 125.4 %all-gather.16.cloned.1.call-start = ((), (), s32[]{:S(2)}) async-start(), calls=%async_computation.10 | async-start | bytes 2621440 | tf_op jit(solution)/shard_map/all_gather | solution.py:293
  45.4 155.3 %all-gather.18.cloned.1.call-start = ((), (), s32[]{:S(2)}) async-start(), calls=%async_computation.11 | async-start | bytes 2621440 | tf_op jit(solution)/shard_map/all_gather | solution.py:1039
  46.0 223.5 %all-gather.22.cloned.1.call-start = ((), (), s32[]{:S(2)}) async-start(), calls=%async_computation.13 | async-start | bytes 2621440 | tf_op jit(solution)/shard_map/all_gather | solution.py:293
  47.6 32.2 %collective-permute-start.31 = (bf16[256,2048]{1,0:T(8,128)(2,1)}, bf16[256,2048]{1,0:T(8,128)(2,1)S(1)}, u32[]{:S(2)}, u32[]{:S(2)}) collective-permute-start(bf16[256,2048]{1,0:T(8,128)(2,1)} %add_convert_fusion.3), channel_id=1, source_target_pairs={{0,1},{1,0},{2,3},{3,2},{4,5},{5,4},{6,7},{7,6},{8,9},{9,8},{10,11... | collective-permute-start | bytes 3145736 | tf_op jit(solution)/shard_map/ppermute | solution.py:327
  78.2 255.3 %all-gather.12.cloned.1.call-start = ((), (), s32[]{:S(2)}) async-start(), calls=%async_computation.4 | async-start | bytes 5242880 | tf_op jit(solution)/shard_map/all_gather | solution.py:1041
  78.3 70.9 %collective-permute-start.37 = (bf16[4,256,1536]{2,1,0:T(8,128)(2,1)}, bf16[4,256,1536]{2,1,0:T(8,128)(2,1)}, u32[]{:S(2)}, u32[]{:S(2)}) collective-permute-start(bf16[4,256,1536]{2,1,0:T(8,128)(2,1)} %bitcast.120), channel_id=1, source_target_pairs={{0,4},{4,0},{1,5},{5,1},{2,6},{6,2},{3,7},{7,3},{8,12},{12,8},{9,1... | collective-permute-start | bytes 9437192 | tf_op jit(solution)/shard_map/ppermute | solution.py:294
  85.3 25.2 %collective-permute-start.35 = (bf16[256,2048]{1,0:T(8,128)(2,1)S(1)}, bf16[256,2048]{1,0:T(8,128)(2,1)S(1)}, u32[]{:S(2)}, u32[]{:S(2)}) collective-permute-start(bf16[256,2048]{1,0:T(8,128)(2,1)S(1)} %bitcast.143), channel_id=1, source_target_pairs={{0,2},{2,0},{1,3},{3,1},{4,6},{6,4},{5,7},{7,5},{8,10},{10,8},{9,1... | collective-permute-start | bytes 3145736 | tf_op jit(solution)/shard_map/ppermute | solution.py:323
  86.8 63.9 %collective-permute-start.34 = (bf16[256,2048]{1,0:T(8,128)(2,1)S(1)}, bf16[256,2048]{1,0:T(8,128)(2,1)}, u32[]{:S(2)}, u32[]{:S(2)}) collective-permute-start(bf16[256,2048]{1,0:T(8,128)(2,1)S(1)} %bitcast.144), channel_id=1, source_target_pairs={{0,1},{1,0},{2,3},{3,2},{4,5},{5,4},{6,7},{7,6},{8,9},{9,8},{10,11... | collective-permute-start | bytes 3145736 | tf_op jit(solution)/shard_map/ppermute | solution.py:327
  110.5 40.1 %collective-permute-start.36 = (bf16[256,2048]{1,0:T(8,128)(2,1)S(1)}, bf16[256,2048]{1,0:T(8,128)(2,1)}, u32[]{:S(2)}, u32[]{:S(2)}) collective-permute-start(bf16[256,2048]{1,0:T(8,128)(2,1)S(1)} %collective-permute-done.35), channel_id=1, source_target_pairs={{0,1},{1,0},{2,3},{3,2},{4,5},{5,4},{6,7},{7,6},{8,9},{9,8},{10,11... | collective-permute-start | bytes 3145736 | tf_op jit(solution)/shard_map/ppermute | solution.py:327
  112.9 376.6 %reduce-scatter.5.cloned.1.call-start = ((), (), s32[]{:S(2)}) async-start(), calls=%async_computation.5 | async-start | bytes 10485760 | tf_op jit(solution)/shard_map/reduce_scatter | solution.py:1099
  113.0 90.3 %collective-permute-start.39 = (bf16[4,128,1024]{2,1,0:T(8,128)(2,1)}, bf16[4,128,1024]{2,1,0:T(8,128)(2,1)}, u32[]{:S(2)}, u32[]{:S(2)}) collective-permute-start(bf16[4,128,1024]{2,1,0:T(8,128)(2,1)} %bitcast.136), channel_id=1, source_target_pairs={{0,2},{2,0},{1,3},{3,1},{4,6},{6,4},{5,7},{7,5},{8,10},{10,8},{9,1... | collective-permute-start | bytes 3145736 | tf_op jit(solution)/shard_map/ppermute | solution.py:960
  149.2 32.8 %collective-permute-start.38 = (bf16[4,128,1024]{2,1,0:T(8,128)(2,1)}, bf16[4,128,1024]{2,1,0:T(8,128)(2,1)}, u32[]{:S(2)}, u32[]{:S(2)}) collective-permute-start(bf16[4,128,1024]{2,1,0:T(8,128)(2,1)} %bitcast.137), channel_id=1, source_target_pairs={{0,4},{4,0},{1,5},{5,1},{2,6},{6,2},{3,7},{7,3},{8,12},{12,8},{9,1... | collective-permute-start | bytes 3145736 | tf_op jit(solution)/shard_map/ppermute | solution.py:294
  170.1 75.0 %collective-permute-start.43 = (bf16[4,256,1024]{2,1,0:T(8,128)(2,1)}, bf16[4,256,1024]{2,1,0:T(8,128)(2,1)}, u32[]{:S(2)}, u32[]{:S(2)}) collective-permute-start(bf16[4,256,1024]{2,1,0:T(8,128)(2,1)} %bitcast.123), channel_id=1, source_target_pairs={{0,4},{4,0},{1,5},{5,1},{2,6},{6,2},{3,7},{7,3},{8,12},{12,8},{9,1... | collective-permute-start | bytes 6291464 | tf_op jit(solution)/shard_map/ppermute | solution.py:294
  200.7 63.5 %collective-permute-start.44 = (bf16[4,256,1024]{2,1,0:T(8,128)(2,1)}, bf16[4,256,1024]{2,1,0:T(8,128)(2,1)}, u32[]{:S(2)}, u32[]{:S(2)}) collective-permute-start(bf16[4,256,1024]{2,1,0:T(8,128)(2,1)} %bitcast.126), channel_id=1, source_target_pairs={{0,4},{4,0},{1,5},{5,1},{2,6},{6,2},{3,7},{7,3},{8,12},{12,8},{9,1... | collective-permute-start | bytes 6291464 | tf_op jit(solution)/shard_map/ppermute | solution.py:1075
  242.9 25.9 %collective-permute-start.42 = (bf16[256,2048]{1,0:T(8,128)(2,1)}, bf16[256,2048]{1,0:T(8,128)(2,1)}, u32[]{:S(2)}, u32[]{:S(2)}) collective-permute-start(bf16[256,2048]{1,0:T(8,128)(2,1)} %get-tuple-element.318), channel_id=1, source_target_pairs={{0,2},{2,0},{1,3},{3,1},{4,6},{6,4},{5,7},{7,5},{8,10},{10,8},{9,1... | collective-permute-start | bytes 3145736 | tf_op jit(solution)/shard_map/ppermute | solution.py:323
  245.1 25.8 %collective-permute-start.41 = (bf16[256,2048]{1,0:T(8,128)(2,1)}, bf16[256,2048]{1,0:T(8,128)(2,1)}, u32[]{:S(2)}, u32[]{:S(2)}) collective-permute-start(bf16[256,2048]{1,0:T(8,128)(2,1)} %get-tuple-element.318), channel_id=1, source_target_pairs={{0,1},{1,0},{2,3},{3,2},{4,5},{5,4},{6,7},{7,6},{8,9},{9,8},{10,11... | collective-permute-start | bytes 3145736 | tf_op jit(solution)/shard_map/ppermute | solution.py:327
  269.5 48.4 %collective-permute-start.46 = (bf16[4,256,1024]{2,1,0:T(8,128)(2,1)}, bf16[4,256,1024]{2,1,0:T(8,128)(2,1)}, u32[]{:S(2)}, u32[]{:S(2)}) collective-permute-start(bf16[4,256,1024]{2,1,0:T(8,128)(2,1)} %bitcast.131), channel_id=1, source_target_pairs={{0,4},{4,0},{1,5},{5,1},{2,6},{6,2},{3,7},{7,3},{8,12},{12,8},{9,1... | collective-permute-start | bytes 6291464 | tf_op jit(solution)/shard_map/ppermute | solution.py:294
  332.6 230.4 %reduce-scatter.7.cloned.1.call-start = ((), (), s32[]{:S(2)}) async-start(), calls=%async_computation.6 | async-start | bytes 5242880 | tf_op jit(solution)/shard_map/reduce_scatter | solution.py:1019
  360.5 118.9 %collective-permute-start.49 = (bf16[4,256,2048]{2,1,0:T(8,128)(2,1)}, bf16[4,256,2048]{2,1,0:T(8,128)(2,1)}, u32[]{:S(2)}, u32[]{:S(2)}) collective-permute-start(bf16[4,256,2048]{2,1,0:T(8,128)(2,1)} %shard_map.245), channel_id=1, source_target_pairs={{0,4},{4,0},{1,5},{5,1},{2,6},{6,2},{3,7},{7,3},{8,12},{12,8},{9,1... | collective-permute-start | bytes 12582920 | tf_op jit(solution)/shard_map/ppermute | solution.py:1011
  388.2 25.4 %collective-permute-start.21 = (bf16[256,2048]{1,0:T(8,128)(2,1)}, bf16[256,2048]{1,0:T(8,128)(2,1)S(1)}, u32[]{:S(2)}, u32[]{:S(2)}) collective-permute-start(bf16[256,2048]{1,0:T(8,128)(2,1)} %get-tuple-element.145), channel_id=1, source_target_pairs={{0,2},{2,0},{1,3},{3,1},{4,6},{6,4},{5,7},{7,5},{8,10},{10,8},{9,1... | collective-permute-start | bytes 3145736 | tf_op jit(solution)/shard_map/cond/branch_1_fun/ppermute | solution.py:1119
  453.4 25.9 %collective-permute-start.48 = (bf16[512,1024]{1,0:T(8,128)(2,1)}, bf16[512,1024]{1,0:T(8,128)(2,1)}, u32[]{:S(2)}, u32[]{:S(2)}) collective-permute-start(bf16[512,1024]{1,0:T(8,128)(2,1)} %get-tuple-element.345), channel_id=1, source_target_pairs={{0,2},{2,0},{1,3},{3,1},{4,6},{6,4},{5,7},{7,5},{8,10},{10,8},{9,1... | collective-permute-start | bytes 3145736 | tf_op jit(solution)/shard_map/ppermute | solution.py:1166
  489.5 143.0 %reduce-scatter.9.cloned.1.call-start = ((), (), s32[]{:S(2)}) async-start(), calls=%async_computation.7 | async-start | bytes 3932160 | tf_op jit(solution)/shard_map/reduce_scatter | solution.py:1019
  489.6 73.4 %collective-permute-start.51 = (bf16[4,256,1536]{2,1,0:T(8,128)(2,1)}, bf16[4,256,1536]{2,1,0:T(8,128)(2,1)}, u32[]{:S(2)}, u32[]{:S(2)}) collective-permute-start(bf16[4,256,1536]{2,1,0:T(8,128)(2,1)} %shard_map.248), channel_id=1, source_target_pairs={{0,4},{4,0},{1,5},{5,1},{2,6},{6,2},{3,7},{7,3},{8,12},{12,8},{9,1... | collective-permute-start | bytes 9437192 | tf_op jit(solution)/shard_map/ppermute | solution.py:1011
  490.3 25.5 %collective-permute-start.50 = (bf16[256,2048]{1,0:T(8,128)(2,1)}, bf16[256,2048]{1,0:T(8,128)(2,1)}, u32[]{:S(2)}, u32[]{:S(2)}) collective-permute-start(bf16[256,2048]{1,0:T(8,128)(2,1)} %get-tuple-element.351), channel_id=1, source_target_pairs={{0,2},{2,0},{1,3},{3,1},{4,6},{6,4},{5,7},{7,5},{8,10},{10,8},{9,1... | collective-permute-start | bytes 3145736 | tf_op jit(solution)/shard_map/ppermute | solution.py:1199
  525.5 25.4 %collective-permute-start.3 = (bf16[256,2048]{1,0:T(8,128)(2,1)}, bf16[256,2048]{1,0:T(8,128)(2,1)S(1)}, u32[]{:S(2)}, u32[]{:S(2)}) collective-permute-start(bf16[256,2048]{1,0:T(8,128)(2,1)} %get-tuple-element.176), channel_id=1, source_target_pairs={{0,2},{2,0},{1,3},{3,1},{4,6},{6,4},{5,7},{7,5},{8,10},{10,8},{9,1... | collective-permute-start | bytes 3145736 | tf_op jit(solution)/shard_map/cond/branch_1_fun/ppermute | solution.py:1203
  571.7 90.9 %reduce-scatter.11.cloned.1.call-start = ((), (), s32[]{:S(2)}) async-start(), calls=%async_computation.8 | async-start | bytes 1310720 | tf_op jit(solution)/shard_map/reduce_scatter | solution.py:1019
  573.3 25.0 %collective-permute-start.4 = (bf16[256,2048]{1,0:T(8,128)(2,1)S(1)}, bf16[256,2048]{1,0:T(8,128)(2,1)S(1)}, u32[]{:S(2)}, u32[]{:S(2)}) collective-permute-start(bf16[256,2048]{1,0:T(8,128)(2,1)S(1)} %slice_bitcast_fusion.1), channel_id=1, source_target_pairs={{0,4},{4,0},{1,5},{5,1},{2,6},{6,2},{3,7},{7,3},{8,12},{12,8},{9,1... | collective-permute-start | bytes 3145736 | tf_op jit(solution)/shard_map/cond/branch_1_fun/ppermute | solution.py:1219
  574.8 24.8 %collective-permute-start.5 = (bf16[256,2048]{1,0:T(8,128)(2,1)S(1)}, bf16[256,2048]{1,0:T(8,128)(2,1)}, u32[]{:S(2)}, u32[]{:S(2)}) collective-permute-start(bf16[256,2048]{1,0:T(8,128)(2,1)S(1)} %copy-done.19), channel_id=1, source_target_pairs={{0,2},{2,0},{1,3},{3,1},{4,6},{6,4},{5,7},{7,5},{8,10},{10,8},{9,1... | collective-permute-start | bytes 3145736 | tf_op jit(solution)/shard_map/cond/branch_1_fun/ppermute | solution.py:1218
  601.1 26.7 %collective-permute-start.15 = (bf16[256,2048]{1,0:T(8,128)(2,1)S(1)}, bf16[256,2048]{1,0:T(8,128)(2,1)}, u32[]{:S(2)}, u32[]{:S(2)}) collective-permute-start(bf16[256,2048]{1,0:T(8,128)(2,1)S(1)} %get-tuple-element.189), channel_id=1, source_target_pairs={{0,2},{2,0},{1,3},{3,1},{4,6},{6,4},{5,7},{7,5},{8,10},{10,8},{9,1... | collective-permute-start | bytes 3145736 | tf_op jit(solution)/shard_map/cond/branch_1_fun/ppermute | solution.py:1251
  604.8 25.1 %collective-permute-start.12 = (bf16[4,128,1024]{2,1,0:T(8,128)(2,1)}, bf16[4,128,1024]{2,1,0:T(8,128)(2,1)}, u32[]{:S(2)}, u32[]{:S(2)}) collective-permute-start(bf16[4,128,1024]{2,1,0:T(8,128)(2,1)} %slice.41), channel_id=1, source_target_pairs={{0,4},{4,0},{1,5},{5,1},{2,6},{6,2},{3,7},{7,3},{8,12},{12,8},{9,1... | collective-permute-start | bytes 3145736 | tf_op jit(solution)/shard_map/cond/branch_1_fun/ppermute | solution.py:1252
  (76 other events, 700.7 us)
Sparse Core Ops, SparseCore 0:
  12.0 66.1 all-gather.13
  80.3 26.5 all-gather.19
  109.1 45.4 all-gather.15
  156.0 44.6 all-gather.17
  202.1 44.6 all-gather.21
  248.8 79.4 all-gather.11
  332.8 143.3 reduce-scatter.4
  489.7 73.3 reduce-scatter.6
  571.8 60.7 reduce-scatter.8
  635.4 27.1 reduce-scatter.10

commit v7 on v6

--- a/solution.py
+++ b/solution.py
@@ -344,7 +344,7 @@
     away, home = parts
     other = lax.ppermute(away, "c", SWAP)
     tokens, model = home.shape[0] // 2, home.shape[1]
-    steps = 4
+    steps = 2
     block = (tokens // steps, model)
 
     def kernel(at_ref, *refs):

time: 694 us -> 693 us (level)
  no operation moved by 1% of the time
where the time goes in v7:
time: 693 us; the launch traced here: 683 us
  waiting for transfers between devices  278 us (40%)
  Pallas kernels  240 us (35%)
  other arithmetic  69.2 us (10%)
  starting transfers between devices  54.3 us (8%)
  local copies, waits for them, and re-layouts  25.4 us (4%)
  between operations  15.2 us (2%)
    pallas_call x8, Pallas kernels, weight_matmul(): pl.pallas_call(kernel, grid_spec=pltpu.PrefetchScalarGridSpec(num_scalar_...  110 us
    pallas_call x6, Pallas kernels, weight_grad(): pl.pallas_call(kernel, grid_spec=pltpu.PrefetchScalarGridSpec(num_scalar_...  59.9 us
    ppermute x4, waiting for transfers between devices, seq_pieces(): return core_pieces(block, after(lax.ppermute(block, 'y', SWAP), *others))  50.1 us
    ppermute x4, waiting for transfers between devices, gather_weight(): return [near, lax.ppermute(after(near, *others), 'x', SWAP)]  37.9 us
    ppermute x1, waiting for transfers between devices, norm_one_back(): away = lax.ppermute(away, 'y', SWAP)  23.7 us
    pallas_call x4, Pallas kernels, widen(): pl.pallas_call(kernel, grid_spec=pltpu.PrefetchScalarGridSpec(num_scalar_...  22.6 us
    ppermute x1, waiting for transfers between devices, split_shards(): up_parts += [up_high, lax.ppermute(after(up_high, mixed_heads), 'x', SWAP)]  19.1 us
    ppermute x1, waiting for transfers between devices, ends(): down_far = lax.ppermute(down_pair[1], 'x', SWAP)  18.2 us
  transfers between devices with their start and end apart: 68, of which 37 were waited for; matrix products, arithmetic and copies ran while one was open for 13% of the time, Pallas kernels for 33%

profile of v7, /device:TPU:0, one launch (start us, length us, event | category | flops | bytes accessed | tf_op | source)
XLA Modules:
  0.0 683.3 jit_solution(4586767584807489904)
XLA Ops:
  30.8 8.9 %collective-permute-done.30 = f32[2304]{0:T(1024)S(1)} collective-permute-done((f32[2304]{0:T(1024)S(1)}, f32[2304]{0:T(1024)S(1)}, u32[]{:S(2)}, u32[]{:S(2)}) %collective-permute-start.30) | collective-permute-done | bytes 9248 | tf_op jit(solution)/shard_map/ppermute | solution.py:289
  47.6 21.6 %collective-permute-done.32 = bf16[256,2048]{1,0:T(8,128)(2,1)S(1)} collective-permute-done((bf16[256,2048]{1,0:T(8,128)(2,1)}, bf16[256,2048]{1,0:T(8,128)(2,1)S(1)}, u32[]{:S(2)}, u32[]{:S(2)}) %collective-permute-start.32) | collective-permute-done | bytes 1048608 | tf_op jit(solution)/shard_map/ppermute | solution.py:323
  69.2 8.9 %all-gather.14.cloned.1.call-done = bf16[1024,1536]{1,0:T(8,128)(2,1)} async-done(((bf16[256,1536]{1,0:T(8,128)(2,1)}), bf16[1024,1536]{1,0:T(8,128)(2,1)}) %all-gather.14.cloned.1.call-update) | async-done | bytes 3145744 | tf_op jit(solution)/shard_map/all_gather | solution.py:293
  86.8 23.7 %collective-permute-done.35 = bf16[256,2048]{1,0:T(8,128)(2,1)S(1)} collective-permute-done((bf16[256,2048]{1,0:T(8,128)(2,1)S(1)}, bf16[256,2048]{1,0:T(8,128)(2,1)S(1)}, u32[]{:S(2)}, u32[]{:S(2)}) %collective-permute-start.35) | collective-permute-done | bytes 1048608 | tf_op jit(solution)/shard_map/ppermute | solution.py:323
  114.5 34.6 %collective-permute-done.37.refs_3_.refs_4_ = bf16[4,256,1536]{2,1,0:T(8,128)(2,1)} collective-permute-done((bf16[4,256,1536]{2,1,0:T(8,128)(2,1)}, bf16[4,256,1536]{2,1,0:T(8,128)(2,1)}, u32[]{:S(2)}, u32[]{:S(2)}) %collective-permute-start.37) | collective-permute-done | bytes 3145760 | tf_op jit(solution)/shard_map/ppermute | solution.py:294
  156.1 13.9 %shard_map.240.q_ref.k_ref.v_ref = bf16[1024,1536]{1,0:T(8,128)(2,1)} custom-call(s32[2,8]{1,0:T(2,128)} %stack.343.refs_0_, bf16[1024,2048]{1,0:T(8,128)(2,1)} %pad_maximum_fusion.3.refs_1_.left_ref, bf16[4,256,1536]{2,1,0:T(8,128)(2,1)} %bitcast.121, bf16[4,256,1536]{2,1,0:T(8,128)(2,1)} %collective-permute-done.37.refs_3_.refs_4_), custom_call_target="tpu_custom_call" | custom-call | flops 64424508 | bytes 136314 | tf_op jit(solution)/shard_map/pallas_call | solution.py:482
  170.6 11.4 %shard_map.241 = (bf16[1024,512]{1,0:T(8,128)(2,1)}, f32[4,1024,1]{2,1,0:T(8,128)}) custom-call(bf16[1024,1536]{1,0:T(8,128)(2,1)} %shard_map.240.q_ref.k_ref.v_ref, bf16[1024,1536]{1,0:T(8,128)(2,1)} %shard_map.240.q_ref.k_ref.v_ref, bf16[1024,1536]{1,0:T(8,128)(2,1)} %shard_map.240.q_ref.k_ref.v_ref, s32[1024,1]{1,0:T(8,128)} %copy.39.qi_ref, ...), custom_call_target="tpu_custom_call" | custom-call | flops 21474836 | bytes 41943 | tf_op jit(solution)/shard_map/pallas_call | solution.py:689
  183.5 17.2 %all-gather.18.cloned.1.call-done = bf16[1024,1024]{1,0:T(8,128)(2,1)} async-done(((bf16[256,1024]{1,0:T(8,128)(2,1)}), bf16[1024,1024]{1,0:T(8,128)(2,1)}) %all-gather.18.cloned.1.call-update) | async-done | bytes 2097168 | tf_op jit(solution)/shard_map/all_gather | solution.py:1039
  206.6 36.3 %conditional.7 = (bf16[256,2048]{1,0:T(8,128)(2,1)}, f32[256,2048]{1,0:T(8,128)}, bf16[512,512]{1,0:T(8,128)(2,1)S(1)}, bf16[512,512]{1,0:T(8,128)(2,1)S(1)}) conditional(s32[]{:T(128)} %bitcast.22, () %tuple.123, (s32[]{:T(128)}, bf16[1024,512]{1,0:T(8,128)(2,1)}, s32[2,16]{1,0:T(2,128)S(1)}, bf16[4,128,1024]{2,1,0:T(8,128)(2,1)}, ...), branch_computations={%region_4.5_spmd, %region_5.8_spmd} | conditional | flops 30912284 | bytes 39470188 | solution.py:303
  209.7 10.6 %collective-permute-done.18 = bf16[512,512]{1,0:T(8,128)(2,1)S(1)} collective-permute-done((bf16[512,512]{1,0:T(8,128)(2,1)S(1)}, bf16[512,512]{1,0:T(8,128)(2,1)S(1)}, u32[]{:S(2)}, u32[]{:S(2)}) %collective-permute-start.18) | collective-permute-done | bytes 524320 | tf_op jit(solution)/shard_map/cond/branch_1_fun/ppermute | solution.py:1054
  245.1 19.1 %collective-permute-done.44.refs_5_.refs_6_ = bf16[4,256,1024]{2,1,0:T(8,128)(2,1)} collective-permute-done((bf16[4,256,1024]{2,1,0:T(8,128)(2,1)}, bf16[4,256,1024]{2,1,0:T(8,128)(2,1)}, u32[]{:S(2)}, u32[]{:S(2)}) %collective-permute-start.44) | collective-permute-done | bytes 2097184 | tf_op jit(solution)/shard_map/ppermute | solution.py:1075
  276.7 20.7 %shard_map.242 = (bf16[1024,2048]{1,0:T(8,128)(2,1)}, f32[1024,2048]{1,0:T(8,128)}) custom-call(s32[2,16]{1,0:T(2,128)} %get-tuple-element.446.refs_0_, bf16[1024,2048]{1,0:T(8,128)(2,1)} %pad_maximum_fusion.5.refs_1_.left_ref, bf16[4,256,1024]{2,1,0:T(8,128)(2,1)} %bitcast.124, bf16[4,256,1024]{2,1,0:T(8,128)(2,1)} %collective-permute-done.43.refs_3_.refs_4_, ...), custom_call_target="tpu_custom_call" | custom-call | flops 85899344 | bytes 251740 | tf_op jit(solution)/shard_map/pallas_call | solution.py:482
  299.8 11.7 %collective-permute-done.47 = bf16[512,512]{1,0:T(8,128)(2,1)} collective-permute-done((bf16[512,512]{1,0:T(8,128)(2,1)S(1)}, bf16[512,512]{1,0:T(8,128)(2,1)}, u32[]{:S(2)}, u32[]{:S(2)}) %collective-permute-start.47) | collective-permute-done | bytes 524320 | tf_op jit(solution)/shard_map/ppermute | solution.py:1091
  317.8 14.8 %shard_map.243 = bf16[8,256,2048]{2,1,0:T(8,128)(2,1)} custom-call(s32[9]{0:T(128)} %stack.340.where_ref, bf16[1024,2048]{1,0:T(8,128)(2,1)S(1)} %copy-done.3, bf16[1024,2048]{1,0:T(8,128)(2,1)} %pad_maximum_fusion.4.right_ref.refs_1_), custom_call_target="tpu_custom_call" | custom-call | flops 85899344 | bytes 251658 | tf_op jit(solution)/shard_map/pallas_call | solution.py:546
  333.5 17.5 %shard_map.244 = (bf16[1024,2048]{1,0:T(8,128)(2,1)}, f32[1,2048]{1,0:T(1,128)S(1)}) custom-call(s32[2,16]{1,0:T(2,128)S(1)} %get-tuple-element.445.refs_0_, bf16[1024,2048]{1,0:T(8,128)(2,1)} %pad_maximum_fusion.4.right_ref.refs_1_, bf16[4,256,1024]{2,1,0:T(8,128)(2,1)} %bitcast.132, bf16[4,256,1024]{2,1,0:T(8,128)(2,1)} %collective-permute-done.46.refs_3_, ...), custom_call_target="tpu_custom_call" | custom-call | flops 85899344 | bytes 251740 | tf_op jit(solution)/shard_map/pallas_call | solution.py:482
  351.0 9.4 %shard_map.245 = bf16[4,256,2048]{2,1,0:T(8,128)(2,1)} custom-call(s32[5]{0:T(128)} %stack.344.where_ref, bf16[1024,2048]{1,0:T(8,128)(2,1)} %pad_maximum_fusion.5.refs_1_.left_ref, bf16[1024,2048]{1,0:T(8,128)(2,1)} %get-tuple-element.335.right_ref.refs_2_), custom_call_target="tpu_custom_call" | custom-call | flops 42949672 | bytes 146800 | tf_op jit(solution)/shard_map/pallas_call | solution.py:546
  362.6 15.8 %shard_map.246 = (bf16[512,2048]{1,0:T(8,128)(2,1)}, bf16[512,2048]{1,0:T(8,128)(2,1)S(1)}) custom-call(s32[2,16]{1,0:T(2,128)} %get-tuple-element.446.refs_0_, s32[4]{0:T(128)} %pad_add_fusion.4.refs_1_, bf16[1024,2048]{1,0:T(8,128)(2,1)} %get-tuple-element.335.right_ref.refs_2_, bf16[4,256,1024]{2,1,0:T(8,128)(2,1)} %bitcast.125, ...), custom_call_target="tpu_custom_call" | custom-call | flops 85899344 | bytes 167772 | tf_op jit(solution)/shard_map/pallas_call | solution.py:482
  378.5 47.2 %conditional.8 = (bf16[512,2048]{1,0:T(8,128)(2,1)}, f32[256,2048]{1,0:T(8,128)}, f32[2048]{0:T(1024)S(1)}, f32[2048]{0:T(1024)S(1)}, bf16[512,2048]{1,0:T(8,128)(2,1)}, /*index=5*/bf16[512,2048]{1,0:T(8,128)(2,1)}) conditional(s32[]{:T(128)} %bitcast.22, () %tuple.118, (s32[]{:T(128)}, s32[]{:T(128)}, bf16[512,2048]{1,0:T(8,128)(2,1)}, ...), branch_computations={%region_8.9_spmd, %region_9.16_spmd} | conditional | flops 104769888 | bytes 83110976 | solution.py:303
  393.5 15.5 %branch_1_fun.11 = (bf16[512,2048]{1,0:T(8,128)(2,1)}, bf16[512,2048]{1,0:T(8,128)(2,1)}) custom-call(s32[2,16]{1,0:T(2,128)S(1)} %get-tuple-element.146.refs_0_, s32[4]{0:T(128)} %pad_add_fusion.refs_1_, bf16[1024,2048]{1,0:T(8,128)(2,1)} %get-tuple-element.148.refs_2_, bf16[4,256,1024]{2,1,0:T(8,128)(2,1)S(1)} %copy-done.9, ...), custom_call_target="tpu_custom_call" | custom-call | flops 85899344 | bytes 167772 | tf_op jit(solution)/shard_map/cond/branch_1_fun/pallas_call | solution.py:482
  425.7 26.7 %conditional.9 = (bf16[1024,512]{1,0:T(8,128)(2,1)}, f32[256,2048]{1,0:T(8,128)}, bf16[256,2048]{1,0:T(8,128)(2,1)}, bf16[512,1024]{1,0:T(8,128)(2,1)}, bf16[512,1024]{1,0:T(8,128)(2,1)S(1)}) conditional(s32[]{:T(128)} %bitcast.22, () %tuple.117, (s32[]{:T(128)}, s32[2,16]{1,0:T(2,128)S(1)}, bf16[512,2048]{1,0:T(8,128)(2,1)}, ...), branch_computations={%region_16.17_spmd, %region_17.18_spmd} | conditional | flops 24096276 | bytes 24227716 | solution.py:303
  454.7 15.6 %shard_map.247.right_ref.refs_2_ = bf16[1024,1536]{1,0:T(8,128)(2,1)} custom-call(bf16[1024,1536]{1,0:T(8,128)(2,1)} %shard_map.240.q_ref.k_ref.v_ref, bf16[1024,1536]{1,0:T(8,128)(2,1)} %shard_map.240.q_ref.k_ref.v_ref, bf16[1024,1536]{1,0:T(8,128)(2,1)} %shard_map.240.q_ref.k_ref.v_ref, bf16[1024,512]{1,0:T(8,128)(2,1)} %get-tuple-element.347.g_ref, ...), custom_call_target="tpu_custom_call" | custom-call | flops 53687092 | bytes 83886 | tf_op jit(solution)/shard_map/pallas_call | solution.py:758
  478.4 10.1 %shard_map.249 = bf16[4,256,2048]{2,1,0:T(8,128)(2,1)} custom-call(s32[5]{0:T(128)} %stack.345.where_ref, bf16[1024,2048]{1,0:T(8,128)(2,1)} %pad_maximum_fusion.5.refs_1_.left_ref, bf16[1024,2048]{1,0:T(8,128)(2,1)} %get-tuple-element.335.right_ref.refs_2_, bf16[4,256,2048]{2,1,0:T(8,128)(2,1)} %collective-permute-done.49.refs_0_), custom_call_target="tpu_custom_call" | custom-call | flops 42949672 | bytes 146800 | tf_op jit(solution)/shard_map/pallas_call | solution.py:546
  493.7 12.3 %shard_map.250 = (bf16[512,2048]{1,0:T(8,128)(2,1)}, bf16[512,2048]{1,0:T(8,128)(2,1)S(1)}) custom-call(s32[2,8]{1,0:T(2,128)} %stack.343.refs_0_, s32[4]{0:T(128)} %pad_add_fusion.4.refs_1_, bf16[1024,1536]{1,0:T(8,128)(2,1)} %shard_map.247.right_ref.refs_2_, bf16[4,256,1536]{2,1,0:T(8,128)(2,1)} %bitcast.122, ...), custom_call_target="tpu_custom_call" | custom-call | flops 64424508 | bytes 136314 | tf_op jit(solution)/shard_map/pallas_call | solution.py:482
  505.9 8.8 %shard_map.251 = bf16[8,128,1024]{2,1,0:T(8,128)(2,1)} custom-call(s32[9]{0:T(128)} %stack.346.where_ref, bf16[1024,1024]{1,0:T(8,128)(2,1)} %pad_maximum_fusion.6.left_ref, bf16[1024,1024]{1,0:T(8,128)(2,1)} %pad_maximum_fusion.7.right_ref), custom_call_target="tpu_custom_call" | custom-call | flops 21474836 | bytes 83886 | tf_op jit(solution)/shard_map/pallas_call | solution.py:546
  514.8 39.4 %conditional.10 = (f32[1,256,2048]{2,1,0:T(8,128)}, f32[2048]{0:T(1024)S(1)}, f32[2048]{0:T(1024)S(1)}) conditional(s32[]{:T(128)} %bitcast.22, () %tuple.152, (s32[]{:T(128)}, bf16[512,2048]{1,0:T(8,128)(2,1)}, bf16[512,2048]{1,0:T(8,128)(2,1)S(1)}, f32[8,256]{1,0:T(8,128)S(1)}, f32[256,2048]{1,0:T(8,128)S(1)}, ...), branch_computations={%region_20.21_spmd, %region_21.28_spmd} | conditional | flops 13103360 | bytes 48339968 | solution.py:303
  525.2 23.7 %collective-permute-done.3 = bf16[256,2048]{1,0:T(8,128)(2,1)S(1)} collective-permute-done((bf16[256,2048]{1,0:T(8,128)(2,1)}, bf16[256,2048]{1,0:T(8,128)(2,1)S(1)}, u32[]{:S(2)}, u32[]{:S(2)}) %collective-permute-start.3) | collective-permute-done | bytes 1048608 | tf_op jit(solution)/shard_map/cond/branch_1_fun/ppermute | solution.py:1203
  570.9 27.8 %conditional.11 = (bf16[1,256,2048]{2,1,0:T(8,128)(2,1)S(1)}, bf16[256,2048]{1,0:T(8,128)(2,1)S(1)}, bf16[256,2048]{1,0:T(8,128)(2,1)}) conditional(s32[]{:T(128)} %bitcast.22, () %tuple.116, (bf16[256,2048]{1,0:T(8,128)(2,1)}, f32[256,2048]{1,0:T(8,128)}, f32[256,2048]{1,0:T(8,128)}, f32[8,2304]{1,0:T(8,128)S(1)}, ...), branch_computations={%region_28.29_spmd, %region_29.30_spmd} | conditional | flops 4718592 | bytes 32546976 | solution.py:303
  579.2 18.2 %collective-permute-done.4 = bf16[256,2048]{1,0:T(8,128)(2,1)S(1)} collective-permute-done((bf16[256,2048]{1,0:T(8,128)(2,1)S(1)}, bf16[256,2048]{1,0:T(8,128)(2,1)S(1)}, u32[]{:S(2)}, u32[]{:S(2)}) %collective-permute-start.4) | collective-permute-done | bytes 1048608 | tf_op jit(solution)/shard_map/cond/branch_1_fun/ppermute | solution.py:1219
  599.7 31.9 %conditional.12 = (bf16[4,128,1024]{2,1,0:T(8,128)(2,1)}, f32[256,8192]{1,0:T(8,128)}, bf16[256,2048]{1,0:T(8,128)(2,1)}, f32[8,2304]{1,0:T(8,128)S(1)}) conditional(s32[]{:T(128)} %bitcast.22, () %tuple.162, (bf16[8,128,1024]{2,1,0:T(8,128)(2,1)}, bf16[256,2048]{1,0:T(8,128)(2,1)}, bf16[256,2048]{1,0:T(8,128)(2,1)}, s32[4]{0:T(128)S(1)}, ...), branch_computations={%region_31.32_spmd, %region_32.34_spmd} | conditional | flops 2664452 | bytes 33979596 | solution.py:303
  616.2 10.7 %collective-permute-done.17 = f32[8,2304]{1,0:T(8,128)S(1)} collective-permute-done((f32[8,2304]{1,0:T(8,128)S(1)}, f32[8,2304]{1,0:T(8,128)S(1)}, u32[]{:S(2)}, u32[]{:S(2)}) %collective-permute-start.17) | collective-permute-done | bytes 73760 | tf_op jit(solution)/shard_map/cond/branch_1_fun/ppermute | solution.py:1250
  631.7 29.0 %conditional.13 = (f32[256,6144]{1,0:T(8,128)}, f32[1024,2048]{1,0:T(8,128)}, f32[4,2304]{1,0:T(4,128)S(1)}) conditional(s32[]{:T(128)} %bitcast.22, () %tuple.161, (bf16[256,1536]{1,0:T(8,128)(2,1)}, f32[8,2304]{1,0:T(8,128)S(1)}, s32[]{:T(128)}, bf16[256,2048]{1,0:T(8,128)(2,1)S(1)}, bf16[256,2048]{1,0:T(8,128)(2,1)}, ...), branch_computations={%region_34.35_spmd, %region_35.36_spmd} | conditional | flops 9223 | bytes 36498960 | solution.py:303
  643.2 8.9 %collective-permute-done.7.refs_2_ = bf16[256,1536]{1,0:T(8,128)(2,1)} collective-permute-done((bf16[256,1536]{1,0:T(8,128)(2,1)}, bf16[256,1536]{1,0:T(8,128)(2,1)}, u32[]{:S(2)}, u32[]{:S(2)}) %collective-permute-start.7) | collective-permute-done | bytes 786464 | tf_op jit(solution)/shard_map/cond/branch_1_fun/ppermute | solution.py:1264
  (359 shorter events, 283.1 us)
Async XLA Ops:
  7.2 71.0 %all-gather.14.cloned.1.call-start = ((), (), s32[]{:S(2)}) async-start(), calls=%async_computation.9 | async-start | bytes 3932160 | tf_op jit(solution)/shard_map/all_gather | solution.py:293
  11.8 101.2 %all-gather.20.cloned.1.call-start = ((), (), s32[]{:S(2)}) async-start(), calls=%async_computation.12 | async-start | bytes 1310720 | tf_op jit(solution)/shard_map/all_gather | solution.py:293
  44.7 125.4 %all-gather.16.cloned.1.call-start = ((), (), s32[]{:S(2)}) async-start(), calls=%async_computation.10 | async-start | bytes 2621440 | tf_op jit(solution)/shard_map/all_gather | solution.py:293
  45.4 155.3 %all-gather.18.cloned.1.call-start = ((), (), s32[]{:S(2)}) async-start(), calls=%async_computation.11 | async-start | bytes 2621440 | tf_op jit(solution)/shard_map/all_gather | solution.py:1039
  46.0 223.5 %all-gather.22.cloned.1.call-start = ((), (), s32[]{:S(2)}) async-start(), calls=%async_computation.13 | async-start | bytes 2621440 | tf_op jit(solution)/shard_map/all_gather | solution.py:293
  47.6 32.2 %collective-permute-start.31 = (bf16[256,2048]{1,0:T(8,128)(2,1)}, bf16[256,2048]{1,0:T(8,128)(2,1)S(1)}, u32[]{:S(2)}, u32[]{:S(2)}) collective-permute-start(bf16[256,2048]{1,0:T(8,128)(2,1)} %add_convert_fusion.3), channel_id=1, source_target_pairs={{0,1},{1,0},{2,3},{3,2},{4,5},{5,4},{6,7},{7,6},{8,9},{9,8},{10,11... | collective-permute-start | bytes 3145736 | tf_op jit(solution)/shard_map/ppermute | solution.py:327
  78.2 255.3 %all-gather.12.cloned.1.call-start = ((), (), s32[]{:S(2)}) async-start(), calls=%async_computation.4 | async-start | bytes 5242880 | tf_op jit(solution)/shard_map/all_gather | solution.py:1041
  78.3 70.9 %collective-permute-start.37 = (bf16[4,256,1536]{2,1,0:T(8,128)(2,1)}, bf16[4,256,1536]{2,1,0:T(8,128)(2,1)}, u32[]{:S(2)}, u32[]{:S(2)}) collective-permute-start(bf16[4,256,1536]{2,1,0:T(8,128)(2,1)} %bitcast.120), channel_id=1, source_target_pairs={{0,4},{4,0},{1,5},{5,1},{2,6},{6,2},{3,7},{7,3},{8,12},{12,8},{9,1... | collective-permute-start | bytes 9437192 | tf_op jit(solution)/shard_map/ppermute | solution.py:294
  85.3 25.2 %collective-permute-start.35 = (bf16[256,2048]{1,0:T(8,128)(2,1)S(1)}, bf16[256,2048]{1,0:T(8,128)(2,1)S(1)}, u32[]{:S(2)}, u32[]{:S(2)}) collective-permute-start(bf16[256,2048]{1,0:T(8,128)(2,1)S(1)} %bitcast.143), channel_id=1, source_target_pairs={{0,2},{2,0},{1,3},{3,1},{4,6},{6,4},{5,7},{7,5},{8,10},{10,8},{9,1... | collective-permute-start | bytes 3145736 | tf_op jit(solution)/shard_map/ppermute | solution.py:323
  86.8 63.9 %collective-permute-start.34 = (bf16[256,2048]{1,0:T(8,128)(2,1)S(1)}, bf16[256,2048]{1,0:T(8,128)(2,1)}, u32[]{:S(2)}, u32[]{:S(2)}) collective-permute-start(bf16[256,2048]{1,0:T(8,128)(2,1)S(1)} %bitcast.144), channel_id=1, source_target_pairs={{0,1},{1,0},{2,3},{3,2},{4,5},{5,4},{6,7},{7,6},{8,9},{9,8},{10,11... | collective-permute-start | bytes 3145736 | tf_op jit(solution)/shard_map/ppermute | solution.py:327
  110.5 40.1 %collective-permute-start.36 = (bf16[256,2048]{1,0:T(8,128)(2,1)S(1)}, bf16[256,2048]{1,0:T(8,128)(2,1)}, u32[]{:S(2)}, u32[]{:S(2)}) collective-permute-start(bf16[256,2048]{1,0:T(8,128)(2,1)S(1)} %collective-permute-done.35), channel_id=1, source_target_pairs={{0,1},{1,0},{2,3},{3,2},{4,5},{5,4},{6,7},{7,6},{8,9},{9,8},{10,11... | collective-permute-start | bytes 3145736 | tf_op jit(solution)/shard_map/ppermute | solution.py:327
  112.9 375.6 %reduce-scatter.5.cloned.1.call-start = ((), (), s32[]{:S(2)}) async-start(), calls=%async_computation.5 | async-start | bytes 10485760 | tf_op jit(solution)/shard_map/reduce_scatter | solution.py:1099
  113.0 90.3 %collective-permute-start.39 = (bf16[4,128,1024]{2,1,0:T(8,128)(2,1)}, bf16[4,128,1024]{2,1,0:T(8,128)(2,1)}, u32[]{:S(2)}, u32[]{:S(2)}) collective-permute-start(bf16[4,128,1024]{2,1,0:T(8,128)(2,1)} %bitcast.136), channel_id=1, source_target_pairs={{0,2},{2,0},{1,3},{3,1},{4,6},{6,4},{5,7},{7,5},{8,10},{10,8},{9,1... | collective-permute-start | bytes 3145736 | tf_op jit(solution)/shard_map/ppermute | solution.py:960
  149.2 32.8 %collective-permute-start.38 = (bf16[4,128,1024]{2,1,0:T(8,128)(2,1)}, bf16[4,128,1024]{2,1,0:T(8,128)(2,1)}, u32[]{:S(2)}, u32[]{:S(2)}) collective-permute-start(bf16[4,128,1024]{2,1,0:T(8,128)(2,1)} %bitcast.137), channel_id=1, source_target_pairs={{0,4},{4,0},{1,5},{5,1},{2,6},{6,2},{3,7},{7,3},{8,12},{12,8},{9,1... | collective-permute-start | bytes 3145736 | tf_op jit(solution)/shard_map/ppermute | solution.py:294
  170.1 75.0 %collective-permute-start.43 = (bf16[4,256,1024]{2,1,0:T(8,128)(2,1)}, bf16[4,256,1024]{2,1,0:T(8,128)(2,1)}, u32[]{:S(2)}, u32[]{:S(2)}) collective-permute-start(bf16[4,256,1024]{2,1,0:T(8,128)(2,1)} %bitcast.123), channel_id=1, source_target_pairs={{0,4},{4,0},{1,5},{5,1},{2,6},{6,2},{3,7},{7,3},{8,12},{12,8},{9,1... | collective-permute-start | bytes 6291464 | tf_op jit(solution)/shard_map/ppermute | solution.py:294
  200.7 63.5 %collective-permute-start.44 = (bf16[4,256,1024]{2,1,0:T(8,128)(2,1)}, bf16[4,256,1024]{2,1,0:T(8,128)(2,1)}, u32[]{:S(2)}, u32[]{:S(2)}) collective-permute-start(bf16[4,256,1024]{2,1,0:T(8,128)(2,1)} %bitcast.126), channel_id=1, source_target_pairs={{0,4},{4,0},{1,5},{5,1},{2,6},{6,2},{3,7},{7,3},{8,12},{12,8},{9,1... | collective-permute-start | bytes 6291464 | tf_op jit(solution)/shard_map/ppermute | solution.py:1075
  242.9 25.9 %collective-permute-start.42 = (bf16[256,2048]{1,0:T(8,128)(2,1)}, bf16[256,2048]{1,0:T(8,128)(2,1)}, u32[]{:S(2)}, u32[]{:S(2)}) collective-permute-start(bf16[256,2048]{1,0:T(8,128)(2,1)} %get-tuple-element.318), channel_id=1, source_target_pairs={{0,2},{2,0},{1,3},{3,1},{4,6},{6,4},{5,7},{7,5},{8,10},{10,8},{9,1... | collective-permute-start | bytes 3145736 | tf_op jit(solution)/shard_map/ppermute | solution.py:323
  245.1 25.8 %collective-permute-start.41 = (bf16[256,2048]{1,0:T(8,128)(2,1)}, bf16[256,2048]{1,0:T(8,128)(2,1)}, u32[]{:S(2)}, u32[]{:S(2)}) collective-permute-start(bf16[256,2048]{1,0:T(8,128)(2,1)} %get-tuple-element.318), channel_id=1, source_target_pairs={{0,1},{1,0},{2,3},{3,2},{4,5},{5,4},{6,7},{7,6},{8,9},{9,8},{10,11... | collective-permute-start | bytes 3145736 | tf_op jit(solution)/shard_map/ppermute | solution.py:327
  269.5 48.4 %collective-permute-start.46 = (bf16[4,256,1024]{2,1,0:T(8,128)(2,1)}, bf16[4,256,1024]{2,1,0:T(8,128)(2,1)}, u32[]{:S(2)}, u32[]{:S(2)}) collective-permute-start(bf16[4,256,1024]{2,1,0:T(8,128)(2,1)} %bitcast.131), channel_id=1, source_target_pairs={{0,4},{4,0},{1,5},{5,1},{2,6},{6,2},{3,7},{7,3},{8,12},{12,8},{9,1... | collective-permute-start | bytes 6291464 | tf_op jit(solution)/shard_map/ppermute | solution.py:294
  332.6 229.5 %reduce-scatter.7.cloned.1.call-start = ((), (), s32[]{:S(2)}) async-start(), calls=%async_computation.6 | async-start | bytes 5242880 | tf_op jit(solution)/shard_map/reduce_scatter | solution.py:1019
  360.5 117.9 %collective-permute-start.49 = (bf16[4,256,2048]{2,1,0:T(8,128)(2,1)}, bf16[4,256,2048]{2,1,0:T(8,128)(2,1)}, u32[]{:S(2)}, u32[]{:S(2)}) collective-permute-start(bf16[4,256,2048]{2,1,0:T(8,128)(2,1)} %shard_map.245), channel_id=1, source_target_pairs={{0,4},{4,0},{1,5},{5,1},{2,6},{6,2},{3,7},{7,3},{8,12},{12,8},{9,1... | collective-permute-start | bytes 12582920 | tf_op jit(solution)/shard_map/ppermute | solution.py:1011
  387.2 25.4 %collective-permute-start.21 = (bf16[256,2048]{1,0:T(8,128)(2,1)}, bf16[256,2048]{1,0:T(8,128)(2,1)S(1)}, u32[]{:S(2)}, u32[]{:S(2)}) collective-permute-start(bf16[256,2048]{1,0:T(8,128)(2,1)} %get-tuple-element.145), channel_id=1, source_target_pairs={{0,2},{2,0},{1,3},{3,1},{4,6},{6,4},{5,7},{7,5},{8,10},{10,8},{9,1... | collective-permute-start | bytes 3145736 | tf_op jit(solution)/shard_map/cond/branch_1_fun/ppermute | solution.py:1119
  452.4 26.0 %collective-permute-start.48 = (bf16[512,1024]{1,0:T(8,128)(2,1)}, bf16[512,1024]{1,0:T(8,128)(2,1)}, u32[]{:S(2)}, u32[]{:S(2)}) collective-permute-start(bf16[512,1024]{1,0:T(8,128)(2,1)} %get-tuple-element.345), channel_id=1, source_target_pairs={{0,2},{2,0},{1,3},{3,1},{4,6},{6,4},{5,7},{7,5},{8,10},{10,8},{9,1... | collective-permute-start | bytes 3145736 | tf_op jit(solution)/shard_map/ppermute | solution.py:1166
  488.6 143.1 %reduce-scatter.9.cloned.1.call-start = ((), (), s32[]{:S(2)}) async-start(), calls=%async_computation.7 | async-start | bytes 3932160 | tf_op jit(solution)/shard_map/reduce_scatter | solution.py:1019
  488.6 73.5 %collective-permute-start.51 = (bf16[4,256,1536]{2,1,0:T(8,128)(2,1)}, bf16[4,256,1536]{2,1,0:T(8,128)(2,1)}, u32[]{:S(2)}, u32[]{:S(2)}) collective-permute-start(bf16[4,256,1536]{2,1,0:T(8,128)(2,1)} %shard_map.248), channel_id=1, source_target_pairs={{0,4},{4,0},{1,5},{5,1},{2,6},{6,2},{3,7},{7,3},{8,12},{12,8},{9,1... | collective-permute-start | bytes 9437192 | tf_op jit(solution)/shard_map/ppermute | solution.py:1011
  489.3 25.5 %collective-permute-start.50 = (bf16[256,2048]{1,0:T(8,128)(2,1)}, bf16[256,2048]{1,0:T(8,128)(2,1)}, u32[]{:S(2)}, u32[]{:S(2)}) collective-permute-start(bf16[256,2048]{1,0:T(8,128)(2,1)} %get-tuple-element.351), channel_id=1, source_target_pairs={{0,2},{2,0},{1,3},{3,1},{4,6},{6,4},{5,7},{7,5},{8,10},{10,8},{9,1... | collective-permute-start | bytes 3145736 | tf_op jit(solution)/shard_map/ppermute | solution.py:1199
  523.4 25.4 %collective-permute-start.3 = (bf16[256,2048]{1,0:T(8,128)(2,1)}, bf16[256,2048]{1,0:T(8,128)(2,1)S(1)}, u32[]{:S(2)}, u32[]{:S(2)}) collective-permute-start(bf16[256,2048]{1,0:T(8,128)(2,1)} %get-tuple-element.176), channel_id=1, source_target_pairs={{0,2},{2,0},{1,3},{3,1},{4,6},{6,4},{5,7},{7,5},{8,10},{10,8},{9,1... | collective-permute-start | bytes 3145736 | tf_op jit(solution)/shard_map/cond/branch_1_fun/ppermute | solution.py:1203
  570.8 90.9 %reduce-scatter.11.cloned.1.call-start = ((), (), s32[]{:S(2)}) async-start(), calls=%async_computation.8 | async-start | bytes 1310720 | tf_op jit(solution)/shard_map/reduce_scatter | solution.py:1019
  572.4 25.0 %collective-permute-start.4 = (bf16[256,2048]{1,0:T(8,128)(2,1)S(1)}, bf16[256,2048]{1,0:T(8,128)(2,1)S(1)}, u32[]{:S(2)}, u32[]{:S(2)}) collective-permute-start(bf16[256,2048]{1,0:T(8,128)(2,1)S(1)} %slice_bitcast_fusion.1), channel_id=1, source_target_pairs={{0,4},{4,0},{1,5},{5,1},{2,6},{6,2},{3,7},{7,3},{8,12},{12,8},{9,1... | collective-permute-start | bytes 3145736 | tf_op jit(solution)/shard_map/cond/branch_1_fun/ppermute | solution.py:1219
  574.0 24.8 %collective-permute-start.5 = (bf16[256,2048]{1,0:T(8,128)(2,1)S(1)}, bf16[256,2048]{1,0:T(8,128)(2,1)}, u32[]{:S(2)}, u32[]{:S(2)}) collective-permute-start(bf16[256,2048]{1,0:T(8,128)(2,1)S(1)} %copy-done.19), channel_id=1, source_target_pairs={{0,2},{2,0},{1,3},{3,1},{4,6},{6,4},{5,7},{7,5},{8,10},{10,8},{9,1... | collective-permute-start | bytes 3145736 | tf_op jit(solution)/shard_map/cond/branch_1_fun/ppermute | solution.py:1218
  600.2 26.7 %collective-permute-start.15 = (bf16[256,2048]{1,0:T(8,128)(2,1)S(1)}, bf16[256,2048]{1,0:T(8,128)(2,1)}, u32[]{:S(2)}, u32[]{:S(2)}) collective-permute-start(bf16[256,2048]{1,0:T(8,128)(2,1)S(1)} %get-tuple-element.189), channel_id=1, source_target_pairs={{0,2},{2,0},{1,3},{3,1},{4,6},{6,4},{5,7},{7,5},{8,10},{10,8},{9,1... | collective-permute-start | bytes 3145736 | tf_op jit(solution)/shard_map/cond/branch_1_fun/ppermute | solution.py:1251
  603.9 25.1 %collective-permute-start.12 = (bf16[4,128,1024]{2,1,0:T(8,128)(2,1)}, bf16[4,128,1024]{2,1,0:T(8,128)(2,1)}, u32[]{:S(2)}, u32[]{:S(2)}) collective-permute-start(bf16[4,128,1024]{2,1,0:T(8,128)(2,1)} %slice.41), channel_id=1, source_target_pairs={{0,4},{4,0},{1,5},{5,1},{2,6},{6,2},{3,7},{7,3},{8,12},{12,8},{9,1... | collective-permute-start | bytes 3145736 | tf_op jit(solution)/shard_map/cond/branch_1_fun/ppermute | solution.py:1252
  (76 other events, 700.7 us)
Sparse Core Ops, SparseCore 0:
  12.0 66.1 all-gather.13
  80.3 26.5 all-gather.19
  109.1 45.4 all-gather.15
  156.0 44.6 all-gather.17
  202.1 44.6 all-gather.21
  248.8 79.4 all-gather.11
  332.8 143.3 reduce-scatter.4
  488.7 73.4 reduce-scatter.6
  570.9 60.7 reduce-scatter.8
  634.5 27.1 reduce-scatter.10
